TPU v7x, 32 devices: a whole 2x2x4 slice. The times are simulated.
32 devices in a mesh: dp: 8 (over y, x, core), layer: 4 (over z).
Axes of the slice: x: 2, y: 2, z: 4, core: 2. Of those that a mesh axis runs over, the one named last changes fastest.
Arguments:
- history: bfloat16 [16, 4096, 2048], P('layer', 'dp'), may hold values from -6 to 6
- mix_weights: float32 [4, 16, 4096], P(None, 'layer', 'dp'), may hold values from -1.5 to 1.5
- segments: int32 [8, 512], P('dp'), may hold values from 0 to 1, never falling along the last dimension, each value on 1 to 511 neighbouring positions
- w_query: float32 [2048, 2048], P('dp', 'layer'), may hold values from -0.125 to 0.125
- w_key: float32 [2048, 2048], P('dp', 'layer'), may hold values from -0.125 to 0.125
- w_value: float32 [2048, 2048], P('dp', 'layer'), may hold values from -0.125 to 0.125
- w_output: float32 [2048, 2048], P('layer', 'dp'), may hold values from -1 to 1
- w_up: float32 [2048, 8192], P('dp', 'layer'), may hold values from -0.125 to 0.125
- w_down: float32 [8192, 2048], P('layer', 'dp'), may hold values from -0.0625 to 0.0625
- norm_gains: float32 [5, 2048], replicated, may hold values from 0.5 to 1.5
- w_first: float32 [2048, 68], replicated, may hold values from -0.125 to 0.125
- w_second: float32 [68, 68], replicated, may hold values from -0.75 to 0.75
- out_cotangent: float32 [4096, 2048], P(('dp', 'layer')), may hold values from -6 to 6
- mix_cotangent: float32 [4096, 68], P(('dp', 'layer')), may hold values from -6 to 6
Outputs:
- block_out: bfloat16 [4096, 2048], P(('dp', 'layer'))
- next_mix: float32 [4096, 68], P(('dp', 'layer'))
- history_grad: bfloat16 [16, 4096, 2048], P('layer', 'dp')
- mix_grad: float32 [4, 16, 4096], P(None, 'layer', 'dp')
- query_grad: float32 [2048, 2048], P('dp', 'layer')
- key_grad: float32 [2048, 2048], P('dp', 'layer')
- value_grad: float32 [2048, 2048], P('dp', 'layer')
- output_grad: float32 [2048, 2048], P('layer', 'dp')
- up_grad: float32 [2048, 8192], P('dp', 'layer')
- down_grad: float32 [8192, 2048], P('layer', 'dp')
- gains_grad: float32 [5, 2048], replicated
- first_grad: float32 [2048, 68], replicated
- second_grad: float32 [68, 68], replicated
Inputs may be any that keep to these rules, and one draw needn't show every extreme that they name: `segments`: ids never fall along a data row; each of the 2 documents of a row is nonempty and holds at most 511 tokens.
All inputs are finite; a program needn't handle non-finite values.
Results may differ from a plain program's by a relative error of at most 0.02.
Values may be sent and summed in bfloat16 or wider, within the bound.
No kernel may reach another device: no remote copies, remote signals or barrier semaphores. Data moves between devices by JAX's collectives and lax.ppermute only.
A program may use at most 192 MiB of HBM per device.

v0:
```python
import math

import jax
import jax.numpy as jnp
from jax import lax
from jax.sharding import PartitionSpec as P

HEAD_DIM = 128
DOCS = 2


highest = lax.Precision.HIGHEST
epsilon = 1e-05


def layer_norm(values, gain_vec):
    centre = values - jnp.mean(values, axis=-1, keepdims=True)
    spread = jnp.mean(centre * centre, axis=-1, keepdims=True)
    return centre * lax.rsqrt(spread + epsilon) * gain_vec


def rms_norm(values, gain_vec):
    square = jnp.mean(values * values, axis=-1, keepdims=True)
    return values * lax.rsqrt(square + epsilon) * gain_vec


def gelu_exact(values):
    return jax.nn.gelu(values, approximate=False)


def doc_angles(seg_row, head_dim, doc_count):
    length = seg_row.shape[0]
    labels = jnp.arange(doc_count, dtype=jnp.int32)
    before = jnp.sum((seg_row[None, :] < labels[:, None]).astype(jnp.int32), axis=1)
    member = (seg_row[:, None] == labels[None, :]).astype(jnp.int32)
    begins = jnp.sum(member * before[None, :], axis=1)
    places = (jnp.arange(length, dtype=jnp.int32) - begins).astype(jnp.float32)
    half_dim = head_dim // 2
    frequency = jnp.exp(
        jnp.arange(half_dim, dtype=jnp.float32) * (-2.0 * math.log(10000.0) / head_dim)
    )
    angles = places[:, None] * frequency[None, :]
    return (jnp.cos(angles)[:, None, :], jnp.sin(angles)[:, None, :])


def rotate(values, cosine, sine):
    half_dim = values.shape[-1] // 2
    first_half = values[..., :half_dim]
    second_half = values[..., half_dim:]
    return jnp.concatenate(
        (first_half * cosine - second_half * sine, second_half * cosine + first_half * sine),
        axis=-1,
    )


def allowed_pairs(seg_row):
    places = jnp.arange(seg_row.shape[0], dtype=jnp.int32)
    return (seg_row[:, None] == seg_row[None, :]) & (places[:, None] >= places[None, :])


def mixer(out_rows, gain_vec, first_matrix, second_matrix):
    hidden = gelu_exact(jnp.dot(rms_norm(out_rows, gain_vec), first_matrix, precision=highest))
    return jnp.dot(hidden, second_matrix, precision=highest)


def plain_dot(left, right):
    return jnp.dot(left, right, preferred_element_type=jnp.float32)


def dot_left_t(left, right):
    return lax.dot_general(
        left, right, (((0,), (0,)), ((), ())), preferred_element_type=jnp.float32
    )


def dot_right_t(left, right):
    return lax.dot_general(
        left, right, (((1,), (1,)), ((), ())), preferred_element_type=jnp.float32
    )


def local(
    history,
    mix_weights,
    segments,
    w_query,
    w_key,
    w_value,
    w_output,
    w_up,
    w_down,
    norm_gains,
    w_first,
    w_second,
    out_cotangent,
    mix_cotangent,
):
    row_tok = history.shape[1]
    head_dim = HEAD_DIM
    scale = head_dim ** (-0.5)
    hist_rows = history.astype(jnp.float32)
    streams = lax.psum_scatter(
        jnp.einsum("sjt,jtd->tsd", mix_weights, hist_rows, precision=highest),
        "layer",
        scatter_dimension=0,
        tiled=True,
    )
    query_low = w_query.astype(jnp.bfloat16)
    key_low = w_key.astype(jnp.bfloat16)
    value_low = w_value.astype(jnp.bfloat16)
    output_low = w_output.astype(jnp.bfloat16)
    up_low = w_up.astype(jnp.bfloat16)
    down_low = w_down.astype(jnp.bfloat16)
    full_query, full_key, full_value, full_output, full_up, full_down = (
        lax.all_gather(query_low, "dp", axis=0, tiled=True),
        lax.all_gather(key_low, "dp", axis=0, tiled=True),
        lax.all_gather(value_low, "dp", axis=0, tiled=True),
        lax.all_gather(output_low, "dp", axis=1, tiled=True),
        lax.all_gather(up_low, "dp", axis=0, tiled=True),
        lax.all_gather(down_low, "dp", axis=1, tiled=True),
    )
    query_norm, query_pull = jax.vjp(layer_norm, streams[:, 0], norm_gains[0])
    key_norm, key_pull = jax.vjp(layer_norm, streams[:, 1], norm_gains[1])
    value_norm, value_pull = jax.vjp(layer_norm, streams[:, 2], norm_gains[2])
    normed = jnp.stack((query_norm, key_norm, value_norm), axis=1).astype(jnp.bfloat16)
    normed_rows = lax.all_gather(normed, "layer", axis=0, tiled=True)
    query_rows = normed_rows[:, 0]
    key_rows = normed_rows[:, 1]
    value_rows = normed_rows[:, 2]
    seg_row = segments[0]
    cosine, sine = doc_angles(seg_row, head_dim, DOCS)
    allowed = allowed_pairs(seg_row)
    local_heads = full_query.shape[1] // head_dim
    query_lin = plain_dot(query_rows, full_query)
    key_lin = plain_dot(key_rows, full_key)
    value_lin = plain_dot(value_rows, full_value).astype(jnp.bfloat16)
    queries = (
        rotate(query_lin.reshape(row_tok, local_heads, head_dim), cosine, sine)
        .astype(jnp.bfloat16)
        .transpose(1, 0, 2)
    )
    keys = (
        rotate(key_lin.reshape(row_tok, local_heads, head_dim), cosine, sine)
        .astype(jnp.bfloat16)
        .transpose(1, 0, 2)
    )
    value_heads = value_lin.reshape(row_tok, local_heads, head_dim).transpose(1, 0, 2)

    def head_scores(head_query, head_key):
        return jnp.where(allowed, dot_right_t(head_query, head_key) * scale, -1e30)

    def head_forward(operands):
        head_query, head_key, head_value = operands
        scores = head_scores(head_query, head_key)
        row_max = jnp.max(scores, axis=1, keepdims=True)
        shifted = jnp.exp(scores - row_max)
        row_sum = jnp.sum(shifted, axis=1, keepdims=True)
        probs = (shifted / row_sum).astype(jnp.bfloat16)
        return (plain_dot(probs, head_value), (row_max + jnp.log(row_sum))[:, 0])

    head_context, log_totals = lax.map(head_forward, (queries, keys, value_heads))
    context = (
        head_context.transpose(1, 0, 2)
        .reshape(row_tok, local_heads * head_dim)
        .astype(jnp.bfloat16)
    )
    attn_branch = lax.psum_scatter(
        plain_dot(context, full_output).astype(jnp.bfloat16),
        "layer",
        scatter_dimension=0,
        tiled=True,
    ).astype(jnp.float32)
    hidden_in = streams[:, 3] + attn_branch
    mlp_norm, mlp_pull = jax.vjp(layer_norm, hidden_in, norm_gains[3])
    mlp_rows = lax.all_gather(mlp_norm.astype(jnp.bfloat16), "layer", axis=0, tiled=True)
    up_proj = plain_dot(mlp_rows, full_up)
    active, gelu_pull = jax.vjp(gelu_exact, up_proj)
    active = active.astype(jnp.bfloat16)
    mlp_branch = lax.psum_scatter(
        plain_dot(active, full_down).astype(jnp.bfloat16), "layer", scatter_dimension=0, tiled=True
    ).astype(jnp.float32)
    block = hidden_in + mlp_branch
    next_mix, mixer_pull = jax.vjp(mixer, block, norm_gains[4], w_first, w_second)
    block_part, mixer_gain_grad, first_grad, second_grad = mixer_pull(mix_cotangent)
    block_grad = out_cotangent + block_part
    branch_rows = lax.all_gather(block_grad.astype(jnp.bfloat16), "layer", axis=0, tiled=True)
    back_query, back_key, back_value, back_output, back_up, back_down = (
        lax.all_gather(query_low, "dp", axis=0, tiled=True),
        lax.all_gather(key_low, "dp", axis=0, tiled=True),
        lax.all_gather(value_low, "dp", axis=0, tiled=True),
        lax.all_gather(output_low, "dp", axis=1, tiled=True),
        lax.all_gather(up_low, "dp", axis=0, tiled=True),
        lax.all_gather(down_low, "dp", axis=1, tiled=True),
    )
    active_grad = dot_right_t(branch_rows, back_down)
    down_grad = dot_left_t(active, branch_rows)
    up_grad_rows = gelu_pull(active_grad)[0].astype(jnp.bfloat16)
    up_grad = dot_left_t(mlp_rows, up_grad_rows)
    mlp_norm_grad = lax.psum_scatter(
        dot_right_t(up_grad_rows, back_up).astype(jnp.bfloat16),
        "layer",
        scatter_dimension=0,
        tiled=True,
    ).astype(jnp.float32)
    hidden_part, mlp_gain_grad = mlp_pull(mlp_norm_grad)
    hidden_grad = block_grad + hidden_part
    hidden_rows = lax.all_gather(hidden_grad.astype(jnp.bfloat16), "layer", axis=0, tiled=True)
    context_grad = dot_right_t(hidden_rows, back_output).astype(jnp.bfloat16)
    output_grad = dot_left_t(context, hidden_rows)
    context_heads = context_grad.reshape(row_tok, local_heads, head_dim).transpose(1, 0, 2)

    def head_backward(operands):
        head_query, head_key, head_value, head_lse, head_grad = operands
        probs = jnp.exp(head_scores(head_query, head_key) - head_lse[:, None])
        prob_grad = dot_right_t(head_grad, head_value)
        value_part = dot_left_t(probs.astype(jnp.bfloat16), head_grad)
        centre = jnp.sum(probs * prob_grad, axis=1, keepdims=True)
        score_grad = (probs * (prob_grad - centre)).astype(jnp.bfloat16)
        query_part = plain_dot(score_grad, head_key) * scale
        key_part = dot_left_t(score_grad, head_query) * scale
        return (query_part, key_part, value_part)

    query_heads, key_heads, value_parts = lax.map(
        head_backward, (queries, keys, value_heads, log_totals, context_heads)
    )

    def unrotate(head_grads):
        turned = rotate(head_grads.transpose(1, 0, 2), cosine, -sine)
        return turned.reshape(row_tok, local_heads * head_dim).astype(jnp.bfloat16)

    query_lin_grad = unrotate(query_heads)
    key_lin_grad = unrotate(key_heads)
    value_lin_grad = (
        value_parts.transpose(1, 0, 2).reshape(row_tok, local_heads * head_dim).astype(jnp.bfloat16)
    )
    query_grad = dot_left_t(query_rows, query_lin_grad)
    key_grad = dot_left_t(key_rows, key_lin_grad)
    value_grad = dot_left_t(value_rows, value_lin_grad)
    normed_grad = lax.psum_scatter(
        jnp.stack(
            (
                dot_right_t(query_lin_grad, back_query),
                dot_right_t(key_lin_grad, back_key),
                dot_right_t(value_lin_grad, back_value),
            ),
            axis=1,
        ).astype(jnp.bfloat16),
        "layer",
        scatter_dimension=0,
        tiled=True,
    ).astype(jnp.float32)
    query_in_grad, query_gain_grad = query_pull(normed_grad[:, 0])
    key_in_grad, key_gain_grad = key_pull(normed_grad[:, 1])
    value_in_grad, value_gain_grad = value_pull(normed_grad[:, 2])
    stream_grads = jnp.stack((query_in_grad, key_in_grad, value_in_grad), axis=1).astype(
        jnp.bfloat16
    )
    stream_rows = lax.all_gather(stream_grads, "layer", axis=0, tiled=True)
    streams_low = jnp.concatenate((stream_rows, hidden_rows[:, None, :]), axis=1)
    streams_wide = streams_low.astype(jnp.float32)
    history_grad = jnp.einsum("sjt,tsd->jtd", mix_weights, streams_wide, precision=highest).astype(
        jnp.bfloat16
    )
    mix_grad = jnp.einsum("jtd,tsd->sjt", history, streams_low, preferred_element_type=jnp.float32)
    query_sum, key_sum, value_sum, output_sum, up_sum, down_sum = (
        lax.psum_scatter(
            query_grad.astype(jnp.bfloat16), "dp", scatter_dimension=0, tiled=True
        ).astype(jnp.float32),
        lax.psum_scatter(
            key_grad.astype(jnp.bfloat16), "dp", scatter_dimension=0, tiled=True
        ).astype(jnp.float32),
        lax.psum_scatter(
            value_grad.astype(jnp.bfloat16), "dp", scatter_dimension=0, tiled=True
        ).astype(jnp.float32),
        lax.psum_scatter(
            output_grad.astype(jnp.bfloat16), "dp", scatter_dimension=1, tiled=True
        ).astype(jnp.float32),
        lax.psum_scatter(
            up_grad.astype(jnp.bfloat16), "dp", scatter_dimension=0, tiled=True
        ).astype(jnp.float32),
        lax.psum_scatter(
            down_grad.astype(jnp.bfloat16), "dp", scatter_dimension=1, tiled=True
        ).astype(jnp.float32),
    )
    gain_grads = jnp.stack(
        (query_gain_grad, key_gain_grad, value_gain_grad, mlp_gain_grad, mixer_gain_grad)
    )
    gains_sum, first_sum, second_sum = lax.psum(
        (gain_grads, first_grad, second_grad), ("dp", "layer")
    )
    return (
        block.astype(jnp.bfloat16),
        next_mix,
        history_grad,
        mix_grad,
        query_sum,
        key_sum,
        value_sum,
        output_sum,
        up_sum,
        down_sum,
        gains_sum,
        first_sum,
        second_sum,
    )


def solution(mesh):
    placed = (
        P("layer", "dp", None),
        P(None, "layer", "dp"),
        P("dp", None),
        P("dp", "layer"),
        P("dp", "layer"),
        P("dp", "layer"),
        P("layer", "dp"),
        P("dp", "layer"),
        P("layer", "dp"),
        P(),
        P(),
        P(),
        P(("dp", "layer"), None),
        P(("dp", "layer"), None),
    )
    return jax.shard_map(
        local,
        mesh=mesh,
        in_specs=placed,
        out_specs=(
            P(("dp", "layer"), None),
            P(("dp", "layer"), None),
            P("layer", "dp", None),
            P(None, "layer", "dp"),
            P("dp", "layer"),
            P("dp", "layer"),
            P("dp", "layer"),
            P("layer", "dp"),
            P("dp", "layer"),
            P("layer", "dp"),
            P(),
            P(),
            P(),
        ),
        check_vma=False,
    )
```

profile of v0, /device:TPU:0, one launch (start us, length us, event | category | flops | bytes accessed | tf_op | source)
XLA Modules:
  0.0 1786.7 jit_solution(6419638943154939091)
XLA Ops:
  9.3 35.2 %fusion.51 = f32[512,4,2048]{2,1,0:T(4,128)} fusion(f32[4,4,512]{0,1,2:T(4,128)S(1)} %copy.116, bf16[4,512,2048]{2,1,0:T(8,128)(2,1)} %param.18), kind=kOutput, calls=%fused_computation.69 | convolution fusion | flops 201326592 | bytes 25198592 | tf_op jit(solution)/shard_map/sjt,jtd->tsd/dot_general | solution.py:103
  48.6 561.1 %all-reduce.7.cloned.1.call-done = f32[512,4,2048]{2,1,0:T(4,128)} async-done(((f32[512,4,2048]{2,1,0:T(4,128)}), f32[512,4,2048]{2,1,0:T(4,128)}) %all-reduce.7.cloned.1.call-update) | async-done | bytes 16777232
  609.6 10.9 fusion.136
  630.0 4.1 copy.103
  634.1 4.0 copy.104
  638.1 101.0 %all-gather.12.cloned.1.call-done = bf16[512,3,2048]{2,0,1:T(8,128)(2,1)} async-done(((bf16[128,3,2048]{2,0,1:T(8,128)(2,1)}), bf16[512,3,2048]{2,0,1:T(8,128)(2,1)}) %all-gather.12.cloned.1.call-update) | async-done | bytes 6291472 | tf_op jit(solution)/shard_map/all_gather | solution.py:126
  739.1 3.7 fusion.65
  742.8 2.9 fusion.62
  747.2 20.3 %all-gather.18.cloned.1.call-done = bf16[2048,512]{1,0:T(8,128)(2,1)} async-done(((bf16[256,512]{1,0:T(8,128)(2,1)}), bf16[2048,512]{1,0:T(8,128)(2,1)}) %all-gather.18.cloned.1.call-update) | async-done | bytes 2097168 | tf_op jit(solution)/shard_map/all_gather | solution.py:117
  767.6 4.3 fusion.78
  772.9 2.0 copy.105
  775.0 18.8 %while.28 = (s32[]{:T(128)}, bf16[4,512,128]{1,2,0:T(8,128)(2,1)}, f32[4,512]{1,0:T(4,128)}, bf16[4,512,128]{2,1,0:T(8,128)(2,1)}, bf16[4,512,128]{2,1,0:T(8,128...) while((s32[]{:T(128)}, bf16[4,512,128]{1,2,0:T(8,128)(2,1)}, ...), condition=%wide.region_12.13_spmd.clone, body=%wide.region_9.12_spmd.clone.sunk | while | flops 137100800 | bytes 3827809 | solution.py:161
  777.8 1.9 fusion.202
  782.4 1.9 fusion.202
  787.1 2.0 fusion.202
  791.9 1.9 fusion.202
  793.8 3.8 all-gather.20.cloned.1.call-done
  797.5 4.4 convolution_convert_fusion.12
  802.0 2.7 convert_element_type.191
  804.7 41.2 %reduce-scatter.11.cloned.1.call-done = bf16[128,2048]{1,0:T(8,128)(2,1)} async-done(((bf16[512,2048]{1,0:T(8,128)(2,1)}), bf16[128,2048]{1,0:T(8,128)(2,1)}) %reduce-scatter.11.cloned.1.call-update) | async-done | bytes 524304 | tf_op jit(solution)/shard_map/reduce_scatter | solution.py:167
  848.9 2.7 convert_element_type.193
  851.9 7.7 all-gather.24.cloned.1.call-done
  859.6 47.7 %all-gather.22.cloned.1.call-done = bf16[512,2048]{1,0:T(8,128)(2,1)} async-done(((bf16[128,2048]{1,0:T(8,128)(2,1)}), bf16[512,2048]{1,0:T(8,128)(2,1)}) %all-gather.22.cloned.1.call-update) | async-done | bytes 2097168 | tf_op jit(solution)/shard_map/all_gather | solution.py:175
  907.3 18.2 %multiply_convert_fusion.1 = (bf16[512,2048]{1,0:T(8,128)(2,1)}, f32[512,2048]{1,0:T(8,128)}, f32[512,2048]{1,0:T(8,128)}) fusion(bf16[512,2048]{1,0:T(8,128)(2,1)} %all-gather.22.cloned.1.call-done, bf16[2048,2048]{1,0:T(8,128)(2,1)} %all-gather.24.cloned.1.call-done), kind=kOutput, calls=%fused_computation.75 | convolution fusion | flops 4363124736 | bytes 20971520 | tf_op jit(solution)/shard_map/dot_general | solution.py:67
  925.5 38.3 %all-gather.26.cloned.1.call-done = bf16[2048,2048]{1,0:T(8,128)(2,1)} async-done(((bf16[2048,256]{1,0:T(8,128)(2,1)}), bf16[2048,2048]{1,0:T(8,128)(2,1)}) %all-gather.26.cloned.1.call-update) | async-done | bytes 8388624 | tf_op jit(solution)/shard_map/all_gather | solution.py:120
  963.8 9.8 convolution_convert_fusion.11
  973.9 43.7 %reduce-scatter.13.cloned.1.call-done = bf16[128,2048]{1,0:T(8,128)(2,1)} async-done(((bf16[512,2048]{1,0:T(8,128)(2,1)}), bf16[128,2048]{1,0:T(8,128)(2,1)}) %reduce-scatter.13.cloned.1.call-update) | async-done | bytes 524304 | tf_op jit(solution)/shard_map/reduce_scatter | solution.py:179
  1020.2 1.9 multiply_reduce_fusion.1
  1022.2 2.6 fusion.131
  1025.3 45.0 %all-gather.28.cloned.1.call-done = bf16[512,2048]{1,0:T(8,128)(2,1)} async-done(((bf16[128,2048]{1,0:T(8,128)(2,1)}), bf16[512,2048]{1,0:T(8,128)(2,1)}) %all-gather.28.cloned.1.call-update) | async-done | bytes 2097168 | tf_op jit(solution)/shard_map/all_gather | solution.py:186
  1070.3 11.9 add_convert_fusion
  1083.5 9.1 convolution_convert_fusion.10
  1092.7 42.7 %reduce-scatter.15.cloned.1.call-done = bf16[128,2048]{1,0:T(8,128)(2,1)} async-done(((bf16[512,2048]{1,0:T(8,128)(2,1)}), bf16[128,2048]{1,0:T(8,128)(2,1)}) %reduce-scatter.15.cloned.1.call-update) | async-done | bytes 524304 | tf_op jit(solution)/shard_map/reduce_scatter | solution.py:199
  1136.8 2.2 fusion.82
  1138.9 2.2 add_convert_fusion.1
  1141.5 45.2 %all-gather.30.cloned.1.call-done = bf16[512,2048]{1,0:T(8,128)(2,1)} async-done(((bf16[128,2048]{1,0:T(8,128)(2,1)}), bf16[512,2048]{1,0:T(8,128)(2,1)}) %all-gather.30.cloned.1.call-update) | async-done | bytes 2097168 | tf_op jit(solution)/shard_map/all_gather | solution.py:207
  1186.6 3.5 convolution_convert_fusion.13
  1192.6 28.7 %while.29 = (s32[]{:T(128)}, f32[4,512,128]{1,2,0:T(8,128)}, f32[4,512,128]{1,2,0:T(8,128)}, bf16[4,512,128]{1,2,0:T(8,128)(2,1)}, bf16[4,512,128]{2,1,0:T(8,128...) while((s32[]{:T(128)}, f32[4,512,128]{1,2,0:T(8,128)}, ...), condition=%wide.region_24.25_spmd.clone, body=%wide.region_22.24_spmd.clone.sunk | while | flops 338820608 | bytes 11683957 | solution.py:223
  1221.3 2.0 multiply_subtract_fusion.1
  1228.4 3.2 pad_maximum_fusion.1
  1231.7 4.5 convolution_convert_fusion.6
  1236.3 2.6 convolution_convert_fusion.3
  1238.9 4.4 convolution_convert_fusion.5
  1243.8 4.4 convolution_convert_fusion.4
  1248.2 8.5 convolution_convert_fusion.1
  1258.4 8.4 convolution_convert_fusion.2
  1267.0 74.2 %reduce-scatter.17.cloned.1.call-done = bf16[128,3,2048]{2,0,1:T(8,128)(2,1)} async-done(((bf16[512,3,2048]{2,0,1:T(8,128)(2,1)}), bf16[128,3,2048]{2,0,1:T(8,128)(2,1)}) %reduce-scatter.17.cloned.1.call-update) | async-done | bytes 1572880 | tf_op jit(solution)/shard_map/reduce_scatter | solution.py:239
  1350.9 1.8 fusion.97
  1352.7 34.5 %reduce-scatter.19.cloned.1.call-done = bf16[256,512]{1,0:T(8,128)(2,1)} async-done(((bf16[2048,512]{1,0:T(8,128)(2,1)}), bf16[256,512]{1,0:T(8,128)(2,1)}) %reduce-scatter.19.cloned.1.call-update) | async-done | bytes 262160 | tf_op jit(solution)/shard_map/reduce_scatter | solution.py:266
  1387.3 1.8 convert_element_type.214
  1389.1 42.7 %reduce-scatter.25.cloned.1.call-done = bf16[512,256]{1,0:T(8,128)(2,1)} async-done(((bf16[512,2048]{1,0:T(8,128)(2,1)}), bf16[512,256]{1,0:T(8,128)(2,1)}) %reduce-scatter.25.cloned.1.call-update) | async-done | bytes 262160 | tf_op jit(solution)/shard_map/reduce_scatter | solution.py:275
  1433.6 43.0 %reduce-scatter.21.cloned.1.call-done = bf16[256,512]{1,0:T(8,128)(2,1)} async-done(((bf16[2048,512]{1,0:T(8,128)(2,1)}), bf16[256,512]{1,0:T(8,128)(2,1)}) %reduce-scatter.21.cloned.1.call-update) | async-done | bytes 262160 | tf_op jit(solution)/shard_map/reduce_scatter | solution.py:269
  1476.6 1.8 convert_element_type.216
  1478.4 42.9 %reduce-scatter.23.cloned.1.call-done = bf16[256,512]{1,0:T(8,128)(2,1)} async-done(((bf16[2048,512]{1,0:T(8,128)(2,1)}), bf16[256,512]{1,0:T(8,128)(2,1)}) %reduce-scatter.23.cloned.1.call-update) | async-done | bytes 262160 | tf_op jit(solution)/shard_map/reduce_scatter | solution.py:272
  1523.1 74.0 %reduce-scatter.29.cloned.1.call-done = bf16[2048,256]{1,0:T(8,128)(2,1)} async-done(((bf16[2048,2048]{1,0:T(8,128)(2,1)}), bf16[2048,256]{1,0:T(8,128)(2,1)}) %reduce-scatter.29.cloned.1.call-update) | async-done | bytes 1048592 | tf_op jit(solution)/shard_map/reduce_scatter | solution.py:281
  1597.1 2.7 convert_element_type.224
  1599.8 72.6 %reduce-scatter.27.cloned.1.call-done = bf16[256,2048]{1,0:T(8,128)(2,1)} async-done(((bf16[2048,2048]{1,0:T(8,128)(2,1)}), bf16[256,2048]{1,0:T(8,128)(2,1)}) %reduce-scatter.27.cloned.1.call-update) | async-done | bytes 1048592 | tf_op jit(solution)/shard_map/reduce_scatter | solution.py:278
  1672.4 2.8 convert_element_type.222
  1675.2 40.9 %all-reduce.1 = (f32[5,2048]{1,0:T(8,128)}, f32[68,68]{1,0:T(8,128)}) all-reduce(f32[5,2048]{1,0:T(8,128)S(1)} %stack.44, f32[68,68]{1,0:T(8,128)S(1)} %fusion.114), channel_id=1, replica_groups=mesh['dp'=8,'layer'=4] {'dp','layer'}, use_global_device_ids=true, to_apply=%region_43.44 | all-reduce | flops 14864 | bytes 118912 | tf_op jit(solution)/shard_map/psum | solution.py:288
  1716.1 6.9 pad_maximum_fusion
  1723.0 20.2 %fusion.73 = f32[4,4,512]{1,0,2:T(4,128)S(1)} fusion(bf16[4,512,2048]{2,1,0:T(8,128)(2,1)} %param.18, bf16[512,4,2048]{2,0,1:T(8,128)(2,1)} %pad_maximum_fusion), kind=kOutput, calls=%fused_computation.124 | convolution fusion | flops 33554432 | bytes 16809984 | tf_op jit(solution)/shard_map/jtd,tsd->sjt/dot_general | solution.py:264
  1743.3 21.7 %fusion.46 = bf16[4,512,2048]{2,0,1:T(4,128)(2,1)} fusion(f32[4,4,512]{0,1,2:T(4,128)S(1)} %copy-done.12, bf16[512,4,2048]{2,0,1:T(8,128)(2,1)S(1)} %copy-done.10), kind=kOutput, calls=%fused_computation.62 | convolution fusion | flops 205520896 | bytes 16809984 | tf_op jit(solution)/shard_map/sjt,tsd->jtd/dot_general | solution.py:261
  1765.0 11.5 copy.119
  1777.4 1.9 copy.251
  (332 shorter events, 89.4 us)
Async XLA Ops:
  8.0 1011.0 %copy-start = (f32[2048,68]{0,1:T(8,128)S(1)}, f32[2048,68]{0,1:T(8,128)}, u32[]{:S(2)}) copy-start(f32[2048,68]{0,1:T(8,128)} %param.28) | copy-start | bytes 1671172
  8.0 601.6 %all-reduce.7.cloned.1.call-start = ((), (), s32[]{:S(2)}) async-start(), calls=%async_computation.32 | async-start | bytes 33554432
  9.3 35.2 %copy-start.11 = (f32[4,4,512]{0,1,2:T(4,128)}, f32[4,4,512]{0,1,2:T(4,128)S(1)}, u32[]{:S(2)}) copy-start(f32[4,4,512]{0,1,2:T(4,128)S(1)} %copy.116) | copy-start | bytes 98308
  44.6 585.4 %all-gather.14.cloned.1.call-start = ((), (), s32[]{:S(2)}) async-start(), calls=%async_computation.11 | async-start | bytes 2359296 | tf_op jit(solution)/shard_map/all_gather | solution.py:115
  46.3 587.8 %all-gather.16.cloned.1.call-start = ((), (), s32[]{:S(2)}) async-start(), calls=%async_computation.12 | async-start | bytes 2359296 | tf_op jit(solution)/shard_map/all_gather | solution.py:116
  47.2 692.0 %all-gather.12.cloned.1.call-start = ((), (), s32[]{:S(2)}) async-start(), calls=%async_computation.10 | async-start | bytes 7864320 | tf_op jit(solution)/shard_map/all_gather | solution.py:126
  47.3 574.8 %copy-start.31 = (f32[1,2048]{1,0:T(1,128)}, f32[1,2048]{1,0:T(1,128)S(1)}, u32[]{:S(2)}) copy-start(f32[1,2048]{1,0:T(1,128)S(1)} %get-tuple-element.366) | copy-start | bytes 24580
  47.3 575.3 %copy-start.29 = (f32[1,2048]{1,0:T(1,128)}, f32[1,2048]{1,0:T(1,128)S(1)}, u32[]{:S(2)}) copy-start(f32[1,2048]{1,0:T(1,128)S(1)} %get-tuple-element.364) | copy-start | bytes 24580
  47.3 575.3 %copy-start.33 = (f32[1,2048]{1,0:T(1,128)}, f32[1,2048]{1,0:T(1,128)S(1)}, u32[]{:S(2)}) copy-start(f32[1,2048]{1,0:T(1,128)S(1)} %get-tuple-element.365) | copy-start | bytes 24580
  47.3 800.5 %copy-start.35 = (f32[1,2048]{1,0:T(1,128)}, f32[1,2048]{1,0:T(1,128)S(1)}, u32[]{:S(2)}) copy-start(f32[1,2048]{1,0:T(1,128)S(1)} %get-tuple-element.367) | copy-start | bytes 24580
  624.8 142.7 %all-gather.18.cloned.1.call-start = ((), (), s32[]{:S(2)}) async-start(), calls=%async_computation.13 | async-start | bytes 2359296 | tf_op jit(solution)/shard_map/all_gather | solution.py:117
  625.7 171.8 %all-gather.20.cloned.1.call-start = ((), (), s32[]{:S(2)}) async-start(), calls=%async_computation.14 | async-start | bytes 2359296 | tf_op jit(solution)/shard_map/all_gather | solution.py:118
  627.7 218.2 %reduce-scatter.11.cloned.1.call-start = ((), (), s32[]{:S(2)}) async-start(), calls=%async_computation.15 | async-start | bytes 2621440 | tf_op jit(solution)/shard_map/reduce_scatter | solution.py:167
  627.8 10.3 copy-start.16
  747.2 24.7 %copy-start.20 = (bf16[512,4,64]{0,2,1:T(8,128)(2,1)S(1)}, bf16[512,4,64]{0,2,1:T(8,128)(2,1)}, u32[]{:S(2)}) copy-start(bf16[512,4,64]{0,2,1:T(8,128)(2,1)} %get-tuple-element.361) | copy-start | bytes 786436
  747.2 24.7 %copy-start.21 = (bf16[512,4,64]{0,2,1:T(8,128)(2,1)S(1)}, bf16[512,4,64]{0,2,1:T(8,128)(2,1)}, u32[]{:S(2)}) copy-start(bf16[512,4,64]{0,2,1:T(8,128)(2,1)} %get-tuple-element.362) | copy-start | bytes 786436
  801.9 57.7 %all-gather.24.cloned.1.call-start = ((), (), s32[]{:S(2)}) async-start(), calls=%async_computation.17 | async-start | bytes 9437184 | tf_op jit(solution)/shard_map/all_gather | solution.py:119
  804.7 102.6 %all-gather.22.cloned.1.call-start = ((), (), s32[]{:S(2)}) async-start(), calls=%async_computation.16 | async-start | bytes 2621440 | tf_op jit(solution)/shard_map/all_gather | solution.py:175
  847.5 77.9 %copy-start.44 = (f32[128]{0:T(128)}, f32[128]{0:T(128)S(1)}, u32[]{:S(2)}) copy-start(f32[128]{0:T(128)S(1)} %broadcast_multiply_fusion) | copy-start | bytes 1540
  847.8 77.7 %copy-start.70 = (f32[128]{0:T(128)}, f32[128]{0:T(128)S(1)}, u32[]{:S(2)}) copy-start(f32[128]{0:T(128)S(1)} %multiply_reduce_fusion.7) | copy-start | bytes 1540
  847.8 77.6 %copy-start.60 = (f32[128]{0:T(128)}, f32[128]{0:T(128)S(1)}, u32[]{:S(2)}) copy-start(f32[128]{0:T(128)S(1)} %fusion.121) | copy-start | bytes 1540
  848.9 114.9 %all-gather.26.cloned.1.call-start = ((), (), s32[]{:S(2)}) async-start(), calls=%async_computation.18 | async-start | bytes 9437184 | tf_op jit(solution)/shard_map/all_gather | solution.py:120
  851.7 166.0 %reduce-scatter.13.cloned.1.call-start = ((), (), s32[]{:S(2)}) async-start(), calls=%async_computation.19 | async-start | bytes 2621440 | tf_op jit(solution)/shard_map/reduce_scatter | solution.py:179
  963.8 9.9 copy-start.37
  963.8 9.9 copy-start.39
  973.7 96.6 %all-gather.28.cloned.1.call-start = ((), (), s32[]{:S(2)}) async-start(), calls=%async_computation.20 | async-start | bytes 2621440 | tf_op jit(solution)/shard_map/all_gather | solution.py:186
  1018.9 5.9 copy-start.8
  1019.0 5.9 copy-start.52
  1024.8 110.6 %reduce-scatter.15.cloned.1.call-start = ((), (), s32[]{:S(2)}) async-start(), calls=%async_computation.21 | async-start | bytes 2621440 | tf_op jit(solution)/shard_map/reduce_scatter | solution.py:199
  1083.5 51.9 %copy-start.36 = (f32[1,2048]{1,0:T(1,128)S(1)}, f32[1,2048]{1,0:T(1,128)}, u32[]{:S(2)}) copy-start(f32[1,2048]{1,0:T(1,128)} %copy-done.35) | copy-start | bytes 24580
  1083.5 51.9 %copy-start.45 = (f32[128]{0:T(128)S(1)}, f32[128]{0:T(128)}, u32[]{:S(2)}) copy-start(f32[128]{0:T(128)} %copy-done.44) | copy-start | bytes 1540
  1083.5 53.2 %copy-start.71 = (f32[128]{0:T(128)S(1)}, f32[128]{0:T(128)}, u32[]{:S(2)}) copy-start(f32[128]{0:T(128)} %copy-done.70) | copy-start | bytes 1540
  1083.5 53.2 %copy-start.61 = (f32[128]{0:T(128)S(1)}, f32[128]{0:T(128)}, u32[]{:S(2)}) copy-start(f32[128]{0:T(128)} %copy-done.60) | copy-start | bytes 1540
  1092.7 93.9 %all-gather.30.cloned.1.call-start = ((), (), s32[]{:S(2)}) async-start(), calls=%async_computation.22 | async-start | bytes 2621440 | tf_op jit(solution)/shard_map/all_gather | solution.py:207
  1141.2 51.4 %copy-start.55 = (s32[1,512]{1,0:T(1,128)S(1)}, s32[1,512]{1,0:T(1,128)}, u32[]{:S(2)}) copy-start(s32[1,512]{1,0:T(1,128)} %param.20) | copy-start | bytes 6148
  1141.2 200.0 %reduce-scatter.17.cloned.1.call-start = ((), (), s32[]{:S(2)}) async-start(), calls=%async_computation.23 | async-start | bytes 7864320 | tf_op jit(solution)/shard_map/reduce_scatter | solution.py:239
  1231.6 4.6 copy-start.18
  1231.6 4.6 copy-start.25
  1231.7 155.6 %reduce-scatter.19.cloned.1.call-start = ((), (), s32[]{:S(2)}) async-start(), calls=%async_computation.25 | async-start | bytes 2359296 | tf_op jit(solution)/shard_map/reduce_scatter | solution.py:266
  1236.2 195.6 %reduce-scatter.25.cloned.1.call-start = ((), (), s32[]{:S(2)}) async-start(), calls=%async_computation.28 | async-start | bytes 2359296 | tf_op jit(solution)/shard_map/reduce_scatter | solution.py:275
  1238.8 237.7 %reduce-scatter.21.cloned.1.call-start = ((), (), s32[]{:S(2)}) async-start(), calls=%async_computation.26 | async-start | bytes 2359296 | tf_op jit(solution)/shard_map/reduce_scatter | solution.py:269
  1243.3 4.9 copy-start.74
  1243.3 278.0 %reduce-scatter.23.cloned.1.call-start = ((), (), s32[]{:S(2)}) async-start(), calls=%async_computation.27 | async-start | bytes 2359296 | tf_op jit(solution)/shard_map/reduce_scatter | solution.py:272
  1248.2 348.9 %reduce-scatter.29.cloned.1.call-start = ((), (), s32[]{:S(2)}) async-start(), calls=%async_computation.30 | async-start | bytes 9437184 | tf_op jit(solution)/shard_map/reduce_scatter | solution.py:281
  1256.8 415.5 %reduce-scatter.27.cloned.1.call-start = ((), (), s32[]{:S(2)}) async-start(), calls=%async_computation.29 | async-start | bytes 9437184 | tf_op jit(solution)/shard_map/reduce_scatter | solution.py:278
  1266.9 76.2 %copy-start.7 = (f32[128,1,2048]{2,1,0:T(1,128)S(1)}, f32[128,1,2048]{2,1,0:T(1,128)}, u32[]{:S(2)}) copy-start(f32[128,1,2048]{2,1,0:T(1,128)} %copy-done.6) | copy-start | bytes 3145732
  1266.9 76.2 %copy-start.30 = (f32[1,2048]{1,0:T(1,128)S(1)}, f32[1,2048]{1,0:T(1,128)}, u32[]{:S(2)}) copy-start(f32[1,2048]{1,0:T(1,128)} %copy-done.29) | copy-start | bytes 24580
  1266.9 76.2 %copy-start.51 = (f32[128]{0:T(128)S(1)}, f32[128]{0:T(128)}, u32[]{:S(2)}) copy-start(f32[128]{0:T(128)} %copy-done.50) | copy-start | bytes 1540
  1266.9 76.8 %copy-start.69 = (f32[128]{0:T(128)S(1)}, f32[128]{0:T(128)}, u32[]{:S(2)}) copy-start(f32[128]{0:T(128)} %copy-done.68) | copy-start | bytes 1540
  1266.9 76.8 %copy-start.3 = (f32[128,1,2048]{2,1,0:T(1,128)S(1)}, f32[128,1,2048]{2,1,0:T(1,128)}, u32[]{:S(2)}) copy-start(f32[128,1,2048]{2,1,0:T(1,128)} %copy-done.2) | copy-start | bytes 3145732
  1266.9 76.8 %copy-start.5 = (f32[128,1,2048]{2,1,0:T(1,128)S(1)}, f32[128,1,2048]{2,1,0:T(1,128)}, u32[]{:S(2)}) copy-start(f32[128,1,2048]{2,1,0:T(1,128)} %copy-done.4) | copy-start | bytes 3145732
  1266.9 76.8 %copy-start.32 = (f32[1,2048]{1,0:T(1,128)S(1)}, f32[1,2048]{1,0:T(1,128)}, u32[]{:S(2)}) copy-start(f32[1,2048]{1,0:T(1,128)} %copy-done.31) | copy-start | bytes 24580
  1266.9 76.8 %copy-start.34 = (f32[1,2048]{1,0:T(1,128)S(1)}, f32[1,2048]{1,0:T(1,128)}, u32[]{:S(2)}) copy-start(f32[1,2048]{1,0:T(1,128)} %copy-done.33) | copy-start | bytes 24580
  1266.9 76.8 %copy-start.47 = (f32[128]{0:T(128)S(1)}, f32[128]{0:T(128)}, u32[]{:S(2)}) copy-start(f32[128]{0:T(128)} %copy-done.46) | copy-start | bytes 1540
  1266.9 76.8 %copy-start.49 = (f32[128]{0:T(128)S(1)}, f32[128]{0:T(128)}, u32[]{:S(2)}) copy-start(f32[128]{0:T(128)} %copy-done.48) | copy-start | bytes 1540
  1267.0 76.8 %copy-start.63 = (f32[128]{0:T(128)S(1)}, f32[128]{0:T(128)}, u32[]{:S(2)}) copy-start(f32[128]{0:T(128)} %copy-done.62) | copy-start | bytes 1540
  1267.0 449.2 %all-gather.32.cloned.1.call-start = ((), (), s32[]{:S(2)}) async-start(), calls=%async_computation.24 | async-start | bytes 7864320 | tf_op jit(solution)/shard_map/all_gather | solution.py:258
  1349.6 427.8 %all-reduce.5.cloned.1.call-start = ((), (), s32[]{:S(2)}) async-start(), calls=%async_computation.31 | async-start | bytes 1179648 | tf_op jit(solution)/shard_map/psum | solution.py:288
  1389.1 286.1 %copy-start.41 = (f32[2048]{0:T(1024)S(1)}, f32[2048]{0:T(1024)}, u32[]{:S(2)}) copy-start(f32[2048]{0:T(1024)} %get-tuple-element.280) | copy-start | bytes 24580
  1389.1 286.1 %copy-start.42 = (f32[2048]{0:T(1024)S(1)}, f32[2048]{0:T(1024)}, u32[]{:S(2)}) copy-start(f32[2048]{0:T(1024)} %get-tuple-element.282) | copy-start | bytes 24580
  1433.6 282.5 %copy-start.19 = (bf16[512,2048]{1,0:T(8,128)(2,1)S(1)}, bf16[512,2048]{1,0:T(8,128)(2,1)}, u32[]{:S(2)}) copy-start(bf16[512,2048]{1,0:T(8,128)(2,1)} %all-gather.30.cloned.1.call-done) | copy-start | bytes 6291460
  1723.0 20.2 %copy-start.10 = (bf16[512,4,2048]{2,0,1:T(8,128)(2,1)S(1)}, bf16[512,4,2048]{2,0,1:T(8,128)(2,1)}, u32[]{:S(2)}) copy-start(bf16[512,4,2048]{2,0,1:T(8,128)(2,1)} %pad_maximum_fusion) | copy-start | bytes 25165828
  1723.0 20.2 %copy-start.12 = (f32[4,4,512]{0,1,2:T(4,128)S(1)}, f32[4,4,512]{0,1,2:T(4,128)}, u32[]{:S(2)}) copy-start(f32[4,4,512]{0,1,2:T(4,128)} %copy-done.11) | copy-start | bytes 98308
  1765.0 14.4 copy-start.1
  (36 other events, 86.4 us)
Sparse Core Ops, SparseCore 0:
  44.7 564.8 all-reduce.6
  802.0 43.8 reduce-scatter.10
  973.8 43.8 reduce-scatter.12
  1025.0 45.2 all-gather.27
  1092.8 42.5 reduce-scatter.14
  1141.3 45.2 all-gather.29
  1231.8 109.4 reduce-scatter.16
  1345.5 41.7 reduce-scatter.18
  1390.5 41.2 reduce-scatter.24
  1435.3 41.2 reduce-scatter.20
  1479.9 41.3 reduce-scatter.22
  1525.0 72.0 reduce-scatter.28
  1601.1 71.2 reduce-scatter.26
Sparse Core Ops, SparseCore 1:
  47.5 30.4 all-gather.13
  80.3 27.7 all-gather.15
  624.9 114.2 all-gather.11
  741.6 25.9 all-gather.17
  769.5 28.0 all-gather.19
  805.3 54.2 all-gather.23
  861.7 45.5 all-gather.21
  909.2 54.6 all-gather.25
  1349.7 115.7 all-gather.31
  1472.1 142.4 all-reduce.4
where the time goes:
time: 1800 us; the launch traced here: 1790 us
  waiting for transfers between devices  1380 us (77%)
  matrix products  221 us (12%)
  other arithmetic  74.1 us (4%)
  local copies, waits for them, and re-layouts  48.7 us (3%)
  blocking collectives  40.9 us (2%)
    unnamed x24, waiting for transfers between devices  561 us
    all_gather x1, waiting for transfers between devices, local(): normed_rows = lax.all_gather(normed, 'layer', axis=0, tiled=True)  101 us
    reduce_scatter x1, waiting for transfers between devices, local(): lax.psum_scatter(jnp.stack((dot_right_t(query_lin_grad, back_query), dot_...  74.2 us
    reduce_scatter x1, waiting for transfers between devices, local(): lax.psum_scatter(down_grad.astype(jnp.bfloat16), 'dp', scatter_dimension=...  74 us
    reduce_scatter x1, waiting for transfers between devices, local(): lax.psum_scatter(up_grad.astype(jnp.bfloat16), 'dp', scatter_dimension=0,...  72.6 us
    dot_general x14, matrix products, plain_dot(): return jnp.dot(left, right, preferred_element_type=jnp.float32)  52.3 us
    all_gather x1, waiting for transfers between devices, local(): lax.all_gather(mlp_norm.astype(jnp.bfloat16), 'layer', axis=0, tiled=True)  47.7 us
    all_gather x1, waiting for transfers between devices, local(): lax.all_gather(hidden_grad.astype(jnp.bfloat16), 'layer', axis=0, tiled=T...  45.2 us
  transfers between devices with their start and end apart: 23, of which 19 were waited for; matrix products, arithmetic and copies ran while one was open for 12% of the time, Pallas kernels for 0%

commit v1 on v0

v1 whole, which is shorter than its diff:
```python
import math

import jax
import jax.numpy as jnp
from jax import lax
from jax.experimental import pallas as pl
from jax.experimental.pallas import tpu as pltpu
from jax.sharding import PartitionSpec as P

HEAD_DIM = 128
DOCS = 2


highest = lax.Precision.HIGHEST
epsilon = 1e-05
bf16 = jnp.bfloat16
f32 = jnp.float32
CHUNK = 16


def rms_norm(values, gain_vec):
    square = jnp.mean(values * values, axis=-1, keepdims=True)
    return values * lax.rsqrt(square + epsilon) * gain_vec


def gelu_exact(values):
    return jax.nn.gelu(values, approximate=False)


def mixer(out_rows, gain_vec, first_matrix, second_matrix):
    hidden = gelu_exact(jnp.dot(rms_norm(out_rows, gain_vec), first_matrix, precision=highest))
    return jnp.dot(hidden, second_matrix, precision=highest)


def plain_dot(left, right):
    return jnp.dot(left, right, preferred_element_type=f32)


def dot_left_t(left, right):
    return lax.dot_general(left, right, (((0,), (0,)), ((), ())), preferred_element_type=f32)


def dot_right_t(left, right):
    return lax.dot_general(left, right, (((1,), (1,)), ((), ())), preferred_element_type=f32)


def gather_blocks(block, count):
    return [block] + [
        lax.ppermute(block, "layer", [(i, (i + k) % count) for i in range(count)])
        for k in range(1, count)
    ]


def gather_line(block, count):
    ups, downs = [block], [block]
    for k in range(1, count):
        ups.append(lax.ppermute(ups[-1], "layer", [(i, i + 1) for i in range(k - 1, count - 1)]))
        downs.append(lax.ppermute(downs[-1], "layer", [(i + 1, i) for i in range(count - k)]))
    return [[block]] + [[ups[k], downs[count - k]] for k in range(1, count)]


def sum_line(blocks, count):
    up = down = None
    for k in range(1, count):
        up = blocks[k] if up is None else blocks[k] + up
        up = lax.ppermute(up, "layer", [(i, i + 1) for i in range(k)])
        down = blocks[count - k] if down is None else blocks[count - k] + down
        down = lax.ppermute(down, "layer", [(i, i - 1) for i in range(count - k, count)])
    return [blocks[0], up, down]


def total_of(pieces):
    total = pieces[0]
    for piece in pieces[1:]:
        total = total + piece
    return total


def after(value, *others):
    anywhere = pl.BlockSpec(memory_space=pl.ANY)
    return pl.pallas_call(
        lambda *refs: None,
        in_specs=[anywhere] * (1 + len(others)),
        out_specs=anywhere,
        out_shape=jax.ShapeDtypeStruct(value.shape, value.dtype),
        input_output_aliases={0: 0},
    )(value, *others)


def return_blocks(blocks, count):
    return [blocks[0]] + [
        lax.ppermute(blocks[k], "layer", [(i, (i - k) % count) for i in range(count)])
        for k in range(1, count)
    ]


def add_blocks(blocks):
    total = blocks[0].astype(f32)
    for block in blocks[1:]:
        total = total + block.astype(f32)
    return total


def vmem(megabytes):
    return pltpu.CompilerParams(vmem_limit_bytes=megabytes << 20)


def row_loop(rows, body, carry):
    return lax.fori_loop(
        0, rows // CHUNK, lambda i, c: body(pl.ds(pl.multiple_of(i * CHUNK, CHUNK), CHUNK), c), carry
    )


def stream_kernel(me_ref, mix_ref, hist_ref, *out_refs, stored, first):
    def body(at, carry):
        mix = mix_ref[at, :]
        totals = [None] * len(out_refs)
        for j in range(stored):
            rows = hist_ref[j, at, :].astype(f32)
            for s in range(len(out_refs)):
                i = (first + s) * stored + j
                term = rows * mix[:, i : i + 1]
                totals[s] = term if j == 0 else totals[s] + term
        for out_ref, total in zip(out_refs, totals):
            out_ref[at, :] = total.astype(bf16)
        return carry

    row_loop(out_refs[0].shape[0], body, 0)


def stream_sums(me, mix_cols, history, first, number, count):
    stored, tokens, width = history.shape
    rows = 128
    steps = tokens // count // rows
    where = lambda i, w: (w[0] - i // steps + count) % count * steps + i % steps
    return pl.pallas_call(
        lambda *refs: stream_kernel(*refs, stored=stored, first=first),
        grid_spec=pltpu.PrefetchScalarGridSpec(
            num_scalar_prefetch=1,
            grid=(tokens // rows,),
            in_specs=[
                pl.BlockSpec((rows, 4 * stored), lambda i, w: (where(i, w), 0)),
                pl.BlockSpec((stored, rows, width), lambda i, w: (0, where(i, w), 0)),
            ],
            out_specs=[pl.BlockSpec((rows, width), lambda i, w: (i, 0))] * number,
        ),
        out_shape=[jax.ShapeDtypeStruct((tokens, width), bf16)] * number,
        compiler_params=vmem(48),
    )(me.astype(jnp.int32).reshape(1), mix_cols, history)


def join_kernel(gain_ref, base_ref, *refs):
    parts, (sum_ref, norm_ref) = refs[:-2], refs[-2:]

    def body(at, carry):
        values = base_ref[at, :].astype(f32) + total_of([p[at, :].astype(f32) for p in parts])
        sum_ref[at, :] = values
        centre = values - jnp.mean(values, axis=1, keepdims=True)
        spread = jnp.mean(centre * centre, axis=1, keepdims=True)
        norm_ref[at, :] = (centre * lax.rsqrt(spread + epsilon) * gain_ref[...]).astype(bf16)
        return carry

    row_loop(base_ref.shape[0], body, 0)


def join_norm(base, parts, gain_vec):
    return pl.pallas_call(
        join_kernel,
        out_shape=[jax.ShapeDtypeStruct(base.shape, f32), jax.ShapeDtypeStruct(base.shape, bf16)],
        compiler_params=vmem(48),
    )(gain_vec[None], base, *parts)


def back_kernel(gain_ref, value_ref, *refs, parts, based):
    part_refs = refs[:parts]
    base_ref = refs[parts] if based else None
    out_ref, dgain_ref = refs[-2:]

    def body(at, dgain):
        values = value_ref[at, :].astype(f32)
        grad = total_of([p[at, :].astype(f32) for p in part_refs])
        centre = values - jnp.mean(values, axis=1, keepdims=True)
        inv = lax.rsqrt(jnp.mean(centre * centre, axis=1, keepdims=True) + epsilon)
        hat = centre * inv
        scaled = grad * gain_ref[...]
        back = (
            scaled
            - jnp.mean(scaled, axis=1, keepdims=True)
            - hat * jnp.mean(scaled * hat, axis=1, keepdims=True)
        ) * inv
        if based:
            back = back + base_ref[at, :]
        out_ref[at, :] = back.astype(bf16)
        return dgain + jnp.sum(grad * hat, axis=0, keepdims=True)

    dgain_ref[...] = row_loop(value_ref.shape[0], body, jnp.zeros(dgain_ref.shape, f32))


def norm_back(values, parts, gain_vec, base=None):
    operands = [gain_vec[None], values] + list(parts) + ([] if base is None else [base])
    back, dgain = pl.pallas_call(
        lambda *refs: back_kernel(*refs, parts=len(parts), based=base is not None),
        out_shape=[
            jax.ShapeDtypeStruct(values.shape, bf16),
            jax.ShapeDtypeStruct((1, values.shape[1]), f32),
        ],
        compiler_params=vmem(48),
    )(*operands)
    return back, dgain[0]


def history_kernel(me_ref, mix_ref, hist_ref, *refs, stored, counts):
    hist_out, mix_out = refs[-2:]
    width = hist_out.shape[2]
    lanes = 256

    def body(at, carry):
        mix = mix_ref[at, :]
        sums = [None] * (4 * stored)
        for c in range(0, width, lanes):
            cols = slice(c, c + lanes)
            wide, first = [], 0
            for n in counts:
                wide.append(total_of([r[at, cols].astype(f32) for r in refs[first : first + n]]))
                first += n
            for j in range(stored):
                stored_rows = hist_ref[j, at, cols].astype(f32)
                total = None
                for s in range(4):
                    i = s * stored + j
                    term = wide[s] * mix[:, i : i + 1]
                    total = term if total is None else total + term
                    product = stored_rows * wide[s]
                    product = total_of([product[:, l : l + 128] for l in range(0, lanes, 128)])
                    sums[i] = product if sums[i] is None else sums[i] + product
                hist_out[j, at, cols] = total.astype(bf16)
        mix_out[at, :] = jnp.concatenate([jnp.sum(v, axis=1, keepdims=True) for v in sums], axis=1)
        return carry

    row_loop(hist_out.shape[1], body, 0)


def history_block(where, mix_cols, history, grads, so_far):
    stored, tokens, width = history.shape
    counts = [len(g) for g in grads]
    pieces = [p for g in grads for p in g]
    block = pieces[0].shape[0]
    rows = 64
    steps = block // rows
    grad_spec = pl.BlockSpec((rows, width), lambda i, w: (i, 0))
    specs = [
        pl.BlockSpec((rows, 4 * stored), lambda i, w: (w[0] * steps + i, 0)),
        pl.BlockSpec((stored, rows, width), lambda i, w: (0, w[0] * steps + i, 0)),
    ] + [grad_spec] * len(pieces)
    operands = [mix_cols, history] + pieces
    aliases = {}
    if so_far is not None:
        specs += [pl.BlockSpec(memory_space=pl.ANY)] * 2
        aliases = {1 + len(operands): 0, 2 + len(operands): 1}
        operands += so_far
    return pl.pallas_call(
        lambda *refs: history_kernel(*refs, stored=stored, counts=counts),
        grid_spec=pltpu.PrefetchScalarGridSpec(
            num_scalar_prefetch=1,
            grid=(steps,),
            in_specs=specs,
            out_specs=[
                pl.BlockSpec((stored, rows, width), lambda i, w: (0, w[0] * steps + i, 0)),
                pl.BlockSpec((rows, 4 * stored), lambda i, w: (w[0] * steps + i, 0)),
            ],
        ),
        out_shape=[
            jax.ShapeDtypeStruct((stored, tokens, width), bf16),
            jax.ShapeDtypeStruct((tokens, 4 * stored), f32),
        ],
        input_output_aliases=aliases,
        compiler_params=vmem(48),
    )(where, *operands)


def turn(values, cosine, sine):
    return values * cosine + pltpu.roll(values, HEAD_DIM // 2, 1) * sine


def score_block(queries, keys, allowed):
    scores = lax.dot_general(
        queries, keys, (((1,), (1,)), ((), ())), preferred_element_type=f32
    ) * (HEAD_DIM ** (-0.5))
    return jnp.where(allowed, scores, -1e30)


def allowed_block(row_ids, col_ids):
    return (row_ids[:, 0:1] == col_ids[0:1, :]) & (row_ids[:, 1:2] >= col_ids[1:2, :])


def attend_kernel(rows_ref, cols_ref, cos_ref, sin_ref, q_ref, k_ref, v_ref, ctx_ref, qr_ref, kr_ref, lse_ref):
    allowed = allowed_block(rows_ref[...], cols_ref[...])
    queries = turn(q_ref[...], cos_ref[...], sin_ref[...]).astype(bf16)
    keys = turn(k_ref[...], cos_ref[...], sin_ref[...]).astype(bf16)
    qr_ref[...] = queries
    kr_ref[...] = keys
    scores = score_block(queries, keys, allowed)
    row_max = jnp.max(scores, axis=1, keepdims=True)
    shifted = jnp.exp(scores - row_max)
    row_sum = jnp.sum(shifted, axis=1, keepdims=True)
    probs = (shifted / row_sum).astype(bf16)
    ctx_ref[...] = jnp.dot(probs, v_ref[...], preferred_element_type=f32).astype(bf16)
    lse_ref[0] = row_max + jnp.log(row_sum)


def attend(row_ids, col_ids, cosine, sine, q_lin, k_lin, v_lin):
    tokens, width = q_lin.shape
    heads = width // HEAD_DIM
    full = lambda a: pl.BlockSpec(a.shape, lambda h: (0,) * a.ndim)
    head = pl.BlockSpec((tokens, HEAD_DIM), lambda h: (0, h))
    return pl.pallas_call(
        attend_kernel,
        grid=(heads,),
        in_specs=[full(row_ids), full(col_ids), full(cosine), full(sine), head, head, head],
        out_specs=[head, head, head, pl.BlockSpec((1, tokens, 1), lambda h: (h, 0, 0))],
        out_shape=[jax.ShapeDtypeStruct((tokens, width), bf16)] * 3
        + [jax.ShapeDtypeStruct((heads, tokens, 1), f32)],
        compiler_params=vmem(56),
    )(row_ids, col_ids, cosine, sine, q_lin, k_lin, v_lin)


def attend_back_kernel(
    rows_ref, cols_ref, cos_ref, sin_ref, q_ref, k_ref, v_ref, lse_ref, grad_ref, dq_ref, dk_ref, dv_ref
):
    allowed = allowed_block(rows_ref[...], cols_ref[...])
    queries, keys, values, grad = q_ref[...], k_ref[...], v_ref[...], grad_ref[...]
    scale = HEAD_DIM ** (-0.5)
    probs = jnp.exp(score_block(queries, keys, allowed) - lse_ref[0])
    prob_grad = lax.dot_general(grad, values, (((1,), (1,)), ((), ())), preferred_element_type=f32)
    dv_ref[...] = lax.dot_general(
        probs.astype(bf16), grad, (((0,), (0,)), ((), ())), preferred_element_type=f32
    ).astype(bf16)
    centre = jnp.sum(probs * prob_grad, axis=1, keepdims=True)
    score_grad = (probs * (prob_grad - centre)).astype(bf16)
    dq = jnp.dot(score_grad, keys, preferred_element_type=f32) * scale
    dk = (
        lax.dot_general(score_grad, queries, (((0,), (0,)), ((), ())), preferred_element_type=f32)
        * scale
    )
    dq_ref[...] = turn(dq, cos_ref[...], -sin_ref[...]).astype(bf16)
    dk_ref[...] = turn(dk, cos_ref[...], -sin_ref[...]).astype(bf16)


def attend_back(row_ids, col_ids, cosine, sine, queries, keys, v_lin, lse, grad):
    tokens, width = queries.shape
    heads = width // HEAD_DIM
    full = lambda a: pl.BlockSpec(a.shape, lambda h: (0,) * a.ndim)
    head = pl.BlockSpec((tokens, HEAD_DIM), lambda h: (0, h))
    return pl.pallas_call(
        attend_back_kernel,
        grid=(heads,),
        in_specs=[full(row_ids), full(col_ids), full(cosine), full(sine), head, head, head]
        + [pl.BlockSpec((1, tokens, 1), lambda h: (h, 0, 0)), head],
        out_specs=[head, head, head],
        out_shape=[jax.ShapeDtypeStruct((tokens, width), bf16)] * 3,
        compiler_params=vmem(56),
    )(row_ids, col_ids, cosine, sine, queries, keys, v_lin, lse, grad)


def places(seg_row):
    length = seg_row.shape[0]
    labels = jnp.arange(DOCS, dtype=jnp.int32)
    before = jnp.sum((seg_row[None, :] < labels[:, None]).astype(jnp.int32), axis=1)
    member = (seg_row[:, None] == labels[None, :]).astype(jnp.int32)
    begins = jnp.sum(member * before[None, :], axis=1)
    return jnp.arange(length, dtype=jnp.int32) - begins


def local(
    history,
    mix_weights,
    segments,
    w_query,
    w_key,
    w_value,
    w_output,
    w_up,
    w_down,
    norm_gains,
    w_first,
    w_second,
    out_cotangent,
    mix_cotangent,
):
    stored, row_tok, width = history.shape
    count = lax.axis_size("layer")
    me = lax.axis_index("layer")
    own_tok = row_tok // count
    order = [(me - k) % count for k in range(count)]

    query_low = jnp.concatenate([w_query, w_key, w_value], axis=1).astype(bf16)
    full_qkv = lax.all_gather(query_low, "dp", axis=0, tiled=True)
    head_cols = w_query.shape[1]
    full_query = full_qkv[:, :head_cols]
    full_key = full_qkv[:, head_cols : 2 * head_cols]
    full_value = full_qkv[:, 2 * head_cols :]
    full_output = lax.all_gather(w_output.astype(bf16), "dp", axis=1, tiled=True)
    full_up = lax.all_gather(w_up.astype(bf16), "dp", axis=0, tiled=True)
    full_down = lax.all_gather(w_down.astype(bf16), "dp", axis=1, tiled=True)

    mix_cols = mix_weights.reshape(4 * stored, row_tok).T
    def block_of(rows, k):
        return rows[k * own_tok : (k + 1) * own_tok]

    def blocks_of(rows):
        return [block_of(rows, k) for k in range(count)]

    shares = list(stream_sums(me, mix_cols, history, 0, 2, count))
    shares += stream_sums(me, mix_cols, history, 2, 2, count)
    stream_own, normed, lin, normed_rows = [], [], [], []
    for s in range(4):
        if s == 2:
            shares[2] = after(shares[2], normed[0])
        if s == 3:
            shares[3] = after(shares[3], normed[1])
        pieces = sum_line(blocks_of(shares[s]), count)
        if s < 3:
            own, norm = join_norm(pieces[0], pieces[1:], norm_gains[s])
            stream_own.append(own)
            normed.append(norm)
        else:
            residual = pieces
    for s, weight in enumerate((full_query, full_key, full_value)):
        rows = jnp.concatenate([total_of(b) for b in gather_line(normed[s], count)], axis=0)
        normed_rows.append(rows)
        lin.append(plain_dot(rows, weight))
    q_lin, k_lin, v_lin = lin[0], lin[1], lin[2].astype(bf16)

    seg_row = segments[0]
    place = places(seg_row)
    index = jnp.arange(row_tok, dtype=jnp.int32)
    ids = jnp.stack([seg_row, index, place])
    ids = jnp.concatenate(
        [lax.dynamic_slice_in_dim(ids, k * own_tok, own_tok, axis=1) for k in order], axis=1
    )
    half = HEAD_DIM // 2
    frequency = jnp.exp(
        jnp.arange(half, dtype=f32) * (-2.0 * math.log(10000.0) / HEAD_DIM)
    )
    angles = ids[2].astype(f32)[:, None] * frequency[None, :]
    cosine, sine = jnp.cos(angles), jnp.sin(angles)
    cosine = jnp.concatenate([cosine, cosine], axis=1)
    sine = jnp.concatenate([-sine, sine], axis=1)
    col_ids = ids[:2]
    row_ids = col_ids.T

    context, queries, keys, lse = attend(row_ids, col_ids, cosine, sine, q_lin, k_lin, v_lin)

    attn = return_blocks(
        [plain_dot(block_of(context, k), full_output).astype(bf16) for k in range(count)], count
    )
    hidden_in, mlp_norm = join_norm(residual[0], residual[1:] + attn, norm_gains[3])
    mlp_blocks = gather_blocks(mlp_norm, count)
    ups, actives, mlp = [], [], []
    for k in range(count):
        up_proj = plain_dot(mlp_blocks[k], full_up)
        active = gelu_exact(up_proj).astype(bf16)
        ups.append(up_proj)
        actives.append(active)
        mlp.append(plain_dot(active, full_down).astype(bf16))
        if k == 0:
            mlp_blocks[1] = after(mlp_blocks[1], mlp[0], *mlp_blocks[2:])
    block = hidden_in + add_blocks(return_blocks(mlp, count))

    next_mix, mixer_pull = jax.vjp(mixer, block, norm_gains[4], w_first, w_second)
    block_part, mixer_gain_grad, first_grad, second_grad = mixer_pull(mix_cotangent)
    block_grad = out_cotangent + block_part
    first_sum = lax.psum(first_grad, ("dp", "layer"))
    branch_blocks = gather_blocks(block_grad.astype(bf16), count)

    up_lows, mlp_backs = [], []
    for k in range(count):
        active_grad = dot_right_t(branch_blocks[k], full_down)
        up_low = jax.vjp(gelu_exact, ups[k])[1](active_grad)[0].astype(bf16)
        up_lows.append(up_low)
        mlp_backs.append(dot_right_t(up_low, full_up).astype(bf16))
        if k == 0:
            branch_blocks[1] = after(branch_blocks[1], mlp_backs[0], *branch_blocks[2:])
    returned = return_blocks(mlp_backs, count)
    branch_rows = jnp.concatenate(branch_blocks, axis=0)
    active_rows = after(jnp.concatenate(actives, axis=0), *mlp_backs)
    down_grad = dot_left_t(active_rows, branch_rows).astype(bf16)
    down_sum = lax.psum_scatter(down_grad, "dp", scatter_dimension=1, tiled=True)
    up_rows = after(jnp.concatenate(up_lows, axis=0), *mlp_backs)
    up_grad = dot_left_t(jnp.concatenate(mlp_blocks, axis=0), up_rows).astype(bf16)
    up_sum = lax.psum_scatter(up_grad, "dp", scatter_dimension=0, tiled=True)
    returned[1] = after(returned[1], down_grad, up_grad)
    hidden_low, mlp_gain_grad = norm_back(hidden_in, returned, norm_gains[3], block_grad)
    hidden_blocks = gather_blocks(hidden_low, count)
    hidden_rows = jnp.concatenate(hidden_blocks, axis=0)
    context_grad = dot_right_t(hidden_rows, full_output).astype(bf16)

    lin_grads = attend_back(
        row_ids, col_ids, cosine, sine, queries, keys, v_lin, lse, context_grad
    )
    lin_grads = [after(lin_grads[0], down_sum), lin_grads[1], lin_grads[2]]

    weights = (full_query, full_key, full_value)
    parts = [dot_right_t(lin_grads[s], weights[s]).astype(bf16) for s in range(3)]
    gain_grads, stream_blocks, early = [], [], None
    for s in range(3):
        share = parts[s]
        if s == 2:
            share = after(share, gained[0])
        gained = norm_back(stream_own[s], sum_line(blocks_of(share), count), norm_gains[s])
        gain_grads.append(gained[1])
        early = gained[0] if early is None else early
        if s < 2:
            stream_blocks.append(gather_line(gained[0], count))
        else:
            stream_blocks.append([[b] for b in gather_blocks(gained[0], count)])
    stream_blocks.append([[b] for b in hidden_blocks])

    held_rows = after(hidden_rows, early)
    output_grad = dot_left_t(context, held_rows).astype(bf16)
    output_sum = lax.psum_scatter(output_grad, "dp", scatter_dimension=1, tiled=True)
    qkv_grad = jnp.concatenate(
        [
            dot_left_t(normed_rows[s], after(lin_grads[s], early)).astype(bf16)
            for s in range(3)
        ],
        axis=1,
    )
    qkv_sum = lax.psum_scatter(qkv_grad, "dp", scatter_dimension=0, tiled=True)
    gain_rows = jnp.stack(gain_grads + [mlp_gain_grad, mixer_gain_grad])
    gains_sum, second_sum = lax.psum((gain_rows, second_grad), ("dp", "layer"))

    so_far = None
    for k in range(count):
        if k == 0:
            stream_blocks[2][0][0] = after(stream_blocks[2][0][0], first_sum, gains_sum)
        so_far = history_block(
            order[k].astype(jnp.int32).reshape(1),
            mix_cols,
            history,
            [stream_blocks[s][k] for s in range(4)],
            so_far,
        )
    history_grad, mix_back = so_far
    mix_grad = mix_back.T.reshape(4, stored, row_tok)

    qkv_sum = qkv_sum.astype(f32)
    return (
        block.astype(bf16),
        next_mix,
        history_grad,
        mix_grad,
        qkv_sum[:, :head_cols],
        qkv_sum[:, head_cols : 2 * head_cols],
        qkv_sum[:, 2 * head_cols :],
        output_sum.astype(f32),
        up_sum.astype(f32),
        down_sum.astype(f32),
        gains_sum,
        first_sum,
        second_sum,
    )


def solution(mesh):
    placed = (
        P("layer", "dp", None),
        P(None, "layer", "dp"),
        P("dp", None),
        P("dp", "layer"),
        P("dp", "layer"),
        P("dp", "layer"),
        P("layer", "dp"),
        P("dp", "layer"),
        P("layer", "dp"),
        P(),
        P(),
        P(),
        P(("dp", "layer"), None),
        P(("dp", "layer"), None),
    )
    return jax.shard_map(
        local,
        mesh=mesh,
        in_specs=placed,
        out_specs=(
            P(("dp", "layer"), None),
            P(("dp", "layer"), None),
            P("layer", "dp", None),
            P(None, "layer", "dp"),
            P("dp", "layer"),
            P("dp", "layer"),
            P("dp", "layer"),
            P("layer", "dp"),
            P("dp", "layer"),
            P("layer", "dp"),
            P(),
            P(),
            P(),
        ),
        check_vma=False,
    )
```

time: 1800 us -> 1020 us (0.57)
  waiting for transfers between devices: 1380 us -> 367 us
  starting transfers between devices: 2.35 us -> 269 us
  matrix products: 221 us -> 142 us
  Pallas kernels: 0 us -> 73.2 us
    unnamed x24 -> x9, waiting for transfers between devices: 561 us -> 0.15 us
    reduce_scatter x10 -> x4, waiting for transfers between devices: 512 us -> 0.03 us  [the longest x1 0.02 us: local(): lax.psum_scatter(down_grad, 'dp', scatter_dimension=1, tiled=True)]
    ppermute x0 -> x93, waiting for transfers between devices: none -> 367 us  [the longest x9 108 us: return_blocks(): lax.ppermute(blocks[k], 'layer', [(i, (i - k) % count) for i in range(cou...]
    all_gather x11 -> x4, waiting for transfers between devices: 309 us -> 0.03 us  [the longest x1 0.02 us: local(): lax.all_gather(w_output.astype(bf16), 'dp', axis=1, tiled=True)]
    ppermute x0 -> x93, starting transfers between devices: none -> 268 us  [the longest x21 121 us: sum_line(): up = lax.ppermute(up, 'layer', [(i, i + 1) for i in range(k)])]
    dot_general x17 -> x15, matrix products: 129 us -> 53.9 us  [plain_dot(): return jnp.dot(left, right, preferred_element_type=f32)]
    pallas_call x0 -> x30, Pallas kernels: none -> 73.2 us  [the longest x4 21.8 us: history_block(): pl.pallas_call(lambda *refs: history_kernel(*refs, stored=stored, counts=...]
    add x4 -> x30, other arithmetic: 0.03 us -> 30.2 us  [the longest x9 14.9 us: total_of(): total = total + piece]
  transfers between devices with their start and end apart: 23 -> 102, of which waited for: 19 -> 38; matrix products, arithmetic and copies ran while one was open for 12% -> 17% of each run, Pallas kernels for 0% -> 7%
where the time goes in v1:
time: 1020 us; the launch traced here: 1010 us
  waiting for transfers between devices  367 us (36%)
  starting transfers between devices  269 us (26%)
  matrix products  142 us (14%)
  Pallas kernels  73.2 us (7%)
  other arithmetic  66.1 us (6%)
  blocking collectives  40.1 us (4%)
  local copies, waits for them, and re-layouts  34.7 us (3%)
  between operations  16.5 us (2%)
    ppermute x21, starting transfers between devices, sum_line(): up = lax.ppermute(up, 'layer', [(i, i + 1) for i in range(k)])  121 us
    ppermute x9, waiting for transfers between devices, return_blocks(): lax.ppermute(blocks[k], 'layer', [(i, (i - k) % count) for i in range(cou...  108 us
    ppermute x21, waiting for transfers between devices, sum_line(): up = lax.ppermute(up, 'layer', [(i, i + 1) for i in range(k)])  103 us
    ppermute x12, waiting for transfers between devices, gather_blocks(): lax.ppermute(block, 'layer', [(i, (i + k) % count) for i in range(count)])  98.3 us
    dot_general x15, matrix products, plain_dot(): return jnp.dot(left, right, preferred_element_type=f32)  53.9 us
    dot_general x12, matrix products, dot_right_t(): lax.dot_general(left, right, (((1,), (1,)), ((), ())), preferred_element_...  48.4 us
    ppermute x15, starting transfers between devices, gather_line(): lax.ppermute(ups[-1], 'layer', [(i, i + 1) for i in range(k - 1, count -...  41.9 us
    ppermute x15, waiting for transfers between devices, gather_line(): lax.ppermute(downs[-1], 'layer', [(i + 1, i) for i in range(count - k)])  41.7 us
  transfers between devices with their start and end apart: 102, of which 38 were waited for; matrix products, arithmetic and copies ran while one was open for 17% of the time, Pallas kernels for 7%

profile of v1, /device:TPU:0, one launch (start us, length us, event | category | flops | bytes accessed | tf_op | source)
XLA Modules:
  0.0 1008.9 jit_solution(9651731562118901492)
XLA Ops:
  16.8 7.7 shard_map.238
  25.3 4.9 collective-permute-start.12
  31.7 9.6 collective-permute-done.12
  45.9 6.8 collective-permute-start
  64.1 5.2 collective-permute-done
  70.2 10.9 %collective-permute-start.1 = (bf16[128,2048]{1,0:T(8,128)(2,1)}, bf16[128,2048]{1,0:T(8,128)(2,1)}, u32[]{:S(2)}, u32[]{:S(2)}) collective-permute-start(bf16[128,2048]{1,0:T(8,128)(2,1)} %slice_add_fusion.13), channel_id=1, source_target_pairs={{0,1},{1,2},{4,5},{5,6},{8,9},{9,10},{12,13},{13,14},{16,17},{17,1... | collective-permute-start | bytes 1572872 | tf_op jit(solution)/shard_map/ppermute | solution.py:66
  81.1 7.3 shard_map.237
  103.6 5.4 collective-permute-start.30
  109.7 5.0 collective-permute-done.5.refs_1_
  126.8 5.6 collective-permute-start.31
  132.6 7.8 collective-permute-start.24
  143.6 4.6 collective-permute-start.18
  148.3 14.7 %collective-permute-start.6 = (bf16[128,2048]{1,0:T(8,128)(2,1)S(1)}, bf16[128,2048]{1,0:T(8,128)(2,1)S(1)}, u32[]{:S(2)}, u32[]{:S(2)}) collective-permute-start(bf16[128,2048]{1,0:T(8,128)(2,1)S(1)} %get-tuple-element.167), channel_id=1, source_target_pairs={{0,1},{4,5},{8,9},{12,13},{16,17},{20,21},{24,25},{28,29}} | collective-permute-start | bytes 1572872 | tf_op jit(solution)/shard_map/ppermute | solution.py:66
  165.7 4.6 collective-permute-start.32
  172.4 12.3 %collective-permute-done.32.refs_0_ = bf16[128,2048]{1,0:T(8,128)(2,1)S(1)} collective-permute-done((bf16[128,2048]{1,0:T(8,128)(2,1)S(1)}, bf16[128,2048]{1,0:T(8,128)(2,1)S(1)}, u32[]{:S(2)}, u32[]{:S(2)}) %collective-permute-start.32) | collective-permute-done | bytes 524320 | tf_op jit(solution)/shard_map/ppermute | solution.py:66
  190.8 9.7 collective-permute-start.36
  229.1 6.4 collective-permute-done.38
  252.8 5.1 collective-permute-done.39
  270.8 7.5 shard_map.244
  280.6 8.5 collective-permute-start.42
  291.2 10.2 %collective-permute-done.42.refs_3_ = bf16[128,2048]{1,0:T(8,128)(2,1)S(1)} collective-permute-done((bf16[128,2048]{1,0:T(8,128)(2,1)S(1)}, bf16[128,2048]{1,0:T(8,128)(2,1)S(1)}, u32[]{:S(2)}, u32[]{:S(2)}) %collective-permute-start.42) | collective-permute-done | bytes 524320 | tf_op jit(solution)/shard_map/ppermute | solution.py:92
  301.5 29.0 %collective-permute-done.43.refs_4_ = bf16[128,2048]{1,0:T(8,128)(2,1)S(1)} collective-permute-done((bf16[128,2048]{1,0:T(8,128)(2,1)S(1)}, bf16[128,2048]{1,0:T(8,128)(2,1)S(1)}, u32[]{:S(2)}, u32[]{:S(2)}) %collective-permute-start.43) | collective-permute-done | bytes 524320 | tf_op jit(solution)/shard_map/ppermute | solution.py:92
  337.6 8.3 multiply_convert_fusion.3
  346.0 5.4 convolution_convert_fusion.16.refs_1_
  351.4 12.0 %collective-permute-done.46.refs_2_ = bf16[128,2048]{1,0:T(8,128)(2,1)S(1)} collective-permute-done((bf16[128,2048]{1,0:T(8,128)(2,1)}, bf16[128,2048]{1,0:T(8,128)(2,1)S(1)}, u32[]{:S(2)}, u32[]{:S(2)}) %collective-permute-start.46) | collective-permute-done | bytes 524320 | tf_op jit(solution)/shard_map/ppermute | solution.py:49
  365.0 8.4 multiply_convert_fusion.2
  373.4 4.8 convolution_convert_fusion.15
  378.2 17.2 %collective-permute-start.48 = (bf16[128,2048]{1,0:T(8,128)(2,1)S(1)}, bf16[128,2048]{1,0:T(8,128)(2,1)S(1)}, u32[]{:S(2)}, u32[]{:S(2)}) collective-permute-start(bf16[128,2048]{1,0:T(8,128)(2,1)S(1)} %convolution_convert_fusion.15), channel_id=1, source_target_pairs={{0,3},{1,0},{2,1},{3,2},{4,7},{5,4},{6,5},{7,6},{8,11},{9,8},{10,9... | collective-permute-start | bytes 1572872 | tf_op jit(solution)/shard_map/ppermute | solution.py:92
  395.3 7.7 multiply_convert_fusion.1
  412.9 26.2 %collective-permute-done.49 = bf16[128,2048]{1,0:T(8,128)(2,1)S(1)} collective-permute-done((bf16[128,2048]{1,0:T(8,128)(2,1)S(1)}, bf16[128,2048]{1,0:T(8,128)(2,1)S(1)}, u32[]{:S(2)}, u32[]{:S(2)}) %collective-permute-start.49) | collective-permute-done | bytes 524320 | tf_op jit(solution)/shard_map/ppermute | solution.py:92
  464.0 28.8 %collective-permute-done.52.refs_2_ = bf16[128,2048]{1,0:T(8,128)(2,1)S(1)} collective-permute-done((bf16[128,2048]{1,0:T(8,128)(2,1)S(1)}, bf16[128,2048]{1,0:T(8,128)(2,1)S(1)}, u32[]{:S(2)}, u32[]{:S(2)}) %collective-permute-start.52) | collective-permute-done | bytes 524320 | tf_op jit(solution)/shard_map/ppermute | solution.py:49
  500.0 7.1 add_convert_fusion.2
  507.9 7.1 convolution_convert_fusion.11.refs_2_
  515.0 10.1 %convolution_convert_fusion.1.refs_1_ = bf16[2048,2048]{1,0:T(8,128)(2,1)} fusion(bf16[512,2048]{1,0:T(8,128)(2,1)} %shard_map.248, bf16[128,2048]{1,0:T(8,128)(2,1)} %copy-done.97, bf16[128,2048]{1,0:T(8,128)(2,1)} %copy-done.98, bf16[128,2048]{1,0:T(8,128)(2,1)} %shard_map.247, bf16[128,2048]{1,0:T(8,128)(2,1)} %copy-done.96), kind=kOutput, calls=%fused_computation.1 | convolution fusion | flops 4307550208 | bytes 12582912 | tf_op jit(solution)/shard_map/dot_general | solution.py:40
  533.7 10.3 %convolution_convert_fusion.refs_2_ = bf16[2048,2048]{1,0:T(8,128)(2,1)} fusion(bf16[512,2048]{1,0:T(8,128)(2,1)} %shard_map.249, bf16[128,2048]{1,0:T(8,128)(2,1)S(1)} %copy-done.85, bf16[128,2048]{1,0:T(8,128)(2,1)S(1)} %copy-done.82, bf16[128,2048]{1,0:T(8,128)(2,1)} %shard_map.246, bf16[128,2048]{1,0:T(8,128)(2,1)} %get-tuple-element.57), kind=kOutput, calls=%fused_computation | convolution fusion | flops 4307550208 | bytes 12582912 | tf_op jit(solution)/shard_map/dot_general | solution.py:40
  546.2 24.1 %collective-permute-done.54.refs_0_ = bf16[128,2048]{1,0:T(8,128)(2,1)S(1)} collective-permute-done((bf16[128,2048]{1,0:T(8,128)(2,1)}, bf16[128,2048]{1,0:T(8,128)(2,1)S(1)}, u32[]{:S(2)}, u32[]{:S(2)}) %collective-permute-start.54) | collective-permute-done | bytes 524320 | tf_op jit(solution)/shard_map/ppermute | solution.py:92
  571.1 18.5 %collective-permute-done.55.refs_4_ = bf16[128,2048]{1,0:T(8,128)(2,1)} collective-permute-done((bf16[128,2048]{1,0:T(8,128)(2,1)}, bf16[128,2048]{1,0:T(8,128)(2,1)}, u32[]{:S(2)}, u32[]{:S(2)}) %collective-permute-start.55) | collective-permute-done | bytes 524320 | tf_op jit(solution)/shard_map/ppermute | solution.py:92
  599.2 12.9 %collective-permute-done.57.refs_8_ = bf16[128,2048]{1,0:T(8,128)(2,1)S(1)} collective-permute-done((bf16[128,2048]{1,0:T(8,128)(2,1)S(1)}, bf16[128,2048]{1,0:T(8,128)(2,1)S(1)}, u32[]{:S(2)}, u32[]{:S(2)}) %collective-permute-start.57) | collective-permute-done | bytes 524320 | tf_op jit(solution)/shard_map/ppermute | solution.py:49
  612.1 23.4 %collective-permute-done.58.refs_8_ = bf16[128,2048]{1,0:T(8,128)(2,1)S(1)} collective-permute-done((bf16[128,2048]{1,0:T(8,128)(2,1)S(1)}, bf16[128,2048]{1,0:T(8,128)(2,1)S(1)}, u32[]{:S(2)}, u32[]{:S(2)}) %collective-permute-start.58) | collective-permute-done | bytes 524320 | tf_op jit(solution)/shard_map/ppermute | solution.py:49
  637.7 7.8 shard_map.252
  649.5 16.0 %collective-permute-start.60 = (bf16[128,2048]{1,0:T(8,128)(2,1)S(1)}, bf16[128,2048]{1,0:T(8,128)(2,1)S(1)}, u32[]{:S(2)}, u32[]{:S(2)}) collective-permute-start(bf16[128,2048]{1,0:T(8,128)(2,1)S(1)} %get-tuple-element.152), channel_id=1, source_target_pairs={{0,1},{4,5},{8,9},{12,13},{16,17},{20,21},{24,25},{28,29}} | collective-permute-start | bytes 1572872 | tf_op jit(solution)/shard_map/ppermute | solution.py:66
  666.2 10.9 %collective-permute-done.60 = bf16[128,2048]{1,0:T(8,128)(2,1)S(1)} collective-permute-done((bf16[128,2048]{1,0:T(8,128)(2,1)S(1)}, bf16[128,2048]{1,0:T(8,128)(2,1)S(1)}, u32[]{:S(2)}, u32[]{:S(2)}) %collective-permute-start.60) | collective-permute-done | bytes 524320 | tf_op jit(solution)/shard_map/ppermute | solution.py:66
  681.8 10.7 %collective-permute-done.61 = bf16[128,2048]{1,0:T(8,128)(2,1)S(1)} collective-permute-done((bf16[128,2048]{1,0:T(8,128)(2,1)S(1)}, bf16[128,2048]{1,0:T(8,128)(2,1)S(1)}, u32[]{:S(2)}, u32[]{:S(2)}) %collective-permute-start.61) | collective-permute-done | bytes 524320 | tf_op jit(solution)/shard_map/ppermute | solution.py:66
  698.4 8.5 collective-permute-done.62.refs_3_
  737.0 11.2 %pad_maximum_fusion = bf16[2048,1536]{0,1:T(8,128)(2,1)} fusion(bf16[2048,512]{0,1:T(8,128)(2,1)S(1)} %convolution_convert_fusion.3, bf16[2048,512]{0,1:T(8,128)(2,1)S(1)} %convolution_convert_fusion.4, bf16[2048,512]{0,1:T(8,128)(2,1)S(1)} %convolution_convert_fusion.5), kind=kLoop, calls=%fused_computation.2 | loop fusion | flops 18874368 | bytes 12582912 | tf_op jit(solution)/shard_map/concatenate | solution.py:522
  755.1 7.5 collective-permute-done.70
  767.3 7.3 collective-permute-done.71
  774.7 5.0 collective-permute-start.72
  781.0 5.4 collective-permute-done.72.refs_3_
  786.4 4.9 collective-permute-done.75.refs_4_
  802.6 7.5 collective-permute-done.80
  816.1 4.6 collective-permute-start.76
  820.7 6.4 collective-permute-done.81
  842.8 6.8 collective-permute-done.82.refs_3_
  854.3 5.3 collective-permute-done.69.refs_4_
  861.7 11.5 %collective-permute-done.88.refs_6_ = bf16[128,2048]{1,0:T(8,128)(2,1)} collective-permute-done((bf16[128,2048]{1,0:T(8,128)(2,1)S(1)}, bf16[128,2048]{1,0:T(8,128)(2,1)}, u32[]{:S(2)}, u32[]{:S(2)}) %collective-permute-start.88) | collective-permute-done | bytes 524320 | tf_op jit(solution)/shard_map/ppermute | solution.py:58
  873.3 8.3 collective-permute-start.89
  883.9 11.1 %collective-permute-start.92 = (bf16[128,2048]{1,0:T(8,128)(2,1)}, bf16[128,2048]{1,0:T(8,128)(2,1)}, u32[]{:S(2)}, u32[]{:S(2)}) collective-permute-start(bf16[128,2048]{1,0:T(8,128)(2,1)} %get-tuple-element.70.refs_0_), channel_id=1, source_target_pairs={{0,1},{1,2},{2,3},{3,0},{4,5},{5,6},{6,7},{7,4},{8,9},{9,10},{10,1... | collective-permute-start | bytes 1572872 | tf_op jit(solution)/shard_map/ppermute | solution.py:49
  900.3 19.4 %collective-permute-done.89.refs_7_ = bf16[128,2048]{1,0:T(8,128)(2,1)S(1)} collective-permute-done((bf16[128,2048]{1,0:T(8,128)(2,1)}, bf16[128,2048]{1,0:T(8,128)(2,1)S(1)}, u32[]{:S(2)}, u32[]{:S(2)}) %collective-permute-start.89) | collective-permute-done | bytes 524320 | tf_op jit(solution)/shard_map/ppermute | solution.py:49
  932.0 40.1 %all-reduce = (f32[5,2048]{1,0:T(8,128)}, f32[68,68]{1,0:T(8,128)}) all-reduce(f32[5,2048]{1,0:T(8,128)S(1)} %stack.10, f32[68,68]{1,0:T(8,128)S(1)} %fusion.72), channel_id=1, replica_groups=mesh['dp'=8,'layer'=4] {'dp','layer'}, use_global_device_ids=true, to_apply=%region_7.8 | all-reduce | flops 14864 | bytes 118912 | tf_op jit(solution)/shard_map/psum | solution.py:531
  973.2 5.2 shard_map.259
  978.5 5.5 shard_map.260
  984.0 5.7 shard_map.261
  989.7 5.4 shard_map.262
  (537 shorter events, 333.0 us)
Async XLA Ops:
  7.2 254.7 %all-gather.5.cloned.1.call-start = ((), (), s32[]{:S(2)}) async-start(), calls=%async_computation.4 | async-start | bytes 7077888 | tf_op jit(solution)/shard_map/all_gather | solution.py:397
  11.7 266.6 %all-gather.7.cloned.1.call-start = ((), (), s32[]{:S(2)}) async-start(), calls=%async_computation.5 | async-start | bytes 2359296 | tf_op jit(solution)/shard_map/all_gather | solution.py:402
  12.6 325.1 %all-gather.9.cloned.1.call-start = ((), (), s32[]{:S(2)}) async-start(), calls=%async_computation.6 | async-start | bytes 9437184 | tf_op jit(solution)/shard_map/all_gather | solution.py:403
  13.8 332.2 %all-gather.11.cloned.1.call-start = ((), (), s32[]{:S(2)}) async-start(), calls=%async_computation.7 | async-start | bytes 9437184 | tf_op jit(solution)/shard_map/all_gather | solution.py:404
  16.6 629.0 %reduce-scatter.5.cloned.1.call-start = ((), (), s32[]{:S(2)}) async-start(), calls=%async_computation.8 | async-start | bytes 9437184 | tf_op jit(solution)/shard_map/reduce_scatter | solution.py:488
  31.0 23.1 %collective-permute-start.16 = (bf16[128,2048]{1,0:T(8,128)(2,1)S(1)}, bf16[128,2048]{1,0:T(8,128)(2,1)S(1)}, u32[]{:S(2)}, u32[]{:S(2)}) collective-permute-start(bf16[128,2048]{1,0:T(8,128)(2,1)S(1)} %get-tuple-element.161), channel_id=1, source_target_pairs={{2,1},{3,2},{6,5},{7,6},{10,9},{11,10},{14,13},{15,14},{18,17},{19... | collective-permute-start | bytes 1572872 | tf_op jit(solution)/shard_map/ppermute | solution.py:68
  45.9 23.5 %collective-permute-start = (bf16[128,2048]{1,0:T(8,128)(2,1)S(1)}, bf16[128,2048]{1,0:T(8,128)(2,1)S(1)}, u32[]{:S(2)}, u32[]{:S(2)}) collective-permute-start(bf16[128,2048]{1,0:T(8,128)(2,1)S(1)} %get-tuple-element.172), channel_id=1, source_target_pairs={{0,1},{4,5},{8,9},{12,13},{16,17},{20,21},{24,25},{28,29}} | collective-permute-start | bytes 1572872 | tf_op jit(solution)/shard_map/ppermute | solution.py:66
  52.6 44.0 %collective-permute-start.4 = (bf16[128,2048]{1,0:T(8,128)(2,1)S(1)}, bf16[128,2048]{1,0:T(8,128)(2,1)}, u32[]{:S(2)}, u32[]{:S(2)}) collective-permute-start(bf16[128,2048]{1,0:T(8,128)(2,1)S(1)} %get-tuple-element.171), channel_id=1, source_target_pairs={{2,1},{3,2},{6,5},{7,6},{10,9},{11,10},{14,13},{15,14},{18,17},{19... | collective-permute-start | bytes 1572872 | tf_op jit(solution)/shard_map/ppermute | solution.py:68
  58.2 32.9 %collective-permute-start.14 = (bf16[128,2048]{1,0:T(8,128)(2,1)S(1)}, bf16[128,2048]{1,0:T(8,128)(2,1)S(1)}, u32[]{:S(2)}, u32[]{:S(2)}) collective-permute-start(bf16[128,2048]{1,0:T(8,128)(2,1)S(1)} %get-tuple-element.159), channel_id=1, source_target_pairs={{0,1},{1,2},{2,3},{4,5},{5,6},{6,7},{8,9},{9,10},{10,11},{12,13},{... | collective-permute-start | bytes 1572872 | tf_op jit(solution)/shard_map/ppermute | solution.py:66
  62.8 28.3 %collective-permute-start.17 = (bf16[128,2048]{1,0:T(8,128)(2,1)S(1)}, bf16[128,2048]{1,0:T(8,128)(2,1)S(1)}, u32[]{:S(2)}, u32[]{:S(2)}) collective-permute-start(bf16[128,2048]{1,0:T(8,128)(2,1)S(1)} %get-tuple-element.158), channel_id=1, source_target_pairs={{1,0},{2,1},{3,2},{5,4},{6,5},{7,6},{9,8},{10,9},{11,10},{13,12},{... | collective-permute-start | bytes 1572872 | tf_op jit(solution)/shard_map/ppermute | solution.py:68
  70.2 26.5 %collective-permute-start.1 = (bf16[128,2048]{1,0:T(8,128)(2,1)}, bf16[128,2048]{1,0:T(8,128)(2,1)}, u32[]{:S(2)}, u32[]{:S(2)}) collective-permute-start(bf16[128,2048]{1,0:T(8,128)(2,1)} %slice_add_fusion.13), channel_id=1, source_target_pairs={{0,1},{1,2},{4,5},{5,6},{8,9},{9,10},{12,13},{13,14},{16,17},{17,1... | collective-permute-start | bytes 1572872 | tf_op jit(solution)/shard_map/ppermute | solution.py:66
  118.4 25.3 %collective-permute-start.25 = (bf16[128,2048]{1,0:T(8,128)(2,1)}, bf16[128,2048]{1,0:T(8,128)(2,1)}, u32[]{:S(2)}, u32[]{:S(2)}) collective-permute-start(bf16[128,2048]{1,0:T(8,128)(2,1)} %get-tuple-element.50.refs_1_), channel_id=1, source_target_pairs={{1,0},{2,1},{3,2},{5,4},{6,5},{7,6},{9,8},{10,9},{11,10},{13,12},{... | collective-permute-start | bytes 1572872 | tf_op jit(solution)/shard_map/ppermute | solution.py:58
  123.3 24.9 %collective-permute-start.34 = (bf16[128,2048]{1,0:T(8,128)(2,1)}, bf16[128,2048]{1,0:T(8,128)(2,1)}, u32[]{:S(2)}, u32[]{:S(2)}) collective-permute-start(bf16[128,2048]{1,0:T(8,128)(2,1)} %get-tuple-element.156), channel_id=1, source_target_pairs={{2,1},{3,2},{6,5},{7,6},{10,9},{11,10},{14,13},{15,14},{18,17},{19... | collective-permute-start | bytes 1572872 | tf_op jit(solution)/shard_map/ppermute | solution.py:68
  126.8 36.2 %collective-permute-start.31 = (bf16[128,2048]{1,0:T(8,128)(2,1)}, bf16[128,2048]{1,0:T(8,128)(2,1)}, u32[]{:S(2)}, u32[]{:S(2)}) collective-permute-start(bf16[128,2048]{1,0:T(8,128)(2,1)} %slice_add_fusion.7), channel_id=1, source_target_pairs={{0,1},{1,2},{4,5},{5,6},{8,9},{9,10},{12,13},{13,14},{16,17},{17,1... | collective-permute-start | bytes 1572872 | tf_op jit(solution)/shard_map/ppermute | solution.py:66
  132.6 33.1 %collective-permute-start.24 = (bf16[128,2048]{1,0:T(8,128)(2,1)}, bf16[128,2048]{1,0:T(8,128)(2,1)S(1)}, u32[]{:S(2)}, u32[]{:S(2)}) collective-permute-start(bf16[128,2048]{1,0:T(8,128)(2,1)} %get-tuple-element.50.refs_1_), channel_id=1, source_target_pairs={{0,1},{1,2},{2,3},{4,5},{5,6},{6,7},{8,9},{9,10},{10,11},{12,13},{... | collective-permute-start | bytes 1572872 | tf_op jit(solution)/shard_map/ppermute | solution.py:57
  140.4 29.9 %collective-permute-start.19 = (bf16[128,2048]{1,0:T(8,128)(2,1)S(1)}, bf16[128,2048]{1,0:T(8,128)(2,1)S(1)}, u32[]{:S(2)}, u32[]{:S(2)}) collective-permute-start(bf16[128,2048]{1,0:T(8,128)(2,1)S(1)} %copy-done.26), channel_id=1, source_target_pairs={{1,0},{2,1},{3,2},{5,4},{6,5},{7,6},{9,8},{10,9},{11,10},{13,12},{... | collective-permute-start | bytes 1572872 | tf_op jit(solution)/shard_map/ppermute | solution.py:58
  143.6 28.1 %collective-permute-start.18 = (bf16[128,2048]{1,0:T(8,128)(2,1)S(1)}, bf16[128,2048]{1,0:T(8,128)(2,1)S(1)}, u32[]{:S(2)}, u32[]{:S(2)}) collective-permute-start(bf16[128,2048]{1,0:T(8,128)(2,1)S(1)} %copy-done.26), channel_id=1, source_target_pairs={{0,1},{1,2},{2,3},{4,5},{5,6},{6,7},{8,9},{9,10},{10,11},{12,13},{... | collective-permute-start | bytes 1572872 | tf_op jit(solution)/shard_map/ppermute | solution.py:57
  148.3 42.5 %collective-permute-start.6 = (bf16[128,2048]{1,0:T(8,128)(2,1)S(1)}, bf16[128,2048]{1,0:T(8,128)(2,1)S(1)}, u32[]{:S(2)}, u32[]{:S(2)}) collective-permute-start(bf16[128,2048]{1,0:T(8,128)(2,1)S(1)} %get-tuple-element.167), channel_id=1, source_target_pairs={{0,1},{4,5},{8,9},{12,13},{16,17},{20,21},{24,25},{28,29}} | collective-permute-start | bytes 1572872 | tf_op jit(solution)/shard_map/ppermute | solution.py:66
  163.0 26.4 %collective-permute-start.26 = (bf16[128,2048]{1,0:T(8,128)(2,1)}, bf16[128,2048]{1,0:T(8,128)(2,1)}, u32[]{:S(2)}, u32[]{:S(2)}) collective-permute-start(bf16[128,2048]{1,0:T(8,128)(2,1)} %collective-permute-done.25), channel_id=1, source_target_pairs={{1,0},{2,1},{5,4},{6,5},{9,8},{10,9},{13,12},{14,13},{17,16},{18,1... | collective-permute-start | bytes 1572872 | tf_op jit(solution)/shard_map/ppermute | solution.py:58
  171.7 30.2 %collective-permute-start.28 = (bf16[128,2048]{1,0:T(8,128)(2,1)S(1)}, bf16[128,2048]{1,0:T(8,128)(2,1)S(1)}, u32[]{:S(2)}, u32[]{:S(2)}) collective-permute-start(bf16[128,2048]{1,0:T(8,128)(2,1)S(1)} %collective-permute-done.24), channel_id=1, source_target_pairs={{1,2},{2,3},{5,6},{6,7},{9,10},{10,11},{13,14},{14,15},{17,18},{18... | collective-permute-start | bytes 1572872 | tf_op jit(solution)/shard_map/ppermute | solution.py:57
  189.5 22.9 %collective-permute-start.37 = (bf16[128,2048]{1,0:T(8,128)(2,1)S(1)}, bf16[128,2048]{1,0:T(8,128)(2,1)}, u32[]{:S(2)}, u32[]{:S(2)}) collective-permute-start(bf16[128,2048]{1,0:T(8,128)(2,1)S(1)} %get-tuple-element.54), channel_id=1, source_target_pairs={{1,0},{2,1},{3,2},{5,4},{6,5},{7,6},{9,8},{10,9},{11,10},{13,12},{... | collective-permute-start | bytes 1572872 | tf_op jit(solution)/shard_map/ppermute | solution.py:58
  190.8 22.9 %collective-permute-start.36 = (bf16[128,2048]{1,0:T(8,128)(2,1)S(1)}, bf16[128,2048]{1,0:T(8,128)(2,1)}, u32[]{:S(2)}, u32[]{:S(2)}) collective-permute-start(bf16[128,2048]{1,0:T(8,128)(2,1)S(1)} %get-tuple-element.54), channel_id=1, source_target_pairs={{0,1},{1,2},{2,3},{4,5},{5,6},{6,7},{8,9},{9,10},{10,11},{12,13},{... | collective-permute-start | bytes 1572872 | tf_op jit(solution)/shard_map/ppermute | solution.py:57
  202.0 25.0 %collective-permute-start.10 = (bf16[128,2048]{1,0:T(8,128)(2,1)}, bf16[128,2048]{1,0:T(8,128)(2,1)}, u32[]{:S(2)}, u32[]{:S(2)}) collective-permute-start(bf16[128,2048]{1,0:T(8,128)(2,1)} %get-tuple-element.166), channel_id=1, source_target_pairs={{2,1},{3,2},{6,5},{7,6},{10,9},{11,10},{14,13},{15,14},{18,17},{19... | collective-permute-start | bytes 1572872 | tf_op jit(solution)/shard_map/ppermute | solution.py:68
  203.4 25.0 %collective-permute-start.7 = (bf16[128,2048]{1,0:T(8,128)(2,1)}, bf16[128,2048]{1,0:T(8,128)(2,1)}, u32[]{:S(2)}, u32[]{:S(2)}) collective-permute-start(bf16[128,2048]{1,0:T(8,128)(2,1)} %slice_add_fusion.9), channel_id=1, source_target_pairs={{0,1},{1,2},{4,5},{5,6},{8,9},{9,10},{12,13},{13,14},{16,17},{17,1... | collective-permute-start | bytes 1572872 | tf_op jit(solution)/shard_map/ppermute | solution.py:66
  212.4 23.2 %collective-permute-start.38 = (bf16[128,2048]{1,0:T(8,128)(2,1)}, bf16[128,2048]{1,0:T(8,128)(2,1)}, u32[]{:S(2)}, u32[]{:S(2)}) collective-permute-start(bf16[128,2048]{1,0:T(8,128)(2,1)} %collective-permute-done.37), channel_id=1, source_target_pairs={{1,0},{2,1},{5,4},{6,5},{9,8},{10,9},{13,12},{14,13},{17,16},{18,1... | collective-permute-start | bytes 1572872 | tf_op jit(solution)/shard_map/ppermute | solution.py:58
  213.7 23.1 %collective-permute-start.40 = (bf16[128,2048]{1,0:T(8,128)(2,1)}, bf16[128,2048]{1,0:T(8,128)(2,1)}, u32[]{:S(2)}, u32[]{:S(2)}) collective-permute-start(bf16[128,2048]{1,0:T(8,128)(2,1)} %collective-permute-done.36), channel_id=1, source_target_pairs={{1,2},{2,3},{5,6},{6,7},{9,10},{10,11},{13,14},{14,15},{17,18},{18... | collective-permute-start | bytes 1572872 | tf_op jit(solution)/shard_map/ppermute | solution.py:57
  235.5 22.4 %collective-permute-start.39 = (bf16[128,2048]{1,0:T(8,128)(2,1)}, bf16[128,2048]{1,0:T(8,128)(2,1)S(1)}, u32[]{:S(2)}, u32[]{:S(2)}) collective-permute-start(bf16[128,2048]{1,0:T(8,128)(2,1)} %collective-permute-done.38), channel_id=1, source_target_pairs={{1,0},{5,4},{9,8},{13,12},{17,16},{21,20},{25,24},{29,28}} | collective-permute-start | bytes 1572872 | tf_op jit(solution)/shard_map/ppermute | solution.py:58
  236.8 23.0 %collective-permute-start.41 = (bf16[128,2048]{1,0:T(8,128)(2,1)}, bf16[128,2048]{1,0:T(8,128)(2,1)S(1)}, u32[]{:S(2)}, u32[]{:S(2)}) collective-permute-start(bf16[128,2048]{1,0:T(8,128)(2,1)} %collective-permute-done.40), channel_id=1, source_target_pairs={{2,3},{6,7},{10,11},{14,15},{18,19},{22,23},{26,27},{30,31}} | collective-permute-start | bytes 1572872 | tf_op jit(solution)/shard_map/ppermute | solution.py:57
  239.8 51.4 %collective-permute-start.11 = (bf16[128,2048]{1,0:T(8,128)(2,1)}, bf16[128,2048]{1,0:T(8,128)(2,1)S(1)}, u32[]{:S(2)}, u32[]{:S(2)}) collective-permute-start(bf16[128,2048]{1,0:T(8,128)(2,1)} %get-tuple-element.163), channel_id=1, source_target_pairs={{1,0},{2,1},{3,2},{5,4},{6,5},{7,6},{9,8},{10,9},{11,10},{13,12},{... | collective-permute-start | bytes 1572872 | tf_op jit(solution)/shard_map/ppermute | solution.py:68
  246.7 44.6 %collective-permute-start.8 = (bf16[128,2048]{1,0:T(8,128)(2,1)}, bf16[128,2048]{1,0:T(8,128)(2,1)S(1)}, u32[]{:S(2)}, u32[]{:S(2)}) collective-permute-start(bf16[128,2048]{1,0:T(8,128)(2,1)} %get-tuple-element.164), channel_id=1, source_target_pairs={{0,1},{1,2},{2,3},{4,5},{5,6},{6,7},{8,9},{9,10},{10,11},{12,13},{... | collective-permute-start | bytes 1572872 | tf_op jit(solution)/shard_map/ppermute | solution.py:66
  289.5 40.9 %collective-permute-start.43 = (bf16[128,2048]{1,0:T(8,128)(2,1)S(1)}, bf16[128,2048]{1,0:T(8,128)(2,1)S(1)}, u32[]{:S(2)}, u32[]{:S(2)}) collective-permute-start(bf16[128,2048]{1,0:T(8,128)(2,1)S(1)} %convolution_convert_fusion.18), channel_id=1, source_target_pairs={{0,2},{1,3},{2,0},{3,1},{4,6},{5,7},{6,4},{7,5},{8,10},{9,11},{10,... | collective-permute-start | bytes 1572872 | tf_op jit(solution)/shard_map/ppermute | solution.py:92
  290.1 40.4 %collective-permute-start.44 = (bf16[128,2048]{1,0:T(8,128)(2,1)S(1)}, bf16[128,2048]{1,0:T(8,128)(2,1)S(1)}, u32[]{:S(2)}, u32[]{:S(2)}) collective-permute-start(bf16[128,2048]{1,0:T(8,128)(2,1)S(1)} %convolution_convert_fusion.17), channel_id=1, source_target_pairs={{0,1},{1,2},{2,3},{3,0},{4,5},{5,6},{6,7},{7,4},{8,9},{9,10},{10,1... | collective-permute-start | bytes 1572872 | tf_op jit(solution)/shard_map/ppermute | solution.py:92
  333.4 30.0 %collective-permute-start.46 = (bf16[128,2048]{1,0:T(8,128)(2,1)}, bf16[128,2048]{1,0:T(8,128)(2,1)S(1)}, u32[]{:S(2)}, u32[]{:S(2)}) collective-permute-start(bf16[128,2048]{1,0:T(8,128)(2,1)} %get-tuple-element.57), channel_id=1, source_target_pairs={{0,2},{1,3},{2,0},{3,1},{4,6},{5,7},{6,4},{7,5},{8,10},{9,11},{10,... | collective-permute-start | bytes 1572872 | tf_op jit(solution)/shard_map/ppermute | solution.py:49
  333.4 30.5 %collective-permute-start.47 = (bf16[128,2048]{1,0:T(8,128)(2,1)}, bf16[128,2048]{1,0:T(8,128)(2,1)S(1)}, u32[]{:S(2)}, u32[]{:S(2)}) collective-permute-start(bf16[128,2048]{1,0:T(8,128)(2,1)} %get-tuple-element.57), channel_id=1, source_target_pairs={{0,3},{1,0},{2,1},{3,2},{4,7},{5,4},{6,5},{7,6},{8,11},{9,8},{10,9... | collective-permute-start | bytes 1572872 | tf_op jit(solution)/shard_map/ppermute | solution.py:49
  378.2 34.7 %collective-permute-start.48 = (bf16[128,2048]{1,0:T(8,128)(2,1)S(1)}, bf16[128,2048]{1,0:T(8,128)(2,1)S(1)}, u32[]{:S(2)}, u32[]{:S(2)}) collective-permute-start(bf16[128,2048]{1,0:T(8,128)(2,1)S(1)} %convolution_convert_fusion.15), channel_id=1, source_target_pairs={{0,3},{1,0},{2,1},{3,2},{4,7},{5,4},{6,5},{7,6},{8,11},{9,8},{10,9... | collective-permute-start | bytes 1572872 | tf_op jit(solution)/shard_map/ppermute | solution.py:92
  404.3 34.8 %collective-permute-start.49 = (bf16[128,2048]{1,0:T(8,128)(2,1)S(1)}, bf16[128,2048]{1,0:T(8,128)(2,1)S(1)}, u32[]{:S(2)}, u32[]{:S(2)}) collective-permute-start(bf16[128,2048]{1,0:T(8,128)(2,1)S(1)} %convolution_convert_fusion.14), channel_id=1, source_target_pairs={{0,2},{1,3},{2,0},{3,1},{4,6},{5,7},{6,4},{7,5},{8,10},{9,11},{10,... | collective-permute-start | bytes 1572872 | tf_op jit(solution)/shard_map/ppermute | solution.py:92
  410.2 28.9 %collective-permute-start.50 = (bf16[128,2048]{1,0:T(8,128)(2,1)S(1)}, bf16[128,2048]{1,0:T(8,128)(2,1)S(1)}, u32[]{:S(2)}, u32[]{:S(2)}) collective-permute-start(bf16[128,2048]{1,0:T(8,128)(2,1)S(1)} %convolution_convert_fusion.13), channel_id=1, source_target_pairs={{0,1},{1,2},{2,3},{3,0},{4,5},{5,6},{6,7},{7,4},{8,9},{9,10},{10,1... | collective-permute-start | bytes 1572872 | tf_op jit(solution)/shard_map/ppermute | solution.py:92
  443.6 49.3 %collective-permute-start.52 = (bf16[128,2048]{1,0:T(8,128)(2,1)S(1)}, bf16[128,2048]{1,0:T(8,128)(2,1)S(1)}, u32[]{:S(2)}, u32[]{:S(2)}) collective-permute-start(bf16[128,2048]{1,0:T(8,128)(2,1)S(1)} %get-tuple-element.126), channel_id=1, source_target_pairs={{0,2},{1,3},{2,0},{3,1},{4,6},{5,7},{6,4},{7,5},{8,10},{9,11},{10,... | collective-permute-start | bytes 1572872 | tf_op jit(solution)/shard_map/ppermute | solution.py:49
  447.0 53.0 %collective-permute-start.51 = (bf16[128,2048]{1,0:T(8,128)(2,1)S(1)}, bf16[128,2048]{1,0:T(8,128)(2,1)}, u32[]{:S(2)}, u32[]{:S(2)}) collective-permute-start(bf16[128,2048]{1,0:T(8,128)(2,1)S(1)} %get-tuple-element.126), channel_id=1, source_target_pairs={{0,1},{1,2},{2,3},{3,0},{4,5},{5,6},{6,7},{7,4},{8,9},{9,10},{10,1... | collective-permute-start | bytes 1572872 | tf_op jit(solution)/shard_map/ppermute | solution.py:49
  525.1 398.7 %all-reduce.3.cloned.1.call-start = ((), (), s32[]{:S(2)}) async-start(), calls=%async_computation.9 | async-start | bytes 2097152 | tf_op jit(solution)/shard_map/psum | solution.py:473
  529.3 399.8 %reduce-scatter.11.cloned.1.call-start = ((), (), s32[]{:S(2)}) async-start(), calls=%async_computation.12 | async-start | bytes 9437184 | tf_op jit(solution)/shard_map/reduce_scatter | solution.py:491
  544.0 451.8 %reduce-scatter.9.cloned.1.call-start = ((), (), s32[]{:S(2)}) async-start(), calls=%async_computation.11 | async-start | bytes 2359296 | tf_op jit(solution)/shard_map/reduce_scatter | solution.py:521
  544.1 26.2 %collective-permute-start.54 = (bf16[128,2048]{1,0:T(8,128)(2,1)}, bf16[128,2048]{1,0:T(8,128)(2,1)S(1)}, u32[]{:S(2)}, u32[]{:S(2)}) collective-permute-start(bf16[128,2048]{1,0:T(8,128)(2,1)} %convolution_convert_fusion.11.refs_2_), channel_id=1, source_target_pairs={{0,3},{1,0},{2,1},{3,2},{4,7},{5,4},{6,5},{7,6},{8,11},{9,8},{10,9... | collective-permute-start | bytes 1572872 | tf_op jit(solution)/shard_map/ppermute | solution.py:92
  544.1 26.9 %collective-permute-start.56 = (bf16[128,2048]{1,0:T(8,128)(2,1)}, bf16[128,2048]{1,0:T(8,128)(2,1)}, u32[]{:S(2)}, u32[]{:S(2)}) collective-permute-start(bf16[128,2048]{1,0:T(8,128)(2,1)} %convolution_convert_fusion.9.refs_4_), channel_id=1, source_target_pairs={{0,1},{1,2},{2,3},{3,0},{4,5},{5,6},{6,7},{7,4},{8,9},{9,10},{10,1... | collective-permute-start | bytes 1572872 | tf_op jit(solution)/shard_map/ppermute | solution.py:92
  546.2 43.4 %collective-permute-start.55 = (bf16[128,2048]{1,0:T(8,128)(2,1)}, bf16[128,2048]{1,0:T(8,128)(2,1)}, u32[]{:S(2)}, u32[]{:S(2)}) collective-permute-start(bf16[128,2048]{1,0:T(8,128)(2,1)} %convolution_convert_fusion.10.refs_3_), channel_id=1, source_target_pairs={{0,2},{1,3},{2,0},{3,1},{4,6},{5,7},{6,4},{7,5},{8,10},{9,11},{10,... | collective-permute-start | bytes 1572872 | tf_op jit(solution)/shard_map/ppermute | solution.py:92
  595.7 39.8 %collective-permute-start.58 = (bf16[128,2048]{1,0:T(8,128)(2,1)S(1)}, bf16[128,2048]{1,0:T(8,128)(2,1)S(1)}, u32[]{:S(2)}, u32[]{:S(2)}) collective-permute-start(bf16[128,2048]{1,0:T(8,128)(2,1)S(1)} %get-tuple-element.62.refs_6_), channel_id=1, source_target_pairs={{0,2},{1,3},{2,0},{3,1},{4,6},{5,7},{6,4},{7,5},{8,10},{9,11},{10,... | collective-permute-start | bytes 1572872 | tf_op jit(solution)/shard_map/ppermute | solution.py:49
  599.1 36.4 %collective-permute-start.59 = (bf16[128,2048]{1,0:T(8,128)(2,1)S(1)}, bf16[128,2048]{1,0:T(8,128)(2,1)S(1)}, u32[]{:S(2)}, u32[]{:S(2)}) collective-permute-start(bf16[128,2048]{1,0:T(8,128)(2,1)S(1)} %get-tuple-element.62.refs_6_), channel_id=1, source_target_pairs={{0,3},{1,0},{2,1},{3,2},{4,7},{5,4},{6,5},{7,6},{8,11},{9,8},{10,9... | collective-permute-start | bytes 1572872 | tf_op jit(solution)/shard_map/ppermute | solution.py:49
  649.5 27.6 %collective-permute-start.60 = (bf16[128,2048]{1,0:T(8,128)(2,1)S(1)}, bf16[128,2048]{1,0:T(8,128)(2,1)S(1)}, u32[]{:S(2)}, u32[]{:S(2)}) collective-permute-start(bf16[128,2048]{1,0:T(8,128)(2,1)S(1)} %get-tuple-element.152), channel_id=1, source_target_pairs={{0,1},{4,5},{8,9},{12,13},{16,17},{20,21},{24,25},{28,29}} | collective-permute-start | bytes 1572872 | tf_op jit(solution)/shard_map/ppermute | solution.py:66
  719.5 278.2 %reduce-scatter.7.cloned.1.call-start = ((), (), s32[]{:S(2)}) async-start(), calls=%async_computation.10 | async-start | bytes 7077888 | tf_op jit(solution)/shard_map/reduce_scatter | solution.py:529
  816.1 22.3 %collective-permute-start.76 = (bf16[128,2048]{1,0:T(8,128)(2,1)S(1)}, bf16[128,2048]{1,0:T(8,128)(2,1)S(1)}, u32[]{:S(2)}, u32[]{:S(2)}) collective-permute-start(bf16[128,2048]{1,0:T(8,128)(2,1)S(1)} %copy-done.15), channel_id=1, source_target_pairs={{0,1},{1,2},{2,3},{4,5},{5,6},{6,7},{8,9},{9,10},{10,11},{12,13},{... | collective-permute-start | bytes 1572872 | tf_op jit(solution)/shard_map/ppermute | solution.py:57
  827.2 22.3 %collective-permute-start.82 = (bf16[128,2048]{1,0:T(8,128)(2,1)S(1)}, bf16[128,2048]{1,0:T(8,128)(2,1)S(1)}, u32[]{:S(2)}, u32[]{:S(2)}) collective-permute-start(bf16[128,2048]{1,0:T(8,128)(2,1)S(1)} %get-tuple-element.139), channel_id=1, source_target_pairs={{0,1},{1,2},{2,3},{4,5},{5,6},{6,7},{8,9},{9,10},{10,11},{12,13},{... | collective-permute-start | bytes 1572872 | tf_op jit(solution)/shard_map/ppermute | solution.py:66
  833.0 26.7 %collective-permute-start.69 = (bf16[128,2048]{1,0:T(8,128)(2,1)S(1)}, bf16[128,2048]{1,0:T(8,128)(2,1)S(1)}, u32[]{:S(2)}, u32[]{:S(2)}) collective-permute-start(bf16[128,2048]{1,0:T(8,128)(2,1)S(1)} %copy-done.9), channel_id=1, source_target_pairs={{1,0},{2,1},{3,2},{5,4},{6,5},{7,6},{9,8},{10,9},{11,10},{13,12},{... | collective-permute-start | bytes 1572872 | tf_op jit(solution)/shard_map/ppermute | solution.py:58
  834.3 39.0 %collective-permute-start.88 = (bf16[128,2048]{1,0:T(8,128)(2,1)S(1)}, bf16[128,2048]{1,0:T(8,128)(2,1)}, u32[]{:S(2)}, u32[]{:S(2)}) collective-permute-start(bf16[128,2048]{1,0:T(8,128)(2,1)S(1)} %collective-permute-done.79.refs_6_), channel_id=1, source_target_pairs={{1,0},{2,1},{5,4},{6,5},{9,8},{10,9},{13,12},{14,13},{17,16},{18,1... | collective-permute-start | bytes 1572872 | tf_op jit(solution)/shard_map/ppermute | solution.py:58
  838.3 43.2 %collective-permute-start.66 = (bf16[128,2048]{1,0:T(8,128)(2,1)S(1)}, bf16[128,2048]{1,0:T(8,128)(2,1)S(1)}, u32[]{:S(2)}, u32[]{:S(2)}) collective-permute-start(bf16[128,2048]{1,0:T(8,128)(2,1)S(1)} %copy-done.9), channel_id=1, source_target_pairs={{0,1},{1,2},{2,3},{4,5},{5,6},{6,7},{8,9},{9,10},{10,11},{12,13},{... | collective-permute-start | bytes 1572872 | tf_op jit(solution)/shard_map/ppermute | solution.py:57
  849.6 34.3 %collective-permute-start.77 = (bf16[128,2048]{1,0:T(8,128)(2,1)S(1)}, bf16[128,2048]{1,0:T(8,128)(2,1)}, u32[]{:S(2)}, u32[]{:S(2)}) collective-permute-start(bf16[128,2048]{1,0:T(8,128)(2,1)S(1)} %collective-permute-done.76.refs_5_), channel_id=1, source_target_pairs={{1,2},{2,3},{5,6},{6,7},{9,10},{10,11},{13,14},{14,15},{17,18},{18... | collective-permute-start | bytes 1572872 | tf_op jit(solution)/shard_map/ppermute | solution.py:57
  854.3 40.6 %collective-permute-start.86 = (bf16[128,2048]{1,0:T(8,128)(2,1)}, bf16[128,2048]{1,0:T(8,128)(2,1)S(1)}, u32[]{:S(2)}, u32[]{:S(2)}) collective-permute-start(bf16[128,2048]{1,0:T(8,128)(2,1)} %get-tuple-element.70.refs_0_), channel_id=1, source_target_pairs={{0,3},{1,0},{2,1},{3,2},{4,7},{5,4},{6,5},{7,6},{8,11},{9,8},{10,9... | collective-permute-start | bytes 1572872 | tf_op jit(solution)/shard_map/ppermute | solution.py:49
  859.7 39.3 %collective-permute-start.87 = (bf16[128,2048]{1,0:T(8,128)(2,1)S(1)}, bf16[128,2048]{1,0:T(8,128)(2,1)}, u32[]{:S(2)}, u32[]{:S(2)}) collective-permute-start(bf16[128,2048]{1,0:T(8,128)(2,1)S(1)} %collective-permute-done.69.refs_4_), channel_id=1, source_target_pairs={{1,0},{2,1},{5,4},{6,5},{9,8},{10,9},{13,12},{14,13},{17,16},{18,1... | collective-permute-start | bytes 1572872 | tf_op jit(solution)/shard_map/ppermute | solution.py:58
  873.3 46.4 %collective-permute-start.89 = (bf16[128,2048]{1,0:T(8,128)(2,1)}, bf16[128,2048]{1,0:T(8,128)(2,1)S(1)}, u32[]{:S(2)}, u32[]{:S(2)}) collective-permute-start(bf16[128,2048]{1,0:T(8,128)(2,1)} %get-tuple-element.70.refs_0_), channel_id=1, source_target_pairs={{0,2},{1,3},{2,0},{3,1},{4,6},{5,7},{6,4},{7,5},{8,10},{9,11},{10,... | collective-permute-start | bytes 1572872 | tf_op jit(solution)/shard_map/ppermute | solution.py:49
  881.6 39.6 %collective-permute-start.67 = (bf16[128,2048]{1,0:T(8,128)(2,1)S(1)}, bf16[128,2048]{1,0:T(8,128)(2,1)}, u32[]{:S(2)}, u32[]{:S(2)}) collective-permute-start(bf16[128,2048]{1,0:T(8,128)(2,1)S(1)} %collective-permute-done.66.refs_3_), channel_id=1, source_target_pairs={{1,2},{2,3},{5,6},{6,7},{9,10},{10,11},{13,14},{14,15},{17,18},{18... | collective-permute-start | bytes 1572872 | tf_op jit(solution)/shard_map/ppermute | solution.py:57
  883.9 88.3 %collective-permute-start.92 = (bf16[128,2048]{1,0:T(8,128)(2,1)}, bf16[128,2048]{1,0:T(8,128)(2,1)}, u32[]{:S(2)}, u32[]{:S(2)}) collective-permute-start(bf16[128,2048]{1,0:T(8,128)(2,1)} %get-tuple-element.70.refs_0_), channel_id=1, source_target_pairs={{0,1},{1,2},{2,3},{3,0},{4,5},{5,6},{6,7},{7,4},{8,9},{9,10},{10,1... | collective-permute-start | bytes 1572872 | tf_op jit(solution)/shard_map/ppermute | solution.py:49
  895.0 83.5 %collective-permute-start.91 = (bf16[128,2048]{1,0:T(8,128)(2,1)}, bf16[128,2048]{1,0:T(8,128)(2,1)}, u32[]{:S(2)}, u32[]{:S(2)}) collective-permute-start(bf16[128,2048]{1,0:T(8,128)(2,1)} %collective-permute-done.88.refs_6_), channel_id=1, source_target_pairs={{1,0},{5,4},{9,8},{13,12},{17,16},{21,20},{25,24},{29,28}} | collective-permute-start | bytes 1572872 | tf_op jit(solution)/shard_map/ppermute | solution.py:58
  899.0 79.4 %collective-permute-start.90 = (bf16[128,2048]{1,0:T(8,128)(2,1)}, bf16[128,2048]{1,0:T(8,128)(2,1)}, u32[]{:S(2)}, u32[]{:S(2)}) collective-permute-start(bf16[128,2048]{1,0:T(8,128)(2,1)} %collective-permute-done.87.refs_4_), channel_id=1, source_target_pairs={{1,0},{5,4},{9,8},{13,12},{17,16},{21,20},{25,24},{29,28}} | collective-permute-start | bytes 1572872 | tf_op jit(solution)/shard_map/ppermute | solution.py:58
  919.7 70.0 %collective-permute-start.78 = (bf16[128,2048]{1,0:T(8,128)(2,1)}, bf16[128,2048]{1,0:T(8,128)(2,1)}, u32[]{:S(2)}, u32[]{:S(2)}) collective-permute-start(bf16[128,2048]{1,0:T(8,128)(2,1)} %collective-permute-done.77.refs_5_), channel_id=1, source_target_pairs={{2,3},{6,7},{10,11},{14,15},{18,19},{22,23},{26,27},{30,31}} | collective-permute-start | bytes 1572872 | tf_op jit(solution)/shard_map/ppermute | solution.py:57
  921.2 68.5 %collective-permute-start.68 = (bf16[128,2048]{1,0:T(8,128)(2,1)}, bf16[128,2048]{1,0:T(8,128)(2,1)}, u32[]{:S(2)}, u32[]{:S(2)}) collective-permute-start(bf16[128,2048]{1,0:T(8,128)(2,1)} %collective-permute-done.67.refs_3_), channel_id=1, source_target_pairs={{2,3},{6,7},{10,11},{14,15},{18,19},{22,23},{26,27},{30,31}} | collective-permute-start | bytes 1572872 | tf_op jit(solution)/shard_map/ppermute | solution.py:57
  (155 other events, 2440.7 us)
Sparse Core Ops, SparseCore 0:
  11.9 48.2 all-gather.4
  62.0 28.1 all-gather.6
  92.7 54.3 all-gather.8
  148.9 55.9 all-gather.10
  525.3 69.5 reduce-scatter.4
  600.7 151.4 all-reduce.2
  755.7 70.2 reduce-scatter.10
  829.6 41.1 reduce-scatter.8
  874.2 61.7 reduce-scatter.6

commit v2 on v1

v2 whole, which is shorter than its diff:
```python
import math

import jax
import jax.numpy as jnp
from jax import lax
from jax.experimental import pallas as pl
from jax.experimental.pallas import tpu as pltpu
from jax.sharding import PartitionSpec as P

HEAD_DIM = 128
DOCS = 2


highest = lax.Precision.HIGHEST
epsilon = 1e-05
bf16 = jnp.bfloat16
f32 = jnp.float32
CHUNK = 16


def rms_norm(values, gain_vec):
    square = jnp.mean(values * values, axis=-1, keepdims=True)
    return values * lax.rsqrt(square + epsilon) * gain_vec


def gelu_exact(values):
    return jax.nn.gelu(values, approximate=False)


def mixer(out_rows, gain_vec, first_matrix, second_matrix):
    hidden = gelu_exact(jnp.dot(rms_norm(out_rows, gain_vec), first_matrix, precision=highest))
    return jnp.dot(hidden, second_matrix, precision=highest)


def plain_dot(left, right):
    return jnp.dot(left, right, preferred_element_type=f32)


def dot_left_t(left, right):
    return lax.dot_general(left, right, (((0,), (0,)), ((), ())), preferred_element_type=f32)


def dot_right_t(left, right):
    return lax.dot_general(left, right, (((1,), (1,)), ((), ())), preferred_element_type=f32)


def total_of(pieces):
    total = pieces[0]
    for piece in pieces[1:]:
        total = total + piece
    return total


def join(values, others):
    anywhere = pl.BlockSpec(memory_space=pl.ANY)
    return list(
        pl.pallas_call(
            lambda *refs: None,
            in_specs=[anywhere] * (len(values) + len(others)),
            out_specs=[anywhere] * len(values),
            out_shape=[jax.ShapeDtypeStruct(v.shape, v.dtype) for v in values],
            input_output_aliases={i: i for i in range(len(values))},
        )(*values, *others)
    )


def after(value, *others):
    return join([value], others)[0]


def gather_line(block, count):
    ups, downs = [block], [block]
    for k in range(1, count):
        ups.append(lax.ppermute(ups[-1], "layer", [(i, i + 1) for i in range(k - 1, count - 1)]))
        downs.append(lax.ppermute(downs[-1], "layer", [(i + 1, i) for i in range(count - k)]))
    return [[block]] + [[ups[k], downs[count - k]] for k in range(1, count)]


def sum_line(blocks, count):
    up = down = None
    for k in range(1, count):
        up = blocks[k] if up is None else blocks[k] + up
        up = lax.ppermute(up, "layer", [(i, i + 1) for i in range(k)])
        down = blocks[count - k] if down is None else blocks[count - k] + down
        down = lax.ppermute(down, "layer", [(i, i - 1) for i in range(count - k, count)])
    return [blocks[0], up, down]


def vmem(megabytes):
    return pltpu.CompilerParams(vmem_limit_bytes=megabytes << 20)


def row_loop(rows, body, carry):
    return lax.fori_loop(
        0, rows // CHUNK, lambda i, c: body(pl.ds(pl.multiple_of(i * CHUNK, CHUNK), CHUNK), c), carry
    )


def stream_kernel(me_ref, mix_ref, hist_ref, *out_refs, stored, first):
    def body(at, carry):
        mix = mix_ref[at, :]
        totals = [None] * len(out_refs)
        for j in range(stored):
            rows = hist_ref[j, at, :].astype(f32)
            for s in range(len(out_refs)):
                i = (first + s) * stored + j
                term = rows * mix[:, i : i + 1]
                totals[s] = term if j == 0 else totals[s] + term
        for out_ref, total in zip(out_refs, totals):
            out_ref[at, :] = total.astype(bf16)
        return carry

    row_loop(out_refs[0].shape[0], body, 0)


def stream_sums(me, mix_cols, history, first, number, count, order=(), tokens_last=False):
    stored, tokens, width = history.shape
    rows = 128
    steps = tokens // count // rows
    where = lambda i, w: (w[0] - i // steps + count) % count * steps + i % steps
    outs = [pl.BlockSpec((rows, width), lambda i, w: (i, 0))] * number
    if tokens_last:
        outs[-1] = pl.BlockSpec((rows, width), lambda i, w: (where(i, w), 0))
    return pl.pallas_call(
        lambda *refs: stream_kernel(*refs[:3], *refs[3 + len(order) :], stored=stored, first=first),
        grid_spec=pltpu.PrefetchScalarGridSpec(
            num_scalar_prefetch=1,
            grid=(tokens // rows,),
            in_specs=[
                pl.BlockSpec((rows, 4 * stored), lambda i, w: (where(i, w), 0)),
                pl.BlockSpec((stored, rows, width), lambda i, w: (0, where(i, w), 0)),
            ]
            + [pl.BlockSpec(memory_space=pl.ANY)] * len(order),
            out_specs=outs,
        ),
        out_shape=[jax.ShapeDtypeStruct((tokens, width), bf16)] * number,
        compiler_params=vmem(48),
    )(me.astype(jnp.int32).reshape(1), mix_cols, history, *order)


def join_kernel(gain_ref, base_ref, *refs):
    parts, (sum_ref, norm_ref) = refs[:-2], refs[-2:]

    def body(at, carry):
        values = base_ref[at, :].astype(f32) + total_of([p[at, :].astype(f32) for p in parts])
        sum_ref[at, :] = values
        centre = values - jnp.mean(values, axis=1, keepdims=True)
        spread = jnp.mean(centre * centre, axis=1, keepdims=True)
        norm_ref[at, :] = (centre * lax.rsqrt(spread + epsilon) * gain_ref[...]).astype(bf16)
        return carry

    row_loop(base_ref.shape[0], body, 0)


def join_norm(base, parts, gain_vec):
    return pl.pallas_call(
        join_kernel,
        out_shape=[jax.ShapeDtypeStruct(base.shape, f32), jax.ShapeDtypeStruct(base.shape, bf16)],
        compiler_params=vmem(48),
    )(gain_vec[None], base, *parts)


def norm_grad(values, grad, gain):
    centre = values - jnp.mean(values, axis=1, keepdims=True)
    inv = lax.rsqrt(jnp.mean(centre * centre, axis=1, keepdims=True) + epsilon)
    hat = centre * inv
    scaled = grad * gain
    back = (
        scaled
        - jnp.mean(scaled, axis=1, keepdims=True)
        - hat * jnp.mean(scaled * hat, axis=1, keepdims=True)
    ) * inv
    return back, jnp.sum(grad * hat, axis=0, keepdims=True)


def back_kernel(gain_ref, value_ref, *refs, parts, based):
    part_refs = refs[:parts]
    base_ref = refs[parts] if based else None
    out_ref, dgain_ref = refs[-2:]

    def body(at, dgain):
        values = value_ref[at, :].astype(f32)
        grad = total_of([p[at, :].astype(f32) for p in part_refs])
        back, dgain_rows = norm_grad(values, grad, gain_ref[...])
        if based:
            back = back + base_ref[at, :]
        out_ref[at, :] = back.astype(bf16)
        return dgain + dgain_rows

    dgain_ref[...] = row_loop(value_ref.shape[0], body, jnp.zeros(dgain_ref.shape, f32))


def norm_back(values, parts, gain_vec, base=None, order=()):
    operands = [gain_vec[None], values] + list(parts) + ([] if base is None else [base])
    number = len(operands)
    back, dgain = pl.pallas_call(
        lambda *refs: back_kernel(
            *refs[:number], *refs[-2:], parts=len(parts), based=base is not None
        ),
        in_specs=[pl.BlockSpec(memory_space=pltpu.VMEM)] * number
        + [pl.BlockSpec(memory_space=pl.ANY)] * len(order),
        out_shape=[
            jax.ShapeDtypeStruct(values.shape, bf16),
            jax.ShapeDtypeStruct((1, values.shape[1]), f32),
        ],
        compiler_params=vmem(48),
    )(*operands, *order)
    return back, dgain[0]


def history_kernel(mix_ref, hist_ref, near_ref, hidden_ref, *refs, stored):
    hist_out, mix_out = refs[-2:]
    width = hist_out.shape[2]
    lanes = 256

    def body(at, carry):
        mix = mix_ref[at, :]
        sums = [None] * (4 * stored)
        for c in range(0, width, lanes):
            cols = slice(c, c + lanes)
            wide = [near_ref[at, s * width + c : s * width + c + lanes].astype(f32) for s in range(3)]
            wide.append(hidden_ref[at, cols].astype(f32))
            for j in range(stored):
                stored_rows = hist_ref[j, at, cols].astype(f32)
                total = None
                for s in range(4):
                    i = s * stored + j
                    term = wide[s] * mix[:, i : i + 1]
                    total = term if total is None else total + term
                    product = stored_rows * wide[s]
                    product = total_of([product[:, l : l + 128] for l in range(0, lanes, 128)])
                    sums[i] = product if sums[i] is None else sums[i] + product
                hist_out[j, at, cols] = total.astype(bf16)
        mix_out[at, :] = jnp.concatenate([jnp.sum(v, axis=1, keepdims=True) for v in sums], axis=1)
        return carry

    row_loop(hist_out.shape[1], body, 0)


def history_grads(mix_cols, history, near, hidden, order):
    stored, tokens, width = history.shape
    rows = 64
    here = lambda i: (i, 0)
    there = lambda i: (0, i, 0)
    return pl.pallas_call(
        lambda *refs: history_kernel(*refs, stored=stored),
        grid=(tokens // rows,),
        in_specs=[
            pl.BlockSpec((rows, 4 * stored), here),
            pl.BlockSpec((stored, rows, width), there),
            pl.BlockSpec((rows, 3 * width), here),
            pl.BlockSpec((rows, width), here),
        ]
        + [pl.BlockSpec(memory_space=pl.ANY)] * len(order),
        out_specs=[
            pl.BlockSpec((stored, rows, width), there),
            pl.BlockSpec((rows, 4 * stored), here),
        ],
        out_shape=[
            jax.ShapeDtypeStruct((stored, tokens, width), bf16),
            jax.ShapeDtypeStruct((tokens, 4 * stored), f32),
        ],
        compiler_params=vmem(48),
    )(mix_cols, history, near, hidden, *order)


def contract_rows(left, right):
    return lax.dot_general(left, right, (((0,), (0,)), ((), ())), preferred_element_type=f32)


def contract_cols(left, right):
    return lax.dot_general(left, right, (((1,), (1,)), ((), ())), preferred_element_type=f32)


def resident(array):
    return pl.BlockSpec(array.shape, lambda i: (0,) * array.ndim)


def mlp_grads(mlp_rows, up_low, branch_rows, active, part):
    tokens, width = mlp_rows.shape
    hidden = active.shape[1]
    rows = 256

    def kernel(mlp_ref, up_ref, branch_ref, active_ref, out_ref):
        out_ref[:, :hidden] = contract_rows(mlp_ref[...], up_ref[...]).astype(bf16)
        out_ref[:, hidden : 2 * hidden] = contract_rows(branch_ref[...], active_ref[...]).astype(bf16)
        out_ref[:, 2 * hidden :] = jnp.zeros((rows, 2 * part - 2 * hidden), bf16)

    side = pl.BlockSpec((tokens, rows), lambda i: (0, i))
    return pl.pallas_call(
        kernel,
        grid=(width // rows,),
        in_specs=[side, resident(up_low), side, resident(active)],
        out_specs=pl.BlockSpec((rows, 2 * part), lambda i: (i, 0)),
        out_shape=jax.ShapeDtypeStruct((width, 3 * part), bf16),
        compiler_params=vmem(56),
    )(mlp_rows, up_low, branch_rows, active)


def attention_grads(so_far, normed_rows, lin_grads, hidden_rows, context, first, part):
    tokens, width = hidden_rows.shape
    heads = context.shape[1]
    rows = 256

    def kernel(q_ref, k_ref, v_ref, dq_ref, dk_ref, dv_ref, hidden_ref, ctx_ref, first_ref, _, out_ref):
        pairs = ((q_ref, dq_ref), (k_ref, dk_ref), (v_ref, dv_ref), (hidden_ref, ctx_ref))
        for s, (left, right) in enumerate(pairs):
            out_ref[:, s * heads : (s + 1) * heads] = contract_rows(left[...], right[...]).astype(bf16)
        out_ref[:, 4 * heads :] = first_ref[...].astype(bf16)

    side = pl.BlockSpec((tokens, rows), lambda i: (0, i))
    return pl.pallas_call(
        kernel,
        grid=(width // rows,),
        in_specs=[side] * 3
        + [resident(lin_grads[0])] * 3
        + [side, resident(context)]
        + [pl.BlockSpec((rows, first.shape[1]), lambda i: (i, 0)), pl.BlockSpec(memory_space=pl.ANY)],
        out_specs=pl.BlockSpec((rows, part), lambda i: (i, 2)),
        out_shape=jax.ShapeDtypeStruct(so_far.shape, bf16),
        input_output_aliases={9: 0},
        compiler_params=vmem(56),
    )(*normed_rows, *lin_grads, hidden_rows, context, first, so_far)


def round_weights(w_up, w_down, w_query, w_key, w_value, w_output, order):
    rows, hidden = w_up.shape
    heads = w_query.shape[1]

    def kernel(up_ref, down_ref, q_ref, k_ref, v_ref, o_ref, _, out_ref):
        out_ref[:, :hidden] = up_ref[...].astype(bf16)
        out_ref[:, hidden : 2 * hidden] = down_ref[...].T.astype(bf16)
        for s, ref in enumerate((q_ref, k_ref, v_ref)):
            out_ref[:, 2 * hidden + s * heads : 2 * hidden + (s + 1) * heads] = ref[...].astype(bf16)
        out_ref[:, 2 * hidden + 3 * heads :] = o_ref[...].T.astype(bf16)

    return pl.pallas_call(
        kernel,
        in_specs=[pl.BlockSpec(memory_space=pltpu.VMEM)] * 6 + [pl.BlockSpec(memory_space=pl.ANY)],
        out_shape=jax.ShapeDtypeStruct((rows, 2 * hidden + 4 * heads), bf16),
        compiler_params=vmem(56),
    )(w_up, w_down, w_query, w_key, w_value, w_output, order)


def project(blocks, full, heads, place, kind):
    pieces = [p for b in blocks for p in b]
    counts = [len(b) for b in blocks]
    block, width = pieces[0].shape
    tokens = block * len(blocks)

    def kernel(full_ref, *refs):
        rows_ref, out_ref = refs[-2:]
        first = 0
        for k, n in enumerate(counts):
            rows_ref[k * block : (k + 1) * block, :] = total_of([r[...] for r in refs[first : first + n]])
            first += n
        out_ref[...] = jnp.dot(rows_ref[...], full_ref[...], preferred_element_type=f32).astype(kind)

    whole = pl.BlockSpec((block, width), lambda i: (0, 0))
    return pl.pallas_call(
        kernel,
        grid=(1,),
        in_specs=[pl.BlockSpec((width, heads), lambda i: (0, place))] + [whole] * len(pieces),
        out_specs=[
            pl.BlockSpec((tokens, width), lambda i: (0, 0)),
            pl.BlockSpec((tokens, heads), lambda i: (0, 0)),
        ],
        out_shape=[
            jax.ShapeDtypeStruct((tokens, width), bf16),
            jax.ShapeDtypeStruct((tokens, heads), kind),
        ],
        compiler_params=vmem(56),
    )(full, *pieces)


def feed_forward(rows, full, hidden):
    tokens, width = rows.shape
    cols = 512
    steps = hidden // cols

    def kernel(rows_ref, up_ref, down_ref, active_ref, slope_ref, out_ref, total_ref):
        step = pl.program_id(0)
        up = jnp.dot(rows_ref[...], up_ref[...], preferred_element_type=f32)
        below = 0.5 * (1.0 + lax.erf(up * (0.5**0.5)))
        active = (up * below).astype(bf16)
        active_ref[...] = active
        slope_ref[...] = below + up * jnp.exp(-0.5 * up * up) * ((2.0 * math.pi) ** -0.5)
        share = contract_cols(active, down_ref[...])

        @pl.when(step == 0)
        def _():
            total_ref[...] = share

        @pl.when(step > 0)
        def _():
            total_ref[...] += share

        @pl.when(step == steps - 1)
        def _():
            out_ref[...] = total_ref[...].astype(bf16)

    part = pl.BlockSpec((tokens, cols), lambda i: (0, i))
    return pl.pallas_call(
        kernel,
        grid=(steps,),
        in_specs=[
            resident(rows),
            pl.BlockSpec((width, cols), lambda i: (0, i)),
            pl.BlockSpec((width, cols), lambda i: (0, steps + i)),
        ],
        out_specs=[part, part, pl.BlockSpec((tokens, width), lambda i: (0, 0))],
        out_shape=[
            jax.ShapeDtypeStruct((tokens, hidden), bf16),
            jax.ShapeDtypeStruct((tokens, hidden), f32),
            jax.ShapeDtypeStruct((tokens, width), bf16),
        ],
        scratch_shapes=[pltpu.VMEM((tokens, width), f32)],
        compiler_params=vmem(60),
    )(rows, full, full)


def feed_back(rows, full, slope):
    tokens, width = rows.shape
    hidden = slope.shape[1]
    cols = 512
    steps = hidden // cols

    def kernel(rows_ref, up_ref, down_ref, slope_ref, low_ref, out_ref, total_ref):
        step = pl.program_id(0)
        grad = jnp.dot(rows_ref[...], down_ref[...], preferred_element_type=f32)
        low = (grad * slope_ref[...]).astype(bf16)
        low_ref[...] = low
        share = contract_cols(low, up_ref[...])

        @pl.when(step == 0)
        def _():
            total_ref[...] = share

        @pl.when(step > 0)
        def _():
            total_ref[...] += share

        @pl.when(step == steps - 1)
        def _():
            out_ref[...] = total_ref[...].astype(bf16)

    part = pl.BlockSpec((tokens, cols), lambda i: (0, i))
    return pl.pallas_call(
        kernel,
        grid=(steps,),
        in_specs=[
            resident(rows),
            pl.BlockSpec((width, cols), lambda i: (0, i)),
            pl.BlockSpec((width, cols), lambda i: (0, steps + i)),
            part,
        ],
        out_specs=[part, pl.BlockSpec((tokens, width), lambda i: (0, 0))],
        out_shape=[
            jax.ShapeDtypeStruct((tokens, hidden), bf16),
            jax.ShapeDtypeStruct((tokens, width), bf16),
        ],
        scratch_shapes=[pltpu.VMEM((tokens, width), f32)],
        compiler_params=vmem(60),
    )(rows, full, full, slope)


def turn(values, cosine, sine):
    return values * cosine + pltpu.roll(values, HEAD_DIM // 2, 1) * sine


def score_block(queries, keys, allowed):
    scores = lax.dot_general(
        queries, keys, (((1,), (1,)), ((), ())), preferred_element_type=f32
    ) * (HEAD_DIM ** (-0.5))
    return jnp.where(allowed, scores, -1e30)


def allowed_block(row_ids, col_ids):
    return (row_ids[:, 0:1] == col_ids[0:1, :]) & (row_ids[:, 1:2] >= col_ids[1:2, :])


def attend_kernel(rows_ref, cols_ref, cos_ref, sin_ref, q_ref, k_ref, v_ref, ctx_ref, qr_ref, kr_ref, lse_ref):
    allowed = allowed_block(rows_ref[...], cols_ref[...])
    queries = turn(q_ref[...], cos_ref[...], sin_ref[...]).astype(bf16)
    keys = turn(k_ref[...], cos_ref[...], sin_ref[...]).astype(bf16)
    qr_ref[...] = queries
    kr_ref[...] = keys
    scores = score_block(queries, keys, allowed)
    row_max = jnp.max(scores, axis=1, keepdims=True)
    shifted = jnp.exp(scores - row_max)
    row_sum = jnp.sum(shifted, axis=1, keepdims=True)
    probs = (shifted / row_sum).astype(bf16)
    ctx_ref[...] = jnp.dot(probs, v_ref[...], preferred_element_type=f32).astype(bf16)
    lse_ref[0] = row_max + jnp.log(row_sum)


def attend(row_ids, col_ids, cosine, sine, q_lin, k_lin, v_lin):
    tokens, width = q_lin.shape
    heads = width // HEAD_DIM
    full = lambda a: pl.BlockSpec(a.shape, lambda h: (0,) * a.ndim)
    head = pl.BlockSpec((tokens, HEAD_DIM), lambda h: (0, h))
    return pl.pallas_call(
        attend_kernel,
        grid=(heads,),
        in_specs=[full(row_ids), full(col_ids), full(cosine), full(sine), head, head, head],
        out_specs=[head, head, head, pl.BlockSpec((1, tokens, 1), lambda h: (h, 0, 0))],
        out_shape=[jax.ShapeDtypeStruct((tokens, width), bf16)] * 3
        + [jax.ShapeDtypeStruct((heads, tokens, 1), f32)],
        compiler_params=vmem(56),
    )(row_ids, col_ids, cosine, sine, q_lin, k_lin, v_lin)


def attend_back_kernel(
    rows_ref, cols_ref, cos_ref, sin_ref, q_ref, k_ref, v_ref, lse_ref, grad_ref, dq_ref, dk_ref, dv_ref
):
    allowed = allowed_block(rows_ref[...], cols_ref[...])
    queries, keys, values, grad = q_ref[...], k_ref[...], v_ref[...], grad_ref[...]
    scale = HEAD_DIM ** (-0.5)
    probs = jnp.exp(score_block(queries, keys, allowed) - lse_ref[0])
    prob_grad = lax.dot_general(grad, values, (((1,), (1,)), ((), ())), preferred_element_type=f32)
    dv_ref[...] = lax.dot_general(
        probs.astype(bf16), grad, (((0,), (0,)), ((), ())), preferred_element_type=f32
    ).astype(bf16)
    centre = jnp.sum(probs * prob_grad, axis=1, keepdims=True)
    score_grad = (probs * (prob_grad - centre)).astype(bf16)
    dq = jnp.dot(score_grad, keys, preferred_element_type=f32) * scale
    dk = (
        lax.dot_general(score_grad, queries, (((0,), (0,)), ((), ())), preferred_element_type=f32)
        * scale
    )
    dq_ref[...] = turn(dq, cos_ref[...], -sin_ref[...]).astype(bf16)
    dk_ref[...] = turn(dk, cos_ref[...], -sin_ref[...]).astype(bf16)


def attend_back(row_ids, col_ids, cosine, sine, queries, keys, v_lin, lse, grad):
    tokens, width = queries.shape
    heads = width // HEAD_DIM
    full = lambda a: pl.BlockSpec(a.shape, lambda h: (0,) * a.ndim)
    head = pl.BlockSpec((tokens, HEAD_DIM), lambda h: (0, h))
    return pl.pallas_call(
        attend_back_kernel,
        grid=(heads,),
        in_specs=[full(row_ids), full(col_ids), full(cosine), full(sine), head, head, head]
        + [pl.BlockSpec((1, tokens, 1), lambda h: (h, 0, 0)), head],
        out_specs=[head, head, head],
        out_shape=[jax.ShapeDtypeStruct((tokens, width), bf16)] * 3,
        compiler_params=vmem(56),
    )(row_ids, col_ids, cosine, sine, queries, keys, v_lin, lse, grad)


def unpack_grads(weight_sum, hidden, heads, part, order):
    rows = weight_sum.shape[0]

    def kernel(sum_ref, *refs):
        up_ref, down_ref, q_ref, k_ref, v_ref, o_ref, first_ref = refs[-7:]
        up_ref[...] = sum_ref[:, :hidden].astype(f32)
        down_ref[...] = sum_ref[:, hidden : 2 * hidden].astype(f32).T
        at = 2 * part
        for ref in (q_ref, k_ref, v_ref):
            ref[...] = sum_ref[:, at : at + heads].astype(f32)
            at += heads
        o_ref[...] = sum_ref[:, at : at + heads].astype(f32).T
        first_ref[...] = sum_ref[:, at + heads :].astype(f32)

    shapes = [(rows, hidden), (hidden, rows)] + [(rows, heads)] * 3
    shapes += [(heads, rows), (rows, 3 * part - 2 * part - 4 * heads)]
    return pl.pallas_call(
        kernel,
        in_specs=[pl.BlockSpec(memory_space=pltpu.VMEM)]
        + [pl.BlockSpec(memory_space=pl.ANY)] * len(order),
        out_shape=[jax.ShapeDtypeStruct(shape, f32) for shape in shapes],
        compiler_params=vmem(56),
    )(weight_sum, *order)


def places(seg_row):
    length = seg_row.shape[0]
    labels = jnp.arange(DOCS, dtype=jnp.int32)
    before = jnp.sum((seg_row[None, :] < labels[:, None]).astype(jnp.int32), axis=1)
    member = (seg_row[:, None] == labels[None, :]).astype(jnp.int32)
    begins = jnp.sum(member * before[None, :], axis=1)
    return jnp.arange(length, dtype=jnp.int32) - begins


def local(
    history,
    mix_weights,
    segments,
    w_query,
    w_key,
    w_value,
    w_output,
    w_up,
    w_down,
    norm_gains,
    w_first,
    w_second,
    out_cotangent,
    mix_cotangent,
):
    stored, row_tok, width = history.shape
    count = lax.axis_size("layer")
    me = lax.axis_index("layer")
    own_tok = row_tok // count
    order = [(me - k) % count for k in range(count)]

    def block_of(rows, k):
        return rows[k * own_tok : (k + 1) * own_tok]

    def blocks_of(rows):
        return [block_of(rows, k) for k in range(count)]

    def reorder(rows):
        return jnp.concatenate(
            [lax.dynamic_slice_in_dim(rows, k * own_tok, own_tok, axis=0) for k in order], axis=0
        )

    mix_cols = mix_weights.reshape(4 * stored, row_tok).T
    shares = stream_sums(me, mix_cols, history, 0, 4, count, tokens_last=True)

    hidden = w_up.shape[1]
    heads = w_query.shape[1]
    low = round_weights(w_up, w_down, w_query, w_key, w_value, w_output, shares[0])
    full = lax.all_gather(low, "dp", axis=0, tiled=True)
    place = 2 * hidden // heads

    def columns(first, number):
        return full[:, first : first + number]

    stream_own, normed, lin, normed_rows = [], [], [], []
    for s in range(3):
        pieces = sum_line(blocks_of(shares[s]), count)
        own, norm = join_norm(pieces[0], pieces[1:], norm_gains[s])
        stream_own.append(own)
        normed.append(norm)
    residual = lax.psum_scatter(
        after(shares[3], *normed), "layer", scatter_dimension=0, tiled=True
    )
    for s in range(3):
        rows, out = project(
            gather_line(normed[s], count), full, heads, place + s, f32 if s < 2 else bf16
        )
        normed_rows.append(rows)
        lin.append(out)
    q_lin, k_lin, v_lin = lin
    q_lin = after(q_lin, residual)

    seg_row = segments[0]
    place = places(seg_row)
    index = jnp.arange(row_tok, dtype=jnp.int32)
    ids = jnp.stack([seg_row, index, place])
    ids = jnp.concatenate(
        [lax.dynamic_slice_in_dim(ids, k * own_tok, own_tok, axis=1) for k in order], axis=1
    )
    half = HEAD_DIM // 2
    frequency = jnp.exp(
        jnp.arange(half, dtype=f32) * (-2.0 * math.log(10000.0) / HEAD_DIM)
    )
    angles = ids[2].astype(f32)[:, None] * frequency[None, :]
    cosine, sine = jnp.cos(angles), jnp.sin(angles)
    cosine = jnp.concatenate([cosine, cosine], axis=1)
    sine = jnp.concatenate([-sine, sine], axis=1)
    col_ids = ids[:2]
    row_ids = col_ids.T

    context, queries, keys, lse = attend(row_ids, col_ids, cosine, sine, q_lin, k_lin, v_lin)

    context = reorder(context)

    def collect(rows):
        return lax.all_gather(rows, "layer", axis=0, tiled=True)

    def spread(rows):
        return lax.psum_scatter(rows.astype(bf16), "layer", scatter_dimension=0, tiled=True)

    out_weight = columns(2 * hidden + 3 * heads, heads)
    attn = spread(dot_right_t(context, out_weight))
    hidden_in, mlp_norm = join_norm(residual, [attn], norm_gains[3])
    mlp_rows = collect(mlp_norm)
    active, slope, mlp_part = feed_forward(mlp_rows, full, hidden)
    block = hidden_in + spread(mlp_part).astype(f32)

    next_mix, mixer_pull = jax.vjp(mixer, block, norm_gains[4], w_first, w_second)
    block_part, mixer_gain_grad, first_grad, second_grad = mixer_pull(mix_cotangent)
    block_grad = out_cotangent + block_part
    branch_rows = collect(block_grad.astype(bf16))
    up_low, mlp_part = feed_back(branch_rows, full, slope)
    mlp_back = spread(mlp_part)
    part = 4 * heads + 128
    weight_grads = mlp_grads(mlp_rows, after(up_low, mlp_part), branch_rows, active, part)
    hidden_low, mlp_gain_grad = norm_back(
        hidden_in, [mlp_back], norm_gains[3], block_grad, [weight_grads]
    )
    hidden_rows = collect(hidden_low)
    context_grad = reorder(plain_dot(hidden_rows, out_weight).astype(bf16))
    lin_grads = attend_back(
        row_ids, col_ids, cosine, sine, queries, keys, v_lin, lse, context_grad
    )
    mixes = first_grad.shape[1]
    first_wide = jnp.pad(first_grad, ((0, 0), (0, 128 - mixes)))
    weight_grads = attention_grads(
        weight_grads, normed_rows, lin_grads, hidden_rows, context, first_wide, part
    )
    weight_sum = lax.psum_scatter(weight_grads, "dp", scatter_dimension=0, tiled=True)

    gain_grads, stream_low = [], []
    for s in range(3):
        share = dot_right_t(lin_grads[s], columns(2 * hidden + s * heads, heads)).astype(bf16)
        low, gain_grad = norm_back(
            stream_own[s], sum_line(blocks_of(share), count), norm_gains[s]
        )
        gain_grads.append(gain_grad)
        stream_low.append(low)
    near = collect(jnp.concatenate(stream_low, axis=1))

    gain_rows = jnp.stack(gain_grads + [mlp_gain_grad, mixer_gain_grad])
    gains_sum, second_sum = lax.psum((gain_rows, second_grad), ("dp", "layer"))
    up_sum, down_sum, *projections, output_sum, first_part = unpack_grads(
        weight_sum, hidden, heads, part, []
    )
    first_sum = total_of(
        [first_part]
        + [
            lax.ppermute(first_part, "layer", [(i, (i + k) % count) for i in range(count)])
            for k in range(1, count)
        ]
    )
    first_sum = lax.all_gather(first_sum[:, :mixes], "dp", axis=0, tiled=True)
    history_grad, mix_back = history_grads(
        mix_cols, history, near, hidden_rows, [output_sum, first_sum, gains_sum]
    )
    mix_grad = mix_back.T.reshape(4, stored, row_tok)
    return (
        block.astype(bf16),
        next_mix,
        history_grad,
        mix_grad,
        *projections,
        output_sum,
        up_sum,
        down_sum,
        gains_sum,
        first_sum,
        second_sum,
    )


def solution(mesh):
    placed = (
        P("layer", "dp", None),
        P(None, "layer", "dp"),
        P("dp", None),
        P("dp", "layer"),
        P("dp", "layer"),
        P("dp", "layer"),
        P("layer", "dp"),
        P("dp", "layer"),
        P("layer", "dp"),
        P(),
        P(),
        P(),
        P(("dp", "layer"), None),
        P(("dp", "layer"), None),
    )
    return jax.shard_map(
        local,
        mesh=mesh,
        in_specs=placed,
        out_specs=(
            P(("dp", "layer"), None),
            P(("dp", "layer"), None),
            P("layer", "dp", None),
            P(None, "layer", "dp"),
            P("dp", "layer"),
            P("dp", "layer"),
            P("dp", "layer"),
            P("layer", "dp"),
            P("dp", "layer"),
            P("layer", "dp"),
            P(),
            P(),
            P(),
        ),
        check_vma=False,
    )
```

time: 1020 us -> 920 us (0.902)
  starting transfers between devices: 269 us -> 136 us
  waiting for transfers between devices: 367 us -> 492 us
  matrix products: 142 us -> 24 us
  Pallas kernels: 73.2 us -> 146 us
  other arithmetic: 66.1 us -> 10.6 us
  blocking collectives: 40.1 us -> 59.8 us
    ppermute x21 -> x3, waiting for transfers between devices: 206 us -> 0.01 us  [local(): lax.ppermute(first_part, 'layer', [(i, (i + k) % count) for i in range(co...]
    reduce_scatter x4 -> x5, waiting for transfers between devices: 0.03 us -> 154 us  [the longest x3 111 us: spread(): lax.psum_scatter(rows.astype(bf16), 'layer', scatter_dimension=0, tiled=T...]
    all_gather x4 -> x5, waiting for transfers between devices: 0.03 us -> 141 us  [the longest x4 141 us: collect(): return lax.all_gather(rows, 'layer', axis=0, tiled=True)]
    pallas_call x24 -> x18, Pallas kernels: 48.8 us -> 123 us  [the longest x1 17.1 us: feed_forward(): pl.pallas_call(kernel, grid=(steps,), in_specs=[resident(rows), pl.BlockS...]
    ppermute x21 -> x3, starting transfers between devices: 63.5 us -> 4.41 us  [local(): lax.ppermute(first_part, 'layer', [(i, (i + k) % count) for i in range(co...]
    dot_general x15 -> x1, matrix products: 53.9 us -> 3.46 us  [plain_dot(): return jnp.dot(left, right, preferred_element_type=f32)]
    ppermute x21 -> x18, starting transfers between devices: 121 us -> 79.1 us  [sum_line(): up = lax.ppermute(up, 'layer', [(i, i + 1) for i in range(k)])]
    dot_general x12 -> x4, matrix products: 48.4 us -> 13.4 us  [dot_right_t(): lax.dot_general(left, right, (((1,), (1,)), ((), ())), preferred_element_...]
  transfers between devices with their start and end apart: 102 -> 67, of which waited for: 38 -> 38; matrix products, arithmetic and copies ran while one was open for 17% -> 3% of each run, Pallas kernels for 7% -> 5%
where the time goes in v2:
time: 920 us; the launch traced here: 912 us
  waiting for transfers between devices  492 us (53%)
  Pallas kernels  146 us (16%)
  starting transfers between devices  136 us (15%)
  blocking collectives  59.8 us (6%)
  local copies, waits for them, and re-layouts  25.4 us (3%)
  matrix products  24 us (3%)
  between operations  17.2 us (2%)
  other arithmetic  10.6 us (1%)
    all_gather x4, waiting for transfers between devices, collect(): return lax.all_gather(rows, 'layer', axis=0, tiled=True)  141 us
    reduce_scatter x3, waiting for transfers between devices, spread(): lax.psum_scatter(rows.astype(bf16), 'layer', scatter_dimension=0, tiled=T...  111 us
    ppermute x18, waiting for transfers between devices, sum_line(): up = lax.ppermute(up, 'layer', [(i, i + 1) for i in range(k)])  105 us
    ppermute x18, starting transfers between devices, sum_line(): up = lax.ppermute(up, 'layer', [(i, i + 1) for i in range(k)])  79.1 us
    ppermute x9, waiting for transfers between devices, gather_line(): lax.ppermute(downs[-1], 'layer', [(i + 1, i) for i in range(count - k)])  69.4 us
    psum x1, blocking collectives, local(): gains_sum, second_sum = lax.psum((gain_rows, second_grad), ('dp', 'layer'))  48.1 us
    reduce_scatter x1, waiting for transfers between devices, local(): lax.psum_scatter(weight_grads, 'dp', scatter_dimension=0, tiled=True)  42.7 us
    ppermute x9, starting transfers between devices, gather_line(): lax.ppermute(ups[-1], 'layer', [(i, i + 1) for i in range(k - 1, count -...  24 us
  transfers between devices with their start and end apart: 67, of which 38 were waited for; matrix products, arithmetic and copies ran while one was open for 3% of the time, Pallas kernels for 5%

profile of v2, /device:TPU:0, one launch (start us, length us, event | category | flops | bytes accessed | tf_op | source)
XLA Modules:
  0.0 911.9 jit_solution(14703195094159920767)
XLA Ops:
  9.0 10.3 %shard_map.237 = (bf16[512,2048]{1,0:T(8,128)(2,1)S(1)}, bf16[512,2048]{1,0:T(8,128)(2,1)S(1)}, bf16[512,2048]{1,0:T(8,128)(2,1)}, bf16[512,2048]{1,0:T(8,128)(2,1)}) custom-call(s32[1]{0:T(128)} %bitcast.refs_0_, f32[512,16]{1,0:T(8,128)S(1)} %bitcast.20, bf16[4,512,2048]{2,1,0:T(8,128)(2,1)} %refs_1_.1), custom_call_target="tpu_custom_call" | custom-call | tf_op jit(solution)/shard_map/pallas_call | solution.py:124
  22.0 5.0 shard_map.242
  32.9 5.6 collective-permute-start
  42.0 8.7 collective-permute-done
  50.8 4.4 collective-permute-start.12
  55.3 6.8 collective-permute-done.6
  62.0 4.4 collective-permute-start.1
  66.5 6.7 collective-permute-done.12
  73.3 6.0 collective-permute-start.7
  84.6 7.1 collective-permute-start.2
  95.9 7.1 collective-permute-start.8
  107.1 7.1 collective-permute-start.14
  123.1 6.3 collective-permute-done.8.refs_0_
  133.0 6.5 collective-permute-done.14.refs_0_
  144.2 5.9 collective-permute-start.18
  151.3 4.6 collective-permute-start.24
  157.2 4.6 collective-permute-start.30
  161.8 9.4 %collective-permute-done.18.refs_1_ = bf16[128,2048]{1,0:T(8,128)(2,1)} collective-permute-done((bf16[128,2048]{1,0:T(8,128)(2,1)S(1)}, bf16[128,2048]{1,0:T(8,128)(2,1)}, u32[]{:S(2)}, u32[]{:S(2)}) %collective-permute-start.18) | collective-permute-done | bytes 524320 | tf_op jit(solution)/shard_map/ppermute | solution.py:74
  172.5 13.0 %collective-permute-done.19.refs_6_ = bf16[128,2048]{1,0:T(8,128)(2,1)} collective-permute-done((bf16[128,2048]{1,0:T(8,128)(2,1)S(1)}, bf16[128,2048]{1,0:T(8,128)(2,1)}, u32[]{:S(2)}, u32[]{:S(2)}) %collective-permute-start.19) | collective-permute-done | bytes 524320 | tf_op jit(solution)/shard_map/ppermute | solution.py:75
  186.8 6.9 collective-permute-done.24.refs_1_
  196.2 10.3 %collective-permute-done.25.refs_6_ = bf16[128,2048]{1,0:T(8,128)(2,1)} collective-permute-done((bf16[128,2048]{1,0:T(8,128)(2,1)S(1)}, bf16[128,2048]{1,0:T(8,128)(2,1)}, u32[]{:S(2)}, u32[]{:S(2)}) %collective-permute-start.25) | collective-permute-done | bytes 524320 | tf_op jit(solution)/shard_map/ppermute | solution.py:75
  207.8 5.8 collective-permute-done.30.refs_1_
  215.0 6.8 collective-permute-done.31.refs_6_
  223.1 9.9 %collective-permute-done.20.refs_4_ = bf16[128,2048]{1,0:T(8,128)(2,1)S(1)} collective-permute-done((bf16[128,2048]{1,0:T(8,128)(2,1)}, bf16[128,2048]{1,0:T(8,128)(2,1)S(1)}, u32[]{:S(2)}, u32[]{:S(2)}) %collective-permute-start.20) | collective-permute-done | bytes 524320 | tf_op jit(solution)/shard_map/ppermute | solution.py:75
  236.5 7.8 collective-permute-done.26.refs_4_
  247.1 8.4 collective-permute-done.32.refs_4_
  258.3 8.5 collective-permute-done.21.refs_2_
  272.1 5.4 shard_map.243
  278.1 5.4 shard_map.245
  287.6 5.2 shard_map.246
  292.8 7.5 shard_map.247
  301.4 4.2 convolution_convert_fusion.3
  305.7 41.8 %reduce-scatter.8.cloned.1.call-done.refs_0_ = bf16[128,2048]{1,0:T(8,128)(2,1)} async-done(((bf16[512,2048]{1,0:T(8,128)(2,1)}), bf16[128,2048]{1,0:T(8,128)(2,1)}) %reduce-scatter.8.cloned.1.call-update) | async-done | bytes 524304 | tf_op jit(solution)/shard_map/reduce_scatter | solution.py:674
  351.2 44.8 %all-gather.8.cloned.1.call-done.rows_ref.mlp_ref = bf16[512,2048]{1,0:T(8,128)(2,1)} async-done(((bf16[128,2048]{1,0:T(8,128)(2,1)}), bf16[512,2048]{1,0:T(8,128)(2,1)}) %all-gather.8.cloned.1.call-update) | async-done | bytes 2097168 | tf_op jit(solution)/shard_map/all_gather | solution.py:671
  396.0 17.1 %shard_map.249 = (bf16[512,2048]{1,0:T(8,128)(2,1)}, f32[512,2048]{1,0:T(8,128)}, bf16[512,2048]{1,0:T(8,128)(2,1)}) custom-call(bf16[512,2048]{1,0:T(8,128)(2,1)} %all-gather.8.cloned.1.call-done.rows_ref.mlp_ref, bf16[2048,6144]{1,0:T(8,128)(2,1)} %all-gather.6.cloned.1.call-done.full_ref.up_ref.down_ref, ...), custom_call_target="tpu_custom_call" | custom-call | tf_op jit(solution)/shard_map/pallas_call | solution.py:403
  414.1 41.5 %reduce-scatter.10.cloned.1.call-done = bf16[128,2048]{1,0:T(8,128)(2,1)} async-done(((bf16[512,2048]{1,0:T(8,128)(2,1)}), bf16[128,2048]{1,0:T(8,128)(2,1)}) %reduce-scatter.10.cloned.1.call-update) | async-done | bytes 524304 | tf_op jit(solution)/shard_map/reduce_scatter | solution.py:674
  461.3 44.6 %all-gather.10.cloned.1.call-done.rows_ref.branch_ref = bf16[512,2048]{1,0:T(8,128)(2,1)} async-done(((bf16[128,2048]{1,0:T(8,128)(2,1)}), bf16[512,2048]{1,0:T(8,128)(2,1)}) %all-gather.10.cloned.1.call-update) | async-done | bytes 2097168 | tf_op jit(solution)/shard_map/all_gather | solution.py:671
  505.9 16.5 %shard_map.250 = (bf16[512,2048]{1,0:T(8,128)(2,1)}, bf16[512,2048]{1,0:T(8,128)(2,1)}) custom-call(bf16[512,2048]{1,0:T(8,128)(2,1)} %all-gather.10.cloned.1.call-done.rows_ref.branch_ref, bf16[2048,6144]{1,0:T(8,128)(2,1)} %all-gather.6.cloned.1.call-done.full_ref.up_ref.down_ref, bf16[2048,6144]{1,0:T(8,128)(2,1)} %all-gather.6.cloned.1.call-done.full_ref.up_ref.down_ref, ...), custom_call_target="tpu_custom_call" | custom-call | tf_op jit(solution)/shard_map/pallas_call | solution.py:448
  522.5 14.8 %shard_map.252.refs_4_._ = bf16[2048,6528]{1,0:T(8,128)(2,1)} custom-call(bf16[512,2048]{1,0:T(8,128)(2,1)} %all-gather.8.cloned.1.call-done.rows_ref.mlp_ref, bf16[512,2048]{1,0:T(8,128)(2,1)} %shard_map.251.up_ref, bf16[512,2048]{1,0:T(8,128)(2,1)} %all-gather.10.cloned.1.call-done.rows_ref.branch_ref, bf16[512,2048]{1,0:T(8,128)(2,1)} %get-tuple-element.81.active_ref), custom_call_target="tpu_custom_call" | custom-call | tf_op jit(solution)/shard_map/pallas_call | solution.py:290
  537.3 27.6 %reduce-scatter.12.cloned.1.call-done.refs_2_ = bf16[128,2048]{1,0:T(8,128)(2,1)} async-done(((bf16[512,2048]{1,0:T(8,128)(2,1)}), bf16[128,2048]{1,0:T(8,128)(2,1)}) %reduce-scatter.12.cloned.1.call-update) | async-done | bytes 524304 | tf_op jit(solution)/shard_map/reduce_scatter | solution.py:674
  574.3 39.9 %all-gather.12.cloned.1.call-done.hidden_ref.refs_3_ = bf16[512,2048]{1,0:T(8,128)(2,1)} async-done(((bf16[128,2048]{1,0:T(8,128)(2,1)}), bf16[512,2048]{1,0:T(8,128)(2,1)}) %all-gather.12.cloned.1.call-update) | async-done | bytes 2097168 | tf_op jit(solution)/shard_map/all_gather | solution.py:671
  618.6 7.8 shard_map.254
  626.3 12.0 %shard_map.258 = bf16[2048,6528]{1,0:T(8,128)(2,1)} custom-call(bf16[512,2048]{1,0:T(8,128)(2,1)} %get-tuple-element.91.q_ref, bf16[512,2048]{1,0:T(8,128)(2,1)} %get-tuple-element.92.k_ref, bf16[512,2048]{1,0:T(8,128)(2,1)} %get-tuple-element.93.v_ref, bf16[512,512]{1,0:T(8,128)(2,1)} %get-tuple-element.83.dq_ref, ...), custom_call_target="tpu_custom_call", output_to_operand_aliasing={{}: (9, {})} | custom-call | tf_op jit(solution)/shard_map/pallas_call | solution.py:312
  658.7 8.6 collective-permute-done.48
  667.2 4.4 collective-permute-start.36
  671.7 6.8 collective-permute-done.42
  678.5 4.4 collective-permute-start.49
  682.9 6.8 collective-permute-done.36
  689.7 4.4 collective-permute-start.43
  696.1 4.8 collective-permute-done.49
  701.1 4.4 collective-permute-start.50
  706.8 5.3 collective-permute-done.43
  712.3 4.4 collective-permute-start.44
  718.2 5.2 collective-permute-done.37
  723.6 4.5 collective-permute-start.38
  728.1 6.5 collective-permute-done.50.refs_3_
  738.5 7.4 collective-permute-done.44.refs_3_
  748.4 6.6 collective-permute-done.38.refs_3_
  759.7 42.7 %reduce-scatter.14.cloned.1.call-done.sum_ref = bf16[256,6528]{1,0:T(8,128)(2,1)} async-done(((bf16[2048,6528]{1,0:T(8,128)(2,1)}), bf16[256,6528]{1,0:T(8,128)(2,1)}) %reduce-scatter.14.cloned.1.call-update) | async-done | bytes 3342352 | tf_op jit(solution)/shard_map/reduce_scatter | solution.py:704
  802.4 5.0 shard_map.259
  812.2 48.1 %all-reduce.1 = (f32[5,2048]{1,0:T(8,128)S(1)}, f32[68,68]{1,0:T(8,128)}) all-reduce(f32[5,2048]{1,0:T(8,128)S(1)} %stack.10, f32[68,68]{1,0:T(8,128)S(1)} %fusion.27), channel_id=1, replica_groups=mesh['dp'=8,'layer'=4] {'dp','layer'}, use_global_device_ids=true, to_apply=%region_10.11 | all-reduce | flops 14864 | bytes 118912 | tf_op jit(solution)/shard_map/psum | solution.py:717
  861.3 11.7 %all_gather.23.refs_5_ = f32[2048,68]{1,0:T(8,128)S(1)} all-gather(f32[256,68]{1,0:T(8,128)S(1)} %slice_add_fusion.12), channel_id=1, replica_groups=mesh['dp'=8,'layer'=4] {'dp'}, dimensions={0}, use_global_device_ids=true | all-gather | bytes 626688 | tf_op jit(solution)/shard_map/all_gather | solution.py:728
  874.2 12.1 %all-gather.14.cloned.1.call-done.refs_2_ = bf16[512,6144]{1,0:T(8,128)(2,1)} async-done(((bf16[128,6144]{1,0:T(8,128)(2,1)}), bf16[512,6144]{1,0:T(8,128)(2,1)}) %all-gather.14.cloned.1.call-update) | async-done | bytes 6291472 | tf_op jit(solution)/shard_map/all_gather | solution.py:671
  887.9 15.5 %shard_map.260 = (bf16[4,512,2048]{2,1,0:T(8,128)(2,1)}, f32[512,16]{1,0:T(8,128)S(1)}) custom-call(f32[512,16]{1,0:T(8,128)S(1)} %bitcast.21, bf16[4,512,2048]{2,1,0:T(8,128)(2,1)} %refs_1_.1, bf16[512,6144]{1,0:T(8,128)(2,1)} %all-gather.14.cloned.1.call-done.refs_2_, bf16[512,2048]{1,0:T(8,128)(2,1)S(1)} %copy-done.4, f32[512,256]{1,0:T(8,128)S(1)} %copy-done.23, ...), custom_call_target="tpu_custom_call" | custom-call | tf_op jit(solution)/shard_map/pallas_call | solution.py:245
  (258 shorter events, 145.2 us)
Async XLA Ops:
  8.0 264.1 %all-gather.6.cloned.1.call-start = ((), (), s32[]{:S(2)}) async-start(), calls=%async_computation.6 | async-start | bytes 28311552 | tf_op jit(solution)/shard_map/all_gather | solution.py:624
  27.0 250.5 %reduce-scatter.6.cloned.1.call-start = ((), (), s32[]{:S(2)}) async-start(), calls=%async_computation.5 | async-start | bytes 2621440 | tf_op jit(solution)/shard_map/reduce_scatter | solution.py:636
  31.4 9.8 %collective-permute-start.15 = (bf16[128,2048]{1,0:T(8,128)(2,1)S(1)}, bf16[128,2048]{1,0:T(8,128)(2,1)S(1)}, u32[]{:S(2)}, u32[]{:S(2)}) collective-permute-start(bf16[128,2048]{1,0:T(8,128)(2,1)S(1)} %slice.125), channel_id=1, source_target_pairs={{3,2},{7,6},{11,10},{15,14},{19,18},{23,22},{27,26},{31,30}} | collective-permute-start | bytes 1572872 | tf_op jit(solution)/shard_map/ppermute | solution.py:85
  32.2 47.1 %collective-permute-start.4 = (bf16[128,2048]{1,0:T(8,128)(2,1)S(1)}, bf16[128,2048]{1,0:T(8,128)(2,1)S(1)}, u32[]{:S(2)}, u32[]{:S(2)}) collective-permute-start(bf16[128,2048]{1,0:T(8,128)(2,1)S(1)} %get-tuple-element.182), channel_id=1, source_target_pairs={{2,1},{3,2},{6,5},{7,6},{10,9},{11,10},{14,13},{15,14},{18,17},{19... | collective-permute-start | bytes 1572872 | tf_op jit(solution)/shard_map/ppermute | solution.py:85
  32.9 17.8 %collective-permute-start = (bf16[128,2048]{1,0:T(8,128)(2,1)S(1)}, bf16[128,2048]{1,0:T(8,128)(2,1)S(1)}, u32[]{:S(2)}, u32[]{:S(2)}) collective-permute-start(bf16[128,2048]{1,0:T(8,128)(2,1)S(1)} %get-tuple-element.183), channel_id=1, source_target_pairs={{0,1},{4,5},{8,9},{12,13},{16,17},{20,21},{24,25},{28,29}} | collective-permute-start | bytes 1572872 | tf_op jit(solution)/shard_map/ppermute | solution.py:83
  38.6 53.1 %collective-permute-start.10 = (bf16[128,2048]{1,0:T(8,128)(2,1)S(1)}, bf16[128,2048]{1,0:T(8,128)(2,1)S(1)}, u32[]{:S(2)}, u32[]{:S(2)}) collective-permute-start(bf16[128,2048]{1,0:T(8,128)(2,1)S(1)} %get-tuple-element.177), channel_id=1, source_target_pairs={{2,1},{3,2},{6,5},{7,6},{10,9},{11,10},{14,13},{15,14},{18,17},{19... | collective-permute-start | bytes 1572872 | tf_op jit(solution)/shard_map/ppermute | solution.py:85
  39.3 22.7 %collective-permute-start.6 = (bf16[128,2048]{1,0:T(8,128)(2,1)S(1)}, bf16[128,2048]{1,0:T(8,128)(2,1)S(1)}, u32[]{:S(2)}, u32[]{:S(2)}) collective-permute-start(bf16[128,2048]{1,0:T(8,128)(2,1)S(1)} %get-tuple-element.178), channel_id=1, source_target_pairs={{0,1},{4,5},{8,9},{12,13},{16,17},{20,21},{24,25},{28,29}} | collective-permute-start | bytes 1572872 | tf_op jit(solution)/shard_map/ppermute | solution.py:83
  41.3 61.6 %collective-permute-start.16 = (bf16[128,2048]{1,0:T(8,128)(2,1)S(1)}, bf16[128,2048]{1,0:T(8,128)(2,1)S(1)}, u32[]{:S(2)}, u32[]{:S(2)}) collective-permute-start(bf16[128,2048]{1,0:T(8,128)(2,1)S(1)} %get-tuple-element.172), channel_id=1, source_target_pairs={{2,1},{3,2},{6,5},{7,6},{10,9},{11,10},{14,13},{15,14},{18,17},{19... | collective-permute-start | bytes 1572872 | tf_op jit(solution)/shard_map/ppermute | solution.py:85
  50.8 22.5 %collective-permute-start.12 = (bf16[128,2048]{1,0:T(8,128)(2,1)S(1)}, bf16[128,2048]{1,0:T(8,128)(2,1)S(1)}, u32[]{:S(2)}, u32[]{:S(2)}) collective-permute-start(bf16[128,2048]{1,0:T(8,128)(2,1)S(1)} %get-tuple-element.173), channel_id=1, source_target_pairs={{0,1},{4,5},{8,9},{12,13},{16,17},{20,21},{24,25},{28,29}} | collective-permute-start | bytes 1572872 | tf_op jit(solution)/shard_map/ppermute | solution.py:83
  62.0 22.5 %collective-permute-start.1 = (bf16[128,2048]{1,0:T(8,128)(2,1)S(1)}, bf16[128,2048]{1,0:T(8,128)(2,1)S(1)}, u32[]{:S(2)}, u32[]{:S(2)}) collective-permute-start(bf16[128,2048]{1,0:T(8,128)(2,1)S(1)} %slice_add_fusion.11), channel_id=1, source_target_pairs={{0,1},{1,2},{4,5},{5,6},{8,9},{9,10},{12,13},{13,14},{16,17},{17,1... | collective-permute-start | bytes 1572872 | tf_op jit(solution)/shard_map/ppermute | solution.py:83
  73.3 22.5 %collective-permute-start.7 = (bf16[128,2048]{1,0:T(8,128)(2,1)S(1)}, bf16[128,2048]{1,0:T(8,128)(2,1)S(1)}, u32[]{:S(2)}, u32[]{:S(2)}) collective-permute-start(bf16[128,2048]{1,0:T(8,128)(2,1)S(1)} %slice_add_fusion.9), channel_id=1, source_target_pairs={{0,1},{1,2},{4,5},{5,6},{8,9},{9,10},{12,13},{13,14},{16,17},{17,1... | collective-permute-start | bytes 1572872 | tf_op jit(solution)/shard_map/ppermute | solution.py:83
  79.4 27.6 %collective-permute-start.13 = (bf16[128,2048]{1,0:T(8,128)(2,1)S(1)}, bf16[128,2048]{1,0:T(8,128)(2,1)S(1)}, u32[]{:S(2)}, u32[]{:S(2)}) collective-permute-start(bf16[128,2048]{1,0:T(8,128)(2,1)S(1)} %slice_add_fusion.7), channel_id=1, source_target_pairs={{0,1},{1,2},{4,5},{5,6},{8,9},{9,10},{12,13},{13,14},{16,17},{17,1... | collective-permute-start | bytes 1572872 | tf_op jit(solution)/shard_map/ppermute | solution.py:83
  84.6 33.6 %collective-permute-start.2 = (bf16[128,2048]{1,0:T(8,128)(2,1)S(1)}, bf16[128,2048]{1,0:T(8,128)(2,1)S(1)}, u32[]{:S(2)}, u32[]{:S(2)}) collective-permute-start(bf16[128,2048]{1,0:T(8,128)(2,1)S(1)} %get-tuple-element.180), channel_id=1, source_target_pairs={{0,1},{1,2},{2,3},{4,5},{5,6},{6,7},{8,9},{9,10},{10,11},{12,13},{... | collective-permute-start | bytes 1572872 | tf_op jit(solution)/shard_map/ppermute | solution.py:83
  91.7 27.8 %collective-permute-start.5 = (bf16[128,2048]{1,0:T(8,128)(2,1)S(1)}, bf16[128,2048]{1,0:T(8,128)(2,1)S(1)}, u32[]{:S(2)}, u32[]{:S(2)}) collective-permute-start(bf16[128,2048]{1,0:T(8,128)(2,1)S(1)} %get-tuple-element.179), channel_id=1, source_target_pairs={{1,0},{2,1},{3,2},{5,4},{6,5},{7,6},{9,8},{10,9},{11,10},{13,12},{... | collective-permute-start | bytes 1572872 | tf_op jit(solution)/shard_map/ppermute | solution.py:85
  95.9 33.5 %collective-permute-start.8 = (bf16[128,2048]{1,0:T(8,128)(2,1)S(1)}, bf16[128,2048]{1,0:T(8,128)(2,1)S(1)}, u32[]{:S(2)}, u32[]{:S(2)}) collective-permute-start(bf16[128,2048]{1,0:T(8,128)(2,1)S(1)} %get-tuple-element.175), channel_id=1, source_target_pairs={{0,1},{1,2},{2,3},{4,5},{5,6},{6,7},{8,9},{9,10},{10,11},{12,13},{... | collective-permute-start | bytes 1572872 | tf_op jit(solution)/shard_map/ppermute | solution.py:83
  103.0 26.4 %collective-permute-start.11 = (bf16[128,2048]{1,0:T(8,128)(2,1)S(1)}, bf16[128,2048]{1,0:T(8,128)(2,1)S(1)}, u32[]{:S(2)}, u32[]{:S(2)}) collective-permute-start(bf16[128,2048]{1,0:T(8,128)(2,1)S(1)} %get-tuple-element.174), channel_id=1, source_target_pairs={{1,0},{2,1},{3,2},{5,4},{6,5},{7,6},{9,8},{10,9},{11,10},{13,12},{... | collective-permute-start | bytes 1572872 | tf_op jit(solution)/shard_map/ppermute | solution.py:85
  107.1 32.4 %collective-permute-start.14 = (bf16[128,2048]{1,0:T(8,128)(2,1)S(1)}, bf16[128,2048]{1,0:T(8,128)(2,1)S(1)}, u32[]{:S(2)}, u32[]{:S(2)}) collective-permute-start(bf16[128,2048]{1,0:T(8,128)(2,1)S(1)} %get-tuple-element.170), channel_id=1, source_target_pairs={{0,1},{1,2},{2,3},{4,5},{5,6},{6,7},{8,9},{9,10},{10,11},{12,13},{... | collective-permute-start | bytes 1572872 | tf_op jit(solution)/shard_map/ppermute | solution.py:83
  118.2 21.3 %collective-permute-start.17 = (bf16[128,2048]{1,0:T(8,128)(2,1)S(1)}, bf16[128,2048]{1,0:T(8,128)(2,1)S(1)}, u32[]{:S(2)}, u32[]{:S(2)}) collective-permute-start(bf16[128,2048]{1,0:T(8,128)(2,1)S(1)} %get-tuple-element.169), channel_id=1, source_target_pairs={{1,0},{2,1},{3,2},{5,4},{6,5},{7,6},{9,8},{10,9},{11,10},{13,12},{... | collective-permute-start | bytes 1572872 | tf_op jit(solution)/shard_map/ppermute | solution.py:85
  143.2 204.4 %reduce-scatter.8.cloned.1.call-start = ((), (), s32[]{:S(2)}) async-start(), calls=%async_computation.7 | async-start | bytes 2621440 | tf_op jit(solution)/shard_map/reduce_scatter | solution.py:674
  144.2 27.1 %collective-permute-start.18 = (bf16[128,2048]{1,0:T(8,128)(2,1)S(1)}, bf16[128,2048]{1,0:T(8,128)(2,1)}, u32[]{:S(2)}, u32[]{:S(2)}) collective-permute-start(bf16[128,2048]{1,0:T(8,128)(2,1)S(1)} %copy-done.14), channel_id=1, source_target_pairs={{0,1},{1,2},{2,3},{4,5},{5,6},{6,7},{8,9},{9,10},{10,11},{12,13},{... | collective-permute-start | bytes 1572872 | tf_op jit(solution)/shard_map/ppermute | solution.py:74
  150.0 35.5 %collective-permute-start.19 = (bf16[128,2048]{1,0:T(8,128)(2,1)S(1)}, bf16[128,2048]{1,0:T(8,128)(2,1)}, u32[]{:S(2)}, u32[]{:S(2)}) collective-permute-start(bf16[128,2048]{1,0:T(8,128)(2,1)S(1)} %copy-done.14), channel_id=1, source_target_pairs={{1,0},{2,1},{3,2},{5,4},{6,5},{7,6},{9,8},{10,9},{11,10},{13,12},{... | collective-permute-start | bytes 1572872 | tf_op jit(solution)/shard_map/ppermute | solution.py:75
  151.3 42.4 %collective-permute-start.24 = (bf16[128,2048]{1,0:T(8,128)(2,1)S(1)}, bf16[128,2048]{1,0:T(8,128)(2,1)S(1)}, u32[]{:S(2)}, u32[]{:S(2)}) collective-permute-start(bf16[128,2048]{1,0:T(8,128)(2,1)S(1)} %copy-done.12), channel_id=1, source_target_pairs={{0,1},{1,2},{2,3},{4,5},{5,6},{6,7},{8,9},{9,10},{10,11},{12,13},{... | collective-permute-start | bytes 1572872 | tf_op jit(solution)/shard_map/ppermute | solution.py:74
  155.9 50.6 %collective-permute-start.25 = (bf16[128,2048]{1,0:T(8,128)(2,1)S(1)}, bf16[128,2048]{1,0:T(8,128)(2,1)}, u32[]{:S(2)}, u32[]{:S(2)}) collective-permute-start(bf16[128,2048]{1,0:T(8,128)(2,1)S(1)} %copy-done.12), channel_id=1, source_target_pairs={{1,0},{2,1},{3,2},{5,4},{6,5},{7,6},{9,8},{10,9},{11,10},{13,12},{... | collective-permute-start | bytes 1572872 | tf_op jit(solution)/shard_map/ppermute | solution.py:75
  157.2 56.3 %collective-permute-start.30 = (bf16[128,2048]{1,0:T(8,128)(2,1)S(1)}, bf16[128,2048]{1,0:T(8,128)(2,1)S(1)}, u32[]{:S(2)}, u32[]{:S(2)}) collective-permute-start(bf16[128,2048]{1,0:T(8,128)(2,1)S(1)} %copy-done.10), channel_id=1, source_target_pairs={{0,1},{1,2},{2,3},{4,5},{5,6},{6,7},{8,9},{9,10},{10,11},{12,13},{... | collective-permute-start | bytes 1572872 | tf_op jit(solution)/shard_map/ppermute | solution.py:74
  171.3 50.6 %collective-permute-start.31 = (bf16[128,2048]{1,0:T(8,128)(2,1)S(1)}, bf16[128,2048]{1,0:T(8,128)(2,1)S(1)}, u32[]{:S(2)}, u32[]{:S(2)}) collective-permute-start(bf16[128,2048]{1,0:T(8,128)(2,1)S(1)} %copy-done.10), channel_id=1, source_target_pairs={{1,0},{2,1},{3,2},{5,4},{6,5},{7,6},{9,8},{10,9},{11,10},{13,12},{... | collective-permute-start | bytes 1572872 | tf_op jit(solution)/shard_map/ppermute | solution.py:75
  185.5 47.5 %collective-permute-start.20 = (bf16[128,2048]{1,0:T(8,128)(2,1)}, bf16[128,2048]{1,0:T(8,128)(2,1)S(1)}, u32[]{:S(2)}, u32[]{:S(2)}) collective-permute-start(bf16[128,2048]{1,0:T(8,128)(2,1)} %collective-permute-done.19.refs_6_), channel_id=1, source_target_pairs={{1,0},{2,1},{5,4},{6,5},{9,8},{10,9},{13,12},{14,13},{17,16},{18,1... | collective-permute-start | bytes 1572872 | tf_op jit(solution)/shard_map/ppermute | solution.py:75
  194.5 40.0 %collective-permute-start.22 = (bf16[128,2048]{1,0:T(8,128)(2,1)}, bf16[128,2048]{1,0:T(8,128)(2,1)}, u32[]{:S(2)}, u32[]{:S(2)}) collective-permute-start(bf16[128,2048]{1,0:T(8,128)(2,1)} %collective-permute-done.18.refs_1_), channel_id=1, source_target_pairs={{1,2},{2,3},{5,6},{6,7},{9,10},{10,11},{13,14},{14,15},{17,18},{18... | collective-permute-start | bytes 1572872 | tf_op jit(solution)/shard_map/ppermute | solution.py:74
  206.5 37.8 %collective-permute-start.26 = (bf16[128,2048]{1,0:T(8,128)(2,1)}, bf16[128,2048]{1,0:T(8,128)(2,1)S(1)}, u32[]{:S(2)}, u32[]{:S(2)}) collective-permute-start(bf16[128,2048]{1,0:T(8,128)(2,1)} %collective-permute-done.25.refs_6_), channel_id=1, source_target_pairs={{1,0},{2,1},{5,4},{6,5},{9,8},{10,9},{13,12},{14,13},{17,16},{18,1... | collective-permute-start | bytes 1572872 | tf_op jit(solution)/shard_map/ppermute | solution.py:75
  213.6 32.2 %collective-permute-start.28 = (bf16[128,2048]{1,0:T(8,128)(2,1)}, bf16[128,2048]{1,0:T(8,128)(2,1)}, u32[]{:S(2)}, u32[]{:S(2)}) collective-permute-start(bf16[128,2048]{1,0:T(8,128)(2,1)} %copy-done.31), channel_id=1, source_target_pairs={{1,2},{2,3},{5,6},{6,7},{9,10},{10,11},{13,14},{14,15},{17,18},{18... | collective-permute-start | bytes 1572872 | tf_op jit(solution)/shard_map/ppermute | solution.py:74
  221.8 33.7 %collective-permute-start.32 = (bf16[128,2048]{1,0:T(8,128)(2,1)S(1)}, bf16[128,2048]{1,0:T(8,128)(2,1)S(1)}, u32[]{:S(2)}, u32[]{:S(2)}) collective-permute-start(bf16[128,2048]{1,0:T(8,128)(2,1)S(1)} %collective-permute-done.31.refs_6_), channel_id=1, source_target_pairs={{1,0},{2,1},{5,4},{6,5},{9,8},{10,9},{13,12},{14,13},{17,16},{18,1... | collective-permute-start | bytes 1572872 | tf_op jit(solution)/shard_map/ppermute | solution.py:75
  233.1 23.9 %collective-permute-start.34 = (bf16[128,2048]{1,0:T(8,128)(2,1)S(1)}, bf16[128,2048]{1,0:T(8,128)(2,1)}, u32[]{:S(2)}, u32[]{:S(2)}) collective-permute-start(bf16[128,2048]{1,0:T(8,128)(2,1)S(1)} %collective-permute-done.30.refs_1_), channel_id=1, source_target_pairs={{1,2},{2,3},{5,6},{6,7},{9,10},{10,11},{13,14},{14,15},{17,18},{18... | collective-permute-start | bytes 1572872 | tf_op jit(solution)/shard_map/ppermute | solution.py:74
  234.5 32.2 %collective-permute-start.21 = (bf16[128,2048]{1,0:T(8,128)(2,1)S(1)}, bf16[128,2048]{1,0:T(8,128)(2,1)S(1)}, u32[]{:S(2)}, u32[]{:S(2)}) collective-permute-start(bf16[128,2048]{1,0:T(8,128)(2,1)S(1)} %collective-permute-done.20.refs_4_), channel_id=1, source_target_pairs={{1,0},{5,4},{9,8},{13,12},{17,16},{21,20},{25,24},{29,28}} | collective-permute-start | bytes 1572872 | tf_op jit(solution)/shard_map/ppermute | solution.py:75
  244.3 27.8 %collective-permute-start.23 = (bf16[128,2048]{1,0:T(8,128)(2,1)}, bf16[128,2048]{1,0:T(8,128)(2,1)}, u32[]{:S(2)}, u32[]{:S(2)}) collective-permute-start(bf16[128,2048]{1,0:T(8,128)(2,1)} %collective-permute-done.22.refs_3_), channel_id=1, source_target_pairs={{2,3},{6,7},{10,11},{14,15},{18,19},{22,23},{26,27},{30,31}} | collective-permute-start | bytes 1572872 | tf_op jit(solution)/shard_map/ppermute | solution.py:74
  245.8 32.3 %collective-permute-start.27 = (bf16[128,2048]{1,0:T(8,128)(2,1)S(1)}, bf16[128,2048]{1,0:T(8,128)(2,1)}, u32[]{:S(2)}, u32[]{:S(2)}) collective-permute-start(bf16[128,2048]{1,0:T(8,128)(2,1)S(1)} %collective-permute-done.26.refs_4_), channel_id=1, source_target_pairs={{1,0},{5,4},{9,8},{13,12},{17,16},{21,20},{25,24},{29,28}} | collective-permute-start | bytes 1572872 | tf_op jit(solution)/shard_map/ppermute | solution.py:75
  255.5 22.6 %collective-permute-start.29 = (bf16[128,2048]{1,0:T(8,128)(2,1)}, bf16[128,2048]{1,0:T(8,128)(2,1)}, u32[]{:S(2)}, u32[]{:S(2)}) collective-permute-start(bf16[128,2048]{1,0:T(8,128)(2,1)} %collective-permute-done.28.refs_3_), channel_id=1, source_target_pairs={{2,3},{6,7},{10,11},{14,15},{18,19},{22,23},{26,27},{30,31}} | collective-permute-start | bytes 1572872 | tf_op jit(solution)/shard_map/ppermute | solution.py:74
  257.0 30.6 %collective-permute-start.33 = (bf16[128,2048]{1,0:T(8,128)(2,1)S(1)}, bf16[128,2048]{1,0:T(8,128)(2,1)}, u32[]{:S(2)}, u32[]{:S(2)}) collective-permute-start(bf16[128,2048]{1,0:T(8,128)(2,1)S(1)} %collective-permute-done.32.refs_4_), channel_id=1, source_target_pairs={{1,0},{5,4},{9,8},{13,12},{17,16},{21,20},{25,24},{29,28}} | collective-permute-start | bytes 1572872 | tf_op jit(solution)/shard_map/ppermute | solution.py:75
  267.6 20.0 %collective-permute-start.35 = (bf16[128,2048]{1,0:T(8,128)(2,1)}, bf16[128,2048]{1,0:T(8,128)(2,1)}, u32[]{:S(2)}, u32[]{:S(2)}) collective-permute-start(bf16[128,2048]{1,0:T(8,128)(2,1)} %collective-permute-done.34.refs_3_), channel_id=1, source_target_pairs={{2,3},{6,7},{10,11},{14,15},{18,19},{22,23},{26,27},{30,31}} | collective-permute-start | bytes 1572872 | tf_op jit(solution)/shard_map/ppermute | solution.py:74
  305.6 90.4 %all-gather.8.cloned.1.call-start = ((), (), s32[]{:S(2)}) async-start(), calls=%async_computation.8 | async-start | bytes 2621440 | tf_op jit(solution)/shard_map/all_gather | solution.py:671
  351.1 104.5 %reduce-scatter.10.cloned.1.call-start = ((), (), s32[]{:S(2)}) async-start(), calls=%async_computation.9 | async-start | bytes 2621440 | tf_op jit(solution)/shard_map/reduce_scatter | solution.py:674
  413.2 92.7 %all-gather.10.cloned.1.call-start = ((), (), s32[]{:S(2)}) async-start(), calls=%async_computation.10 | async-start | bytes 2621440 | tf_op jit(solution)/shard_map/all_gather | solution.py:671
  461.0 103.9 %reduce-scatter.12.cloned.1.call-start = ((), (), s32[]{:S(2)}) async-start(), calls=%async_computation.11 | async-start | bytes 2621440 | tf_op jit(solution)/shard_map/reduce_scatter | solution.py:674
  522.4 91.7 %all-gather.12.cloned.1.call-start = ((), (), s32[]{:S(2)}) async-start(), calls=%async_computation.12 | async-start | bytes 2621440 | tf_op jit(solution)/shard_map/all_gather | solution.py:671
  569.3 233.1 %reduce-scatter.14.cloned.1.call-start = ((), (), s32[]{:S(2)}) async-start(), calls=%async_computation.14 | async-start | bytes 30081024 | tf_op jit(solution)/shard_map/reduce_scatter | solution.py:704
  638.4 247.9 %all-gather.14.cloned.1.call-start = ((), (), s32[]{:S(2)}) async-start(), calls=%async_computation.13 | async-start | bytes 7864320 | tf_op jit(solution)/shard_map/all_gather | solution.py:671
  642.4 8.7 collective-permute-start.51
  646.2 9.0 collective-permute-start.45
  651.1 43.0 %collective-permute-start.52 = (bf16[128,2048]{1,0:T(8,128)(2,1)S(1)}, bf16[128,2048]{1,0:T(8,128)(2,1)S(1)}, u32[]{:S(2)}, u32[]{:S(2)}) collective-permute-start(bf16[128,2048]{1,0:T(8,128)(2,1)S(1)} %get-tuple-element.167), channel_id=1, source_target_pairs={{2,1},{3,2},{6,5},{7,6},{10,9},{11,10},{14,13},{15,14},{18,17},{19... | collective-permute-start | bytes 1572872 | tf_op jit(solution)/shard_map/ppermute | solution.py:85
  651.8 15.4 %collective-permute-start.48 = (bf16[128,2048]{1,0:T(8,128)(2,1)S(1)}, bf16[128,2048]{1,0:T(8,128)(2,1)S(1)}, u32[]{:S(2)}, u32[]{:S(2)}) collective-permute-start(bf16[128,2048]{1,0:T(8,128)(2,1)S(1)} %get-tuple-element.168), channel_id=1, source_target_pairs={{0,1},{4,5},{8,9},{12,13},{16,17},{20,21},{24,25},{28,29}} | collective-permute-start | bytes 1572872 | tf_op jit(solution)/shard_map/ppermute | solution.py:83
  655.3 50.3 %collective-permute-start.46 = (bf16[128,2048]{1,0:T(8,128)(2,1)S(1)}, bf16[128,2048]{1,0:T(8,128)(2,1)S(1)}, u32[]{:S(2)}, u32[]{:S(2)}) collective-permute-start(bf16[128,2048]{1,0:T(8,128)(2,1)S(1)} %get-tuple-element.162), channel_id=1, source_target_pairs={{2,1},{3,2},{6,5},{7,6},{10,9},{11,10},{14,13},{15,14},{18,17},{19... | collective-permute-start | bytes 1572872 | tf_op jit(solution)/shard_map/ppermute | solution.py:85
  656.0 22.5 %collective-permute-start.42 = (bf16[128,2048]{1,0:T(8,128)(2,1)S(1)}, bf16[128,2048]{1,0:T(8,128)(2,1)S(1)}, u32[]{:S(2)}, u32[]{:S(2)}) collective-permute-start(bf16[128,2048]{1,0:T(8,128)(2,1)S(1)} %get-tuple-element.163), channel_id=1, source_target_pairs={{0,1},{4,5},{8,9},{12,13},{16,17},{20,21},{24,25},{28,29}} | collective-permute-start | bytes 1572872 | tf_op jit(solution)/shard_map/ppermute | solution.py:83
  658.0 58.8 %collective-permute-start.40 = (bf16[128,2048]{1,0:T(8,128)(2,1)S(1)}, bf16[128,2048]{1,0:T(8,128)(2,1)S(1)}, u32[]{:S(2)}, u32[]{:S(2)}) collective-permute-start(bf16[128,2048]{1,0:T(8,128)(2,1)S(1)} %get-tuple-element.157), channel_id=1, source_target_pairs={{2,1},{3,2},{6,5},{7,6},{10,9},{11,10},{14,13},{15,14},{18,17},{19... | collective-permute-start | bytes 1572872 | tf_op jit(solution)/shard_map/ppermute | solution.py:85
  667.2 22.5 %collective-permute-start.36 = (bf16[128,2048]{1,0:T(8,128)(2,1)S(1)}, bf16[128,2048]{1,0:T(8,128)(2,1)S(1)}, u32[]{:S(2)}, u32[]{:S(2)}) collective-permute-start(bf16[128,2048]{1,0:T(8,128)(2,1)S(1)} %get-tuple-element.158), channel_id=1, source_target_pairs={{0,1},{4,5},{8,9},{12,13},{16,17},{20,21},{24,25},{28,29}} | collective-permute-start | bytes 1572872 | tf_op jit(solution)/shard_map/ppermute | solution.py:83
  678.5 22.5 %collective-permute-start.49 = (bf16[128,2048]{1,0:T(8,128)(2,1)S(1)}, bf16[128,2048]{1,0:T(8,128)(2,1)S(1)}, u32[]{:S(2)}, u32[]{:S(2)}) collective-permute-start(bf16[128,2048]{1,0:T(8,128)(2,1)S(1)} %slice_add_fusion.1), channel_id=1, source_target_pairs={{0,1},{1,2},{4,5},{5,6},{8,9},{9,10},{12,13},{13,14},{16,17},{17,1... | collective-permute-start | bytes 1572872 | tf_op jit(solution)/shard_map/ppermute | solution.py:83
  689.7 22.5 %collective-permute-start.43 = (bf16[128,2048]{1,0:T(8,128)(2,1)S(1)}, bf16[128,2048]{1,0:T(8,128)(2,1)S(1)}, u32[]{:S(2)}, u32[]{:S(2)}) collective-permute-start(bf16[128,2048]{1,0:T(8,128)(2,1)S(1)} %slice_add_fusion.3), channel_id=1, source_target_pairs={{0,1},{1,2},{4,5},{5,6},{8,9},{9,10},{12,13},{13,14},{16,17},{17,1... | collective-permute-start | bytes 1572872 | tf_op jit(solution)/shard_map/ppermute | solution.py:83
  694.2 29.2 %collective-permute-start.37 = (bf16[128,2048]{1,0:T(8,128)(2,1)S(1)}, bf16[128,2048]{1,0:T(8,128)(2,1)S(1)}, u32[]{:S(2)}, u32[]{:S(2)}) collective-permute-start(bf16[128,2048]{1,0:T(8,128)(2,1)S(1)} %slice_add_fusion.5), channel_id=1, source_target_pairs={{0,1},{1,2},{4,5},{5,6},{8,9},{9,10},{12,13},{13,14},{16,17},{17,1... | collective-permute-start | bytes 1572872 | tf_op jit(solution)/shard_map/ppermute | solution.py:83
  701.1 33.5 %collective-permute-start.50 = (bf16[128,2048]{1,0:T(8,128)(2,1)S(1)}, bf16[128,2048]{1,0:T(8,128)(2,1)S(1)}, u32[]{:S(2)}, u32[]{:S(2)}) collective-permute-start(bf16[128,2048]{1,0:T(8,128)(2,1)S(1)} %get-tuple-element.165), channel_id=1, source_target_pairs={{0,1},{1,2},{2,3},{4,5},{5,6},{6,7},{8,9},{9,10},{10,11},{12,13},{... | collective-permute-start | bytes 1572872 | tf_op jit(solution)/shard_map/ppermute | solution.py:83
  705.5 30.4 %collective-permute-start.53 = (bf16[128,2048]{1,0:T(8,128)(2,1)S(1)}, bf16[128,2048]{1,0:T(8,128)(2,1)S(1)}, u32[]{:S(2)}, u32[]{:S(2)}) collective-permute-start(bf16[128,2048]{1,0:T(8,128)(2,1)S(1)} %get-tuple-element.164), channel_id=1, source_target_pairs={{1,0},{2,1},{3,2},{5,4},{6,5},{7,6},{9,8},{10,9},{11,10},{13,12},{... | collective-permute-start | bytes 1572872 | tf_op jit(solution)/shard_map/ppermute | solution.py:85
  712.3 33.6 %collective-permute-start.44 = (bf16[128,2048]{1,0:T(8,128)(2,1)S(1)}, bf16[128,2048]{1,0:T(8,128)(2,1)S(1)}, u32[]{:S(2)}, u32[]{:S(2)}) collective-permute-start(bf16[128,2048]{1,0:T(8,128)(2,1)S(1)} %get-tuple-element.160), channel_id=1, source_target_pairs={{0,1},{1,2},{2,3},{4,5},{5,6},{6,7},{8,9},{9,10},{10,11},{12,13},{... | collective-permute-start | bytes 1572872 | tf_op jit(solution)/shard_map/ppermute | solution.py:83
  716.8 29.1 %collective-permute-start.47 = (bf16[128,2048]{1,0:T(8,128)(2,1)S(1)}, bf16[128,2048]{1,0:T(8,128)(2,1)S(1)}, u32[]{:S(2)}, u32[]{:S(2)}) collective-permute-start(bf16[128,2048]{1,0:T(8,128)(2,1)S(1)} %get-tuple-element.159), channel_id=1, source_target_pairs={{1,0},{2,1},{3,2},{5,4},{6,5},{7,6},{9,8},{10,9},{11,10},{13,12},{... | collective-permute-start | bytes 1572872 | tf_op jit(solution)/shard_map/ppermute | solution.py:85
  723.6 31.4 %collective-permute-start.38 = (bf16[128,2048]{1,0:T(8,128)(2,1)S(1)}, bf16[128,2048]{1,0:T(8,128)(2,1)S(1)}, u32[]{:S(2)}, u32[]{:S(2)}) collective-permute-start(bf16[128,2048]{1,0:T(8,128)(2,1)S(1)} %get-tuple-element.155), channel_id=1, source_target_pairs={{0,1},{1,2},{2,3},{4,5},{5,6},{6,7},{8,9},{9,10},{10,11},{12,13},{... | collective-permute-start | bytes 1572872 | tf_op jit(solution)/shard_map/ppermute | solution.py:83
  734.6 20.3 %collective-permute-start.41 = (bf16[128,2048]{1,0:T(8,128)(2,1)S(1)}, bf16[128,2048]{1,0:T(8,128)(2,1)S(1)}, u32[]{:S(2)}, u32[]{:S(2)}) collective-permute-start(bf16[128,2048]{1,0:T(8,128)(2,1)S(1)} %get-tuple-element.154), channel_id=1, source_target_pairs={{1,0},{2,1},{3,2},{5,4},{6,5},{7,6},{9,8},{10,9},{11,10},{13,12},{... | collective-permute-start | bytes 1572872 | tf_op jit(solution)/shard_map/ppermute | solution.py:85
  807.4 52.9 %collective-permute-start.56 = (f32[256,128]{1,0:T(8,128)}, f32[256,128]{1,0:T(8,128)S(1)}, u32[]{:S(2)}, u32[]{:S(2)}) collective-permute-start(f32[256,128]{1,0:T(8,128)} %get-tuple-element.95), channel_id=1, source_target_pairs={{0,3},{1,0},{2,1},{3,2},{4,7},{5,4},{6,5},{7,6},{8,11},{9,8},{10,9... | collective-permute-start | bytes 393224 | tf_op jit(solution)/shard_map/ppermute | solution.py:724
  810.8 49.5 %collective-permute-start.55 = (f32[256,128]{1,0:T(8,128)}, f32[256,128]{1,0:T(8,128)S(1)}, u32[]{:S(2)}, u32[]{:S(2)}) collective-permute-start(f32[256,128]{1,0:T(8,128)} %get-tuple-element.95), channel_id=1, source_target_pairs={{0,2},{1,3},{2,0},{3,1},{4,6},{5,7},{6,4},{7,5},{8,10},{9,11},{10,... | collective-permute-start | bytes 393224 | tf_op jit(solution)/shard_map/ppermute | solution.py:724
  810.8 49.5 %collective-permute-start.54 = (f32[256,128]{1,0:T(8,128)}, f32[256,128]{1,0:T(8,128)S(1)}, u32[]{:S(2)}, u32[]{:S(2)}) collective-permute-start(f32[256,128]{1,0:T(8,128)} %get-tuple-element.95), channel_id=1, source_target_pairs={{0,1},{1,2},{2,3},{3,0},{4,5},{5,6},{6,7},{7,4},{8,9},{9,10},{10,1... | collective-permute-start | bytes 393224 | tf_op jit(solution)/shard_map/ppermute | solution.py:724
  (46 other events, 1147.0 us)
Sparse Core Ops, SparseCore 0:
  27.1 128.0 all-gather.5
  638.5 163.8 reduce-scatter.13
Sparse Core Ops, SparseCore 1:
  143.2 75.2 reduce-scatter.5
  305.7 41.7 reduce-scatter.7
  351.2 44.8 all-gather.7
  413.3 42.3 reduce-scatter.9
  461.1 44.8 all-gather.9
  522.5 42.3 reduce-scatter.11
  569.4 44.7 all-gather.11
  758.9 127.3 all-gather.13

commit v3 on v2

v3 whole, which is shorter than its diff:
```python
import math

import jax
import jax.numpy as jnp
from jax import lax
from jax.experimental import pallas as pl
from jax.experimental.pallas import tpu as pltpu
from jax.sharding import PartitionSpec as P

HEAD_DIM = 128
DOCS = 2


highest = lax.Precision.HIGHEST
epsilon = 1e-05
bf16 = jnp.bfloat16
f32 = jnp.float32
CHUNK = 16


def rms_norm(values, gain_vec):
    square = jnp.mean(values * values, axis=-1, keepdims=True)
    return values * lax.rsqrt(square + epsilon) * gain_vec


def gelu_exact(values):
    return jax.nn.gelu(values, approximate=False)


def mixer(out_rows, gain_vec, first_matrix, second_matrix):
    hidden = gelu_exact(jnp.dot(rms_norm(out_rows, gain_vec), first_matrix, precision=highest))
    return jnp.dot(hidden, second_matrix, precision=highest)


def plain_dot(left, right):
    return jnp.dot(left, right, preferred_element_type=f32)


def dot_left_t(left, right):
    return lax.dot_general(left, right, (((0,), (0,)), ((), ())), preferred_element_type=f32)


def dot_right_t(left, right):
    return lax.dot_general(left, right, (((1,), (1,)), ((), ())), preferred_element_type=f32)


def doubling_sum(value, axis):
    size = lax.axis_size(axis)
    step = 1
    while step < size:
        value = value + lax.ppermute(value, axis, [(i, i ^ step) for i in range(size)])
        step *= 2
    return value


def total_of(pieces):
    total = pieces[0]
    for piece in pieces[1:]:
        total = total + piece
    return total


def join(values, others):
    anywhere = pl.BlockSpec(memory_space=pl.ANY)
    return list(
        pl.pallas_call(
            lambda *refs: None,
            in_specs=[anywhere] * (len(values) + len(others)),
            out_specs=[anywhere] * len(values),
            out_shape=[jax.ShapeDtypeStruct(v.shape, v.dtype) for v in values],
            input_output_aliases={i: i for i in range(len(values))},
        )(*values, *others)
    )


def after(value, *others):
    return join([value], others)[0]


def sum_line(blocks, count):
    up = down = None
    for k in range(1, count):
        up = blocks[k] if up is None else blocks[k] + up
        up = lax.ppermute(up, "layer", [(i, i + 1) for i in range(k)])
        down = blocks[count - k] if down is None else blocks[count - k] + down
        down = lax.ppermute(down, "layer", [(i, i - 1) for i in range(count - k, count)])
    return [blocks[0], up, down]


def vmem(megabytes):
    return pltpu.CompilerParams(vmem_limit_bytes=megabytes << 20)


def row_loop(rows, body, carry):
    return lax.fori_loop(
        0, rows // CHUNK, lambda i, c: body(pl.ds(pl.multiple_of(i * CHUNK, CHUNK), CHUNK), c), carry
    )


def stream_kernel(mix_ref, hist_ref, near_ref, rest_ref, *, stored):
    width = rest_ref.shape[1]
    lanes = 512

    def body(at, carry):
        mix = mix_ref[at, :]
        for c in range(0, width, lanes):
            rows = [hist_ref[j, at, c : c + lanes].astype(f32) for j in range(stored)]
            for s in range(4):
                total = total_of(
                    [rows[j] * mix[:, s * stored + j : s * stored + j + 1] for j in range(stored)]
                ).astype(bf16)
                if s < 3:
                    near_ref[at, s * width + c : s * width + c + lanes] = total
                else:
                    rest_ref[at, c : c + lanes] = total
        return carry

    row_loop(rest_ref.shape[0], body, 0)


def stream_sums(mix_cols, history):
    stored, tokens, width = history.shape
    rows = 128
    here = lambda i: (i, 0)
    return pl.pallas_call(
        lambda *refs: stream_kernel(*refs, stored=stored),
        grid=(tokens // rows,),
        in_specs=[
            pl.BlockSpec((rows, 4 * stored), here),
            pl.BlockSpec((stored, rows, width), lambda i: (0, i, 0)),
        ],
        out_specs=[pl.BlockSpec((rows, 3 * width), here), pl.BlockSpec((rows, width), here)],
        out_shape=[
            jax.ShapeDtypeStruct((tokens, 3 * width), bf16),
            jax.ShapeDtypeStruct((tokens, width), bf16),
        ],
        compiler_params=vmem(48),
    )(mix_cols, history)


def streams_norm(values, gains):
    width = gains.shape[1]

    def kernel(gain_ref, value_ref, norm_ref):
        for s in range(3):
            cols = slice(s * width, (s + 1) * width)

            def body(at, carry, s=s, cols=cols):
                rows = value_ref[at, cols].astype(f32)
                centre = rows - jnp.mean(rows, axis=1, keepdims=True)
                spread = jnp.mean(centre * centre, axis=1, keepdims=True)
                normed = centre * lax.rsqrt(spread + epsilon) * gain_ref[s : s + 1, :]
                norm_ref[at, cols] = normed.astype(bf16)
                return carry

            row_loop(value_ref.shape[0], body, 0)

    return pl.pallas_call(
        kernel,
        out_shape=jax.ShapeDtypeStruct(values.shape, bf16),
        compiler_params=vmem(48),
    )(gains, values)


def row_norm(values, gain_vec):
    def kernel(gain_ref, value_ref, norm_ref):
        def body(at, carry):
            rows = value_ref[at, :].astype(f32)
            centre = rows - jnp.mean(rows, axis=1, keepdims=True)
            spread = jnp.mean(centre * centre, axis=1, keepdims=True)
            norm_ref[at, :] = (centre * lax.rsqrt(spread + epsilon) * gain_ref[...]).astype(bf16)
            return carry

        row_loop(value_ref.shape[0], body, 0)

    return pl.pallas_call(
        kernel,
        out_shape=jax.ShapeDtypeStruct(values.shape, bf16),
        compiler_params=vmem(48),
    )(gain_vec[None], values)


def norm_grad(values, grad, gain):
    centre = values - jnp.mean(values, axis=1, keepdims=True)
    inv = lax.rsqrt(jnp.mean(centre * centre, axis=1, keepdims=True) + epsilon)
    hat = centre * inv
    scaled = grad * gain
    back = (
        scaled
        - jnp.mean(scaled, axis=1, keepdims=True)
        - hat * jnp.mean(scaled * hat, axis=1, keepdims=True)
    ) * inv
    return back, jnp.sum(grad * hat, axis=0, keepdims=True)


def back_kernel(gain_ref, value_ref, *refs, parts, based):
    part_refs = refs[:parts]
    base_ref = refs[parts] if based else None
    out_ref, dgain_ref = refs[-2:]

    def body(at, dgain):
        values = value_ref[at, :].astype(f32)
        grad = total_of([p[at, :].astype(f32) for p in part_refs])
        back, dgain_rows = norm_grad(values, grad, gain_ref[...])
        if based:
            back = back + base_ref[at, :]
        out_ref[at, :] = back.astype(bf16)
        return dgain + dgain_rows

    dgain_ref[...] = row_loop(value_ref.shape[0], body, jnp.zeros(dgain_ref.shape, f32))


def norm_back(values, parts, gain_vec, base=None, order=()):
    width = gain_vec.shape[0]
    operands = [gain_vec[None], values] + list(parts) + ([] if base is None else [base])
    arrays, specs = [], []
    for operand in operands:
        array, column = operand if isinstance(operand, tuple) else (operand, 0)
        rows = 1 if array.shape[0] == 1 else values_rows(values)
        arrays.append(array)
        specs.append(pl.BlockSpec((rows, width), lambda i, column=column: (0, column)))
    number = len(arrays)
    rows = values_rows(values)
    whole = lambda i: (0, 0)
    back, dgain = pl.pallas_call(
        lambda *refs: back_kernel(
            *refs[:number], *refs[-2:], parts=len(parts), based=base is not None
        ),
        grid=(1,),
        in_specs=specs + [pl.BlockSpec(memory_space=pl.ANY)] * len(order),
        out_specs=[pl.BlockSpec((rows, width), whole), pl.BlockSpec((1, width), whole)],
        out_shape=[
            jax.ShapeDtypeStruct((rows, width), bf16),
            jax.ShapeDtypeStruct((1, width), f32),
        ],
        compiler_params=vmem(48),
    )(*arrays, *order)
    return back, dgain[0]


def values_rows(values):
    return (values[0] if isinstance(values, tuple) else values).shape[0]


def history_kernel(mix_ref, hist_ref, *refs, stored):
    grad_refs, (hist_out, mix_out) = refs[:4], refs[-2:]
    rows, width = hist_out.shape[1:]
    lanes = 512
    group = 64

    token = lax.broadcasted_iota(jnp.int32, (group, stored * group), 0)
    other = lax.broadcasted_iota(jnp.int32, (group, stored * group), 1)
    for g in range(0, rows, group):
        grads = jnp.concatenate([r[g : g + group, :] for r in grad_refs], axis=0)
        stored_rows = jnp.concatenate([hist_ref[j, g : g + group, :] for j in range(stored)], axis=0)
        pairs = contract_cols(grads, stored_rows)
        columns = []
        for s in range(4):
            part = pairs[s * group : (s + 1) * group, :]
            for j in range(stored):
                kept = jnp.where(other == token + j * group, part, 0.0)
                columns.append(jnp.sum(kept, axis=1, keepdims=True))
        mix_out[g : g + group, :] = jnp.concatenate(columns, axis=1)

    def body(at, carry):
        mix = mix_ref[at, :]
        for c in range(0, width, lanes):
            cols = slice(c, c + lanes)
            wide = [r[at, cols].astype(f32) for r in grad_refs]
            for j in range(stored):
                total = total_of(
                    [wide[s] * mix[:, s * stored + j : s * stored + j + 1] for s in range(4)]
                )
                hist_out[j, at, cols] = total.astype(bf16)
        return carry

    row_loop(rows, body, 0)


def history_grads(mix_cols, history, grads, order):
    stored, tokens, width = history.shape
    rows = 128
    here = lambda i: (i, 0)
    there = lambda i: (0, i, 0)
    return pl.pallas_call(
        lambda *refs: history_kernel(*refs, stored=stored),
        grid=(tokens // rows,),
        in_specs=[
            pl.BlockSpec((rows, 4 * stored), here),
            pl.BlockSpec((stored, rows, width), there),
        ]
        + [pl.BlockSpec((rows, width), lambda i, column=column: (i, column)) for _, column in grads]
        + [pl.BlockSpec(memory_space=pl.ANY)] * len(order),
        out_specs=[
            pl.BlockSpec((stored, rows, width), there),
            pl.BlockSpec((rows, 4 * stored), here),
        ],
        out_shape=[
            jax.ShapeDtypeStruct((stored, tokens, width), bf16),
            jax.ShapeDtypeStruct((tokens, 4 * stored), f32),
        ],
        compiler_params=vmem(48),
    )(mix_cols, history, *[g for g, _ in grads], *order)


def contract_rows(left, right):
    return lax.dot_general(left, right, (((0,), (0,)), ((), ())), preferred_element_type=f32)


def contract_cols(left, right):
    return lax.dot_general(left, right, (((1,), (1,)), ((), ())), preferred_element_type=f32)


def mlp_grads(mlp_rows, up_low, branch_rows, active, part):
    tokens, width = mlp_rows.shape
    hidden = active.shape[1]
    rows = 256

    def kernel(mlp_ref, up_ref, branch_ref, active_ref, out_ref):
        out_ref[:, :hidden] = contract_rows(mlp_ref[...], up_ref[...]).astype(bf16)
        out_ref[:, hidden : 2 * hidden] = contract_rows(branch_ref[...], active_ref[...]).astype(bf16)
        out_ref[:, 2 * hidden :] = jnp.zeros((rows, 2 * part - 2 * hidden), bf16)

    side = pl.BlockSpec((tokens, rows), lambda i: (0, i))
    return pl.pallas_call(
        kernel,
        grid=(width // rows,),
        in_specs=[side, resident(up_low), side, resident(active)],
        out_specs=pl.BlockSpec((rows, 2 * part), lambda i: (i, 0)),
        out_shape=jax.ShapeDtypeStruct((width, 3 * part), bf16),
        compiler_params=vmem(56),
    )(mlp_rows, up_low, branch_rows, active)


def attention_grads(so_far, near, lin_grads, hidden_rows, context, first, part, order):
    tokens, width = hidden_rows.shape
    heads = context.shape[1]
    rows = 256

    def kernel(q_ref, k_ref, v_ref, dq_ref, dk_ref, dv_ref, hidden_ref, ctx_ref, first_ref, *refs):
        out_ref = refs[-1]
        pairs = ((q_ref, dq_ref), (k_ref, dk_ref), (v_ref, dv_ref), (hidden_ref, ctx_ref))
        for s, (left, right) in enumerate(pairs):
            out_ref[:, s * heads : (s + 1) * heads] = contract_rows(left[...], right[...]).astype(bf16)
        out_ref[:, 4 * heads :] = first_ref[...].astype(bf16)

    side = pl.BlockSpec((tokens, rows), lambda i: (0, i))
    return pl.pallas_call(
        kernel,
        grid=(width // rows,),
        in_specs=[
            pl.BlockSpec((tokens, rows), lambda i, s=s: (0, s * (width // rows) + i))
            for s in range(3)
        ]
        + [resident(lin_grads[0])] * 3
        + [side, resident(context)]
        + [pl.BlockSpec((rows, first.shape[1]), lambda i: (i, 0))]
        + [pl.BlockSpec(memory_space=pl.ANY)] * (1 + len(order)),
        out_specs=pl.BlockSpec((rows, part), lambda i: (i, 2)),
        out_shape=jax.ShapeDtypeStruct(so_far.shape, bf16),
        input_output_aliases={9: 0},
        compiler_params=vmem(56),
    )(near, near, near, *lin_grads, hidden_rows, context, first, so_far, *order)


def round_weights(weights, turned, order):
    heights = [w.shape[1] if t else w.shape[0] for w, t in zip(weights, turned)]
    widths = [w.shape[0] if t else w.shape[1] for w, t in zip(weights, turned)]
    number = len(weights)

    def kernel(*refs):
        at = 0
        for ref, t, size in zip(refs[:number], turned, widths):
            value = ref[...].T if t else ref[...]
            refs[-1][:, at : at + size] = value.astype(bf16)
            at += size

    return pl.pallas_call(
        kernel,
        in_specs=[pl.BlockSpec(memory_space=pltpu.VMEM)] * number
        + [pl.BlockSpec(memory_space=pl.ANY)] * len(order),
        out_shape=jax.ShapeDtypeStruct((heights[0], sum(widths)), bf16),
        compiler_params=vmem(56),
    )(*weights, *order)


def feed_forward(rows, full, up_first):
    tokens, width = rows.shape
    hidden = (full.shape[1] - up_first) // 2
    cols = 512
    first = up_first // cols
    steps = hidden // cols

    def kernel(rows_ref, up_ref, down_ref, active_ref, slope_ref, out_ref, total_ref):
        step = pl.program_id(0)
        up = jnp.dot(rows_ref[...], up_ref[...], preferred_element_type=f32)
        below = 0.5 * (1.0 + lax.erf(up * (0.5**0.5)))
        active = (up * below).astype(bf16)
        active_ref[...] = active
        slope_ref[...] = below + up * jnp.exp(-0.5 * up * up) * ((2.0 * math.pi) ** -0.5)
        share = contract_cols(active, down_ref[...])

        @pl.when(step == 0)
        def _():
            total_ref[...] = share

        @pl.when(step > 0)
        def _():
            total_ref[...] += share

        @pl.when(step == steps - 1)
        def _():
            out_ref[...] = total_ref[...].astype(bf16)

    part = pl.BlockSpec((tokens, cols), lambda i: (0, i))
    return pl.pallas_call(
        kernel,
        grid=(steps,),
        in_specs=[
            resident(rows),
            pl.BlockSpec((width, cols), lambda i: (0, first + i)),
            pl.BlockSpec((width, cols), lambda i: (0, first + steps + i)),
        ],
        out_specs=[part, part, pl.BlockSpec((tokens, width), lambda i: (0, 0))],
        out_shape=[
            jax.ShapeDtypeStruct((tokens, hidden), bf16),
            jax.ShapeDtypeStruct((tokens, hidden), f32),
            jax.ShapeDtypeStruct((tokens, width), bf16),
        ],
        scratch_shapes=[pltpu.VMEM((tokens, width), f32)],
        compiler_params=vmem(60),
    )(rows, full, full)


def feed_back(rows, full, up_first, slope):
    tokens, width = rows.shape
    hidden = slope.shape[1]
    cols = 512
    first = up_first // cols
    steps = hidden // cols

    def kernel(rows_ref, up_ref, down_ref, slope_ref, *refs):
        low_ref, out_ref, total_ref = refs[-3:]
        step = pl.program_id(0)
        grad = jnp.dot(rows_ref[...], down_ref[...], preferred_element_type=f32)
        low = (grad * slope_ref[...]).astype(bf16)
        low_ref[...] = low
        share = contract_cols(low, up_ref[...])

        @pl.when(step == 0)
        def _():
            total_ref[...] = share

        @pl.when(step > 0)
        def _():
            total_ref[...] += share

        @pl.when(step == steps - 1)
        def _():
            out_ref[...] = total_ref[...].astype(bf16)

    part = pl.BlockSpec((tokens, cols), lambda i: (0, i))
    return pl.pallas_call(
        kernel,
        grid=(steps,),
        in_specs=[
            resident(rows),
            pl.BlockSpec((width, cols), lambda i: (0, first + i)),
            pl.BlockSpec((width, cols), lambda i: (0, first + steps + i)),
            part,
        ],
        out_specs=[part, pl.BlockSpec((tokens, width), lambda i: (0, 0))],
        out_shape=[
            jax.ShapeDtypeStruct((tokens, hidden), bf16),
            jax.ShapeDtypeStruct((tokens, width), bf16),
        ],
        scratch_shapes=[pltpu.VMEM((tokens, width), f32)],
        compiler_params=vmem(60),
    )(rows, full, full, slope)


def turn(values, cosine, sine):
    return values * cosine + pltpu.roll(values, HEAD_DIM // 2, 1) * sine


def score_block(queries, keys, allowed):
    scores = lax.dot_general(
        queries, keys, (((1,), (1,)), ((), ())), preferred_element_type=f32
    ) * (HEAD_DIM ** (-0.5))
    return jnp.where(allowed, scores, -1e30)


def allowed_block(row_ids, col_ids):
    return (row_ids[:, 0:1] == col_ids[0:1, :]) & (row_ids[:, 1:2] >= col_ids[1:2, :])


GROUP = 2


def attend_kernel(
    rows_ref, cols_ref, cos_ref, sin_ref, near_ref, rest_ref, wq_ref, wk_ref, wv_ref, wo_ref,
    ctx_ref, qr_ref, kr_ref, v_ref, lse_ref, out_ref, total_ref,
):
    step = pl.program_id(0)
    width = out_ref.shape[1]
    allowed = allowed_block(rows_ref[...], cols_ref[...])

    def lin(s, weight_ref):
        rows = near_ref[:, s * width : (s + 1) * width]
        return jnp.dot(rows, weight_ref[...], preferred_element_type=f32)

    q_lin, k_lin = lin(0, wq_ref), lin(1, wk_ref)
    v_ref[...] = lin(2, wv_ref).astype(bf16)
    for g in range(GROUP):
        cols = slice(g * HEAD_DIM, (g + 1) * HEAD_DIM)
        queries = turn(q_lin[:, cols], cos_ref[...], sin_ref[...]).astype(bf16)
        keys = turn(k_lin[:, cols], cos_ref[...], sin_ref[...]).astype(bf16)
        qr_ref[:, cols] = queries
        kr_ref[:, cols] = keys
        scores = score_block(queries, keys, allowed)
        row_max = jnp.max(scores, axis=1, keepdims=True)
        shifted = jnp.exp(scores - row_max)
        row_sum = jnp.sum(shifted, axis=1, keepdims=True)
        probs = (shifted / row_sum).astype(bf16)
        context = jnp.dot(probs, v_ref[:, cols], preferred_element_type=f32)
        ctx_ref[:, cols] = context.astype(bf16)
        lse_ref[g] = row_max + jnp.log(row_sum)
    share = contract_cols(ctx_ref[...], wo_ref[...])

    @pl.when(step == 0)
    def _():
        total_ref[...] = share + rest_ref[...].astype(f32)

    @pl.when(step > 0)
    def _():
        total_ref[...] += share

    @pl.when(step == pl.num_programs(0) - 1)
    def _():
        out_ref[...] = total_ref[...].astype(bf16)


def resident(array):
    return pl.BlockSpec(
        array.shape, lambda i: (0,) * array.ndim, pipeline_mode=pl.Buffered(buffer_count=1)
    )


def head_columns(full, first):
    lanes = GROUP * HEAD_DIM
    return pl.BlockSpec((full.shape[0], lanes), lambda h: (0, first // lanes + h))


def attend(row_ids, col_ids, cosine, sine, near, rest, full, heads):
    tokens, width = rest.shape
    head = pl.BlockSpec((tokens, GROUP * HEAD_DIM), lambda h: (0, h))
    fixed = [row_ids, col_ids, cosine, sine, near, rest]

    return pl.pallas_call(
        attend_kernel,
        grid=(heads // HEAD_DIM // GROUP,),
        in_specs=[resident(a) for a in fixed]
        + [head_columns(full, s * heads) for s in range(4)],
        out_specs=[head] * 4
        + [
            pl.BlockSpec((GROUP, tokens, 1), lambda h: (h, 0, 0)),
            pl.BlockSpec((tokens, width), lambda h: (0, 0)),
        ],
        out_shape=[jax.ShapeDtypeStruct((tokens, heads), bf16)] * 4
        + [
            jax.ShapeDtypeStruct((heads // HEAD_DIM, tokens, 1), f32),
            jax.ShapeDtypeStruct((tokens, width), bf16),
        ],
        scratch_shapes=[pltpu.VMEM((tokens, width), f32)],
        compiler_params=vmem(60),
    )(*fixed, *[full] * 4)


def attend_back_kernel(
    rows_ref, cols_ref, cos_ref, sin_ref, hidden_ref, wo_ref, q_ref, k_ref, v_ref, lse_ref,
    dq_ref, dk_ref, dv_ref,
):
    allowed = allowed_block(rows_ref[...], cols_ref[...])
    scale = HEAD_DIM ** (-0.5)
    grads = jnp.dot(hidden_ref[...], wo_ref[...], preferred_element_type=f32).astype(bf16)
    for g in range(GROUP):
        cols = slice(g * HEAD_DIM, (g + 1) * HEAD_DIM)
        queries, keys, values, grad = q_ref[:, cols], k_ref[:, cols], v_ref[:, cols], grads[:, cols]
        probs = jnp.exp(score_block(queries, keys, allowed) - lse_ref[g])
        prob_grad = contract_cols(grad, values)
        dv_ref[:, cols] = contract_rows(probs.astype(bf16), grad).astype(bf16)
        centre = jnp.sum(probs * prob_grad, axis=1, keepdims=True)
        score_grad = (probs * (prob_grad - centre)).astype(bf16)
        dq = jnp.dot(score_grad, keys, preferred_element_type=f32) * scale
        dk = contract_rows(score_grad, queries) * scale
        dq_ref[:, cols] = turn(dq, cos_ref[...], -sin_ref[...]).astype(bf16)
        dk_ref[:, cols] = turn(dk, cos_ref[...], -sin_ref[...]).astype(bf16)


def attend_back(row_ids, col_ids, cosine, sine, hidden_rows, full, queries, keys, values, lse):
    tokens, heads = queries.shape
    head = pl.BlockSpec((tokens, GROUP * HEAD_DIM), lambda h: (0, h))
    fixed = [row_ids, col_ids, cosine, sine, hidden_rows]

    return pl.pallas_call(
        attend_back_kernel,
        grid=(heads // HEAD_DIM // GROUP,),
        in_specs=[resident(a) for a in fixed]
        + [head_columns(full, 3 * heads), head, head, head]
        + [pl.BlockSpec((GROUP, tokens, 1), lambda h: (h, 0, 0))],
        out_specs=[head, head, head],
        out_shape=[jax.ShapeDtypeStruct((tokens, heads), bf16)] * 3,
        compiler_params=vmem(60),
    )(*fixed, full, queries, keys, values, lse)


def stream_shares(where, lin_grads, full):
    tokens, heads = lin_grads[0].shape
    width = full.shape[0]
    count = where.shape[0]
    block = tokens // count

    def kernel(where_ref, dq_ref, dk_ref, dv_ref, full_ref, *out_refs):
        for s, ref in enumerate((dq_ref, dk_ref, dv_ref)):

            @pl.when(pl.program_id(0) == s)
            def _(ref=ref, out_ref=out_refs[s]):
                share = contract_cols(ref[...], full_ref[...]).astype(bf16)
                for j in range(count):
                    at = pl.ds(pl.multiple_of(where_ref[j] * block, block), block)
                    out_ref[at, :] = share[j * block : (j + 1) * block, :]

    fixed = pl.BlockSpec(
        (tokens, heads), lambda s, w: (0, 0), pipeline_mode=pl.Buffered(buffer_count=1)
    )
    return pl.pallas_call(
        kernel,
        grid_spec=pltpu.PrefetchScalarGridSpec(
            num_scalar_prefetch=1,
            grid=(3,),
            in_specs=[fixed] * 3 + [pl.BlockSpec((width, heads), lambda s, w: (0, s))],
            out_specs=[pl.BlockSpec((tokens, width), lambda s, w: (0, 0))] * 3,
        ),
        out_shape=[jax.ShapeDtypeStruct((tokens, width), bf16)] * 3,
        compiler_params=vmem(56),
    )(where, *lin_grads, full)


def unpack_grads(weight_sum, hidden, heads, part, mixes, order):
    rows = weight_sum.shape[0]

    def kernel(sum_ref, *refs):
        up_ref, down_ref, q_ref, k_ref, v_ref, o_ref, first_ref = refs[-7:]
        up_ref[...] = sum_ref[:, :hidden].astype(f32)
        down_ref[...] = sum_ref[:, hidden : 2 * hidden].astype(f32).T
        at = 2 * part
        for ref in (q_ref, k_ref, v_ref):
            ref[...] = sum_ref[:, at : at + heads].astype(f32)
            at += heads
        o_ref[...] = sum_ref[:, at : at + heads].astype(f32).T
        first_ref[...] = sum_ref[:, at + heads :].astype(f32).T[: first_ref.shape[0], :]

    shapes = [(rows, hidden), (hidden, rows)] + [(rows, heads)] * 3
    shapes += [(heads, rows), (mixes + -mixes % 8, rows)]
    return pl.pallas_call(
        kernel,
        in_specs=[pl.BlockSpec(memory_space=pltpu.VMEM)]
        + [pl.BlockSpec(memory_space=pl.ANY)] * len(order),
        out_shape=[jax.ShapeDtypeStruct(shape, f32) for shape in shapes],
        compiler_params=vmem(56),
    )(weight_sum, *order)


def places(seg_row):
    length = seg_row.shape[0]
    labels = jnp.arange(DOCS, dtype=jnp.int32)
    before = jnp.sum((seg_row[None, :] < labels[:, None]).astype(jnp.int32), axis=1)
    member = (seg_row[:, None] == labels[None, :]).astype(jnp.int32)
    begins = jnp.sum(member * before[None, :], axis=1)
    return jnp.arange(length, dtype=jnp.int32) - begins


def local(
    history,
    mix_weights,
    segments,
    w_query,
    w_key,
    w_value,
    w_output,
    w_up,
    w_down,
    norm_gains,
    w_first,
    w_second,
    out_cotangent,
    mix_cotangent,
):
    stored, row_tok, width = history.shape
    count = lax.axis_size("layer")
    me = lax.axis_index("layer")
    own_tok = row_tok // count
    order = [(me - k) % count for k in range(count)]

    def block_of(rows, k):
        return rows[k * own_tok : (k + 1) * own_tok]

    def blocks_of(rows):
        return [block_of(rows, k) for k in range(count)]

    def collect(rows):
        return lax.all_gather(rows, "layer", axis=0, tiled=True)

    def spread(rows):
        return lax.psum_scatter(rows, "layer", scatter_dimension=0, tiled=True)

    hidden = w_up.shape[1]
    heads = w_query.shape[1]
    mix_cols = mix_weights.reshape(4 * stored, row_tok).T
    near_shares, rest_share = stream_sums(mix_cols, history)
    low = round_weights(
        [w_query, w_key, w_value, w_output, w_up, w_down],
        [False, False, False, True, False, True],
        [near_shares],
    )
    full = lax.all_gather(low, "dp", axis=0, tiled=True)
    stream_own = spread(near_shares)
    normed_rows = collect(after(streams_norm(stream_own, norm_gains[:3]), full))

    seg_row = segments[0]
    place_row = places(seg_row)
    col_ids = jnp.stack([seg_row, jnp.arange(row_tok, dtype=jnp.int32)])
    half = HEAD_DIM // 2
    frequency = jnp.exp(jnp.arange(half, dtype=f32) * (-2.0 * math.log(10000.0) / HEAD_DIM))
    angles = place_row.astype(f32)[:, None] * frequency[None, :]
    cosine, sine = jnp.cos(angles), jnp.sin(angles)
    cosine = jnp.concatenate([cosine, cosine], axis=1)
    sine = jnp.concatenate([-sine, sine], axis=1)
    row_ids = col_ids.T

    context, queries, keys, values, lse, hidden_part = attend(
        row_ids, col_ids, cosine, sine, normed_rows, rest_share, full, heads
    )
    hidden_in = spread(hidden_part)
    mlp_norm = row_norm(hidden_in, norm_gains[3])
    mlp_rows = collect(mlp_norm)
    active, slope, mlp_part = feed_forward(mlp_rows, full, 4 * heads)
    block = hidden_in.astype(f32) + spread(mlp_part).astype(f32)

    next_mix, mixer_pull = jax.vjp(mixer, block, norm_gains[4], w_first, w_second)
    block_part, mixer_gain_grad, first_grad, second_grad = mixer_pull(mix_cotangent)
    block_grad = out_cotangent + block_part
    branch_rows = collect(block_grad.astype(bf16))
    up_low, mlp_part = feed_back(branch_rows, full, 4 * heads, slope)
    mlp_back = spread(mlp_part)
    part = 4 * heads + 128
    weight_grads = mlp_grads(mlp_rows, after(up_low, mlp_part), branch_rows, active, part)
    hidden_low, mlp_gain_grad = norm_back(
        hidden_in, [mlp_back], norm_gains[3], block_grad, [weight_grads]
    )
    hidden_rows = collect(hidden_low)
    lin_grads = attend_back(
        row_ids, col_ids, cosine, sine, hidden_rows, full, queries, keys, values, lse
    )
    table = jnp.stack(order).astype(jnp.int32)
    stream_parts = stream_shares(table, lin_grads, full)
    mixes = first_grad.shape[1]
    weight_grads = attention_grads(
        weight_grads,
        normed_rows,
        lin_grads,
        hidden_rows,
        context,
        jnp.pad(first_grad, ((0, 0), (0, 128 - mixes))),
        part,
        [stream_parts[0]],
    )
    weight_sum = lax.psum_scatter(weight_grads, "dp", scatter_dimension=0, tiled=True)
    gain_grads, stream_low = [], []
    for s in range(3):
        low, gain_grad = norm_back(
            (stream_own, s), sum_line(blocks_of(stream_parts[s]), count), norm_gains[s]
        )
        gain_grads.append(gain_grad)
        stream_low.append(low)
    near = collect(jnp.concatenate(stream_low, axis=1))

    gain_rows = jnp.stack(gain_grads + [mlp_gain_grad, mixer_gain_grad])
    lines = -(-mixes * mixes // width)
    second_flat = jnp.pad(second_grad.reshape(-1), (0, lines * width - mixes * mixes))
    small = jnp.concatenate([gain_rows, second_flat.reshape(lines, width)])
    small = doubling_sum(doubling_sum(small, "dp"), "layer")
    up_sum, down_sum, *projections, output_sum, first_part = unpack_grads(
        weight_sum, hidden, heads, part, mixes, [small]
    )
    gains_sum = small[:5]
    second_sum = small[5:].reshape(-1)[: mixes * mixes].reshape(mixes, mixes)
    first_sum = lax.all_gather(doubling_sum(first_part, "layer"), "dp", axis=1, tiled=True)[:mixes].T
    history_grad, mix_back = history_grads(
        mix_cols,
        history,
        [(near, 0), (near, 1), (near, 2), (hidden_rows, 0)],
        [output_sum, first_sum, small],
    )
    mix_grad = mix_back.T.reshape(4, stored, row_tok)
    return (
        block.astype(bf16),
        next_mix,
        history_grad,
        mix_grad,
        *projections,
        output_sum,
        up_sum,
        down_sum,
        gains_sum,
        first_sum,
        second_sum,
    )


def solution(mesh):
    placed = (
        P("layer", "dp", None),
        P(None, "layer", "dp"),
        P("dp", None),
        P("dp", "layer"),
        P("dp", "layer"),
        P("dp", "layer"),
        P("layer", "dp"),
        P("dp", "layer"),
        P("layer", "dp"),
        P(),
        P(),
        P(),
        P(("dp", "layer"), None),
        P(("dp", "layer"), None),
    )
    return jax.shard_map(
        local,
        mesh=mesh,
        in_specs=placed,
        out_specs=(
            P(("dp", "layer"), None),
            P(("dp", "layer"), None),
            P("layer", "dp", None),
            P(None, "layer", "dp"),
            P("dp", "layer"),
            P("dp", "layer"),
            P("dp", "layer"),
            P("layer", "dp"),
            P("dp", "layer"),
            P("layer", "dp"),
            P(),
            P(),
            P(),
        ),
        check_vma=False,
    )
```

time: 920 us -> 896 us (0.974)
  waiting for transfers between devices: 492 us -> 619 us
  starting transfers between devices: 136 us -> 59.6 us
  blocking collectives: 59.8 us -> 10.8 us
  matrix products: 24 us -> 7.24 us
    all_gather x4 -> x5, waiting for transfers between devices: 141 us -> 265 us  [collect(): return lax.all_gather(rows, 'layer', axis=0, tiled=True)]
    reduce_scatter x4, waiting for transfers between devices: 111 us -> 219 us  [spread(): return lax.psum_scatter(rows, 'layer', scatter_dimension=0, tiled=True)]
    ppermute x18 -> x9, waiting for transfers between devices: 105 us -> 54.1 us  [sum_line(): up = lax.ppermute(up, 'layer', [(i, i + 1) for i in range(k)])]
    ppermute x21 -> x7, waiting for transfers between devices: 91.5 us -> 42.4 us  [doubling_sum(): lax.ppermute(value, axis, [(i, i ^ step) for i in range(size)])]
    psum x1 -> x0, blocking collectives: 48.1 us -> none  [local(): gains_sum, second_sum = lax.psum((gain_rows, second_grad), ('dp', 'layer'))]
    ppermute x18 -> x9, starting transfers between devices: 79.1 us -> 37.2 us  [sum_line(): up = lax.ppermute(up, 'layer', [(i, i + 1) for i in range(k)])]
    ppermute x21 -> x7, starting transfers between devices: 39.9 us -> 12.9 us  [doubling_sum(): lax.ppermute(value, axis, [(i, i ^ step) for i in range(size)])]
    reduce_scatter x1, waiting for transfers between devices: 42.7 us -> 25.2 us  [local(): lax.psum_scatter(weight_grads, 'dp', scatter_dimension=0, tiled=True)]
  transfers between devices with their start and end apart: 67 -> 36, of which waited for: 38 -> 27; matrix products, arithmetic and copies ran while one was open for 3% -> 2% of each run, Pallas kernels for 5% -> 4%
where the time goes in v3:
time: 896 us; the launch traced here: 894 us
  waiting for transfers between devices  619 us (69%)
  Pallas kernels  150 us (17%)
  starting transfers between devices  59.6 us (7%)
  local copies, waits for them, and re-layouts  21.9 us (2%)
  between operations  16 us (2%)
  blocking collectives  10.8 us (1%)
  other arithmetic  10.4 us (1%)
    all_gather x5, waiting for transfers between devices, collect(): return lax.all_gather(rows, 'layer', axis=0, tiled=True)  265 us
    reduce_scatter x4, waiting for transfers between devices, spread(): return lax.psum_scatter(rows, 'layer', scatter_dimension=0, tiled=True)  219 us
    ppermute x9, waiting for transfers between devices, sum_line(): up = lax.ppermute(up, 'layer', [(i, i + 1) for i in range(k)])  54.1 us
    ppermute x7, waiting for transfers between devices, doubling_sum(): lax.ppermute(value, axis, [(i, i ^ step) for i in range(size)])  42.4 us
    ppermute x9, starting transfers between devices, sum_line(): up = lax.ppermute(up, 'layer', [(i, i + 1) for i in range(k)])  37.2 us
    reduce_scatter x1, waiting for transfers between devices, local(): lax.psum_scatter(weight_grads, 'dp', scatter_dimension=0, tiled=True)  25.2 us
  transfers between devices with their start and end apart: 36, of which 27 were waited for; matrix products, arithmetic and copies ran while one was open for 2% of the time, Pallas kernels for 4%

profile of v3, /device:TPU:0, one launch (start us, length us, event | category | flops | bytes accessed | tf_op | source)
XLA Modules:
  0.0 894.3 jit_solution(1824761063242384343)
XLA Ops:
  9.0 10.2 %shard_map.237 = (bf16[512,6144]{1,0:T(8,128)(2,1)}, bf16[512,2048]{1,0:T(8,128)(2,1)S(1)}) custom-call(f32[512,16]{1,0:T(8,128)S(1)} %bitcast.20, bf16[4,512,2048]{2,1,0:T(8,128)(2,1)} %refs_1_.5), custom_call_target="tpu_custom_call" | custom-call | tf_op jit(solution)/shard_map/pallas_call | solution.py:125
  20.6 5.0 shard_map.239
  26.5 107.7 %reduce-scatter.6.cloned.1.call-done.value_ref.refs_1_ = bf16[128,6144]{1,0:T(8,128)(2,1)} async-done(((bf16[512,6144]{1,0:T(8,128)(2,1)}), bf16[128,6144]{1,0:T(8,128)(2,1)}) %reduce-scatter.6.cloned.1.call-update) | async-done | bytes 1572880 | tf_op jit(solution)/shard_map/reduce_scatter | solution.py:715
  134.2 1.6 copy-done.2
  135.8 5.0 shard_map.238.refs_0_
  141.9 11.7 %all-gather.7.cloned.1.call-done.refs_1_.wq_ref.wk_ref.wv_ref.wo_ref.up_ref.down_ref.full_ref = bf16[2048,6144]{1,0:T(8,128)(2,1)} async-done(((bf16[256,6144]{1,0:T(8,128)(2,1)}), bf16[2048,6144]{1,0:T(8,128)(2,1)}) %all-gather.7.cloned.1.call-update) | async-done | bytes 25165840 | tf_op jit(solution)/shard_map/all_gather | solution.py:726
  157.4 111.7 %all-gather.9.cloned.1.call-done.near_ref.q_ref.k_ref.v_ref = bf16[512,6144]{1,0:T(8,128)(2,1)} async-done(((bf16[128,6144]{1,0:T(8,128)(2,1)}), bf16[512,6144]{1,0:T(8,128)(2,1)}) %all-gather.9.cloned.1.call-update) | async-done | bytes 6291472 | tf_op jit(solution)/shard_map/all_gather | solution.py:712
  269.2 16.7 %shard_map.241 = (bf16[512,512]{1,0:T(8,128)(2,1)}, bf16[512,512]{1,0:T(8,128)(2,1)}, bf16[512,512]{1,0:T(8,128)(2,1)}, bf16[512,512]{1,0:T(8,128)(2,1)}, f32[4,...) custom-call(s32[512,2]{1,0:T(8,128)} %copy.47.rows_ref, s32[2,512]{1,0:T(2,128)} %get-tuple-element.149.cols_ref, ...), custom_call_target="tpu_custom_call" | custom-call | tf_op jit(solution)/shard_map/pallas_call | solution.py:559
  286.0 42.2 %reduce-scatter.8.cloned.1.call-done.value_ref.refs_1_ = bf16[128,2048]{1,0:T(8,128)(2,1)} async-done(((bf16[512,2048]{1,0:T(8,128)(2,1)}), bf16[128,2048]{1,0:T(8,128)(2,1)}) %reduce-scatter.8.cloned.1.call-update) | async-done | bytes 524304 | tf_op jit(solution)/shard_map/reduce_scatter | solution.py:715
  329.2 2.4 shard_map.242
  331.7 45.4 %all-gather.11.cloned.1.call-done.rows_ref.mlp_ref = bf16[512,2048]{1,0:T(8,128)(2,1)} async-done(((bf16[128,2048]{1,0:T(8,128)(2,1)}), bf16[512,2048]{1,0:T(8,128)(2,1)}) %all-gather.11.cloned.1.call-update) | async-done | bytes 2097168 | tf_op jit(solution)/shard_map/all_gather | solution.py:712
  377.1 17.1 %shard_map.243 = (bf16[512,2048]{1,0:T(8,128)(2,1)}, f32[512,2048]{1,0:T(8,128)}, bf16[512,2048]{1,0:T(8,128)(2,1)}) custom-call(bf16[512,2048]{1,0:T(8,128)(2,1)} %all-gather.11.cloned.1.call-done.rows_ref.mlp_ref, bf16[2048,6144]{1,0:T(8,128)(2,1)} %all-gather.7.cloned.1.call-done.refs_1_.wq_ref.wk_ref.wv_ref.wo_ref.up_ref.down_ref.full_ref, ...), custom_call_target="tpu_custom_call" | custom-call | tf_op jit(solution)/shard_map/pallas_call | solution.py:416
  395.2 41.8 %reduce-scatter.10.cloned.1.call-done = bf16[128,2048]{1,0:T(8,128)(2,1)} async-done(((bf16[512,2048]{1,0:T(8,128)(2,1)}), bf16[128,2048]{1,0:T(8,128)(2,1)}) %reduce-scatter.10.cloned.1.call-update) | async-done | bytes 524304 | tf_op jit(solution)/shard_map/reduce_scatter | solution.py:715
  438.5 2.5 fusion.3
  440.9 1.5 multiply_reduce_fusion
  443.9 45.4 %all-gather.13.cloned.1.call-done.rows_ref.branch_ref = bf16[512,2048]{1,0:T(8,128)(2,1)} async-done(((bf16[128,2048]{1,0:T(8,128)(2,1)}), bf16[512,2048]{1,0:T(8,128)(2,1)}) %all-gather.13.cloned.1.call-update) | async-done | bytes 2097168 | tf_op jit(solution)/shard_map/all_gather | solution.py:712
  489.2 16.5 %shard_map.244 = (bf16[512,2048]{1,0:T(8,128)(2,1)}, bf16[512,2048]{1,0:T(8,128)(2,1)}) custom-call(bf16[512,2048]{1,0:T(8,128)(2,1)} %all-gather.13.cloned.1.call-done.rows_ref.branch_ref, bf16[2048,6144]{1,0:T(8,128)(2,1)} %all-gather.7.cloned.1.call-done.refs_1_.wq_ref.wk_ref.wv_ref.wo_ref.up_ref.down_ref.full_ref, ...), custom_call_target="tpu_custom_call" | custom-call | tf_op jit(solution)/shard_map/pallas_call | solution.py:463
  505.9 14.9 %shard_map.246.refs_4_.refs_0_ = bf16[2048,6528]{1,0:T(8,128)(2,1)} custom-call(bf16[512,2048]{1,0:T(8,128)(2,1)} %all-gather.11.cloned.1.call-done.rows_ref.mlp_ref, bf16[512,2048]{1,0:T(8,128)(2,1)} %shard_map.245.up_ref, bf16[512,2048]{1,0:T(8,128)(2,1)} %all-gather.13.cloned.1.call-done.rows_ref.branch_ref, bf16[512,2048]{1,0:T(8,128)(2,1)} %get-tuple-element.56.active_ref), custom_call_target="tpu_custom_call" | custom-call | tf_op jit(solution)/shard_map/pallas_call | solution.py:325
  520.8 27.8 %reduce-scatter.12.cloned.1.call-done.refs_2_ = bf16[128,2048]{1,0:T(8,128)(2,1)} async-done(((bf16[512,2048]{1,0:T(8,128)(2,1)}), bf16[128,2048]{1,0:T(8,128)(2,1)}) %reduce-scatter.12.cloned.1.call-update) | async-done | bytes 524304 | tf_op jit(solution)/shard_map/reduce_scatter | solution.py:715
  549.6 3.4 shard_map.247
  554.0 1.9 fusion.1
  556.9 41.4 %all-gather.15.cloned.1.call-done.hidden_ref.refs_5_ = bf16[512,2048]{1,0:T(8,128)(2,1)} async-done(((bf16[128,2048]{1,0:T(8,128)(2,1)}), bf16[512,2048]{1,0:T(8,128)(2,1)}) %all-gather.15.cloned.1.call-update) | async-done | bytes 2097168 | tf_op jit(solution)/shard_map/all_gather | solution.py:712
  598.4 9.8 %shard_map.248 = (bf16[512,512]{1,0:T(8,128)(2,1)}, bf16[512,512]{1,0:T(8,128)(2,1)}, bf16[512,512]{1,0:T(8,128)(2,1)}) custom-call(s32[512,2]{1,0:T(8,128)} %copy.47.rows_ref, s32[2,512]{1,0:T(2,128)} %get-tuple-element.149.cols_ref, f32[512,128]{1,0:T(8,128)} %get-tuple-element.155.cos_ref, f32[512,128]{1,0:T(8,128)} %get-tuple-element.156.sin_ref, ...), custom_call_target="tpu_custom_call" | custom-call | tf_op jit(solution)/shard_map/pallas_call | solution.py:605
  608.2 9.6 %shard_map.249 = (bf16[512,2048]{1,0:T(8,128)(2,1)}, bf16[512,2048]{1,0:T(8,128)(2,1)}, bf16[512,2048]{1,0:T(8,128)(2,1)}) custom-call(s32[4]{0:T(128)} %pad_add_fusion.1.where_ref, bf16[512,512]{1,0:T(8,128)(2,1)} %get-tuple-element.62.dq_ref, bf16[512,512]{1,0:T(8,128)(2,1)} %get-tuple-element.63.dk_ref, bf16[512,512]{1,0:T(8,128)(2,1)} %get-tuple-element.64.dv_ref, ...), custom_call_target="tpu_custom_call" | custom-call | tf_op jit(solution)/shard_map/pallas_call | solution.py:636
  617.8 12.1 %shard_map.253 = bf16[2048,6528]{1,0:T(8,128)(2,1)} custom-call(bf16[512,6144]{1,0:T(8,128)(2,1)} %all-gather.9.cloned.1.call-done.near_ref.q_ref.k_ref.v_ref, bf16[512,6144]{1,0:T(8,128)(2,1)} %all-gather.9.cloned.1.call-done.near_ref.q_ref.k_ref.v_ref, ...), custom_call_target="tpu_custom_call", output_to_operand_aliasing={{}: (9, {})} | custom-call | tf_op jit(solution)/shard_map/pallas_call | solution.py:348
  636.8 2.4 collective-permute-start.12
  640.0 1.9 collective-permute-start.6
  642.7 8.8 collective-permute-done.12
  651.5 4.4 collective-permute-start
  656.0 6.7 collective-permute-done.6
  662.7 4.4 collective-permute-start.13
  667.2 6.8 collective-permute-done
  674.0 4.8 collective-permute-start.7
  678.8 1.9 collective-permute-start.1
  680.8 4.5 collective-permute-done.13
  685.4 5.8 collective-permute-start.14
  692.5 4.0 collective-permute-done.7
  696.6 5.8 collective-permute-start.8
  703.9 3.8 collective-permute-done.1
  707.8 5.8 collective-permute-start.2
  713.6 5.3 collective-permute-done.14.refs_3_
  718.9 1.5 collective-permute-start.5
  720.5 2.6 shard_map.252
  723.1 7.1 collective-permute-done.8.refs_3_
  730.2 2.6 shard_map.251
  732.7 7.2 collective-permute-done.2.refs_3_
  740.0 2.6 shard_map.250
  745.7 1.7 collective-permute-start.19
  747.3 2.7 collective-permute-done.19
  750.0 1.7 collective-permute-start.20
  751.7 2.7 collective-permute-done.20
  754.4 2.6 collective-permute-start.21
  756.9 3.5 collective-permute-done.21
  760.4 4.2 collective-permute-start.22
  764.7 4.4 collective-permute-done.22
  769.7 25.2 %reduce-scatter.14.cloned.1.call-done.sum_ref = bf16[256,6528]{1,0:T(8,128)(2,1)} async-done(((bf16[2048,6528]{1,0:T(8,128)(2,1)}), bf16[256,6528]{1,0:T(8,128)(2,1)}) %reduce-scatter.14.cloned.1.call-update) | async-done | bytes 3342352 | tf_op jit(solution)/shard_map/reduce_scatter | solution.py:778
  794.9 5.0 shard_map.254
  800.8 1.6 collective-permute-start.23
  802.4 14.4 %collective-permute-done.23 = f32[72,256]{0,1:T(8,128)S(1)} collective-permute-done((f32[72,256]{0,1:T(8,128)S(1)}, f32[72,256]{0,1:T(8,128)S(1)}, u32[]{:S(2)}, u32[]{:S(2)}) %collective-permute-start.23) | collective-permute-done | bytes 73760 | tf_op jit(solution)/shard_map/ppermute | solution.py:51
  819.7 13.6 %collective-permute-done.24 = f32[72,256]{0,1:T(8,128)S(1)} collective-permute-done((f32[72,256]{0,1:T(8,128)S(1)}, f32[72,256]{0,1:T(8,128)S(1)}, u32[]{:S(2)}, u32[]{:S(2)}) %collective-permute-start.24) | collective-permute-done | bytes 73760 | tf_op jit(solution)/shard_map/ppermute | solution.py:51
  833.3 10.8 %all_gather.27 = f32[72,2048]{0,1:T(8,128)S(1)} all-gather(f32[72,256]{0,1:T(8,128)S(1)} %add.132), channel_id=1, replica_groups=mesh['dp'=8,'layer'=4] {'dp'}, dimensions={1}, use_global_device_ids=true | all-gather | bytes 663552 | tf_op jit(solution)/shard_map/all_gather | solution.py:798
  845.2 2.6 copy.53
  847.8 21.5 %all-gather.17.cloned.1.call-done.refs_2_.refs_3_.refs_4_ = bf16[512,6144]{1,0:T(8,128)(2,1)} async-done(((bf16[128,6144]{1,0:T(8,128)(2,1)}), bf16[512,6144]{1,0:T(8,128)(2,1)}) %all-gather.17.cloned.1.call-update) | async-done | bytes 6291472 | tf_op jit(solution)/shard_map/all_gather | solution.py:712
  870.5 14.3 %shard_map.255 = (bf16[4,512,2048]{2,1,0:T(8,128)(2,1)}, f32[512,16]{1,0:T(8,128)S(1)}) custom-call(f32[512,16]{1,0:T(8,128)S(1)} %bitcast.21, bf16[4,512,2048]{2,1,0:T(8,128)(2,1)} %refs_1_.5, bf16[512,6144]{1,0:T(8,128)(2,1)} %all-gather.17.cloned.1.call-done.refs_2_.refs_3_.refs_4_, ...), custom_call_target="tpu_custom_call" | custom-call | tf_op jit(solution)/shard_map/pallas_call | solution.py:285
  (147 shorter events, 40.1 us)
Async XLA Ops:
  8.0 430.4 %copy-start = (f32[2048,68]{0,1:T(8,128)S(1)}, f32[2048,68]{0,1:T(8,128)}, u32[]{:S(2)}) copy-start(f32[2048,68]{0,1:T(8,128)} %param.24) | copy-start | bytes 1671172
  8.0 126.1 %reduce-scatter.6.cloned.1.call-start = ((), (), s32[]{:S(2)}) async-start(), calls=%async_computation.5 | async-start | bytes 7864320 | tf_op jit(solution)/shard_map/reduce_scatter | solution.py:715
  9.0 10.2 %copy-start.9 = (f32[16,512]{0,1:T(8,128)}, f32[16,512]{0,1:T(8,128)S(1)}, u32[]{:S(2)}) copy-start(f32[16,512]{0,1:T(8,128)S(1)} %copy.46) | copy-start | bytes 98308
  19.2 1.3 copy-start.11
  20.6 133.1 %all-gather.7.cloned.1.call-start = ((), (), s32[]{:S(2)}) async-start(), calls=%async_computation.6 | async-start | bytes 28311552 | tf_op jit(solution)/shard_map/all_gather | solution.py:726
  25.7 0.8 copy-start.21
  25.7 243.5 %all-gather.9.cloned.1.call-start = ((), (), s32[]{:S(2)}) async-start(), calls=%async_computation.7 | async-start | bytes 7864320 | tf_op jit(solution)/shard_map/all_gather | solution.py:712
  134.2 1.6 copy-start.2
  140.8 1.1 copy-start.7
  141.9 11.8 %copy-start.24 = (s32[1,512]{1,0:T(1,128)S(1)}, s32[1,512]{1,0:T(1,128)}, u32[]{:S(2)}) copy-start(s32[1,512]{1,0:T(1,128)} %param.16) | copy-start | bytes 6148
  153.7 174.5 %reduce-scatter.8.cloned.1.call-start = ((), (), s32[]{:S(2)}) async-start(), calls=%async_computation.8 | async-start | bytes 2621440 | tf_op jit(solution)/shard_map/reduce_scatter | solution.py:715
  285.9 91.2 %all-gather.11.cloned.1.call-start = ((), (), s32[]{:S(2)}) async-start(), calls=%async_computation.9 | async-start | bytes 2621440 | tf_op jit(solution)/shard_map/all_gather | solution.py:712
  328.2 1.0 copy-start.4
  331.7 105.4 %reduce-scatter.10.cloned.1.call-start = ((), (), s32[]{:S(2)}) async-start(), calls=%async_computation.10 | async-start | bytes 2621440 | tf_op jit(solution)/shard_map/reduce_scatter | solution.py:715
  394.2 0.8 copy-start.22
  394.2 0.8 copy-start.23
  394.3 42.8 %copy-start.5 = (bf16[128,2048]{1,0:T(8,128)(2,1)S(1)}, bf16[128,2048]{1,0:T(8,128)(2,1)}, u32[]{:S(2)}) copy-start(bf16[128,2048]{1,0:T(8,128)(2,1)} %reduce-scatter.8.cloned.1.call-done.value_ref.refs_1_) | copy-start | bytes 1572868
  394.3 94.9 %all-gather.13.cloned.1.call-start = ((), (), s32[]{:S(2)}) async-start(), calls=%async_computation.11 | async-start | bytes 2621440 | tf_op jit(solution)/shard_map/all_gather | solution.py:712
  437.1 3.9 copy-start.17
  438.5 4.0 copy-start.20
  443.8 104.7 %reduce-scatter.12.cloned.1.call-start = ((), (), s32[]{:S(2)}) async-start(), calls=%async_computation.12 | async-start | bytes 2621440 | tf_op jit(solution)/shard_map/reduce_scatter | solution.py:715
  505.8 92.6 %all-gather.15.cloned.1.call-start = ((), (), s32[]{:S(2)}) async-start(), calls=%async_computation.13 | async-start | bytes 2621440 | tf_op jit(solution)/shard_map/all_gather | solution.py:712
  548.5 1.0 copy-start.14
  553.0 241.9 %reduce-scatter.14.cloned.1.call-start = ((), (), s32[]{:S(2)}) async-start(), calls=%async_computation.15 | async-start | bytes 30081024 | tf_op jit(solution)/shard_map/reduce_scatter | solution.py:778
  629.9 239.4 %all-gather.17.cloned.1.call-start = ((), (), s32[]{:S(2)}) async-start(), calls=%async_computation.14 | async-start | bytes 7864320 | tf_op jit(solution)/shard_map/all_gather | solution.py:712
  630.0 3.9 copy-start.16
  631.2 3.5 collective-permute-start.15
  633.0 6.2 copy-start.18
  633.0 6.2 collective-permute-start.9
  633.9 8.0 collective-permute-start.3
  636.1 42.7 %collective-permute-start.16 = (bf16[128,2048]{1,0:T(8,128)(2,1)S(1)}, bf16[128,2048]{1,0:T(8,128)(2,1)S(1)}, u32[]{:S(2)}, u32[]{:S(2)}) collective-permute-start(bf16[128,2048]{1,0:T(8,128)(2,1)S(1)} %get-tuple-element.141), channel_id=1, source_target_pairs={{2,1},{3,2},{6,5},{7,6},{10,9},{11,10},{14,13},{15,14},{18,17},{19... | collective-permute-start | bytes 1572872 | tf_op jit(solution)/shard_map/ppermute | solution.py:86
  636.8 19.1 %copy-start.19 = (bf16[512,2048]{1,0:T(8,128)(2,1)S(1)}, bf16[512,2048]{1,0:T(8,128)(2,1)}, u32[]{:S(2)}) copy-start(bf16[512,2048]{1,0:T(8,128)(2,1)} %get-tuple-element.69) | copy-start | bytes 6291460
  636.8 14.7 %collective-permute-start.12 = (bf16[128,2048]{1,0:T(8,128)(2,1)S(1)}, bf16[128,2048]{1,0:T(8,128)(2,1)S(1)}, u32[]{:S(2)}, u32[]{:S(2)}) collective-permute-start(bf16[128,2048]{1,0:T(8,128)(2,1)S(1)} %get-tuple-element.142), channel_id=1, source_target_pairs={{0,1},{4,5},{8,9},{12,13},{16,17},{20,21},{24,25},{28,29}} | collective-permute-start | bytes 1572872 | tf_op jit(solution)/shard_map/ppermute | solution.py:84
  639.3 51.9 %collective-permute-start.10 = (bf16[128,2048]{1,0:T(8,128)(2,1)S(1)}, bf16[128,2048]{1,0:T(8,128)(2,1)S(1)}, u32[]{:S(2)}, u32[]{:S(2)}) collective-permute-start(bf16[128,2048]{1,0:T(8,128)(2,1)S(1)} %get-tuple-element.136), channel_id=1, source_target_pairs={{2,1},{3,2},{6,5},{7,6},{10,9},{11,10},{14,13},{15,14},{18,17},{19... | collective-permute-start | bytes 1572872 | tf_op jit(solution)/shard_map/ppermute | solution.py:86
  640.0 22.7 %collective-permute-start.6 = (bf16[128,2048]{1,0:T(8,128)(2,1)S(1)}, bf16[128,2048]{1,0:T(8,128)(2,1)S(1)}, u32[]{:S(2)}, u32[]{:S(2)}) collective-permute-start(bf16[128,2048]{1,0:T(8,128)(2,1)S(1)} %get-tuple-element.137), channel_id=1, source_target_pairs={{0,1},{4,5},{8,9},{12,13},{16,17},{20,21},{24,25},{28,29}} | collective-permute-start | bytes 1572872 | tf_op jit(solution)/shard_map/ppermute | solution.py:84
  642.0 60.4 %collective-permute-start.4 = (bf16[128,2048]{1,0:T(8,128)(2,1)S(1)}, bf16[128,2048]{1,0:T(8,128)(2,1)S(1)}, u32[]{:S(2)}, u32[]{:S(2)}) collective-permute-start(bf16[128,2048]{1,0:T(8,128)(2,1)S(1)} %get-tuple-element.131), channel_id=1, source_target_pairs={{2,1},{3,2},{6,5},{7,6},{10,9},{11,10},{14,13},{15,14},{18,17},{19... | collective-permute-start | bytes 1572872 | tf_op jit(solution)/shard_map/ppermute | solution.py:86
  651.5 22.5 %collective-permute-start = (bf16[128,2048]{1,0:T(8,128)(2,1)S(1)}, bf16[128,2048]{1,0:T(8,128)(2,1)S(1)}, u32[]{:S(2)}, u32[]{:S(2)}) collective-permute-start(bf16[128,2048]{1,0:T(8,128)(2,1)S(1)} %get-tuple-element.132), channel_id=1, source_target_pairs={{0,1},{4,5},{8,9},{12,13},{16,17},{20,21},{24,25},{28,29}} | collective-permute-start | bytes 1572872 | tf_op jit(solution)/shard_map/ppermute | solution.py:84
  662.7 22.5 %collective-permute-start.13 = (bf16[128,2048]{1,0:T(8,128)(2,1)S(1)}, bf16[128,2048]{1,0:T(8,128)(2,1)S(1)}, u32[]{:S(2)}, u32[]{:S(2)}) collective-permute-start(bf16[128,2048]{1,0:T(8,128)(2,1)S(1)} %slice_add_fusion.1), channel_id=1, source_target_pairs={{0,1},{1,2},{4,5},{5,6},{8,9},{9,10},{12,13},{13,14},{16,17},{17,1... | collective-permute-start | bytes 1572872 | tf_op jit(solution)/shard_map/ppermute | solution.py:84
  674.0 22.5 %collective-permute-start.7 = (bf16[128,2048]{1,0:T(8,128)(2,1)S(1)}, bf16[128,2048]{1,0:T(8,128)(2,1)S(1)}, u32[]{:S(2)}, u32[]{:S(2)}) collective-permute-start(bf16[128,2048]{1,0:T(8,128)(2,1)S(1)} %slice_add_fusion.3), channel_id=1, source_target_pairs={{0,1},{1,2},{4,5},{5,6},{8,9},{9,10},{12,13},{13,14},{16,17},{17,1... | collective-permute-start | bytes 1572872 | tf_op jit(solution)/shard_map/ppermute | solution.py:84
  678.8 28.9 %collective-permute-start.1 = (bf16[128,2048]{1,0:T(8,128)(2,1)S(1)}, bf16[128,2048]{1,0:T(8,128)(2,1)S(1)}, u32[]{:S(2)}, u32[]{:S(2)}) collective-permute-start(bf16[128,2048]{1,0:T(8,128)(2,1)S(1)} %slice_add_fusion.5), channel_id=1, source_target_pairs={{0,1},{1,2},{4,5},{5,6},{8,9},{9,10},{12,13},{13,14},{16,17},{17,1... | collective-permute-start | bytes 1572872 | tf_op jit(solution)/shard_map/ppermute | solution.py:84
  685.4 33.6 %collective-permute-start.14 = (bf16[128,2048]{1,0:T(8,128)(2,1)S(1)}, bf16[128,2048]{1,0:T(8,128)(2,1)S(1)}, u32[]{:S(2)}, u32[]{:S(2)}) collective-permute-start(bf16[128,2048]{1,0:T(8,128)(2,1)S(1)} %get-tuple-element.139), channel_id=1, source_target_pairs={{0,1},{1,2},{2,3},{4,5},{5,6},{6,7},{8,9},{9,10},{10,11},{12,13},{... | collective-permute-start | bytes 1572872 | tf_op jit(solution)/shard_map/ppermute | solution.py:84
  691.2 29.3 %collective-permute-start.17 = (bf16[128,2048]{1,0:T(8,128)(2,1)S(1)}, bf16[128,2048]{1,0:T(8,128)(2,1)S(1)}, u32[]{:S(2)}, u32[]{:S(2)}) collective-permute-start(bf16[128,2048]{1,0:T(8,128)(2,1)S(1)} %get-tuple-element.138), channel_id=1, source_target_pairs={{1,0},{2,1},{3,2},{5,4},{6,5},{7,6},{9,8},{10,9},{11,10},{13,12},{... | collective-permute-start | bytes 1572872 | tf_op jit(solution)/shard_map/ppermute | solution.py:86
  696.6 33.6 %collective-permute-start.8 = (bf16[128,2048]{1,0:T(8,128)(2,1)S(1)}, bf16[128,2048]{1,0:T(8,128)(2,1)S(1)}, u32[]{:S(2)}, u32[]{:S(2)}) collective-permute-start(bf16[128,2048]{1,0:T(8,128)(2,1)S(1)} %get-tuple-element.134), channel_id=1, source_target_pairs={{0,1},{1,2},{2,3},{4,5},{5,6},{6,7},{8,9},{9,10},{10,11},{12,13},{... | collective-permute-start | bytes 1572872 | tf_op jit(solution)/shard_map/ppermute | solution.py:84
  702.4 18.1 %copy-start.3 = (bf16[128,6144]{1,0:T(8,128)(2,1)S(1)}, bf16[128,6144]{1,0:T(8,128)(2,1)}, u32[]{:S(2)}) copy-start(bf16[128,6144]{1,0:T(8,128)(2,1)} %reduce-scatter.6.cloned.1.call-done.value_ref.refs_1_) | copy-start | bytes 4718596
  702.4 27.7 %collective-permute-start.11 = (bf16[128,2048]{1,0:T(8,128)(2,1)S(1)}, bf16[128,2048]{1,0:T(8,128)(2,1)S(1)}, u32[]{:S(2)}, u32[]{:S(2)}) collective-permute-start(bf16[128,2048]{1,0:T(8,128)(2,1)S(1)} %get-tuple-element.133), channel_id=1, source_target_pairs={{1,0},{2,1},{3,2},{5,4},{6,5},{7,6},{9,8},{10,9},{11,10},{13,12},{... | collective-permute-start | bytes 1572872 | tf_op jit(solution)/shard_map/ppermute | solution.py:86
  707.8 32.1 %collective-permute-start.2 = (bf16[128,2048]{1,0:T(8,128)(2,1)S(1)}, bf16[128,2048]{1,0:T(8,128)(2,1)S(1)}, u32[]{:S(2)}, u32[]{:S(2)}) collective-permute-start(bf16[128,2048]{1,0:T(8,128)(2,1)S(1)} %get-tuple-element.129), channel_id=1, source_target_pairs={{0,1},{1,2},{2,3},{4,5},{5,6},{6,7},{8,9},{9,10},{10,11},{12,13},{... | collective-permute-start | bytes 1572872 | tf_op jit(solution)/shard_map/ppermute | solution.py:84
  718.9 21.0 %collective-permute-start.5 = (bf16[128,2048]{1,0:T(8,128)(2,1)S(1)}, bf16[128,2048]{1,0:T(8,128)(2,1)S(1)}, u32[]{:S(2)}, u32[]{:S(2)}) collective-permute-start(bf16[128,2048]{1,0:T(8,128)(2,1)S(1)} %get-tuple-element.128), channel_id=1, source_target_pairs={{1,0},{2,1},{3,2},{5,4},{6,5},{7,6},{9,8},{10,9},{11,10},{13,12},{... | collective-permute-start | bytes 1572872 | tf_op jit(solution)/shard_map/ppermute | solution.py:86
  744.3 1.3 collective-permute-start.18
  745.7 4.3 collective-permute-start.19
  750.0 4.3 collective-permute-start.20
  754.4 6.1 collective-permute-start.21
  760.4 8.6 collective-permute-start.22
  769.7 49.2 %copy-start.12 = (f32[8,2048]{1,0:T(8,128)S(1)}, f32[8,2048]{1,0:T(8,128)}, u32[]{:S(2)}) copy-start(f32[8,2048]{1,0:T(8,128)} %add.130.refs_0_.refs_8_) | copy-start | bytes 196612
  800.8 16.0 %collective-permute-start.23 = (f32[72,256]{0,1:T(8,128)S(1)}, f32[72,256]{0,1:T(8,128)S(1)}, u32[]{:S(2)}, u32[]{:S(2)}) collective-permute-start(f32[72,256]{0,1:T(8,128)S(1)} %copy.51), channel_id=1, source_target_pairs={{0,1},{1,0},{2,3},{3,2},{4,5},{5,4},{6,7},{7,6},{8,9},{9,8},{10,11... | collective-permute-start | bytes 221192 | tf_op jit(solution)/shard_map/ppermute | solution.py:51
  816.9 16.4 %collective-permute-start.24 = (f32[72,256]{0,1:T(8,128)S(1)}, f32[72,256]{0,1:T(8,128)S(1)}, u32[]{:S(2)}, u32[]{:S(2)}) collective-permute-start(f32[72,256]{0,1:T(8,128)S(1)} %add.131), channel_id=1, source_target_pairs={{0,2},{1,3},{2,0},{3,1},{4,6},{5,7},{6,4},{7,5},{8,10},{9,11},{10,... | collective-permute-start | bytes 221192 | tf_op jit(solution)/shard_map/ppermute | solution.py:51
  844.1 25.2 %copy-start.6 = (bf16[512,2048]{1,0:T(8,128)(2,1)S(1)}, bf16[512,2048]{1,0:T(8,128)(2,1)}, u32[]{:S(2)}) copy-start(bf16[512,2048]{1,0:T(8,128)(2,1)} %all-gather.15.cloned.1.call-done.hidden_ref.refs_5_) | copy-start | bytes 6291460
  844.1 25.2 %copy-start.10 = (f32[16,512]{0,1:T(8,128)S(1)}, f32[16,512]{0,1:T(8,128)}, u32[]{:S(2)}) copy-start(f32[16,512]{0,1:T(8,128)} %copy-done.9) | copy-start | bytes 98308
  844.1 25.2 %copy-start.13 = (f32[512,256]{1,0:T(8,128)S(1)}, f32[512,256]{1,0:T(8,128)}, u32[]{:S(2)}) copy-start(f32[512,256]{1,0:T(8,128)} %get-tuple-element.118.refs_6_) | copy-start | bytes 1572868
  869.3 1.2 copy-start.8
  870.5 16.7 %copy-start.1 = (f32[2048,68]{0,1:T(8,128)S(1)}, f32[2048,68]{0,1:T(8,128)}, u32[]{:S(2)}) copy-start(f32[2048,68]{0,1:T(8,128)} %param.24) | copy-start | bytes 1671172
  884.8 0.7 copy-start.15
Sparse Core Ops, SparseCore 0:
  20.7 113.4 reduce-scatter.5
  153.8 115.3 all-gather.8
  286.1 42.0 reduce-scatter.7
  331.8 45.2 all-gather.10
  394.4 42.6 reduce-scatter.9
  443.9 45.2 all-gather.12
  505.9 42.5 reduce-scatter.11
  553.1 45.2 all-gather.14
  743.9 125.2 all-gather.16
Sparse Core Ops, SparseCore 1:
  25.8 127.8 all-gather.6
  630.0 164.8 reduce-scatter.13

commit v4 on v3

--- a/solution.py
+++ b/solution.py
@@ -77,14 +77,14 @@
     return join([value], others)[0]
 
 
-def sum_line(blocks, count):
-    up = down = None
-    for k in range(1, count):
-        up = blocks[k] if up is None else blocks[k] + up
-        up = lax.ppermute(up, "layer", [(i, i + 1) for i in range(k)])
-        down = blocks[count - k] if down is None else blocks[count - k] + down
-        down = lax.ppermute(down, "layer", [(i, i - 1) for i in range(count - k, count)])
-    return [blocks[0], up, down]
+def sum_hop(blocks, k, came, count):
+    up, down = blocks[k], blocks[count - k]
+    if came:
+        up, down = up + came[0], down + came[1]
+    return [
+        lax.ppermute(up, "layer", [(i, i + 1) for i in range(k)]),
+        lax.ppermute(down, "layer", [(i, i - 1) for i in range(count - k, count)]),
+    ]
 
 
 def vmem(megabytes):
@@ -139,24 +139,26 @@
 
 
 def streams_norm(values, gains):
-    width = gains.shape[1]
+    block, width = values.shape[0], gains.shape[1]
 
     def kernel(gain_ref, value_ref, norm_ref):
-        for s in range(3):
-            cols = slice(s * width, (s + 1) * width)
-
-            def body(at, carry, s=s, cols=cols):
-                rows = value_ref[at, cols].astype(f32)
-                centre = rows - jnp.mean(rows, axis=1, keepdims=True)
-                spread = jnp.mean(centre * centre, axis=1, keepdims=True)
-                normed = centre * lax.rsqrt(spread + epsilon) * gain_ref[s : s + 1, :]
-                norm_ref[at, cols] = normed.astype(bf16)
-                return carry
-
-            row_loop(value_ref.shape[0], body, 0)
-
-    return pl.pallas_call(
-        kernel,
+        gain = gain_ref[pl.ds(pl.program_id(0), 1), :]
+
+        def body(at, carry):
+            rows = value_ref[at, :].astype(f32)
+            centre = rows - jnp.mean(rows, axis=1, keepdims=True)
+            spread = jnp.mean(centre * centre, axis=1, keepdims=True)
+            norm_ref[at, :] = (centre * lax.rsqrt(spread + epsilon) * gain).astype(bf16)
+            return carry
+
+        row_loop(block, body, 0)
+
+    stream = pl.BlockSpec((block, width), lambda s: (0, s))
+    return pl.pallas_call(
+        kernel,
+        grid=(3,),
+        in_specs=[pl.BlockSpec(gains.shape, lambda s: (0, 0)), stream],
+        out_specs=stream,
         out_shape=jax.ShapeDtypeStruct(values.shape, bf16),
         compiler_params=vmem(48),
     )(gains, values)
@@ -311,38 +313,39 @@
     return lax.dot_general(left, right, (((1,), (1,)), ((), ())), preferred_element_type=f32)
 
 
-def mlp_grads(mlp_rows, up_low, branch_rows, active, part):
+def mlp_grads(mlp_rows, up_low, branch_rows, active, first):
     tokens, width = mlp_rows.shape
     hidden = active.shape[1]
     rows = 256
-
-    def kernel(mlp_ref, up_ref, branch_ref, active_ref, out_ref):
+    total = 2 * hidden + first.shape[1]
+
+    def kernel(mlp_ref, up_ref, branch_ref, active_ref, first_ref, out_ref):
         out_ref[:, :hidden] = contract_rows(mlp_ref[...], up_ref[...]).astype(bf16)
         out_ref[:, hidden : 2 * hidden] = contract_rows(branch_ref[...], active_ref[...]).astype(bf16)
-        out_ref[:, 2 * hidden :] = jnp.zeros((rows, 2 * part - 2 * hidden), bf16)
+        out_ref[:, 2 * hidden :] = first_ref[...].astype(bf16)
 
     side = pl.BlockSpec((tokens, rows), lambda i: (0, i))
     return pl.pallas_call(
         kernel,
         grid=(width // rows,),
-        in_specs=[side, resident(up_low), side, resident(active)],
-        out_specs=pl.BlockSpec((rows, 2 * part), lambda i: (i, 0)),
-        out_shape=jax.ShapeDtypeStruct((width, 3 * part), bf16),
+        in_specs=[side, resident(up_low), side, resident(active)]
+        + [pl.BlockSpec((rows, first.shape[1]), lambda i: (i, 0))],
+        out_specs=pl.BlockSpec((rows, total), lambda i: (i, 0)),
+        out_shape=jax.ShapeDtypeStruct((width, total), bf16),
         compiler_params=vmem(56),
-    )(mlp_rows, up_low, branch_rows, active)
-
-
-def attention_grads(so_far, near, lin_grads, hidden_rows, context, first, part, order):
+    )(mlp_rows, up_low, branch_rows, active, first)
+
+
+def attention_grads(near, lin_grads, hidden_rows, context, order):
     tokens, width = hidden_rows.shape
     heads = context.shape[1]
     rows = 256
 
-    def kernel(q_ref, k_ref, v_ref, dq_ref, dk_ref, dv_ref, hidden_ref, ctx_ref, first_ref, *refs):
+    def kernel(q_ref, k_ref, v_ref, dq_ref, dk_ref, dv_ref, hidden_ref, ctx_ref, *refs):
         out_ref = refs[-1]
         pairs = ((q_ref, dq_ref), (k_ref, dk_ref), (v_ref, dv_ref), (hidden_ref, ctx_ref))
         for s, (left, right) in enumerate(pairs):
             out_ref[:, s * heads : (s + 1) * heads] = contract_rows(left[...], right[...]).astype(bf16)
-        out_ref[:, 4 * heads :] = first_ref[...].astype(bf16)
 
     side = pl.BlockSpec((tokens, rows), lambda i: (0, i))
     return pl.pallas_call(
@@ -354,13 +357,11 @@
         ]
         + [resident(lin_grads[0])] * 3
         + [side, resident(context)]
-        + [pl.BlockSpec((rows, first.shape[1]), lambda i: (i, 0))]
-        + [pl.BlockSpec(memory_space=pl.ANY)] * (1 + len(order)),
-        out_specs=pl.BlockSpec((rows, part), lambda i: (i, 2)),
-        out_shape=jax.ShapeDtypeStruct(so_far.shape, bf16),
-        input_output_aliases={9: 0},
+        + [pl.BlockSpec(memory_space=pl.ANY)] * len(order),
+        out_specs=pl.BlockSpec((rows, 4 * heads), lambda i: (i, 0)),
+        out_shape=jax.ShapeDtypeStruct((width, 4 * heads), bf16),
         compiler_params=vmem(56),
-    )(near, near, near, *lin_grads, hidden_rows, context, first, so_far, *order)
+    )(near, near, near, *lin_grads, hidden_rows, context, *order)
 
 
 def round_weights(weights, turned, order):
@@ -646,29 +647,39 @@
     )(where, *lin_grads, full)
 
 
-def unpack_grads(weight_sum, hidden, heads, part, mixes, order):
-    rows = weight_sum.shape[0]
-
-    def kernel(sum_ref, *refs):
-        up_ref, down_ref, q_ref, k_ref, v_ref, o_ref, first_ref = refs[-7:]
+def unpack_mlp(mlp_sum, hidden, mixes):
+    rows = mlp_sum.shape[0]
+
+    def kernel(sum_ref, up_ref, down_ref, first_ref):
         up_ref[...] = sum_ref[:, :hidden].astype(f32)
         down_ref[...] = sum_ref[:, hidden : 2 * hidden].astype(f32).T
-        at = 2 * part
-        for ref in (q_ref, k_ref, v_ref):
-            ref[...] = sum_ref[:, at : at + heads].astype(f32)
-            at += heads
-        o_ref[...] = sum_ref[:, at : at + heads].astype(f32).T
-        first_ref[...] = sum_ref[:, at + heads :].astype(f32).T[: first_ref.shape[0], :]
-
-    shapes = [(rows, hidden), (hidden, rows)] + [(rows, heads)] * 3
-    shapes += [(heads, rows), (mixes + -mixes % 8, rows)]
-    return pl.pallas_call(
-        kernel,
-        in_specs=[pl.BlockSpec(memory_space=pltpu.VMEM)]
-        + [pl.BlockSpec(memory_space=pl.ANY)] * len(order),
+        first_ref[...] = sum_ref[:, 2 * hidden :].astype(f32).T[: first_ref.shape[0], :]
+
+    return pl.pallas_call(
+        kernel,
+        out_shape=[
+            jax.ShapeDtypeStruct((rows, hidden), f32),
+            jax.ShapeDtypeStruct((hidden, rows), f32),
+            jax.ShapeDtypeStruct((mixes + -mixes % 8, rows), f32),
+        ],
+        compiler_params=vmem(56),
+    )(mlp_sum)
+
+
+def unpack_attention(attention_sum, heads):
+    rows = attention_sum.shape[0]
+
+    def kernel(sum_ref, q_ref, k_ref, v_ref, o_ref):
+        for s, ref in enumerate((q_ref, k_ref, v_ref)):
+            ref[...] = sum_ref[:, s * heads : (s + 1) * heads].astype(f32)
+        o_ref[...] = sum_ref[:, 3 * heads :].astype(f32).T
+
+    shapes = [(rows, heads)] * 3 + [(heads, rows)]
+    return pl.pallas_call(
+        kernel,
         out_shape=[jax.ShapeDtypeStruct(shape, f32) for shape in shapes],
         compiler_params=vmem(56),
-    )(weight_sum, *order)
+    )(attention_sum)
 
 
 def places(seg_row):
@@ -753,10 +764,11 @@
     branch_rows = collect(block_grad.astype(bf16))
     up_low, mlp_part = feed_back(branch_rows, full, 4 * heads, slope)
     mlp_back = spread(mlp_part)
-    part = 4 * heads + 128
-    weight_grads = mlp_grads(mlp_rows, after(up_low, mlp_part), branch_rows, active, part)
+    mixes = first_grad.shape[1]
+    first_wide = jnp.pad(first_grad, ((0, 0), (0, -mixes % 128)))
+    mlp_grad = mlp_grads(mlp_rows, after(up_low, mlp_part), branch_rows, active, first_wide)
     hidden_low, mlp_gain_grad = norm_back(
-        hidden_in, [mlp_back], norm_gains[3], block_grad, [weight_grads]
+        hidden_in, [mlp_back], norm_gains[3], block_grad, [mlp_grad]
     )
     hidden_rows = collect(hidden_low)
     lin_grads = attend_back(
@@ -764,23 +776,14 @@
     )
     table = jnp.stack(order).astype(jnp.int32)
     stream_parts = stream_shares(table, lin_grads, full)
-    mixes = first_grad.shape[1]
-    weight_grads = attention_grads(
-        weight_grads,
-        normed_rows,
-        lin_grads,
-        hidden_rows,
-        context,
-        jnp.pad(first_grad, ((0, 0), (0, 128 - mixes))),
-        part,
-        [stream_parts[0]],
-    )
-    weight_sum = lax.psum_scatter(weight_grads, "dp", scatter_dimension=0, tiled=True)
+    mlp_sum = lax.psum_scatter(mlp_grad, "dp", scatter_dimension=0, tiled=True)
     gain_grads, stream_low = [], []
     for s in range(3):
-        low, gain_grad = norm_back(
-            (stream_own, s), sum_line(blocks_of(stream_parts[s]), count), norm_gains[s]
-        )
+        blocks = blocks_of(stream_parts[s])
+        came = []
+        for k in range(1, count):
+            came = sum_hop(blocks, k, came, count)
+        low, gain_grad = norm_back((stream_own, s), blocks[:1] + came, norm_gains[s])
         gain_grads.append(gain_grad)
         stream_low.append(low)
     near = collect(jnp.concatenate(stream_low, axis=1))
@@ -789,19 +792,22 @@
     lines = -(-mixes * mixes // width)
     second_flat = jnp.pad(second_grad.reshape(-1), (0, lines * width - mixes * mixes))
     small = jnp.concatenate([gain_rows, second_flat.reshape(lines, width)])
-    small = doubling_sum(doubling_sum(small, "dp"), "layer")
-    up_sum, down_sum, *projections, output_sum, first_part = unpack_grads(
-        weight_sum, hidden, heads, part, mixes, [small]
-    )
+    small = doubling_sum(doubling_sum(small, "layer"), "dp")
     gains_sum = small[:5]
     second_sum = small[5:].reshape(-1)[: mixes * mixes].reshape(mixes, mixes)
+    attention_grad = attention_grads(
+        normed_rows, lin_grads, hidden_rows, context, stream_low + [mlp_sum]
+    )
+    attention_sum = lax.psum_scatter(attention_grad, "dp", scatter_dimension=0, tiled=True)
+    up_sum, down_sum, first_part = unpack_mlp(mlp_sum, hidden, mixes)
     first_sum = lax.all_gather(doubling_sum(first_part, "layer"), "dp", axis=1, tiled=True)[:mixes].T
     history_grad, mix_back = history_grads(
         mix_cols,
         history,
         [(near, 0), (near, 1), (near, 2), (hidden_rows, 0)],
-        [output_sum, first_sum, small],
-    )
+        [down_sum, first_sum, small, attention_grad],
+    )
+    *projections, output_sum = unpack_attention(attention_sum, heads)
     mix_grad = mix_back.T.reshape(4, stored, row_tok)
     return (
         block.astype(bf16),

time: 896 us -> 887 us (0.990)
  waiting for transfers between devices: 619 us -> 600 us
    reduce_scatter x1 -> x2, waiting for transfers between devices: 25.2 us -> 0.02 us  [the longest x1 0.02 us: local(): mlp_sum = lax.psum_scatter(mlp_grad, 'dp', scatter_dimension=0, tiled=True)]
    all_gather x5, waiting for transfers between devices: 265 us -> 279 us  [collect(): return lax.all_gather(rows, 'layer', axis=0, tiled=True)]
  transfers between devices with their start and end apart: 36 -> 37, of which waited for: 27 -> 24; matrix products, arithmetic and copies ran while one was open for 2% -> 2% of each run, Pallas kernels for 4% -> 9%
where the time goes in v4:
time: 887 us; the launch traced here: 885 us
  waiting for transfers between devices  600 us (68%)
  Pallas kernels  152 us (17%)
  starting transfers between devices  60.8 us (7%)
  local copies, waits for them, and re-layouts  21.8 us (2%)
  blocking collectives  16.5 us (2%)
  between operations  16.3 us (2%)
  other arithmetic  10 us (1%)
    all_gather x5, waiting for transfers between devices, collect(): return lax.all_gather(rows, 'layer', axis=0, tiled=True)  279 us
    reduce_scatter x4, waiting for transfers between devices, spread(): return lax.psum_scatter(rows, 'layer', scatter_dimension=0, tiled=True)  216 us
    ppermute x9, waiting for transfers between devices, sum_hop(): lax.ppermute(up, 'layer', [(i, i + 1) for i in range(k)])  52.1 us
    ppermute x7, waiting for transfers between devices, doubling_sum(): lax.ppermute(value, axis, [(i, i ^ step) for i in range(size)])  40.7 us
    ppermute x9, starting transfers between devices, sum_hop(): lax.ppermute(up, 'layer', [(i, i + 1) for i in range(k)])  39.7 us
  transfers between devices with their start and end apart: 37, of which 24 were waited for; matrix products, arithmetic and copies ran while one was open for 2% of the time, Pallas kernels for 9%

profile of v4, /device:TPU:0, one launch (start us, length us, event | category | flops | bytes accessed | tf_op | source)
XLA Modules:
  0.0 885.2 jit_solution(9693032262169841385)
XLA Ops:
  9.0 10.1 %shard_map.237 = (bf16[512,6144]{1,0:T(8,128)(2,1)}, bf16[512,2048]{1,0:T(8,128)(2,1)S(1)}) custom-call(f32[512,16]{1,0:T(8,128)S(1)} %bitcast.20, bf16[4,512,2048]{2,1,0:T(8,128)(2,1)} %refs_1_.5), custom_call_target="tpu_custom_call" | custom-call | tf_op jit(solution)/shard_map/pallas_call | solution.py:125
  20.5 5.1 shard_map.239
  26.5 107.7 %reduce-scatter.7.cloned.1.call-done.value_ref.refs_1_ = bf16[128,6144]{1,0:T(8,128)(2,1)} async-done(((bf16[512,6144]{1,0:T(8,128)(2,1)}), bf16[128,6144]{1,0:T(8,128)(2,1)}) %reduce-scatter.7.cloned.1.call-update) | async-done | bytes 1572880 | tf_op jit(solution)/shard_map/reduce_scatter | solution.py:726
  134.1 1.6 copy-done.2
  135.7 5.3 shard_map.238.refs_0_
  142.1 11.5 %all-gather.7.cloned.1.call-done.refs_1_.wq_ref.wk_ref.wv_ref.wo_ref.up_ref.down_ref.full_ref = bf16[2048,6144]{1,0:T(8,128)(2,1)} async-done(((bf16[256,6144]{1,0:T(8,128)(2,1)}), bf16[2048,6144]{1,0:T(8,128)(2,1)}) %all-gather.7.cloned.1.call-update) | async-done | bytes 25165840 | tf_op jit(solution)/shard_map/all_gather | solution.py:737
  157.4 111.7 %all-gather.9.cloned.1.call-done.near_ref.q_ref.k_ref.v_ref = bf16[512,6144]{1,0:T(8,128)(2,1)} async-done(((bf16[128,6144]{1,0:T(8,128)(2,1)}), bf16[512,6144]{1,0:T(8,128)(2,1)}) %all-gather.9.cloned.1.call-update) | async-done | bytes 6291472 | tf_op jit(solution)/shard_map/all_gather | solution.py:723
  269.1 16.7 %shard_map.241 = (bf16[512,512]{1,0:T(8,128)(2,1)}, bf16[512,512]{1,0:T(8,128)(2,1)}, bf16[512,512]{1,0:T(8,128)(2,1)}, bf16[512,512]{1,0:T(8,128)(2,1)}, f32[4,...) custom-call(s32[512,2]{1,0:T(8,128)} %copy.46.rows_ref, s32[2,512]{1,0:T(2,128)} %get-tuple-element.149.cols_ref, ...), custom_call_target="tpu_custom_call" | custom-call | tf_op jit(solution)/shard_map/pallas_call | solution.py:560
  286.0 42.2 %reduce-scatter.9.cloned.1.call-done.value_ref.refs_1_ = bf16[128,2048]{1,0:T(8,128)(2,1)} async-done(((bf16[512,2048]{1,0:T(8,128)(2,1)}), bf16[128,2048]{1,0:T(8,128)(2,1)}) %reduce-scatter.9.cloned.1.call-update) | async-done | bytes 524304 | tf_op jit(solution)/shard_map/reduce_scatter | solution.py:726
  329.2 2.4 shard_map.242
  331.7 45.4 %all-gather.11.cloned.1.call-done.rows_ref.mlp_ref = bf16[512,2048]{1,0:T(8,128)(2,1)} async-done(((bf16[128,2048]{1,0:T(8,128)(2,1)}), bf16[512,2048]{1,0:T(8,128)(2,1)}) %all-gather.11.cloned.1.call-update) | async-done | bytes 2097168 | tf_op jit(solution)/shard_map/all_gather | solution.py:723
  377.1 17.1 %shard_map.243 = (bf16[512,2048]{1,0:T(8,128)(2,1)}, f32[512,2048]{1,0:T(8,128)}, bf16[512,2048]{1,0:T(8,128)(2,1)}) custom-call(bf16[512,2048]{1,0:T(8,128)(2,1)} %all-gather.11.cloned.1.call-done.rows_ref.mlp_ref, bf16[2048,6144]{1,0:T(8,128)(2,1)} %all-gather.7.cloned.1.call-done.refs_1_.wq_ref.wk_ref.wv_ref.wo_ref.up_ref.down_ref.full_ref, ...), custom_call_target="tpu_custom_call" | custom-call | tf_op jit(solution)/shard_map/pallas_call | solution.py:417
  395.2 41.8 %reduce-scatter.11.cloned.1.call-done = bf16[128,2048]{1,0:T(8,128)(2,1)} async-done(((bf16[512,2048]{1,0:T(8,128)(2,1)}), bf16[128,2048]{1,0:T(8,128)(2,1)}) %reduce-scatter.11.cloned.1.call-update) | async-done | bytes 524304 | tf_op jit(solution)/shard_map/reduce_scatter | solution.py:726
  437.0 1.4 multiply_reduce_fusion.2
  438.4 2.5 fusion.3
  440.9 1.4 multiply_reduce_fusion
  443.8 45.4 %all-gather.13.cloned.1.call-done.rows_ref.branch_ref = bf16[512,2048]{1,0:T(8,128)(2,1)} async-done(((bf16[128,2048]{1,0:T(8,128)(2,1)}), bf16[512,2048]{1,0:T(8,128)(2,1)}) %all-gather.13.cloned.1.call-update) | async-done | bytes 2097168 | tf_op jit(solution)/shard_map/all_gather | solution.py:723
  489.2 16.5 %shard_map.244 = (bf16[512,2048]{1,0:T(8,128)(2,1)}, bf16[512,2048]{1,0:T(8,128)(2,1)}) custom-call(bf16[512,2048]{1,0:T(8,128)(2,1)} %all-gather.13.cloned.1.call-done.rows_ref.branch_ref, bf16[2048,6144]{1,0:T(8,128)(2,1)} %all-gather.7.cloned.1.call-done.refs_1_.wq_ref.wk_ref.wv_ref.wo_ref.up_ref.down_ref.full_ref, ...), custom_call_target="tpu_custom_call" | custom-call | tf_op jit(solution)/shard_map/pallas_call | solution.py:464
  505.7 1.9 fusion.1
  508.7 15.5 %shard_map.246.refs_4_ = bf16[2048,4224]{1,0:T(8,128)(2,1)} custom-call(bf16[512,2048]{1,0:T(8,128)(2,1)} %all-gather.11.cloned.1.call-done.rows_ref.mlp_ref, bf16[512,2048]{1,0:T(8,128)(2,1)} %shard_map.245.up_ref, bf16[512,2048]{1,0:T(8,128)(2,1)} %all-gather.13.cloned.1.call-done.rows_ref.branch_ref, bf16[512,2048]{1,0:T(8,128)(2,1)} %get-tuple-element.56.active_ref, ...), custom_call_target="tpu_custom_call" | custom-call | tf_op jit(solution)/shard_map/pallas_call | solution.py:328
  524.2 24.2 %reduce-scatter.13.cloned.1.call-done.refs_2_ = bf16[128,2048]{1,0:T(8,128)(2,1)} async-done(((bf16[512,2048]{1,0:T(8,128)(2,1)}), bf16[128,2048]{1,0:T(8,128)(2,1)}) %reduce-scatter.13.cloned.1.call-update) | async-done | bytes 524304 | tf_op jit(solution)/shard_map/reduce_scatter | solution.py:726
  549.4 3.4 shard_map.247
  554.4 43.9 %all-gather.15.cloned.1.call-done.hidden_ref.refs_5_ = bf16[512,2048]{1,0:T(8,128)(2,1)} async-done(((bf16[128,2048]{1,0:T(8,128)(2,1)}), bf16[512,2048]{1,0:T(8,128)(2,1)}) %all-gather.15.cloned.1.call-update) | async-done | bytes 2097168 | tf_op jit(solution)/shard_map/all_gather | solution.py:723
  598.2 10.1 %shard_map.248 = (bf16[512,512]{1,0:T(8,128)(2,1)}, bf16[512,512]{1,0:T(8,128)(2,1)}, bf16[512,512]{1,0:T(8,128)(2,1)}) custom-call(s32[512,2]{1,0:T(8,128)} %copy.46.rows_ref, s32[2,512]{1,0:T(2,128)} %get-tuple-element.149.cols_ref, f32[512,128]{1,0:T(8,128)} %get-tuple-element.155.cos_ref, f32[512,128]{1,0:T(8,128)} %get-tuple-element.156.sin_ref, ...), custom_call_target="tpu_custom_call" | custom-call | tf_op jit(solution)/shard_map/pallas_call | solution.py:606
  608.3 9.6 %shard_map.249 = (bf16[512,2048]{1,0:T(8,128)(2,1)}, bf16[512,2048]{1,0:T(8,128)(2,1)}, bf16[512,2048]{1,0:T(8,128)(2,1)}) custom-call(s32[4]{0:T(128)} %pad_add_fusion.1.where_ref, bf16[512,512]{1,0:T(8,128)(2,1)} %get-tuple-element.62.dq_ref, bf16[512,512]{1,0:T(8,128)(2,1)} %get-tuple-element.63.dk_ref, bf16[512,512]{1,0:T(8,128)(2,1)} %get-tuple-element.64.dv_ref, ...), custom_call_target="tpu_custom_call" | custom-call | tf_op jit(solution)/shard_map/pallas_call | solution.py:637
  622.6 1.5 slice_add_fusion
  624.9 2.5 collective-permute-start.12
  628.2 1.9 collective-permute-start.6
  630.9 8.8 collective-permute-done.12
  639.7 4.4 collective-permute-start
  644.2 6.7 collective-permute-done.6
  650.9 4.4 collective-permute-start.13
  655.4 6.7 collective-permute-done
  662.2 4.9 collective-permute-start.7
  667.1 1.9 collective-permute-start.1
  669.1 4.3 collective-permute-done.13
  674.9 6.5 collective-permute-start.14
  681.4 3.3 collective-permute-done.7
  686.1 6.7 collective-permute-start.8
  692.8 3.1 collective-permute-done.1
  697.3 6.5 collective-permute-start.2
  703.9 3.3 collective-permute-done.14.refs_3_
  707.1 2.6 shard_map.252
  709.7 8.6 collective-permute-done.8.refs_3_
  718.3 2.6 shard_map.251
  720.9 7.3 collective-permute-done.2.refs_3_
  728.2 2.6 shard_map.250
  732.5 12.0 %shard_map.254.refs_9_ = bf16[2048,2048]{1,0:T(8,128)(2,1)} custom-call(bf16[512,6144]{1,0:T(8,128)(2,1)} %all-gather.9.cloned.1.call-done.near_ref.q_ref.k_ref.v_ref, bf16[512,6144]{1,0:T(8,128)(2,1)} %all-gather.9.cloned.1.call-done.near_ref.q_ref.k_ref.v_ref, bf16[512,6144]{1,0:T(8,128)(2,1)} %all-gather.9.cloned.1.call-done.near_ref.q_ref.k_ref.v_ref, ...), custom_call_target="tpu_custom_call" | custom-call | tf_op jit(solution)/shard_map/pallas_call | solution.py:351
  745.0 2.5 collective-permute-start.20
  747.5 3.9 collective-permute-done.20
  751.4 5.9 collective-permute-start.21
  757.3 7.4 collective-permute-done.21
  764.8 4.0 shard_map.253
  769.9 1.5 collective-permute-start.23
  771.5 4.5 collective-permute-done.23
  775.9 1.5 collective-permute-start.24
  777.5 10.5 %collective-permute-done.18 = f32[72,256]{0,1:T(8,128)S(1)} collective-permute-done((f32[72,256]{0,1:T(8,128)S(1)}, f32[72,256]{0,1:T(8,128)S(1)}, u32[]{:S(2)}, u32[]{:S(2)}) %collective-permute-start.18) | collective-permute-done | bytes 73760 | tf_op jit(solution)/shard_map/ppermute | solution.py:51
  789.8 14.5 %collective-permute-done.19 = f32[72,256]{0,1:T(8,128)S(1)} collective-permute-done((f32[72,256]{0,1:T(8,128)S(1)}, f32[72,256]{0,1:T(8,128)S(1)}, u32[]{:S(2)}, u32[]{:S(2)}) %collective-permute-start.19) | collective-permute-done | bytes 73760 | tf_op jit(solution)/shard_map/ppermute | solution.py:51
  804.3 16.5 %all_gather.27 = f32[72,2048]{0,1:T(8,128)S(1)} all-gather(f32[72,256]{0,1:T(8,128)S(1)} %add.129), channel_id=1, replica_groups=mesh['dp'=8,'layer'=4] {'dp'}, dimensions={1}, use_global_device_ids=true | all-gather | bytes 663552 | tf_op jit(solution)/shard_map/all_gather | solution.py:803
  821.9 2.4 copy.52
  824.3 33.0 %all-gather.17.cloned.1.call-done.refs_2_.refs_3_.refs_4_ = bf16[512,6144]{1,0:T(8,128)(2,1)} async-done(((bf16[128,6144]{1,0:T(8,128)(2,1)}), bf16[512,6144]{1,0:T(8,128)(2,1)}) %all-gather.17.cloned.1.call-update) | async-done | bytes 6291472 | tf_op jit(solution)/shard_map/all_gather | solution.py:723
  858.6 1.6 copy-done.12
  860.1 14.3 %shard_map.255 = (bf16[4,512,2048]{2,1,0:T(8,128)(2,1)}, f32[512,16]{1,0:T(8,128)S(1)}) custom-call(f32[512,16]{1,0:T(8,128)S(1)} %bitcast.21, bf16[4,512,2048]{2,1,0:T(8,128)(2,1)} %refs_1_.5, bf16[512,6144]{1,0:T(8,128)(2,1)} %all-gather.17.cloned.1.call-done.refs_2_.refs_3_.refs_4_, ...), custom_call_target="tpu_custom_call" | custom-call | tf_op jit(solution)/shard_map/pallas_call | solution.py:287
  875.2 2.6 shard_map.256
  (151 shorter events, 35.0 us)
Async XLA Ops:
  8.0 430.4 %copy-start = (f32[2048,68]{0,1:T(8,128)S(1)}, f32[2048,68]{0,1:T(8,128)}, u32[]{:S(2)}) copy-start(f32[2048,68]{0,1:T(8,128)} %param.24) | copy-start | bytes 1671172
  8.0 126.1 %reduce-scatter.7.cloned.1.call-start = ((), (), s32[]{:S(2)}) async-start(), calls=%async_computation.6 | async-start | bytes 7864320 | tf_op jit(solution)/shard_map/reduce_scatter | solution.py:726
  19.1 1.3 copy-start.13
  20.5 133.1 %all-gather.7.cloned.1.call-start = ((), (), s32[]{:S(2)}) async-start(), calls=%async_computation.7 | async-start | bytes 28311552 | tf_op jit(solution)/shard_map/all_gather | solution.py:737
  25.6 0.8 copy-start.21
  25.6 243.5 %all-gather.9.cloned.1.call-start = ((), (), s32[]{:S(2)}) async-start(), calls=%async_computation.8 | async-start | bytes 7864320 | tf_op jit(solution)/shard_map/all_gather | solution.py:723
  134.1 1.6 copy-start.2
  141.0 1.1 copy-start.7
  142.1 11.6 %copy-start.24 = (s32[1,512]{1,0:T(1,128)S(1)}, s32[1,512]{1,0:T(1,128)}, u32[]{:S(2)}) copy-start(s32[1,512]{1,0:T(1,128)} %param.16) | copy-start | bytes 6148
  153.6 174.5 %reduce-scatter.9.cloned.1.call-start = ((), (), s32[]{:S(2)}) async-start(), calls=%async_computation.9 | async-start | bytes 2621440 | tf_op jit(solution)/shard_map/reduce_scatter | solution.py:726
  285.9 91.2 %all-gather.11.cloned.1.call-start = ((), (), s32[]{:S(2)}) async-start(), calls=%async_computation.10 | async-start | bytes 2621440 | tf_op jit(solution)/shard_map/all_gather | solution.py:723
  328.1 1.0 copy-start.5
  331.6 105.4 %reduce-scatter.11.cloned.1.call-start = ((), (), s32[]{:S(2)}) async-start(), calls=%async_computation.11 | async-start | bytes 2621440 | tf_op jit(solution)/shard_map/reduce_scatter | solution.py:726
  394.2 0.8 copy-start.22
  394.2 0.8 copy-start.23
  394.2 42.8 %copy-start.6 = (bf16[128,2048]{1,0:T(8,128)(2,1)S(1)}, bf16[128,2048]{1,0:T(8,128)(2,1)}, u32[]{:S(2)}) copy-start(bf16[128,2048]{1,0:T(8,128)(2,1)} %reduce-scatter.9.cloned.1.call-done.value_ref.refs_1_) | copy-start | bytes 1572868
  394.2 94.9 %all-gather.13.cloned.1.call-start = ((), (), s32[]{:S(2)}) async-start(), calls=%async_computation.12 | async-start | bytes 2621440 | tf_op jit(solution)/shard_map/all_gather | solution.py:723
  437.0 3.9 copy-start.16
  438.4 4.0 copy-start.20
  443.7 104.6 %reduce-scatter.13.cloned.1.call-start = ((), (), s32[]{:S(2)}) async-start(), calls=%async_computation.13 | async-start | bytes 2621440 | tf_op jit(solution)/shard_map/reduce_scatter | solution.py:726
  505.7 92.6 %all-gather.15.cloned.1.call-start = ((), (), s32[]{:S(2)}) async-start(), calls=%async_computation.14 | async-start | bytes 2621440 | tf_op jit(solution)/shard_map/all_gather | solution.py:723
  548.4 1.0 copy-start.14
  552.8 179.7 %reduce-scatter.15.cloned.1.call-start = ((), (), s32[]{:S(2)}) async-start(), calls=%async_computation.16 | async-start | bytes 19464192 | tf_op jit(solution)/shard_map/reduce_scatter | solution.py:779
  553.4 303.9 %all-gather.17.cloned.1.call-start = ((), (), s32[]{:S(2)}) async-start(), calls=%async_computation.15 | async-start | bytes 7864320 | tf_op jit(solution)/shard_map/all_gather | solution.py:723
  617.9 3.9 copy-start.17
  619.1 3.5 collective-permute-start.15
  621.0 6.4 copy-start.18
  621.0 6.4 collective-permute-start.9
  621.9 8.2 collective-permute-start.3
  624.1 43.0 %collective-permute-start.16 = (bf16[128,2048]{1,0:T(8,128)(2,1)S(1)}, bf16[128,2048]{1,0:T(8,128)(2,1)S(1)}, u32[]{:S(2)}, u32[]{:S(2)}) collective-permute-start(bf16[128,2048]{1,0:T(8,128)(2,1)S(1)} %get-tuple-element.141), channel_id=1, source_target_pairs={{2,1},{3,2},{6,5},{7,6},{10,9},{11,10},{14,13},{15,14},{18,17},{19... | collective-permute-start | bytes 1572872 | tf_op jit(solution)/shard_map/ppermute | solution.py:86
  624.8 19.3 %copy-start.19 = (bf16[512,2048]{1,0:T(8,128)(2,1)S(1)}, bf16[512,2048]{1,0:T(8,128)(2,1)}, u32[]{:S(2)}) copy-start(bf16[512,2048]{1,0:T(8,128)(2,1)} %get-tuple-element.69) | copy-start | bytes 6291460
  624.9 14.8 %collective-permute-start.12 = (bf16[128,2048]{1,0:T(8,128)(2,1)S(1)}, bf16[128,2048]{1,0:T(8,128)(2,1)S(1)}, u32[]{:S(2)}, u32[]{:S(2)}) collective-permute-start(bf16[128,2048]{1,0:T(8,128)(2,1)S(1)} %get-tuple-element.142), channel_id=1, source_target_pairs={{0,1},{4,5},{8,9},{12,13},{16,17},{20,21},{24,25},{28,29}} | collective-permute-start | bytes 1572872 | tf_op jit(solution)/shard_map/ppermute | solution.py:85
  627.5 47.3 %collective-permute-start.10 = (bf16[128,2048]{1,0:T(8,128)(2,1)S(1)}, bf16[128,2048]{1,0:T(8,128)(2,1)S(1)}, u32[]{:S(2)}, u32[]{:S(2)}) collective-permute-start(bf16[128,2048]{1,0:T(8,128)(2,1)S(1)} %get-tuple-element.136), channel_id=1, source_target_pairs={{2,1},{3,2},{6,5},{7,6},{10,9},{11,10},{14,13},{15,14},{18,17},{19... | collective-permute-start | bytes 1572872 | tf_op jit(solution)/shard_map/ppermute | solution.py:86
  628.2 22.7 %collective-permute-start.6 = (bf16[128,2048]{1,0:T(8,128)(2,1)S(1)}, bf16[128,2048]{1,0:T(8,128)(2,1)S(1)}, u32[]{:S(2)}, u32[]{:S(2)}) collective-permute-start(bf16[128,2048]{1,0:T(8,128)(2,1)S(1)} %get-tuple-element.137), channel_id=1, source_target_pairs={{0,1},{4,5},{8,9},{12,13},{16,17},{20,21},{24,25},{28,29}} | collective-permute-start | bytes 1572872 | tf_op jit(solution)/shard_map/ppermute | solution.py:85
  630.2 55.9 %collective-permute-start.4 = (bf16[128,2048]{1,0:T(8,128)(2,1)S(1)}, bf16[128,2048]{1,0:T(8,128)(2,1)S(1)}, u32[]{:S(2)}, u32[]{:S(2)}) collective-permute-start(bf16[128,2048]{1,0:T(8,128)(2,1)S(1)} %get-tuple-element.131), channel_id=1, source_target_pairs={{2,1},{3,2},{6,5},{7,6},{10,9},{11,10},{14,13},{15,14},{18,17},{19... | collective-permute-start | bytes 1572872 | tf_op jit(solution)/shard_map/ppermute | solution.py:86
  639.7 22.5 %collective-permute-start = (bf16[128,2048]{1,0:T(8,128)(2,1)S(1)}, bf16[128,2048]{1,0:T(8,128)(2,1)S(1)}, u32[]{:S(2)}, u32[]{:S(2)}) collective-permute-start(bf16[128,2048]{1,0:T(8,128)(2,1)S(1)} %get-tuple-element.132), channel_id=1, source_target_pairs={{0,1},{4,5},{8,9},{12,13},{16,17},{20,21},{24,25},{28,29}} | collective-permute-start | bytes 1572872 | tf_op jit(solution)/shard_map/ppermute | solution.py:85
  650.9 22.5 %collective-permute-start.13 = (bf16[128,2048]{1,0:T(8,128)(2,1)S(1)}, bf16[128,2048]{1,0:T(8,128)(2,1)S(1)}, u32[]{:S(2)}, u32[]{:S(2)}) collective-permute-start(bf16[128,2048]{1,0:T(8,128)(2,1)S(1)} %slice_add_fusion.1), channel_id=1, source_target_pairs={{0,1},{1,2},{4,5},{5,6},{8,9},{9,10},{12,13},{13,14},{16,17},{17,1... | collective-permute-start | bytes 1572872 | tf_op jit(solution)/shard_map/ppermute | solution.py:85
  662.2 22.5 %collective-permute-start.7 = (bf16[128,2048]{1,0:T(8,128)(2,1)S(1)}, bf16[128,2048]{1,0:T(8,128)(2,1)S(1)}, u32[]{:S(2)}, u32[]{:S(2)}) collective-permute-start(bf16[128,2048]{1,0:T(8,128)(2,1)S(1)} %slice_add_fusion.3), channel_id=1, source_target_pairs={{0,1},{1,2},{4,5},{5,6},{8,9},{9,10},{12,13},{13,14},{16,17},{17,1... | collective-permute-start | bytes 1572872 | tf_op jit(solution)/shard_map/ppermute | solution.py:85
  667.1 28.7 %collective-permute-start.1 = (bf16[128,2048]{1,0:T(8,128)(2,1)S(1)}, bf16[128,2048]{1,0:T(8,128)(2,1)S(1)}, u32[]{:S(2)}, u32[]{:S(2)}) collective-permute-start(bf16[128,2048]{1,0:T(8,128)(2,1)S(1)} %slice_add_fusion.5), channel_id=1, source_target_pairs={{0,1},{1,2},{4,5},{5,6},{8,9},{9,10},{12,13},{13,14},{16,17},{17,1... | collective-permute-start | bytes 1572872 | tf_op jit(solution)/shard_map/ppermute | solution.py:85
  673.5 23.8 %collective-permute-start.17 = (bf16[128,2048]{1,0:T(8,128)(2,1)S(1)}, bf16[128,2048]{1,0:T(8,128)(2,1)S(1)}, u32[]{:S(2)}, u32[]{:S(2)}) collective-permute-start(bf16[128,2048]{1,0:T(8,128)(2,1)S(1)} %get-tuple-element.138), channel_id=1, source_target_pairs={{1,0},{2,1},{3,2},{5,4},{6,5},{7,6},{9,8},{10,9},{11,10},{13,12},{... | collective-permute-start | bytes 1572872 | tf_op jit(solution)/shard_map/ppermute | solution.py:86
  674.9 32.3 %collective-permute-start.14 = (bf16[128,2048]{1,0:T(8,128)(2,1)S(1)}, bf16[128,2048]{1,0:T(8,128)(2,1)S(1)}, u32[]{:S(2)}, u32[]{:S(2)}) collective-permute-start(bf16[128,2048]{1,0:T(8,128)(2,1)S(1)} %get-tuple-element.139), channel_id=1, source_target_pairs={{0,1},{1,2},{2,3},{4,5},{5,6},{6,7},{8,9},{9,10},{10,11},{12,13},{... | collective-permute-start | bytes 1572872 | tf_op jit(solution)/shard_map/ppermute | solution.py:85
  684.8 24.9 %collective-permute-start.11 = (bf16[128,2048]{1,0:T(8,128)(2,1)S(1)}, bf16[128,2048]{1,0:T(8,128)(2,1)S(1)}, u32[]{:S(2)}, u32[]{:S(2)}) collective-permute-start(bf16[128,2048]{1,0:T(8,128)(2,1)S(1)} %get-tuple-element.133), channel_id=1, source_target_pairs={{1,0},{2,1},{3,2},{5,4},{6,5},{7,6},{9,8},{10,9},{11,10},{13,12},{... | collective-permute-start | bytes 1572872 | tf_op jit(solution)/shard_map/ppermute | solution.py:86
  686.1 21.0 %copy-start.3 = (bf16[128,6144]{1,0:T(8,128)(2,1)S(1)}, bf16[128,6144]{1,0:T(8,128)(2,1)}, u32[]{:S(2)}) copy-start(bf16[128,6144]{1,0:T(8,128)(2,1)} %reduce-scatter.7.cloned.1.call-done.value_ref.refs_1_) | copy-start | bytes 4718596
  686.1 32.2 %collective-permute-start.8 = (bf16[128,2048]{1,0:T(8,128)(2,1)S(1)}, bf16[128,2048]{1,0:T(8,128)(2,1)S(1)}, u32[]{:S(2)}, u32[]{:S(2)}) collective-permute-start(bf16[128,2048]{1,0:T(8,128)(2,1)S(1)} %get-tuple-element.134), channel_id=1, source_target_pairs={{0,1},{1,2},{2,3},{4,5},{5,6},{6,7},{8,9},{9,10},{10,11},{12,13},{... | collective-permute-start | bytes 1572872 | tf_op jit(solution)/shard_map/ppermute | solution.py:85
  696.0 24.9 %collective-permute-start.5 = (bf16[128,2048]{1,0:T(8,128)(2,1)S(1)}, bf16[128,2048]{1,0:T(8,128)(2,1)S(1)}, u32[]{:S(2)}, u32[]{:S(2)}) collective-permute-start(bf16[128,2048]{1,0:T(8,128)(2,1)S(1)} %get-tuple-element.128), channel_id=1, source_target_pairs={{1,0},{2,1},{3,2},{5,4},{6,5},{7,6},{9,8},{10,9},{11,10},{13,12},{... | collective-permute-start | bytes 1572872 | tf_op jit(solution)/shard_map/ppermute | solution.py:86
  697.3 30.9 %collective-permute-start.2 = (bf16[128,2048]{1,0:T(8,128)(2,1)S(1)}, bf16[128,2048]{1,0:T(8,128)(2,1)S(1)}, u32[]{:S(2)}, u32[]{:S(2)}) collective-permute-start(bf16[128,2048]{1,0:T(8,128)(2,1)S(1)} %get-tuple-element.129), channel_id=1, source_target_pairs={{0,1},{1,2},{2,3},{4,5},{5,6},{6,7},{8,9},{9,10},{10,11},{12,13},{... | collective-permute-start | bytes 1572872 | tf_op jit(solution)/shard_map/ppermute | solution.py:85
  709.7 21.1 %copy-start.9 = (bf16[128,2048]{1,0:T(8,128)(2,1)}, bf16[128,2048]{1,0:T(8,128)(2,1)S(1)}, u32[]{:S(2)}) copy-start(bf16[128,2048]{1,0:T(8,128)(2,1)S(1)} %get-tuple-element.70.refs_2_) | copy-start | bytes 1572868
  720.9 11.2 %copy-start.10 = (bf16[128,2048]{1,0:T(8,128)(2,1)}, bf16[128,2048]{1,0:T(8,128)(2,1)S(1)}, u32[]{:S(2)}) copy-start(bf16[128,2048]{1,0:T(8,128)(2,1)S(1)} %get-tuple-element.68.refs_1_) | copy-start | bytes 1572868
  730.8 1.3 copy-start.11
  732.1 143.0 %reduce-scatter.17.cloned.1.call-start = ((), (), s32[]{:S(2)}) async-start(), calls=%async_computation.17 | async-start | bytes 9437184 | tf_op jit(solution)/shard_map/reduce_scatter | solution.py:801
  745.0 6.4 collective-permute-start.20
  751.4 13.3 %collective-permute-start.21 = (f32[8,2048]{1,0:T(8,128)S(1)}, f32[8,2048]{1,0:T(8,128)S(1)}, u32[]{:S(2)}, u32[]{:S(2)}) collective-permute-start(f32[8,2048]{1,0:T(8,128)S(1)} %add.130), channel_id=1, source_target_pairs={{0,2},{1,3},{2,0},{3,1},{4,6},{5,7},{6,4},{7,5},{8,10},{9,11},{10,... | collective-permute-start | bytes 196616 | tf_op jit(solution)/shard_map/ppermute | solution.py:51
  764.8 5.2 collective-permute-start.22
  769.8 18.1 %collective-permute-start.18 = (f32[72,256]{0,1:T(8,128)S(1)}, f32[72,256]{0,1:T(8,128)S(1)}, u32[]{:S(2)}, u32[]{:S(2)}) collective-permute-start(f32[72,256]{0,1:T(8,128)S(1)} %copy.50), channel_id=1, source_target_pairs={{0,1},{1,0},{2,3},{3,2},{4,5},{5,4},{6,7},{7,6},{8,9},{9,8},{10,11... | collective-permute-start | bytes 221192 | tf_op jit(solution)/shard_map/ppermute | solution.py:51
  769.9 6.0 collective-permute-start.23
  775.9 13.0 %collective-permute-start.24 = (f32[8,2048]{1,0:T(8,128)S(1)}, f32[8,2048]{1,0:T(8,128)S(1)}, u32[]{:S(2)}, u32[]{:S(2)}) collective-permute-start(f32[8,2048]{1,0:T(8,128)S(1)} %add.133), channel_id=1, source_target_pairs={{0,16},{4,20},{8,24},{12,28},{16,0},{20,4},{24,8},{28,12},{1,17},{... | collective-permute-start | bytes 196616 | tf_op jit(solution)/shard_map/ppermute | solution.py:51
  788.0 16.3 %collective-permute-start.19 = (f32[72,256]{0,1:T(8,128)S(1)}, f32[72,256]{0,1:T(8,128)S(1)}, u32[]{:S(2)}, u32[]{:S(2)}) collective-permute-start(f32[72,256]{0,1:T(8,128)S(1)} %add.128), channel_id=1, source_target_pairs={{0,2},{1,3},{2,0},{3,1},{4,6},{5,7},{6,4},{7,5},{8,10},{9,11},{10,... | collective-permute-start | bytes 221192 | tf_op jit(solution)/shard_map/ppermute | solution.py:51
  789.0 68.3 %copy-start.15 = (f32[8,2048]{1,0:T(8,128)}, f32[8,2048]{1,0:T(8,128)S(1)}, u32[]{:S(2)}) copy-start(f32[8,2048]{1,0:T(8,128)S(1)} %add.134.refs_8_) | copy-start | bytes 196612
  820.8 36.5 %copy-start.4 = (bf16[512,2048]{1,0:T(8,128)(2,1)S(1)}, bf16[512,2048]{1,0:T(8,128)(2,1)}, u32[]{:S(2)}) copy-start(bf16[512,2048]{1,0:T(8,128)(2,1)} %all-gather.15.cloned.1.call-done.hidden_ref.refs_5_) | copy-start | bytes 6291460
  857.3 1.2 copy-start.8
  858.6 1.6 copy-start.12
  860.1 17.7 %copy-start.1 = (f32[2048,68]{0,1:T(8,128)S(1)}, f32[2048,68]{0,1:T(8,128)}, u32[]{:S(2)}) copy-start(f32[2048,68]{0,1:T(8,128)} %param.24) | copy-start | bytes 1671172
Sparse Core Ops, SparseCore 0:
  20.6 113.4 reduce-scatter.6
  153.7 115.3 all-gather.8
  286.0 42.0 reduce-scatter.8
  331.8 45.2 all-gather.10
  394.4 42.6 reduce-scatter.10
  443.8 45.2 all-gather.12
  505.8 42.5 reduce-scatter.12
  552.9 45.2 all-gather.14
  732.2 125.0 all-gather.16
Sparse Core Ops, SparseCore 1:
  25.7 127.8 all-gather.6
  557.4 117.7 reduce-scatter.14
  744.6 78.0 reduce-scatter.16

commit v5 on v4

--- a/solution.py
+++ b/solution.py
@@ -97,45 +97,41 @@
     )
 
 
-def stream_kernel(mix_ref, hist_ref, near_ref, rest_ref, *, stored):
-    width = rest_ref.shape[1]
+def stream_kernel(mix_ref, hist_ref, *refs, stored, streams):
+    out_ref = refs[-1]
+    width = hist_ref.shape[2]
     lanes = 512
 
     def body(at, carry):
         mix = mix_ref[at, :]
         for c in range(0, width, lanes):
             rows = [hist_ref[j, at, c : c + lanes].astype(f32) for j in range(stored)]
-            for s in range(4):
+            for n, s in enumerate(streams):
                 total = total_of(
                     [rows[j] * mix[:, s * stored + j : s * stored + j + 1] for j in range(stored)]
-                ).astype(bf16)
-                if s < 3:
-                    near_ref[at, s * width + c : s * width + c + lanes] = total
-                else:
-                    rest_ref[at, c : c + lanes] = total
+                )
+                out_ref[at, n * width + c : n * width + c + lanes] = total.astype(bf16)
         return carry
 
-    row_loop(rest_ref.shape[0], body, 0)
-
-
-def stream_sums(mix_cols, history):
+    row_loop(out_ref.shape[0], body, 0)
+
+
+def stream_sums(mix_cols, history, streams, order):
     stored, tokens, width = history.shape
     rows = 128
     here = lambda i: (i, 0)
     return pl.pallas_call(
-        lambda *refs: stream_kernel(*refs, stored=stored),
+        lambda *refs: stream_kernel(*refs, stored=stored, streams=streams),
         grid=(tokens // rows,),
         in_specs=[
             pl.BlockSpec((rows, 4 * stored), here),
             pl.BlockSpec((stored, rows, width), lambda i: (0, i, 0)),
-        ],
-        out_specs=[pl.BlockSpec((rows, 3 * width), here), pl.BlockSpec((rows, width), here)],
-        out_shape=[
-            jax.ShapeDtypeStruct((tokens, 3 * width), bf16),
-            jax.ShapeDtypeStruct((tokens, width), bf16),
-        ],
+        ]
+        + [pl.BlockSpec(memory_space=pl.ANY)] * len(order),
+        out_specs=pl.BlockSpec((rows, len(streams) * width), here),
+        out_shape=jax.ShapeDtypeStruct((tokens, len(streams) * width), bf16),
         compiler_params=vmem(48),
-    )(mix_cols, history)
+    )(mix_cols, history, *order)
 
 
 def streams_norm(values, gains):
@@ -728,7 +724,7 @@
     hidden = w_up.shape[1]
     heads = w_query.shape[1]
     mix_cols = mix_weights.reshape(4 * stored, row_tok).T
-    near_shares, rest_share = stream_sums(mix_cols, history)
+    near_shares = stream_sums(mix_cols, history, (0, 1, 2), [])
     low = round_weights(
         [w_query, w_key, w_value, w_output, w_up, w_down],
         [False, False, False, True, False, True],
@@ -736,6 +732,7 @@
     )
     full = lax.all_gather(low, "dp", axis=0, tiled=True)
     stream_own = spread(near_shares)
+    rest_share = stream_sums(mix_cols, history, (3,), [near_shares, low])
     normed_rows = collect(after(streams_norm(stream_own, norm_gains[:3]), full))
 
     seg_row = segments[0]
@@ -805,7 +802,7 @@
         mix_cols,
         history,
         [(near, 0), (near, 1), (near, 2), (hidden_rows, 0)],
-        [down_sum, first_sum, small, attention_grad],
+        [down_sum[:8], first_sum[:8], small, attention_grad],
     )
     *projections, output_sum = unpack_attention(attention_sum, heads)
     mix_grad = mix_back.T.reshape(4, stored, row_tok)

time: 887 us -> 882 us (level)
  waiting for transfers between devices: 600 us -> 590 us
    all_gather x5, waiting for transfers between devices: 279 us -> 270 us  [collect(): return lax.all_gather(rows, 'layer', axis=0, tiled=True)]
  transfers between devices with their start and end apart: 37 -> 37, of which waited for: 24 -> 24; matrix products, arithmetic and copies ran while one was open for 2% -> 2% of each run, Pallas kernels for 9% -> 10%
where the time goes in v5:
time: 882 us; the launch traced here: 880 us
  waiting for transfers between devices  590 us (67%)
  Pallas kernels  158 us (18%)
  starting transfers between devices  60.9 us (7%)
  local copies, waits for them, and re-layouts  21.5 us (2%)
  blocking collectives  16.5 us (2%)
  between operations  16.3 us (2%)
  other arithmetic  10 us (1%)
    all_gather x5, waiting for transfers between devices, collect(): return lax.all_gather(rows, 'layer', axis=0, tiled=True)  270 us
    reduce_scatter x4, waiting for transfers between devices, spread(): return lax.psum_scatter(rows, 'layer', scatter_dimension=0, tiled=True)  216 us
    ppermute x9, waiting for transfers between devices, sum_hop(): lax.ppermute(up, 'layer', [(i, i + 1) for i in range(k)])  52 us
    ppermute x7, waiting for transfers between devices, doubling_sum(): lax.ppermute(value, axis, [(i, i ^ step) for i in range(size)])  40.1 us
    ppermute x9, starting transfers between devices, sum_hop(): lax.ppermute(up, 'layer', [(i, i + 1) for i in range(k)])  39.8 us
  transfers between devices with their start and end apart: 37, of which 24 were waited for; matrix products, arithmetic and copies ran while one was open for 2% of the time, Pallas kernels for 10%

profile of v5, /device:TPU:0, one launch (start us, length us, event | category | flops | bytes accessed | tf_op | source)
XLA Modules:
  0.0 880.4 jit_solution(13161305261271759229)
XLA Ops:
  9.0 9.3 %shard_map.237.refs_6_.refs_2_ = bf16[512,6144]{1,0:T(8,128)(2,1)} custom-call(f32[512,16]{1,0:T(8,128)S(1)} %bitcast.20, bf16[4,512,2048]{2,1,0:T(8,128)(2,1)} %refs_1_.7), custom_call_target="tpu_custom_call" | custom-call | tf_op jit(solution)/shard_map/pallas_call | solution.py:123
  18.4 5.1 shard_map.239.refs_3_
  24.3 107.6 %reduce-scatter.7.cloned.1.call-done.value_ref.refs_1_ = bf16[128,6144]{1,0:T(8,128)(2,1)} async-done(((bf16[512,6144]{1,0:T(8,128)(2,1)}), bf16[128,6144]{1,0:T(8,128)(2,1)}) %reduce-scatter.7.cloned.1.call-update) | async-done | bytes 1572880 | tf_op jit(solution)/shard_map/reduce_scatter | solution.py:722
  132.0 1.6 copy-done.3
  133.6 5.3 shard_map.238.refs_0_
  140.0 11.5 %all-gather.7.cloned.1.call-done.refs_1_.wq_ref.wk_ref.wv_ref.wo_ref.up_ref.down_ref.full_ref = bf16[2048,6144]{1,0:T(8,128)(2,1)} async-done(((bf16[256,6144]{1,0:T(8,128)(2,1)}), bf16[2048,6144]{1,0:T(8,128)(2,1)}) %all-gather.7.cloned.1.call-update) | async-done | bytes 25165840 | tf_op jit(solution)/shard_map/all_gather | solution.py:733
  151.6 1.9 copy-done.2
  153.5 6.4 shard_map.241.rest_ref
  164.9 102.1 %all-gather.9.cloned.1.call-done.near_ref.q_ref.k_ref.v_ref = bf16[512,6144]{1,0:T(8,128)(2,1)} async-done(((bf16[128,6144]{1,0:T(8,128)(2,1)}), bf16[512,6144]{1,0:T(8,128)(2,1)}) %all-gather.9.cloned.1.call-update) | async-done | bytes 6291472 | tf_op jit(solution)/shard_map/all_gather | solution.py:719
  267.0 16.7 %shard_map.242 = (bf16[512,512]{1,0:T(8,128)(2,1)}, bf16[512,512]{1,0:T(8,128)(2,1)}, bf16[512,512]{1,0:T(8,128)(2,1)}, bf16[512,512]{1,0:T(8,128)(2,1)}, f32[4,...) custom-call(s32[512,2]{1,0:T(8,128)} %copy.46.rows_ref, s32[2,512]{1,0:T(2,128)} %get-tuple-element.145.cols_ref, ...), custom_call_target="tpu_custom_call" | custom-call | tf_op jit(solution)/shard_map/pallas_call | solution.py:556
  283.9 42.2 %reduce-scatter.9.cloned.1.call-done.value_ref.refs_1_ = bf16[128,2048]{1,0:T(8,128)(2,1)} async-done(((bf16[512,2048]{1,0:T(8,128)(2,1)}), bf16[128,2048]{1,0:T(8,128)(2,1)}) %reduce-scatter.9.cloned.1.call-update) | async-done | bytes 524304 | tf_op jit(solution)/shard_map/reduce_scatter | solution.py:722
  327.1 2.4 shard_map.243
  329.6 45.4 %all-gather.11.cloned.1.call-done.rows_ref.mlp_ref = bf16[512,2048]{1,0:T(8,128)(2,1)} async-done(((bf16[128,2048]{1,0:T(8,128)(2,1)}), bf16[512,2048]{1,0:T(8,128)(2,1)}) %all-gather.11.cloned.1.call-update) | async-done | bytes 2097168 | tf_op jit(solution)/shard_map/all_gather | solution.py:719
  375.0 17.1 %shard_map.244 = (bf16[512,2048]{1,0:T(8,128)(2,1)}, f32[512,2048]{1,0:T(8,128)}, bf16[512,2048]{1,0:T(8,128)(2,1)}) custom-call(bf16[512,2048]{1,0:T(8,128)(2,1)} %all-gather.11.cloned.1.call-done.rows_ref.mlp_ref, bf16[2048,6144]{1,0:T(8,128)(2,1)} %all-gather.7.cloned.1.call-done.refs_1_.wq_ref.wk_ref.wv_ref.wo_ref.up_ref.down_ref.full_ref, ...), custom_call_target="tpu_custom_call" | custom-call | tf_op jit(solution)/shard_map/pallas_call | solution.py:413
  393.1 41.8 %reduce-scatter.11.cloned.1.call-done = bf16[128,2048]{1,0:T(8,128)(2,1)} async-done(((bf16[512,2048]{1,0:T(8,128)(2,1)}), bf16[128,2048]{1,0:T(8,128)(2,1)}) %reduce-scatter.11.cloned.1.call-update) | async-done | bytes 524304 | tf_op jit(solution)/shard_map/reduce_scatter | solution.py:722
  436.4 2.5 fusion.3
  438.9 1.5 multiply_reduce_fusion
  441.8 45.4 %all-gather.13.cloned.1.call-done.rows_ref.branch_ref = bf16[512,2048]{1,0:T(8,128)(2,1)} async-done(((bf16[128,2048]{1,0:T(8,128)(2,1)}), bf16[512,2048]{1,0:T(8,128)(2,1)}) %all-gather.13.cloned.1.call-update) | async-done | bytes 2097168 | tf_op jit(solution)/shard_map/all_gather | solution.py:719
  487.2 16.5 %shard_map.245 = (bf16[512,2048]{1,0:T(8,128)(2,1)}, bf16[512,2048]{1,0:T(8,128)(2,1)}) custom-call(bf16[512,2048]{1,0:T(8,128)(2,1)} %all-gather.13.cloned.1.call-done.rows_ref.branch_ref, bf16[2048,6144]{1,0:T(8,128)(2,1)} %all-gather.7.cloned.1.call-done.refs_1_.wq_ref.wk_ref.wv_ref.wo_ref.up_ref.down_ref.full_ref, ...), custom_call_target="tpu_custom_call" | custom-call | tf_op jit(solution)/shard_map/pallas_call | solution.py:460
  503.7 1.9 fusion.1
  506.7 15.5 %shard_map.247.refs_4_ = bf16[2048,4224]{1,0:T(8,128)(2,1)} custom-call(bf16[512,2048]{1,0:T(8,128)(2,1)} %all-gather.11.cloned.1.call-done.rows_ref.mlp_ref, bf16[512,2048]{1,0:T(8,128)(2,1)} %shard_map.246.up_ref, bf16[512,2048]{1,0:T(8,128)(2,1)} %all-gather.13.cloned.1.call-done.rows_ref.branch_ref, bf16[512,2048]{1,0:T(8,128)(2,1)} %get-tuple-element.52.active_ref, ...), custom_call_target="tpu_custom_call" | custom-call | tf_op jit(solution)/shard_map/pallas_call | solution.py:324
  522.2 24.2 %reduce-scatter.13.cloned.1.call-done.refs_2_ = bf16[128,2048]{1,0:T(8,128)(2,1)} async-done(((bf16[512,2048]{1,0:T(8,128)(2,1)}), bf16[128,2048]{1,0:T(8,128)(2,1)}) %reduce-scatter.13.cloned.1.call-update) | async-done | bytes 524304 | tf_op jit(solution)/shard_map/reduce_scatter | solution.py:722
  547.5 3.4 shard_map.248
  552.4 43.8 %all-gather.15.cloned.1.call-done.hidden_ref.refs_5_ = bf16[512,2048]{1,0:T(8,128)(2,1)} async-done(((bf16[128,2048]{1,0:T(8,128)(2,1)}), bf16[512,2048]{1,0:T(8,128)(2,1)}) %all-gather.15.cloned.1.call-update) | async-done | bytes 2097168 | tf_op jit(solution)/shard_map/all_gather | solution.py:719
  596.2 10.1 %shard_map.249 = (bf16[512,512]{1,0:T(8,128)(2,1)}, bf16[512,512]{1,0:T(8,128)(2,1)}, bf16[512,512]{1,0:T(8,128)(2,1)}) custom-call(s32[512,2]{1,0:T(8,128)} %copy.46.rows_ref, s32[2,512]{1,0:T(2,128)} %get-tuple-element.145.cols_ref, f32[512,128]{1,0:T(8,128)} %get-tuple-element.151.cos_ref, f32[512,128]{1,0:T(8,128)} %get-tuple-element.152.sin_ref, ...), custom_call_target="tpu_custom_call" | custom-call | tf_op jit(solution)/shard_map/pallas_call | solution.py:602
  606.3 9.6 %shard_map.250 = (bf16[512,2048]{1,0:T(8,128)(2,1)}, bf16[512,2048]{1,0:T(8,128)(2,1)}, bf16[512,2048]{1,0:T(8,128)(2,1)}) custom-call(s32[4]{0:T(128)} %pad_add_fusion.1.where_ref, bf16[512,512]{1,0:T(8,128)(2,1)} %get-tuple-element.58.dq_ref, bf16[512,512]{1,0:T(8,128)(2,1)} %get-tuple-element.59.dk_ref, bf16[512,512]{1,0:T(8,128)(2,1)} %get-tuple-element.60.dv_ref, ...), custom_call_target="tpu_custom_call" | custom-call | tf_op jit(solution)/shard_map/pallas_call | solution.py:633
  620.6 1.5 slice_add_fusion
  622.8 2.5 collective-permute-start.12
  626.2 1.9 collective-permute-start.6
  628.9 8.8 collective-permute-done.12
  637.7 4.4 collective-permute-start
  642.2 6.7 collective-permute-done.6
  648.9 4.4 collective-permute-start.13
  653.4 6.7 collective-permute-done
  660.2 4.9 collective-permute-start.7
  665.1 1.9 collective-permute-start.1
  667.1 4.3 collective-permute-done.13
  672.9 6.5 collective-permute-start.14
  679.5 3.2 collective-permute-done.7
  684.2 6.7 collective-permute-start.8
  690.8 3.0 collective-permute-done.1
  695.3 6.5 collective-permute-start.2
  701.9 3.2 collective-permute-done.14.refs_3_
  705.1 2.6 shard_map.253
  707.7 8.6 collective-permute-done.8.refs_3_
  716.3 2.6 shard_map.252
  718.9 7.3 collective-permute-done.2.refs_3_
  726.2 2.6 shard_map.251
  730.5 12.0 %shard_map.255.refs_9_ = bf16[2048,2048]{1,0:T(8,128)(2,1)} custom-call(bf16[512,6144]{1,0:T(8,128)(2,1)} %all-gather.9.cloned.1.call-done.near_ref.q_ref.k_ref.v_ref, bf16[512,6144]{1,0:T(8,128)(2,1)} %all-gather.9.cloned.1.call-done.near_ref.q_ref.k_ref.v_ref, bf16[512,6144]{1,0:T(8,128)(2,1)} %all-gather.9.cloned.1.call-done.near_ref.q_ref.k_ref.v_ref, ...), custom_call_target="tpu_custom_call" | custom-call | tf_op jit(solution)/shard_map/pallas_call | solution.py:347
  743.0 2.5 collective-permute-start.20
  745.6 3.9 collective-permute-done.20
  749.4 5.9 collective-permute-start.21
  755.3 7.4 collective-permute-done.21
  762.9 4.0 shard_map.254
  768.0 1.5 collective-permute-start.23
  769.5 4.5 collective-permute-done.23
  774.0 1.5 collective-permute-start.24
  775.5 10.5 %collective-permute-done.18 = f32[72,256]{0,1:T(8,128)S(1)} collective-permute-done((f32[72,256]{0,1:T(8,128)S(1)}, f32[72,256]{0,1:T(8,128)S(1)}, u32[]{:S(2)}, u32[]{:S(2)}) %collective-permute-start.18) | collective-permute-done | bytes 73760 | tf_op jit(solution)/shard_map/ppermute | solution.py:51
  788.5 13.8 %collective-permute-done.19 = f32[72,256]{0,1:T(8,128)S(1)} collective-permute-done((f32[72,256]{0,1:T(8,128)S(1)}, f32[72,256]{0,1:T(8,128)S(1)}, u32[]{:S(2)}, u32[]{:S(2)}) %collective-permute-start.19) | collective-permute-done | bytes 73760 | tf_op jit(solution)/shard_map/ppermute | solution.py:51
  802.3 16.5 %all_gather.27 = f32[72,2048]{0,1:T(8,128)S(1)} all-gather(f32[72,256]{0,1:T(8,128)S(1)} %add.129), channel_id=1, replica_groups=mesh['dp'=8,'layer'=4] {'dp'}, dimensions={1}, use_global_device_ids=true | all-gather | bytes 663552 | tf_op jit(solution)/shard_map/all_gather | solution.py:800
  819.9 2.4 copy.52
  822.3 33.0 %all-gather.17.cloned.1.call-done.refs_2_.refs_3_.refs_4_ = bf16[512,6144]{1,0:T(8,128)(2,1)} async-done(((bf16[128,6144]{1,0:T(8,128)(2,1)}), bf16[512,6144]{1,0:T(8,128)(2,1)}) %all-gather.17.cloned.1.call-update) | async-done | bytes 6291472 | tf_op jit(solution)/shard_map/all_gather | solution.py:719
  855.3 14.3 %shard_map.256 = (bf16[4,512,2048]{2,1,0:T(8,128)(2,1)}, f32[512,16]{1,0:T(8,128)S(1)}) custom-call(f32[512,16]{1,0:T(8,128)S(1)} %bitcast.22, bf16[4,512,2048]{2,1,0:T(8,128)(2,1)} %refs_1_.7, bf16[512,6144]{1,0:T(8,128)(2,1)} %all-gather.17.cloned.1.call-done.refs_2_.refs_3_.refs_4_, ...), custom_call_target="tpu_custom_call" | custom-call | tf_op jit(solution)/shard_map/pallas_call | solution.py:283
  870.4 2.6 shard_map.257
  (154 shorter events, 35.9 us)
Async XLA Ops:
  8.0 428.3 %copy-start = (f32[2048,68]{0,1:T(8,128)S(1)}, f32[2048,68]{0,1:T(8,128)}, u32[]{:S(2)}) copy-start(f32[2048,68]{0,1:T(8,128)} %param.24) | copy-start | bytes 1671172
  8.0 124.0 %reduce-scatter.7.cloned.1.call-start = ((), (), s32[]{:S(2)}) async-start(), calls=%async_computation.6 | async-start | bytes 7864320 | tf_op jit(solution)/shard_map/reduce_scatter | solution.py:722
  18.4 133.1 %all-gather.7.cloned.1.call-start = ((), (), s32[]{:S(2)}) async-start(), calls=%async_computation.7 | async-start | bytes 28311552 | tf_op jit(solution)/shard_map/all_gather | solution.py:733
  23.5 0.8 copy-start.21
  23.5 243.5 %all-gather.9.cloned.1.call-start = ((), (), s32[]{:S(2)}) async-start(), calls=%async_computation.8 | async-start | bytes 7864320 | tf_op jit(solution)/shard_map/all_gather | solution.py:719
  132.0 1.6 copy-start.3
  138.8 1.1 copy-start.8
  151.5 174.6 %reduce-scatter.9.cloned.1.call-start = ((), (), s32[]{:S(2)}) async-start(), calls=%async_computation.9 | async-start | bytes 2621440 | tf_op jit(solution)/shard_map/reduce_scatter | solution.py:722
  151.6 1.9 copy-start.2
  153.5 7.8 copy-start.24
  159.9 1.3 copy-start.9
  283.8 91.2 %all-gather.11.cloned.1.call-start = ((), (), s32[]{:S(2)}) async-start(), calls=%async_computation.10 | async-start | bytes 2621440 | tf_op jit(solution)/shard_map/all_gather | solution.py:719
  326.1 1.0 copy-start.6
  329.6 105.4 %reduce-scatter.11.cloned.1.call-start = ((), (), s32[]{:S(2)}) async-start(), calls=%async_computation.11 | async-start | bytes 2621440 | tf_op jit(solution)/shard_map/reduce_scatter | solution.py:722
  392.1 0.8 copy-start.22
  392.1 0.8 copy-start.23
  392.1 42.8 %copy-start.7 = (bf16[128,2048]{1,0:T(8,128)(2,1)S(1)}, bf16[128,2048]{1,0:T(8,128)(2,1)}, u32[]{:S(2)}) copy-start(bf16[128,2048]{1,0:T(8,128)(2,1)} %reduce-scatter.9.cloned.1.call-done.value_ref.refs_1_) | copy-start | bytes 1572868
  392.2 95.0 %all-gather.13.cloned.1.call-start = ((), (), s32[]{:S(2)}) async-start(), calls=%async_computation.12 | async-start | bytes 2621440 | tf_op jit(solution)/shard_map/all_gather | solution.py:719
  435.0 3.9 copy-start.15
  436.3 4.0 copy-start.20
  441.8 104.7 %reduce-scatter.13.cloned.1.call-start = ((), (), s32[]{:S(2)}) async-start(), calls=%async_computation.13 | async-start | bytes 2621440 | tf_op jit(solution)/shard_map/reduce_scatter | solution.py:722
  503.7 92.6 %all-gather.15.cloned.1.call-start = ((), (), s32[]{:S(2)}) async-start(), calls=%async_computation.14 | async-start | bytes 2621440 | tf_op jit(solution)/shard_map/all_gather | solution.py:719
  546.4 1.0 copy-start.13
  550.9 179.6 %reduce-scatter.15.cloned.1.call-start = ((), (), s32[]{:S(2)}) async-start(), calls=%async_computation.16 | async-start | bytes 19464192 | tf_op jit(solution)/shard_map/reduce_scatter | solution.py:776
  551.5 303.9 %all-gather.17.cloned.1.call-start = ((), (), s32[]{:S(2)}) async-start(), calls=%async_computation.15 | async-start | bytes 7864320 | tf_op jit(solution)/shard_map/all_gather | solution.py:719
  615.9 3.9 copy-start.16
  617.2 3.5 collective-permute-start.15
  619.0 6.4 copy-start.17
  619.0 6.4 collective-permute-start.9
  619.9 8.2 collective-permute-start.3
  622.1 43.0 %collective-permute-start.16 = (bf16[128,2048]{1,0:T(8,128)(2,1)S(1)}, bf16[128,2048]{1,0:T(8,128)(2,1)S(1)}, u32[]{:S(2)}, u32[]{:S(2)}) collective-permute-start(bf16[128,2048]{1,0:T(8,128)(2,1)S(1)} %get-tuple-element.137), channel_id=1, source_target_pairs={{2,1},{3,2},{6,5},{7,6},{10,9},{11,10},{14,13},{15,14},{18,17},{19... | collective-permute-start | bytes 1572872 | tf_op jit(solution)/shard_map/ppermute | solution.py:86
  622.8 19.3 %copy-start.18 = (bf16[512,2048]{1,0:T(8,128)(2,1)S(1)}, bf16[512,2048]{1,0:T(8,128)(2,1)}, u32[]{:S(2)}) copy-start(bf16[512,2048]{1,0:T(8,128)(2,1)} %get-tuple-element.65) | copy-start | bytes 6291460
  622.8 14.9 %collective-permute-start.12 = (bf16[128,2048]{1,0:T(8,128)(2,1)S(1)}, bf16[128,2048]{1,0:T(8,128)(2,1)S(1)}, u32[]{:S(2)}, u32[]{:S(2)}) collective-permute-start(bf16[128,2048]{1,0:T(8,128)(2,1)S(1)} %get-tuple-element.138), channel_id=1, source_target_pairs={{0,1},{4,5},{8,9},{12,13},{16,17},{20,21},{24,25},{28,29}} | collective-permute-start | bytes 1572872 | tf_op jit(solution)/shard_map/ppermute | solution.py:85
  625.5 47.4 %collective-permute-start.10 = (bf16[128,2048]{1,0:T(8,128)(2,1)S(1)}, bf16[128,2048]{1,0:T(8,128)(2,1)S(1)}, u32[]{:S(2)}, u32[]{:S(2)}) collective-permute-start(bf16[128,2048]{1,0:T(8,128)(2,1)S(1)} %get-tuple-element.132), channel_id=1, source_target_pairs={{2,1},{3,2},{6,5},{7,6},{10,9},{11,10},{14,13},{15,14},{18,17},{19... | collective-permute-start | bytes 1572872 | tf_op jit(solution)/shard_map/ppermute | solution.py:86
  626.2 22.7 %collective-permute-start.6 = (bf16[128,2048]{1,0:T(8,128)(2,1)S(1)}, bf16[128,2048]{1,0:T(8,128)(2,1)S(1)}, u32[]{:S(2)}, u32[]{:S(2)}) collective-permute-start(bf16[128,2048]{1,0:T(8,128)(2,1)S(1)} %get-tuple-element.133), channel_id=1, source_target_pairs={{0,1},{4,5},{8,9},{12,13},{16,17},{20,21},{24,25},{28,29}} | collective-permute-start | bytes 1572872 | tf_op jit(solution)/shard_map/ppermute | solution.py:85
  628.2 55.9 %collective-permute-start.4 = (bf16[128,2048]{1,0:T(8,128)(2,1)S(1)}, bf16[128,2048]{1,0:T(8,128)(2,1)S(1)}, u32[]{:S(2)}, u32[]{:S(2)}) collective-permute-start(bf16[128,2048]{1,0:T(8,128)(2,1)S(1)} %get-tuple-element.127), channel_id=1, source_target_pairs={{2,1},{3,2},{6,5},{7,6},{10,9},{11,10},{14,13},{15,14},{18,17},{19... | collective-permute-start | bytes 1572872 | tf_op jit(solution)/shard_map/ppermute | solution.py:86
  637.7 22.5 %collective-permute-start = (bf16[128,2048]{1,0:T(8,128)(2,1)S(1)}, bf16[128,2048]{1,0:T(8,128)(2,1)S(1)}, u32[]{:S(2)}, u32[]{:S(2)}) collective-permute-start(bf16[128,2048]{1,0:T(8,128)(2,1)S(1)} %get-tuple-element.128), channel_id=1, source_target_pairs={{0,1},{4,5},{8,9},{12,13},{16,17},{20,21},{24,25},{28,29}} | collective-permute-start | bytes 1572872 | tf_op jit(solution)/shard_map/ppermute | solution.py:85
  648.9 22.5 %collective-permute-start.13 = (bf16[128,2048]{1,0:T(8,128)(2,1)S(1)}, bf16[128,2048]{1,0:T(8,128)(2,1)S(1)}, u32[]{:S(2)}, u32[]{:S(2)}) collective-permute-start(bf16[128,2048]{1,0:T(8,128)(2,1)S(1)} %slice_add_fusion.1), channel_id=1, source_target_pairs={{0,1},{1,2},{4,5},{5,6},{8,9},{9,10},{12,13},{13,14},{16,17},{17,1... | collective-permute-start | bytes 1572872 | tf_op jit(solution)/shard_map/ppermute | solution.py:85
  660.2 22.5 %collective-permute-start.7 = (bf16[128,2048]{1,0:T(8,128)(2,1)S(1)}, bf16[128,2048]{1,0:T(8,128)(2,1)S(1)}, u32[]{:S(2)}, u32[]{:S(2)}) collective-permute-start(bf16[128,2048]{1,0:T(8,128)(2,1)S(1)} %slice_add_fusion.3), channel_id=1, source_target_pairs={{0,1},{1,2},{4,5},{5,6},{8,9},{9,10},{12,13},{13,14},{16,17},{17,1... | collective-permute-start | bytes 1572872 | tf_op jit(solution)/shard_map/ppermute | solution.py:85
  665.1 28.7 %collective-permute-start.1 = (bf16[128,2048]{1,0:T(8,128)(2,1)S(1)}, bf16[128,2048]{1,0:T(8,128)(2,1)S(1)}, u32[]{:S(2)}, u32[]{:S(2)}) collective-permute-start(bf16[128,2048]{1,0:T(8,128)(2,1)S(1)} %slice_add_fusion.5), channel_id=1, source_target_pairs={{0,1},{1,2},{4,5},{5,6},{8,9},{9,10},{12,13},{13,14},{16,17},{17,1... | collective-permute-start | bytes 1572872 | tf_op jit(solution)/shard_map/ppermute | solution.py:85
  671.6 23.7 %collective-permute-start.17 = (bf16[128,2048]{1,0:T(8,128)(2,1)S(1)}, bf16[128,2048]{1,0:T(8,128)(2,1)S(1)}, u32[]{:S(2)}, u32[]{:S(2)}) collective-permute-start(bf16[128,2048]{1,0:T(8,128)(2,1)S(1)} %get-tuple-element.134), channel_id=1, source_target_pairs={{1,0},{2,1},{3,2},{5,4},{6,5},{7,6},{9,8},{10,9},{11,10},{13,12},{... | collective-permute-start | bytes 1572872 | tf_op jit(solution)/shard_map/ppermute | solution.py:86
  672.9 32.2 %collective-permute-start.14 = (bf16[128,2048]{1,0:T(8,128)(2,1)S(1)}, bf16[128,2048]{1,0:T(8,128)(2,1)S(1)}, u32[]{:S(2)}, u32[]{:S(2)}) collective-permute-start(bf16[128,2048]{1,0:T(8,128)(2,1)S(1)} %get-tuple-element.135), channel_id=1, source_target_pairs={{0,1},{1,2},{2,3},{4,5},{5,6},{6,7},{8,9},{9,10},{10,11},{12,13},{... | collective-permute-start | bytes 1572872 | tf_op jit(solution)/shard_map/ppermute | solution.py:85
  682.8 24.9 %collective-permute-start.11 = (bf16[128,2048]{1,0:T(8,128)(2,1)S(1)}, bf16[128,2048]{1,0:T(8,128)(2,1)S(1)}, u32[]{:S(2)}, u32[]{:S(2)}) collective-permute-start(bf16[128,2048]{1,0:T(8,128)(2,1)S(1)} %get-tuple-element.129), channel_id=1, source_target_pairs={{1,0},{2,1},{3,2},{5,4},{6,5},{7,6},{9,8},{10,9},{11,10},{13,12},{... | collective-permute-start | bytes 1572872 | tf_op jit(solution)/shard_map/ppermute | solution.py:86
  684.1 21.0 %copy-start.4 = (bf16[128,6144]{1,0:T(8,128)(2,1)S(1)}, bf16[128,6144]{1,0:T(8,128)(2,1)}, u32[]{:S(2)}) copy-start(bf16[128,6144]{1,0:T(8,128)(2,1)} %reduce-scatter.7.cloned.1.call-done.value_ref.refs_1_) | copy-start | bytes 4718596
  684.2 32.2 %collective-permute-start.8 = (bf16[128,2048]{1,0:T(8,128)(2,1)S(1)}, bf16[128,2048]{1,0:T(8,128)(2,1)S(1)}, u32[]{:S(2)}, u32[]{:S(2)}) collective-permute-start(bf16[128,2048]{1,0:T(8,128)(2,1)S(1)} %get-tuple-element.130), channel_id=1, source_target_pairs={{0,1},{1,2},{2,3},{4,5},{5,6},{6,7},{8,9},{9,10},{10,11},{12,13},{... | collective-permute-start | bytes 1572872 | tf_op jit(solution)/shard_map/ppermute | solution.py:85
  694.0 24.9 %collective-permute-start.5 = (bf16[128,2048]{1,0:T(8,128)(2,1)S(1)}, bf16[128,2048]{1,0:T(8,128)(2,1)S(1)}, u32[]{:S(2)}, u32[]{:S(2)}) collective-permute-start(bf16[128,2048]{1,0:T(8,128)(2,1)S(1)} %get-tuple-element.124), channel_id=1, source_target_pairs={{1,0},{2,1},{3,2},{5,4},{6,5},{7,6},{9,8},{10,9},{11,10},{13,12},{... | collective-permute-start | bytes 1572872 | tf_op jit(solution)/shard_map/ppermute | solution.py:86
  695.3 30.9 %collective-permute-start.2 = (bf16[128,2048]{1,0:T(8,128)(2,1)S(1)}, bf16[128,2048]{1,0:T(8,128)(2,1)S(1)}, u32[]{:S(2)}, u32[]{:S(2)}) collective-permute-start(bf16[128,2048]{1,0:T(8,128)(2,1)S(1)} %get-tuple-element.125), channel_id=1, source_target_pairs={{0,1},{1,2},{2,3},{4,5},{5,6},{6,7},{8,9},{9,10},{10,11},{12,13},{... | collective-permute-start | bytes 1572872 | tf_op jit(solution)/shard_map/ppermute | solution.py:85
  707.7 21.1 %copy-start.10 = (bf16[128,2048]{1,0:T(8,128)(2,1)}, bf16[128,2048]{1,0:T(8,128)(2,1)S(1)}, u32[]{:S(2)}) copy-start(bf16[128,2048]{1,0:T(8,128)(2,1)S(1)} %get-tuple-element.66.refs_2_) | copy-start | bytes 1572868
  718.9 11.2 %copy-start.11 = (bf16[128,2048]{1,0:T(8,128)(2,1)}, bf16[128,2048]{1,0:T(8,128)(2,1)S(1)}, u32[]{:S(2)}) copy-start(bf16[128,2048]{1,0:T(8,128)(2,1)S(1)} %get-tuple-element.64.refs_1_) | copy-start | bytes 1572868
  728.8 1.3 copy-start.12
  730.1 140.2 %reduce-scatter.17.cloned.1.call-start = ((), (), s32[]{:S(2)}) async-start(), calls=%async_computation.17 | async-start | bytes 9437184 | tf_op jit(solution)/shard_map/reduce_scatter | solution.py:798
  743.0 6.4 collective-permute-start.20
  749.4 13.3 %collective-permute-start.21 = (f32[8,2048]{1,0:T(8,128)S(1)}, f32[8,2048]{1,0:T(8,128)S(1)}, u32[]{:S(2)}, u32[]{:S(2)}) collective-permute-start(f32[8,2048]{1,0:T(8,128)S(1)} %add.130), channel_id=1, source_target_pairs={{0,2},{1,3},{2,0},{3,1},{4,6},{5,7},{6,4},{7,5},{8,10},{9,11},{10,... | collective-permute-start | bytes 196616 | tf_op jit(solution)/shard_map/ppermute | solution.py:51
  762.8 5.2 collective-permute-start.22
  767.9 18.1 %collective-permute-start.18 = (f32[72,256]{0,1:T(8,128)S(1)}, f32[72,256]{0,1:T(8,128)S(1)}, u32[]{:S(2)}, u32[]{:S(2)}) collective-permute-start(f32[72,256]{0,1:T(8,128)S(1)} %copy.50), channel_id=1, source_target_pairs={{0,1},{1,0},{2,3},{3,2},{4,5},{5,4},{6,7},{7,6},{8,9},{9,8},{10,11... | collective-permute-start | bytes 221192 | tf_op jit(solution)/shard_map/ppermute | solution.py:51
  768.0 6.0 collective-permute-start.23
  774.0 13.0 %collective-permute-start.24 = (f32[8,2048]{1,0:T(8,128)S(1)}, f32[8,2048]{1,0:T(8,128)S(1)}, u32[]{:S(2)}, u32[]{:S(2)}) collective-permute-start(f32[8,2048]{1,0:T(8,128)S(1)} %add.133), channel_id=1, source_target_pairs={{0,16},{4,20},{8,24},{12,28},{16,0},{20,4},{24,8},{28,12},{1,17},{... | collective-permute-start | bytes 196616 | tf_op jit(solution)/shard_map/ppermute | solution.py:51
  786.0 16.3 %collective-permute-start.19 = (f32[72,256]{0,1:T(8,128)S(1)}, f32[72,256]{0,1:T(8,128)S(1)}, u32[]{:S(2)}, u32[]{:S(2)}) collective-permute-start(f32[72,256]{0,1:T(8,128)S(1)} %add.128), channel_id=1, source_target_pairs={{0,2},{1,3},{2,0},{3,1},{4,6},{5,7},{6,4},{7,5},{8,10},{9,11},{10,... | collective-permute-start | bytes 221192 | tf_op jit(solution)/shard_map/ppermute | solution.py:51
  787.0 68.3 %copy-start.14 = (f32[8,2048]{1,0:T(8,128)}, f32[8,2048]{1,0:T(8,128)S(1)}, u32[]{:S(2)}) copy-start(f32[8,2048]{1,0:T(8,128)S(1)} %add.134.refs_8_) | copy-start | bytes 196612
  818.8 36.5 %copy-start.5 = (bf16[512,2048]{1,0:T(8,128)(2,1)S(1)}, bf16[512,2048]{1,0:T(8,128)(2,1)}, u32[]{:S(2)}) copy-start(bf16[512,2048]{1,0:T(8,128)(2,1)} %all-gather.15.cloned.1.call-done.hidden_ref.refs_5_) | copy-start | bytes 6291460
  818.9 1.0 copy-start.19
  855.3 17.7 %copy-start.1 = (f32[2048,68]{0,1:T(8,128)S(1)}, f32[2048,68]{0,1:T(8,128)}, u32[]{:S(2)}) copy-start(f32[2048,68]{0,1:T(8,128)} %param.24) | copy-start | bytes 1671172
Sparse Core Ops, SparseCore 0:
  18.5 113.4 reduce-scatter.6
  151.6 115.3 all-gather.8
  283.9 42.1 reduce-scatter.8
  329.7 45.2 all-gather.10
  392.3 42.6 reduce-scatter.10
  441.9 45.2 all-gather.12
  503.8 42.5 reduce-scatter.12
  551.0 45.2 all-gather.14
  730.3 125.0 all-gather.16
Sparse Core Ops, SparseCore 1:
  23.6 127.8 all-gather.6
  555.4 117.7 reduce-scatter.14
  742.6 78.0 reduce-scatter.16

commit v6 on v5

--- a/solution.py
+++ b/solution.py
@@ -92,9 +92,12 @@
 
 
 def row_loop(rows, body, carry):
-    return lax.fori_loop(
-        0, rows // CHUNK, lambda i, c: body(pl.ds(pl.multiple_of(i * CHUNK, CHUNK), CHUNK), c), carry
-    )
+    def turn_of(i, c):
+        for n in range(2):
+            c = body(pl.ds(pl.multiple_of((2 * i + n) * CHUNK, CHUNK), CHUNK), c)
+        return c
+
+    return lax.fori_loop(0, rows // CHUNK // 2, turn_of, carry)
 
 
 def stream_kernel(mix_ref, hist_ref, *refs, stored, streams):
@@ -621,11 +624,13 @@
         for s, ref in enumerate((dq_ref, dk_ref, dv_ref)):
 
             @pl.when(pl.program_id(0) == s)
-            def _(ref=ref, out_ref=out_refs[s]):
+            def _(ref=ref, out_ref=out_refs[3 * s], leave_refs=out_refs[3 * s + 1 : 3 * s + 3]):
                 share = contract_cols(ref[...], full_ref[...]).astype(bf16)
                 for j in range(count):
                     at = pl.ds(pl.multiple_of(where_ref[j] * block, block), block)
                     out_ref[at, :] = share[j * block : (j + 1) * block, :]
+                for k, leave_ref in zip((1, count - 1), leave_refs):
+                    leave_ref[...] = out_ref[k * block : (k + 1) * block, :]
 
     fixed = pl.BlockSpec(
         (tokens, heads), lambda s, w: (0, 0), pipeline_mode=pl.Buffered(buffer_count=1)
@@ -636,9 +641,17 @@
             num_scalar_prefetch=1,
             grid=(3,),
             in_specs=[fixed] * 3 + [pl.BlockSpec((width, heads), lambda s, w: (0, s))],
-            out_specs=[pl.BlockSpec((tokens, width), lambda s, w: (0, 0))] * 3,
+            out_specs=(
+                [pl.BlockSpec((tokens, width), lambda s, w: (0, 0))]
+                + [pl.BlockSpec((block, width), lambda s, w: (0, 0))] * 2
+            )
+            * 3,
         ),
-        out_shape=[jax.ShapeDtypeStruct((tokens, width), bf16)] * 3,
+        out_shape=(
+            [jax.ShapeDtypeStruct((tokens, width), bf16)]
+            + [jax.ShapeDtypeStruct((block, width), bf16)] * 2
+        )
+        * 3,
         compiler_params=vmem(56),
     )(where, *lin_grads, full)
 
@@ -707,6 +720,7 @@
     count = lax.axis_size("layer")
     me = lax.axis_index("layer")
     own_tok = row_tok // count
+    last = count - 1
     order = [(me - k) % count for k in range(count)]
 
     def block_of(rows, k):
@@ -776,7 +790,8 @@
     mlp_sum = lax.psum_scatter(mlp_grad, "dp", scatter_dimension=0, tiled=True)
     gain_grads, stream_low = [], []
     for s in range(3):
-        blocks = blocks_of(stream_parts[s])
+        blocks = blocks_of(stream_parts[3 * s])
+        blocks[1], blocks[last] = stream_parts[3 * s + 1 : 3 * s + 3]
         came = []
         for k in range(1, count):
             came = sum_hop(blocks, k, came, count)

time: 882 us -> 872 us (0.989)
    ppermute x9, waiting for transfers between devices: 52 us -> 39.1 us  [sum_hop(): lax.ppermute(up, 'layer', [(i, i + 1) for i in range(k)])]
    ppermute x9, starting transfers between devices: 39.8 us -> 50.3 us  [sum_hop(): lax.ppermute(up, 'layer', [(i, i + 1) for i in range(k)])]
where the time goes in v6:
time: 872 us; the launch traced here: 871 us
  waiting for transfers between devices  585 us (67%)
  Pallas kernels  150 us (17%)
  starting transfers between devices  65.9 us (8%)
  local copies, waits for them, and re-layouts  19.2 us (2%)
  blocking collectives  16.5 us (2%)
  between operations  16.4 us (2%)
  other arithmetic  10.1 us (1%)
    all_gather x5, waiting for transfers between devices, collect(): return lax.all_gather(rows, 'layer', axis=0, tiled=True)  271 us
    reduce_scatter x4, waiting for transfers between devices, spread(): return lax.psum_scatter(rows, 'layer', scatter_dimension=0, tiled=True)  216 us
    ppermute x9, starting transfers between devices, sum_hop(): lax.ppermute(up, 'layer', [(i, i + 1) for i in range(k)])  50.3 us
    ppermute x7, waiting for transfers between devices, doubling_sum(): lax.ppermute(value, axis, [(i, i ^ step) for i in range(size)])  45.2 us
    ppermute x9, waiting for transfers between devices, sum_hop(): lax.ppermute(up, 'layer', [(i, i + 1) for i in range(k)])  39.1 us
  transfers between devices with their start and end apart: 37, of which 24 were waited for; matrix products, arithmetic and copies ran while one was open for 2% of the time, Pallas kernels for 10%

profile of v6, /device:TPU:0, one launch (start us, length us, event | category | flops | bytes accessed | tf_op | source)
XLA Modules:
  0.0 870.5 jit_solution(7229011403698071521)
XLA Ops:
  9.0 8.9 %shard_map.237.refs_6_.refs_2_ = bf16[512,6144]{1,0:T(8,128)(2,1)} custom-call(f32[512,16]{1,0:T(8,128)S(1)} %bitcast.20, bf16[4,512,2048]{2,1,0:T(8,128)(2,1)} %refs_1_.7), custom_call_target="tpu_custom_call" | custom-call | tf_op jit(solution)/shard_map/pallas_call | solution.py:126
  18.0 5.1 shard_map.239.refs_3_
  23.9 107.7 %reduce-scatter.7.cloned.1.call-done.value_ref.refs_1_ = bf16[128,6144]{1,0:T(8,128)(2,1)} async-done(((bf16[512,6144]{1,0:T(8,128)(2,1)}), bf16[128,6144]{1,0:T(8,128)(2,1)}) %reduce-scatter.7.cloned.1.call-update) | async-done | bytes 1572880 | tf_op jit(solution)/shard_map/reduce_scatter | solution.py:736
  131.5 1.6 copy-done.3
  133.1 3.0 shard_map.238.refs_0_
  137.3 13.7 %all-gather.7.cloned.1.call-done.refs_1_.wq_ref.wk_ref.wv_ref.wo_ref.up_ref.down_ref.full_ref = bf16[2048,6144]{1,0:T(8,128)(2,1)} async-done(((bf16[256,6144]{1,0:T(8,128)(2,1)}), bf16[2048,6144]{1,0:T(8,128)(2,1)}) %all-gather.7.cloned.1.call-update) | async-done | bytes 25165840 | tf_op jit(solution)/shard_map/all_gather | solution.py:747
  151.1 1.9 copy-done.2
  153.0 5.4 shard_map.241.rest_ref
  163.5 103.1 %all-gather.9.cloned.1.call-done.near_ref.q_ref.k_ref.v_ref = bf16[512,6144]{1,0:T(8,128)(2,1)} async-done(((bf16[128,6144]{1,0:T(8,128)(2,1)}), bf16[512,6144]{1,0:T(8,128)(2,1)}) %all-gather.9.cloned.1.call-update) | async-done | bytes 6291472 | tf_op jit(solution)/shard_map/all_gather | solution.py:733
  266.6 16.7 %shard_map.242 = (bf16[512,512]{1,0:T(8,128)(2,1)}, bf16[512,512]{1,0:T(8,128)(2,1)}, bf16[512,512]{1,0:T(8,128)(2,1)}, bf16[512,512]{1,0:T(8,128)(2,1)}, f32[4,...) custom-call(s32[512,2]{1,0:T(8,128)} %copy.46.rows_ref, s32[2,512]{1,0:T(2,128)} %get-tuple-element.151.cols_ref, ...), custom_call_target="tpu_custom_call" | custom-call | tf_op jit(solution)/shard_map/pallas_call | solution.py:559
  283.4 42.2 %reduce-scatter.9.cloned.1.call-done.value_ref.refs_1_ = bf16[128,2048]{1,0:T(8,128)(2,1)} async-done(((bf16[512,2048]{1,0:T(8,128)(2,1)}), bf16[128,2048]{1,0:T(8,128)(2,1)}) %reduce-scatter.9.cloned.1.call-update) | async-done | bytes 524304 | tf_op jit(solution)/shard_map/reduce_scatter | solution.py:736
  326.6 1.7 shard_map.243
  328.4 45.4 %all-gather.11.cloned.1.call-done.rows_ref.mlp_ref = bf16[512,2048]{1,0:T(8,128)(2,1)} async-done(((bf16[128,2048]{1,0:T(8,128)(2,1)}), bf16[512,2048]{1,0:T(8,128)(2,1)}) %all-gather.11.cloned.1.call-update) | async-done | bytes 2097168 | tf_op jit(solution)/shard_map/all_gather | solution.py:733
  373.8 17.1 %shard_map.244 = (bf16[512,2048]{1,0:T(8,128)(2,1)}, f32[512,2048]{1,0:T(8,128)}, bf16[512,2048]{1,0:T(8,128)(2,1)}) custom-call(bf16[512,2048]{1,0:T(8,128)(2,1)} %all-gather.11.cloned.1.call-done.rows_ref.mlp_ref, bf16[2048,6144]{1,0:T(8,128)(2,1)} %all-gather.7.cloned.1.call-done.refs_1_.wq_ref.wk_ref.wv_ref.wo_ref.up_ref.down_ref.full_ref, ...), custom_call_target="tpu_custom_call" | custom-call | tf_op jit(solution)/shard_map/pallas_call | solution.py:416
  391.9 41.8 %reduce-scatter.11.cloned.1.call-done = bf16[128,2048]{1,0:T(8,128)(2,1)} async-done(((bf16[512,2048]{1,0:T(8,128)(2,1)}), bf16[128,2048]{1,0:T(8,128)(2,1)}) %reduce-scatter.11.cloned.1.call-update) | async-done | bytes 524304 | tf_op jit(solution)/shard_map/reduce_scatter | solution.py:736
  433.7 1.4 multiply_reduce_fusion.2
  435.1 2.5 fusion.3
  437.6 1.5 multiply_reduce_fusion
  439.1 1.4 fusion.32
  440.6 45.4 %all-gather.13.cloned.1.call-done.rows_ref.branch_ref = bf16[512,2048]{1,0:T(8,128)(2,1)} async-done(((bf16[128,2048]{1,0:T(8,128)(2,1)}), bf16[512,2048]{1,0:T(8,128)(2,1)}) %all-gather.13.cloned.1.call-update) | async-done | bytes 2097168 | tf_op jit(solution)/shard_map/all_gather | solution.py:733
  485.9 16.5 %shard_map.245 = (bf16[512,2048]{1,0:T(8,128)(2,1)}, bf16[512,2048]{1,0:T(8,128)(2,1)}) custom-call(bf16[512,2048]{1,0:T(8,128)(2,1)} %all-gather.13.cloned.1.call-done.rows_ref.branch_ref, bf16[2048,6144]{1,0:T(8,128)(2,1)} %all-gather.7.cloned.1.call-done.refs_1_.wq_ref.wk_ref.wv_ref.wo_ref.up_ref.down_ref.full_ref, ...), custom_call_target="tpu_custom_call" | custom-call | tf_op jit(solution)/shard_map/pallas_call | solution.py:463
  502.5 1.9 fusion.1
  505.5 15.5 %shard_map.247.refs_4_ = bf16[2048,4224]{1,0:T(8,128)(2,1)} custom-call(bf16[512,2048]{1,0:T(8,128)(2,1)} %all-gather.11.cloned.1.call-done.rows_ref.mlp_ref, bf16[512,2048]{1,0:T(8,128)(2,1)} %shard_map.246.up_ref, bf16[512,2048]{1,0:T(8,128)(2,1)} %all-gather.13.cloned.1.call-done.rows_ref.branch_ref, bf16[512,2048]{1,0:T(8,128)(2,1)} %get-tuple-element.58.active_ref, ...), custom_call_target="tpu_custom_call" | custom-call | tf_op jit(solution)/shard_map/pallas_call | solution.py:327
  521.0 24.2 %reduce-scatter.13.cloned.1.call-done.refs_2_ = bf16[128,2048]{1,0:T(8,128)(2,1)} async-done(((bf16[512,2048]{1,0:T(8,128)(2,1)}), bf16[128,2048]{1,0:T(8,128)(2,1)}) %reduce-scatter.13.cloned.1.call-update) | async-done | bytes 524304 | tf_op jit(solution)/shard_map/reduce_scatter | solution.py:736
  546.2 2.3 shard_map.248
  550.1 43.8 %all-gather.15.cloned.1.call-done.hidden_ref.refs_5_ = bf16[512,2048]{1,0:T(8,128)(2,1)} async-done(((bf16[128,2048]{1,0:T(8,128)(2,1)}), bf16[512,2048]{1,0:T(8,128)(2,1)}) %all-gather.15.cloned.1.call-update) | async-done | bytes 2097168 | tf_op jit(solution)/shard_map/all_gather | solution.py:733
  593.9 10.1 %shard_map.249 = (bf16[512,512]{1,0:T(8,128)(2,1)}, bf16[512,512]{1,0:T(8,128)(2,1)}, bf16[512,512]{1,0:T(8,128)(2,1)}) custom-call(s32[512,2]{1,0:T(8,128)} %copy.46.rows_ref, s32[2,512]{1,0:T(2,128)} %get-tuple-element.151.cols_ref, f32[512,128]{1,0:T(8,128)} %get-tuple-element.157.cos_ref, f32[512,128]{1,0:T(8,128)} %get-tuple-element.158.sin_ref, ...), custom_call_target="tpu_custom_call" | custom-call | tf_op jit(solution)/shard_map/pallas_call | solution.py:605
  604.0 10.7 %shard_map.250 = (bf16[512,2048]{1,0:T(8,128)(2,1)}, bf16[128,2048]{1,0:T(8,128)(2,1)}, bf16[128,2048]{1,0:T(8,128)(2,1)}, bf16[512,2048]{1,0:T(8,128)(2,1)}, bf...) custom-call(s32[4]{0:T(128)} %pad_add_fusion.1.where_ref, ...), custom_call_target="tpu_custom_call" | custom-call | tf_op jit(solution)/shard_map/pallas_call | solution.py:638
  615.5 2.0 collective-permute-start
  618.2 1.3 collective-permute-start.6
  620.3 1.3 collective-permute-start.12
  621.6 8.6 collective-permute-done
  630.2 1.4 slice_add_fusion.4
  632.4 4.9 collective-permute-start.1
  637.3 4.1 collective-permute-done.6
  642.4 7.8 collective-permute-start.7
  650.3 2.4 collective-permute-done.12
  653.7 8.0 collective-permute-start.13
  661.8 1.9 collective-permute-done.1
  665.2 8.5 collective-permute-start.2
  676.4 8.3 collective-permute-start.8
  684.9 1.4 collective-permute-done.13
  687.7 8.1 collective-permute-start.14
  695.8 1.7 collective-permute-done.2.refs_3_
  697.5 1.5 shard_map.251
  699.0 9.7 %collective-permute-done.8.refs_3_ = bf16[128,2048]{1,0:T(8,128)(2,1)S(1)} collective-permute-done((bf16[128,2048]{1,0:T(8,128)(2,1)S(1)}, bf16[128,2048]{1,0:T(8,128)(2,1)S(1)}, u32[]{:S(2)}, u32[]{:S(2)}) %collective-permute-start.8) | collective-permute-done | bytes 524320 | tf_op jit(solution)/shard_map/ppermute | solution.py:85
  708.7 1.5 shard_map.252
  710.2 8.3 collective-permute-done.14.refs_3_
  718.5 1.5 shard_map.253
  721.7 12.0 %shard_map.255.refs_9_ = bf16[2048,2048]{1,0:T(8,128)(2,1)} custom-call(bf16[512,6144]{1,0:T(8,128)(2,1)} %all-gather.9.cloned.1.call-done.near_ref.q_ref.k_ref.v_ref, bf16[512,6144]{1,0:T(8,128)(2,1)} %all-gather.9.cloned.1.call-done.near_ref.q_ref.k_ref.v_ref, bf16[512,6144]{1,0:T(8,128)(2,1)} %all-gather.9.cloned.1.call-done.near_ref.q_ref.k_ref.v_ref, ...), custom_call_target="tpu_custom_call" | custom-call | tf_op jit(solution)/shard_map/pallas_call | solution.py:350
  734.2 2.5 collective-permute-start.20
  736.8 9.3 %collective-permute-done.20 = f32[8,2048]{1,0:T(8,128)S(1)} collective-permute-done((f32[8,2048]{1,0:T(8,128)S(1)}, f32[8,2048]{1,0:T(8,128)S(1)}, u32[]{:S(2)}, u32[]{:S(2)}) %collective-permute-start.20) | collective-permute-done | bytes 65568 | tf_op jit(solution)/shard_map/ppermute | solution.py:51
  746.2 7.1 collective-permute-done.21
  753.4 4.0 shard_map.254
  758.5 1.5 collective-permute-start.23
  760.0 4.5 collective-permute-done.23
  764.5 1.5 collective-permute-start.24
  766.0 10.5 %collective-permute-done.18 = f32[72,256]{0,1:T(8,128)S(1)} collective-permute-done((f32[72,256]{0,1:T(8,128)S(1)}, f32[72,256]{0,1:T(8,128)S(1)}, u32[]{:S(2)}, u32[]{:S(2)}) %collective-permute-start.18) | collective-permute-done | bytes 73760 | tf_op jit(solution)/shard_map/ppermute | solution.py:51
  779.0 13.8 %collective-permute-done.19 = f32[72,256]{0,1:T(8,128)S(1)} collective-permute-done((f32[72,256]{0,1:T(8,128)S(1)}, f32[72,256]{0,1:T(8,128)S(1)}, u32[]{:S(2)}, u32[]{:S(2)}) %collective-permute-start.19) | collective-permute-done | bytes 73760 | tf_op jit(solution)/shard_map/ppermute | solution.py:51
  792.8 16.5 %all_gather.27 = f32[72,2048]{0,1:T(8,128)S(1)} all-gather(f32[72,256]{0,1:T(8,128)S(1)} %add.129), channel_id=1, replica_groups=mesh['dp'=8,'layer'=4] {'dp'}, dimensions={1}, use_global_device_ids=true | all-gather | bytes 663552 | tf_op jit(solution)/shard_map/all_gather | solution.py:815
  810.4 2.4 copy.52
  812.8 33.0 %all-gather.17.cloned.1.call-done.refs_2_.refs_3_.refs_4_ = bf16[512,6144]{1,0:T(8,128)(2,1)} async-done(((bf16[128,6144]{1,0:T(8,128)(2,1)}), bf16[512,6144]{1,0:T(8,128)(2,1)}) %all-gather.17.cloned.1.call-update) | async-done | bytes 6291472 | tf_op jit(solution)/shard_map/all_gather | solution.py:733
  845.8 14.0 %shard_map.256 = (bf16[4,512,2048]{2,1,0:T(8,128)(2,1)}, f32[512,16]{1,0:T(8,128)S(1)}) custom-call(f32[512,16]{1,0:T(8,128)S(1)} %bitcast.22, bf16[4,512,2048]{2,1,0:T(8,128)(2,1)} %refs_1_.7, bf16[512,6144]{1,0:T(8,128)(2,1)} %all-gather.17.cloned.1.call-done.refs_2_.refs_3_.refs_4_, ...), custom_call_target="tpu_custom_call" | custom-call | tf_op jit(solution)/shard_map/pallas_call | solution.py:286
  860.5 2.6 shard_map.257
  (161 shorter events, 32.4 us)
Async XLA Ops:
  8.0 427.1 %copy-start = (f32[2048,68]{0,1:T(8,128)S(1)}, f32[2048,68]{0,1:T(8,128)}, u32[]{:S(2)}) copy-start(f32[2048,68]{0,1:T(8,128)} %param.24) | copy-start | bytes 1671172
  8.0 123.5 %reduce-scatter.7.cloned.1.call-start = ((), (), s32[]{:S(2)}) async-start(), calls=%async_computation.6 | async-start | bytes 7864320 | tf_op jit(solution)/shard_map/reduce_scatter | solution.py:736
  17.9 133.1 %all-gather.7.cloned.1.call-start = ((), (), s32[]{:S(2)}) async-start(), calls=%async_computation.7 | async-start | bytes 28311552 | tf_op jit(solution)/shard_map/all_gather | solution.py:747
  23.1 243.5 %all-gather.9.cloned.1.call-start = ((), (), s32[]{:S(2)}) async-start(), calls=%async_computation.8 | async-start | bytes 7864320 | tf_op jit(solution)/shard_map/all_gather | solution.py:733
  131.5 1.6 copy-start.3
  136.2 1.1 copy-start.8
  151.1 174.5 %reduce-scatter.9.cloned.1.call-start = ((), (), s32[]{:S(2)}) async-start(), calls=%async_computation.9 | async-start | bytes 2621440 | tf_op jit(solution)/shard_map/reduce_scatter | solution.py:736
  151.1 1.9 copy-start.2
  153.0 6.8 copy-start.29
  158.4 1.3 copy-start.9
  283.3 90.4 %all-gather.11.cloned.1.call-start = ((), (), s32[]{:S(2)}) async-start(), calls=%async_computation.10 | async-start | bytes 2621440 | tf_op jit(solution)/shard_map/all_gather | solution.py:733
  325.6 1.0 copy-start.6
  328.4 105.4 %reduce-scatter.11.cloned.1.call-start = ((), (), s32[]{:S(2)}) async-start(), calls=%async_computation.11 | async-start | bytes 2621440 | tf_op jit(solution)/shard_map/reduce_scatter | solution.py:736
  390.9 42.8 %copy-start.7 = (bf16[128,2048]{1,0:T(8,128)(2,1)S(1)}, bf16[128,2048]{1,0:T(8,128)(2,1)}, u32[]{:S(2)}) copy-start(bf16[128,2048]{1,0:T(8,128)(2,1)} %reduce-scatter.9.cloned.1.call-done.value_ref.refs_1_) | copy-start | bytes 1572868
  390.9 95.0 %all-gather.13.cloned.1.call-start = ((), (), s32[]{:S(2)}) async-start(), calls=%async_computation.12 | async-start | bytes 2621440 | tf_op jit(solution)/shard_map/all_gather | solution.py:733
  433.7 3.9 copy-start.15
  435.1 4.0 copy-start.17
  440.5 104.7 %reduce-scatter.13.cloned.1.call-start = ((), (), s32[]{:S(2)}) async-start(), calls=%async_computation.13 | async-start | bytes 2621440 | tf_op jit(solution)/shard_map/reduce_scatter | solution.py:736
  502.4 91.5 %all-gather.15.cloned.1.call-start = ((), (), s32[]{:S(2)}) async-start(), calls=%async_computation.14 | async-start | bytes 2621440 | tf_op jit(solution)/shard_map/all_gather | solution.py:733
  545.2 1.0 copy-start.13
  548.5 173.2 %reduce-scatter.15.cloned.1.call-start = ((), (), s32[]{:S(2)}) async-start(), calls=%async_computation.16 | async-start | bytes 19464192 | tf_op jit(solution)/shard_map/reduce_scatter | solution.py:790
  549.1 296.7 %all-gather.17.cloned.1.call-start = ((), (), s32[]{:S(2)}) async-start(), calls=%async_computation.15 | async-start | bytes 7864320 | tf_op jit(solution)/shard_map/all_gather | solution.py:733
  614.7 26.7 %copy-start.19 = (bf16[512,2048]{1,0:T(8,128)(2,1)S(1)}, bf16[512,2048]{1,0:T(8,128)(2,1)}, u32[]{:S(2)}) copy-start(bf16[512,2048]{1,0:T(8,128)(2,1)} %get-tuple-element.71) | copy-start | bytes 6291460
  614.7 5.6 collective-permute-start.3
  615.5 14.6 %collective-permute-start = (bf16[128,2048]{1,0:T(8,128)(2,1)}, bf16[128,2048]{1,0:T(8,128)(2,1)S(1)}, u32[]{:S(2)}, u32[]{:S(2)}) collective-permute-start(bf16[128,2048]{1,0:T(8,128)(2,1)} %get-tuple-element.69), channel_id=1, source_target_pairs={{0,1},{4,5},{8,9},{12,13},{16,17},{20,21},{24,25},{28,29}} | collective-permute-start | bytes 1572872 | tf_op jit(solution)/shard_map/ppermute | solution.py:85
  617.5 14.8 %collective-permute-start.9 = (bf16[128,2048]{1,0:T(8,128)(2,1)}, bf16[128,2048]{1,0:T(8,128)(2,1)S(1)}, u32[]{:S(2)}, u32[]{:S(2)}) collective-permute-start(bf16[128,2048]{1,0:T(8,128)(2,1)} %get-tuple-element.72), channel_id=1, source_target_pairs={{3,2},{7,6},{11,10},{15,14},{19,18},{23,22},{27,26},{31,30}} | collective-permute-start | bytes 1572872 | tf_op jit(solution)/shard_map/ppermute | solution.py:86
  618.2 23.2 %collective-permute-start.6 = (bf16[128,2048]{1,0:T(8,128)(2,1)}, bf16[128,2048]{1,0:T(8,128)(2,1)S(1)}, u32[]{:S(2)}, u32[]{:S(2)}) collective-permute-start(bf16[128,2048]{1,0:T(8,128)(2,1)} %get-tuple-element.73), channel_id=1, source_target_pairs={{0,1},{4,5},{8,9},{12,13},{16,17},{20,21},{24,25},{28,29}} | collective-permute-start | bytes 1572872 | tf_op jit(solution)/shard_map/ppermute | solution.py:85
  619.6 22.8 %collective-permute-start.15 = (bf16[128,2048]{1,0:T(8,128)(2,1)}, bf16[128,2048]{1,0:T(8,128)(2,1)S(1)}, u32[]{:S(2)}, u32[]{:S(2)}) collective-permute-start(bf16[128,2048]{1,0:T(8,128)(2,1)} %get-tuple-element.76), channel_id=1, source_target_pairs={{3,2},{7,6},{11,10},{15,14},{19,18},{23,22},{27,26},{31,30}} | collective-permute-start | bytes 1572872 | tf_op jit(solution)/shard_map/ppermute | solution.py:86
  620.3 32.4 %collective-permute-start.12 = (bf16[128,2048]{1,0:T(8,128)(2,1)}, bf16[128,2048]{1,0:T(8,128)(2,1)S(1)}, u32[]{:S(2)}, u32[]{:S(2)}) collective-permute-start(bf16[128,2048]{1,0:T(8,128)(2,1)} %get-tuple-element.77), channel_id=1, source_target_pairs={{0,1},{4,5},{8,9},{12,13},{16,17},{20,21},{24,25},{28,29}} | collective-permute-start | bytes 1572872 | tf_op jit(solution)/shard_map/ppermute | solution.py:85
  631.5 21.1 %copy-start.18 = (bf16[512,2048]{1,0:T(8,128)(2,1)S(1)}, bf16[512,2048]{1,0:T(8,128)(2,1)}, u32[]{:S(2)}) copy-start(bf16[512,2048]{1,0:T(8,128)(2,1)} %get-tuple-element.75) | copy-start | bytes 6291460
  631.5 22.1 %collective-permute-start.4 = (bf16[128,2048]{1,0:T(8,128)(2,1)S(1)}, bf16[128,2048]{1,0:T(8,128)(2,1)S(1)}, u32[]{:S(2)}, u32[]{:S(2)}) collective-permute-start(bf16[128,2048]{1,0:T(8,128)(2,1)S(1)} %get-tuple-element.136), channel_id=1, source_target_pairs={{2,1},{3,2},{6,5},{7,6},{10,9},{11,10},{14,13},{15,14},{18,17},{19... | collective-permute-start | bytes 1572872 | tf_op jit(solution)/shard_map/ppermute | solution.py:86
  632.4 31.4 %collective-permute-start.1 = (bf16[128,2048]{1,0:T(8,128)(2,1)S(1)}, bf16[128,2048]{1,0:T(8,128)(2,1)S(1)}, u32[]{:S(2)}, u32[]{:S(2)}) collective-permute-start(bf16[128,2048]{1,0:T(8,128)(2,1)S(1)} %get-tuple-element.137), channel_id=1, source_target_pairs={{0,1},{1,2},{4,5},{5,6},{8,9},{9,10},{12,13},{13,14},{16,17},{17,1... | collective-permute-start | bytes 1572872 | tf_op jit(solution)/shard_map/ppermute | solution.py:85
  641.5 20.1 %copy-start.25 = (bf16[128,2048]{1,0:T(8,128)(2,1)S(1)}, bf16[128,2048]{1,0:T(8,128)(2,1)}, u32[]{:S(2)}) copy-start(bf16[128,2048]{1,0:T(8,128)(2,1)} %get-tuple-element.69) | copy-start | bytes 1572868
  641.6 23.7 %collective-permute-start.10 = (bf16[128,2048]{1,0:T(8,128)(2,1)S(1)}, bf16[128,2048]{1,0:T(8,128)(2,1)S(1)}, u32[]{:S(2)}, u32[]{:S(2)}) collective-permute-start(bf16[128,2048]{1,0:T(8,128)(2,1)S(1)} %get-tuple-element.139), channel_id=1, source_target_pairs={{2,1},{3,2},{6,5},{7,6},{10,9},{11,10},{14,13},{15,14},{18,17},{19... | collective-permute-start | bytes 1572872 | tf_op jit(solution)/shard_map/ppermute | solution.py:86
  642.4 32.6 %collective-permute-start.7 = (bf16[128,2048]{1,0:T(8,128)(2,1)S(1)}, bf16[128,2048]{1,0:T(8,128)(2,1)S(1)}, u32[]{:S(2)}, u32[]{:S(2)}) collective-permute-start(bf16[128,2048]{1,0:T(8,128)(2,1)S(1)} %get-tuple-element.140), channel_id=1, source_target_pairs={{0,1},{1,2},{4,5},{5,6},{8,9},{9,10},{12,13},{13,14},{16,17},{17,1... | collective-permute-start | bytes 1572872 | tf_op jit(solution)/shard_map/ppermute | solution.py:85
  652.6 12.4 %copy-start.24 = (bf16[128,2048]{1,0:T(8,128)(2,1)S(1)}, bf16[128,2048]{1,0:T(8,128)(2,1)}, u32[]{:S(2)}) copy-start(bf16[128,2048]{1,0:T(8,128)(2,1)} %get-tuple-element.68) | copy-start | bytes 1572868
  652.8 20.9 %copy-start.23 = (bf16[128,2048]{1,0:T(8,128)(2,1)S(1)}, bf16[128,2048]{1,0:T(8,128)(2,1)}, u32[]{:S(2)}) copy-start(bf16[128,2048]{1,0:T(8,128)(2,1)} %get-tuple-element.73) | copy-start | bytes 1572868
  652.8 23.6 %collective-permute-start.16 = (bf16[128,2048]{1,0:T(8,128)(2,1)S(1)}, bf16[128,2048]{1,0:T(8,128)(2,1)S(1)}, u32[]{:S(2)}, u32[]{:S(2)}) collective-permute-start(bf16[128,2048]{1,0:T(8,128)(2,1)S(1)} %get-tuple-element.142), channel_id=1, source_target_pairs={{2,1},{3,2},{6,5},{7,6},{10,9},{11,10},{14,13},{15,14},{18,17},{19... | collective-permute-start | bytes 1572872 | tf_op jit(solution)/shard_map/ppermute | solution.py:86
  653.7 22.6 %copy-start.22 = (bf16[128,2048]{1,0:T(8,128)(2,1)S(1)}, bf16[128,2048]{1,0:T(8,128)(2,1)}, u32[]{:S(2)}) copy-start(bf16[128,2048]{1,0:T(8,128)(2,1)} %get-tuple-element.72) | copy-start | bytes 1572868
  653.7 32.5 %collective-permute-start.13 = (bf16[128,2048]{1,0:T(8,128)(2,1)S(1)}, bf16[128,2048]{1,0:T(8,128)(2,1)S(1)}, u32[]{:S(2)}, u32[]{:S(2)}) collective-permute-start(bf16[128,2048]{1,0:T(8,128)(2,1)S(1)} %get-tuple-element.143), channel_id=1, source_target_pairs={{0,1},{1,2},{4,5},{5,6},{8,9},{9,10},{12,13},{13,14},{16,17},{17,1... | collective-permute-start | bytes 1572872 | tf_op jit(solution)/shard_map/ppermute | solution.py:85
  661.8 22.9 %copy-start.21 = (bf16[128,2048]{1,0:T(8,128)(2,1)S(1)}, bf16[128,2048]{1,0:T(8,128)(2,1)}, u32[]{:S(2)}) copy-start(bf16[128,2048]{1,0:T(8,128)(2,1)} %get-tuple-element.77) | copy-start | bytes 1572868
  663.8 23.9 %collective-permute-start.5 = (bf16[128,2048]{1,0:T(8,128)(2,1)S(1)}, bf16[128,2048]{1,0:T(8,128)(2,1)S(1)}, u32[]{:S(2)}, u32[]{:S(2)}) collective-permute-start(bf16[128,2048]{1,0:T(8,128)(2,1)S(1)} %add.119), channel_id=1, source_target_pairs={{1,0},{2,1},{3,2},{5,4},{6,5},{7,6},{9,8},{10,9},{11,10},{13,12},{... | collective-permute-start | bytes 1572872 | tf_op jit(solution)/shard_map/ppermute | solution.py:86
  665.2 22.3 %copy-start.20 = (bf16[128,2048]{1,0:T(8,128)(2,1)S(1)}, bf16[128,2048]{1,0:T(8,128)(2,1)}, u32[]{:S(2)}) copy-start(bf16[128,2048]{1,0:T(8,128)(2,1)} %get-tuple-element.76) | copy-start | bytes 1572868
  665.2 32.3 %collective-permute-start.2 = (bf16[128,2048]{1,0:T(8,128)(2,1)S(1)}, bf16[128,2048]{1,0:T(8,128)(2,1)S(1)}, u32[]{:S(2)}, u32[]{:S(2)}) collective-permute-start(bf16[128,2048]{1,0:T(8,128)(2,1)S(1)} %add.117), channel_id=1, source_target_pairs={{0,1},{1,2},{2,3},{4,5},{5,6},{6,7},{8,9},{9,10},{10,11},{12,13},{... | collective-permute-start | bytes 1572872 | tf_op jit(solution)/shard_map/ppermute | solution.py:85
  673.9 23.6 %copy-start.4 = (bf16[128,6144]{1,0:T(8,128)(2,1)S(1)}, bf16[128,6144]{1,0:T(8,128)(2,1)}, u32[]{:S(2)}) copy-start(bf16[128,6144]{1,0:T(8,128)(2,1)} %reduce-scatter.7.cloned.1.call-done.value_ref.refs_1_) | copy-start | bytes 4718596
  675.0 24.0 %collective-permute-start.11 = (bf16[128,2048]{1,0:T(8,128)(2,1)S(1)}, bf16[128,2048]{1,0:T(8,128)(2,1)S(1)}, u32[]{:S(2)}, u32[]{:S(2)}) collective-permute-start(bf16[128,2048]{1,0:T(8,128)(2,1)S(1)} %add.123), channel_id=1, source_target_pairs={{1,0},{2,1},{3,2},{5,4},{6,5},{7,6},{9,8},{10,9},{11,10},{13,12},{... | collective-permute-start | bytes 1572872 | tf_op jit(solution)/shard_map/ppermute | solution.py:86
  676.4 32.3 %collective-permute-start.8 = (bf16[128,2048]{1,0:T(8,128)(2,1)S(1)}, bf16[128,2048]{1,0:T(8,128)(2,1)S(1)}, u32[]{:S(2)}, u32[]{:S(2)}) collective-permute-start(bf16[128,2048]{1,0:T(8,128)(2,1)S(1)} %add.121), channel_id=1, source_target_pairs={{0,1},{1,2},{2,3},{4,5},{5,6},{6,7},{8,9},{9,10},{10,11},{12,13},{... | collective-permute-start | bytes 1572872 | tf_op jit(solution)/shard_map/ppermute | solution.py:85
  686.2 24.0 %collective-permute-start.17 = (bf16[128,2048]{1,0:T(8,128)(2,1)S(1)}, bf16[128,2048]{1,0:T(8,128)(2,1)S(1)}, u32[]{:S(2)}, u32[]{:S(2)}) collective-permute-start(bf16[128,2048]{1,0:T(8,128)(2,1)S(1)} %add.127), channel_id=1, source_target_pairs={{1,0},{2,1},{3,2},{5,4},{6,5},{7,6},{9,8},{10,9},{11,10},{13,12},{... | collective-permute-start | bytes 1572872 | tf_op jit(solution)/shard_map/ppermute | solution.py:86
  687.7 30.8 %collective-permute-start.14 = (bf16[128,2048]{1,0:T(8,128)(2,1)S(1)}, bf16[128,2048]{1,0:T(8,128)(2,1)S(1)}, u32[]{:S(2)}, u32[]{:S(2)}) collective-permute-start(bf16[128,2048]{1,0:T(8,128)(2,1)S(1)} %add.125), channel_id=1, source_target_pairs={{0,1},{1,2},{2,3},{4,5},{5,6},{6,7},{8,9},{9,10},{10,11},{12,13},{... | collective-permute-start | bytes 1572872 | tf_op jit(solution)/shard_map/ppermute | solution.py:85
  699.0 21.1 %copy-start.10 = (bf16[128,2048]{1,0:T(8,128)(2,1)}, bf16[128,2048]{1,0:T(8,128)(2,1)S(1)}, u32[]{:S(2)}) copy-start(bf16[128,2048]{1,0:T(8,128)(2,1)S(1)} %get-tuple-element.70.refs_0_) | copy-start | bytes 1572868
  710.2 11.1 %copy-start.11 = (bf16[128,2048]{1,0:T(8,128)(2,1)}, bf16[128,2048]{1,0:T(8,128)(2,1)S(1)}, u32[]{:S(2)}) copy-start(bf16[128,2048]{1,0:T(8,128)(2,1)S(1)} %get-tuple-element.74.refs_1_) | copy-start | bytes 1572868
  720.0 1.3 copy-start.12
  721.4 139.2 %reduce-scatter.17.cloned.1.call-start = ((), (), s32[]{:S(2)}) async-start(), calls=%async_computation.17 | async-start | bytes 9437184 | tf_op jit(solution)/shard_map/reduce_scatter | solution.py:813
  734.2 11.8 %collective-permute-start.20 = (f32[8,2048]{1,0:T(8,128)S(1)}, f32[8,2048]{1,0:T(8,128)S(1)}, u32[]{:S(2)}, u32[]{:S(2)}) collective-permute-start(f32[8,2048]{1,0:T(8,128)S(1)} %concatenate.15), channel_id=1, source_target_pairs={{0,1},{1,0},{2,3},{3,2},{4,5},{5,4},{6,7},{7,6},{8,9},{9,8},{10,11... | collective-permute-start | bytes 196616 | tf_op jit(solution)/shard_map/ppermute | solution.py:51
  746.1 7.2 collective-permute-start.21
  753.3 5.2 collective-permute-start.22
  758.4 18.1 %collective-permute-start.18 = (f32[72,256]{0,1:T(8,128)S(1)}, f32[72,256]{0,1:T(8,128)S(1)}, u32[]{:S(2)}, u32[]{:S(2)}) collective-permute-start(f32[72,256]{0,1:T(8,128)S(1)} %copy.50), channel_id=1, source_target_pairs={{0,1},{1,0},{2,3},{3,2},{4,5},{5,4},{6,7},{7,6},{8,9},{9,8},{10,11... | collective-permute-start | bytes 221192 | tf_op jit(solution)/shard_map/ppermute | solution.py:51
  758.5 6.0 collective-permute-start.23
  764.5 13.0 %collective-permute-start.24 = (f32[8,2048]{1,0:T(8,128)S(1)}, f32[8,2048]{1,0:T(8,128)S(1)}, u32[]{:S(2)}, u32[]{:S(2)}) collective-permute-start(f32[8,2048]{1,0:T(8,128)S(1)} %add.133), channel_id=1, source_target_pairs={{0,16},{4,20},{8,24},{12,28},{16,0},{20,4},{24,8},{28,12},{1,17},{... | collective-permute-start | bytes 196616 | tf_op jit(solution)/shard_map/ppermute | solution.py:51
  776.5 16.3 %collective-permute-start.19 = (f32[72,256]{0,1:T(8,128)S(1)}, f32[72,256]{0,1:T(8,128)S(1)}, u32[]{:S(2)}, u32[]{:S(2)}) collective-permute-start(f32[72,256]{0,1:T(8,128)S(1)} %add.128), channel_id=1, source_target_pairs={{0,2},{1,3},{2,0},{3,1},{4,6},{5,7},{6,4},{7,5},{8,10},{9,11},{10,... | collective-permute-start | bytes 221192 | tf_op jit(solution)/shard_map/ppermute | solution.py:51
  777.5 68.3 %copy-start.14 = (f32[8,2048]{1,0:T(8,128)}, f32[8,2048]{1,0:T(8,128)S(1)}, u32[]{:S(2)}) copy-start(f32[8,2048]{1,0:T(8,128)S(1)} %add.134.refs_8_) | copy-start | bytes 196612
  809.3 36.5 %copy-start.5 = (bf16[512,2048]{1,0:T(8,128)(2,1)S(1)}, bf16[512,2048]{1,0:T(8,128)(2,1)}, u32[]{:S(2)}) copy-start(bf16[512,2048]{1,0:T(8,128)(2,1)} %all-gather.15.cloned.1.call-done.hidden_ref.refs_5_) | copy-start | bytes 6291460
  809.4 1.0 copy-start.16
  845.8 17.4 %copy-start.1 = (f32[2048,68]{0,1:T(8,128)S(1)}, f32[2048,68]{0,1:T(8,128)}, u32[]{:S(2)}) copy-start(f32[2048,68]{0,1:T(8,128)} %param.24) | copy-start | bytes 1671172
  (3 other events, 2.4 us)
Sparse Core Ops, SparseCore 0:
  18.1 113.4 reduce-scatter.6
  151.2 115.3 all-gather.8
  283.4 42.1 reduce-scatter.8
  328.5 45.2 all-gather.10
  391.1 42.6 reduce-scatter.10
  440.6 45.2 all-gather.12
  502.6 42.5 reduce-scatter.12
  548.6 45.2 all-gather.14
  721.5 124.2 all-gather.16
Sparse Core Ops, SparseCore 1:
  23.2 127.8 all-gather.6
  553.1 117.7 reduce-scatter.14
  733.8 77.2 reduce-scatter.16

commit v7 on v6

--- a/solution.py
+++ b/solution.py
@@ -375,10 +375,18 @@
             refs[-1][:, at : at + size] = value.astype(bf16)
             at += size
 
-    return pl.pallas_call(
-        kernel,
-        in_specs=[pl.BlockSpec(memory_space=pltpu.VMEM)] * number
+    block = min(128, heights[0])
+    return pl.pallas_call(
+        kernel,
+        grid=(heights[0] // block,),
+        in_specs=[
+            pl.BlockSpec((size, block), lambda i: (0, i))
+            if t
+            else pl.BlockSpec((block, size), lambda i: (i, 0))
+            for t, size in zip(turned, widths)
+        ]
         + [pl.BlockSpec(memory_space=pl.ANY)] * len(order),
+        out_specs=pl.BlockSpec((block, sum(widths)), lambda i: (i, 0)),
         out_shape=jax.ShapeDtypeStruct((heights[0], sum(widths)), bf16),
         compiler_params=vmem(56),
     )(*weights, *order)

time: 872 us -> 871 us (level)
  no operation moved by 1% of the time
where the time goes in v7:
time: 871 us; the launch traced here: 870 us
  waiting for transfers between devices  585 us (67%)
  Pallas kernels  149 us (17%)
  starting transfers between devices  65.9 us (8%)
  local copies, waits for them, and re-layouts  19 us (2%)
  blocking collectives  16.5 us (2%)
  between operations  16.4 us (2%)
  other arithmetic  10.1 us (1%)
    all_gather x5, waiting for transfers between devices, collect(): return lax.all_gather(rows, 'layer', axis=0, tiled=True)  271 us
    reduce_scatter x4, waiting for transfers between devices, spread(): return lax.psum_scatter(rows, 'layer', scatter_dimension=0, tiled=True)  217 us
    ppermute x9, starting transfers between devices, sum_hop(): lax.ppermute(up, 'layer', [(i, i + 1) for i in range(k)])  50.3 us
    ppermute x7, waiting for transfers between devices, doubling_sum(): lax.ppermute(value, axis, [(i, i ^ step) for i in range(size)])  45.2 us
    ppermute x9, waiting for transfers between devices, sum_hop(): lax.ppermute(up, 'layer', [(i, i + 1) for i in range(k)])  39.1 us
  transfers between devices with their start and end apart: 37, of which 24 were waited for; matrix products, arithmetic and copies ran while one was open for 2% of the time, Pallas kernels for 10%

profile of v7, /device:TPU:0, one launch (start us, length us, event | category | flops | bytes accessed | tf_op | source)
XLA Modules:
  0.0 869.7 jit_solution(7397234394163295016)
XLA Ops:
  9.0 8.9 %shard_map.237.refs_6_.refs_2_ = bf16[512,6144]{1,0:T(8,128)(2,1)} custom-call(f32[512,16]{1,0:T(8,128)S(1)} %bitcast.20, bf16[4,512,2048]{2,1,0:T(8,128)(2,1)} %refs_1_.7), custom_call_target="tpu_custom_call" | custom-call | tf_op jit(solution)/shard_map/pallas_call | solution.py:126
  18.0 4.3 shard_map.239.refs_3_
  23.1 108.4 %reduce-scatter.7.cloned.1.call-done.value_ref.refs_1_ = bf16[128,6144]{1,0:T(8,128)(2,1)} async-done(((bf16[512,6144]{1,0:T(8,128)(2,1)}), bf16[128,6144]{1,0:T(8,128)(2,1)}) %reduce-scatter.7.cloned.1.call-update) | async-done | bytes 1572880 | tf_op jit(solution)/shard_map/reduce_scatter | solution.py:744
  131.5 1.5 copy-done.3
  133.0 3.0 shard_map.238.refs_0_
  137.2 13.1 %all-gather.7.cloned.1.call-done.refs_1_.wq_ref.wk_ref.wv_ref.wo_ref.up_ref.down_ref.full_ref = bf16[2048,6144]{1,0:T(8,128)(2,1)} async-done(((bf16[256,6144]{1,0:T(8,128)(2,1)}), bf16[2048,6144]{1,0:T(8,128)(2,1)}) %all-gather.7.cloned.1.call-update) | async-done | bytes 25165840 | tf_op jit(solution)/shard_map/all_gather | solution.py:755
  150.3 1.9 copy-done.2
  152.2 5.4 shard_map.241.rest_ref
  162.7 103.1 %all-gather.9.cloned.1.call-done.near_ref.q_ref.k_ref.v_ref = bf16[512,6144]{1,0:T(8,128)(2,1)} async-done(((bf16[128,6144]{1,0:T(8,128)(2,1)}), bf16[512,6144]{1,0:T(8,128)(2,1)}) %all-gather.9.cloned.1.call-update) | async-done | bytes 6291472 | tf_op jit(solution)/shard_map/all_gather | solution.py:741
  265.8 16.7 %shard_map.242 = (bf16[512,512]{1,0:T(8,128)(2,1)}, bf16[512,512]{1,0:T(8,128)(2,1)}, bf16[512,512]{1,0:T(8,128)(2,1)}, bf16[512,512]{1,0:T(8,128)(2,1)}, f32[4,...) custom-call(s32[512,2]{1,0:T(8,128)} %copy.46.rows_ref, s32[2,512]{1,0:T(2,128)} %get-tuple-element.151.cols_ref, ...), custom_call_target="tpu_custom_call" | custom-call | tf_op jit(solution)/shard_map/pallas_call | solution.py:567
  282.6 42.2 %reduce-scatter.9.cloned.1.call-done.value_ref.refs_1_ = bf16[128,2048]{1,0:T(8,128)(2,1)} async-done(((bf16[512,2048]{1,0:T(8,128)(2,1)}), bf16[128,2048]{1,0:T(8,128)(2,1)}) %reduce-scatter.9.cloned.1.call-update) | async-done | bytes 524304 | tf_op jit(solution)/shard_map/reduce_scatter | solution.py:744
  325.9 1.7 shard_map.243
  327.6 45.4 %all-gather.11.cloned.1.call-done.rows_ref.mlp_ref = bf16[512,2048]{1,0:T(8,128)(2,1)} async-done(((bf16[128,2048]{1,0:T(8,128)(2,1)}), bf16[512,2048]{1,0:T(8,128)(2,1)}) %all-gather.11.cloned.1.call-update) | async-done | bytes 2097168 | tf_op jit(solution)/shard_map/all_gather | solution.py:741
  373.0 17.1 %shard_map.244 = (bf16[512,2048]{1,0:T(8,128)(2,1)}, f32[512,2048]{1,0:T(8,128)}, bf16[512,2048]{1,0:T(8,128)(2,1)}) custom-call(bf16[512,2048]{1,0:T(8,128)(2,1)} %all-gather.11.cloned.1.call-done.rows_ref.mlp_ref, bf16[2048,6144]{1,0:T(8,128)(2,1)} %all-gather.7.cloned.1.call-done.refs_1_.wq_ref.wk_ref.wv_ref.wo_ref.up_ref.down_ref.full_ref, ...), custom_call_target="tpu_custom_call" | custom-call | tf_op jit(solution)/shard_map/pallas_call | solution.py:424
  391.1 41.8 %reduce-scatter.11.cloned.1.call-done = bf16[128,2048]{1,0:T(8,128)(2,1)} async-done(((bf16[512,2048]{1,0:T(8,128)(2,1)}), bf16[128,2048]{1,0:T(8,128)(2,1)}) %reduce-scatter.11.cloned.1.call-update) | async-done | bytes 524304 | tf_op jit(solution)/shard_map/reduce_scatter | solution.py:744
  432.9 1.4 multiply_reduce_fusion.2
  434.3 2.5 fusion.3
  436.8 1.5 multiply_reduce_fusion
  438.3 1.4 fusion.32
  439.8 45.4 %all-gather.13.cloned.1.call-done.rows_ref.branch_ref = bf16[512,2048]{1,0:T(8,128)(2,1)} async-done(((bf16[128,2048]{1,0:T(8,128)(2,1)}), bf16[512,2048]{1,0:T(8,128)(2,1)}) %all-gather.13.cloned.1.call-update) | async-done | bytes 2097168 | tf_op jit(solution)/shard_map/all_gather | solution.py:741
  485.2 16.5 %shard_map.245 = (bf16[512,2048]{1,0:T(8,128)(2,1)}, bf16[512,2048]{1,0:T(8,128)(2,1)}) custom-call(bf16[512,2048]{1,0:T(8,128)(2,1)} %all-gather.13.cloned.1.call-done.rows_ref.branch_ref, bf16[2048,6144]{1,0:T(8,128)(2,1)} %all-gather.7.cloned.1.call-done.refs_1_.wq_ref.wk_ref.wv_ref.wo_ref.up_ref.down_ref.full_ref, ...), custom_call_target="tpu_custom_call" | custom-call | tf_op jit(solution)/shard_map/pallas_call | solution.py:471
  501.7 1.9 fusion.1
  504.7 15.5 %shard_map.247.refs_4_ = bf16[2048,4224]{1,0:T(8,128)(2,1)} custom-call(bf16[512,2048]{1,0:T(8,128)(2,1)} %all-gather.11.cloned.1.call-done.rows_ref.mlp_ref, bf16[512,2048]{1,0:T(8,128)(2,1)} %shard_map.246.up_ref, bf16[512,2048]{1,0:T(8,128)(2,1)} %all-gather.13.cloned.1.call-done.rows_ref.branch_ref, bf16[512,2048]{1,0:T(8,128)(2,1)} %get-tuple-element.58.active_ref, ...), custom_call_target="tpu_custom_call" | custom-call | tf_op jit(solution)/shard_map/pallas_call | solution.py:327
  520.2 24.2 %reduce-scatter.13.cloned.1.call-done.refs_2_ = bf16[128,2048]{1,0:T(8,128)(2,1)} async-done(((bf16[512,2048]{1,0:T(8,128)(2,1)}), bf16[128,2048]{1,0:T(8,128)(2,1)}) %reduce-scatter.13.cloned.1.call-update) | async-done | bytes 524304 | tf_op jit(solution)/shard_map/reduce_scatter | solution.py:744
  545.4 2.3 shard_map.248
  549.3 43.8 %all-gather.15.cloned.1.call-done.hidden_ref.refs_5_ = bf16[512,2048]{1,0:T(8,128)(2,1)} async-done(((bf16[128,2048]{1,0:T(8,128)(2,1)}), bf16[512,2048]{1,0:T(8,128)(2,1)}) %all-gather.15.cloned.1.call-update) | async-done | bytes 2097168 | tf_op jit(solution)/shard_map/all_gather | solution.py:741
  593.1 10.1 %shard_map.249 = (bf16[512,512]{1,0:T(8,128)(2,1)}, bf16[512,512]{1,0:T(8,128)(2,1)}, bf16[512,512]{1,0:T(8,128)(2,1)}) custom-call(s32[512,2]{1,0:T(8,128)} %copy.46.rows_ref, s32[2,512]{1,0:T(2,128)} %get-tuple-element.151.cols_ref, f32[512,128]{1,0:T(8,128)} %get-tuple-element.157.cos_ref, f32[512,128]{1,0:T(8,128)} %get-tuple-element.158.sin_ref, ...), custom_call_target="tpu_custom_call" | custom-call | tf_op jit(solution)/shard_map/pallas_call | solution.py:613
  603.2 10.7 %shard_map.250 = (bf16[512,2048]{1,0:T(8,128)(2,1)}, bf16[128,2048]{1,0:T(8,128)(2,1)}, bf16[128,2048]{1,0:T(8,128)(2,1)}, bf16[512,2048]{1,0:T(8,128)(2,1)}, bf...) custom-call(s32[4]{0:T(128)} %pad_add_fusion.1.where_ref, ...), custom_call_target="tpu_custom_call" | custom-call | tf_op jit(solution)/shard_map/pallas_call | solution.py:646
  614.7 2.0 collective-permute-start
  617.5 1.3 collective-permute-start.6
  619.5 1.3 collective-permute-start.12
  620.8 8.6 collective-permute-done
  629.4 1.4 slice_add_fusion.4
  631.6 4.9 collective-permute-start.1
  636.5 4.1 collective-permute-done.6
  641.6 7.8 collective-permute-start.7
  649.5 2.4 collective-permute-done.12
  652.9 8.0 collective-permute-start.13
  661.1 1.9 collective-permute-done.1
  664.4 8.5 collective-permute-start.2
  675.7 8.3 collective-permute-start.8
  684.1 1.4 collective-permute-done.13
  686.9 8.1 collective-permute-start.14
  695.0 1.7 collective-permute-done.2.refs_3_
  696.7 1.5 shard_map.251
  698.2 9.7 %collective-permute-done.8.refs_3_ = bf16[128,2048]{1,0:T(8,128)(2,1)S(1)} collective-permute-done((bf16[128,2048]{1,0:T(8,128)(2,1)S(1)}, bf16[128,2048]{1,0:T(8,128)(2,1)S(1)}, u32[]{:S(2)}, u32[]{:S(2)}) %collective-permute-start.8) | collective-permute-done | bytes 524320 | tf_op jit(solution)/shard_map/ppermute | solution.py:85
  707.9 1.5 shard_map.252
  709.4 8.3 collective-permute-done.14.refs_3_
  717.7 1.5 shard_map.253
  720.9 12.0 %shard_map.255.refs_9_ = bf16[2048,2048]{1,0:T(8,128)(2,1)} custom-call(bf16[512,6144]{1,0:T(8,128)(2,1)} %all-gather.9.cloned.1.call-done.near_ref.q_ref.k_ref.v_ref, bf16[512,6144]{1,0:T(8,128)(2,1)} %all-gather.9.cloned.1.call-done.near_ref.q_ref.k_ref.v_ref, bf16[512,6144]{1,0:T(8,128)(2,1)} %all-gather.9.cloned.1.call-done.near_ref.q_ref.k_ref.v_ref, ...), custom_call_target="tpu_custom_call" | custom-call | tf_op jit(solution)/shard_map/pallas_call | solution.py:350
  733.5 2.5 collective-permute-start.20
  736.0 9.3 %collective-permute-done.20 = f32[8,2048]{1,0:T(8,128)S(1)} collective-permute-done((f32[8,2048]{1,0:T(8,128)S(1)}, f32[8,2048]{1,0:T(8,128)S(1)}, u32[]{:S(2)}, u32[]{:S(2)}) %collective-permute-start.20) | collective-permute-done | bytes 65568 | tf_op jit(solution)/shard_map/ppermute | solution.py:51
  745.4 7.1 collective-permute-done.21
  752.6 4.0 shard_map.254
  757.7 1.5 collective-permute-start.23
  759.2 4.5 collective-permute-done.23
  763.7 1.5 collective-permute-start.24
  765.2 10.5 %collective-permute-done.18 = f32[72,256]{0,1:T(8,128)S(1)} collective-permute-done((f32[72,256]{0,1:T(8,128)S(1)}, f32[72,256]{0,1:T(8,128)S(1)}, u32[]{:S(2)}, u32[]{:S(2)}) %collective-permute-start.18) | collective-permute-done | bytes 73760 | tf_op jit(solution)/shard_map/ppermute | solution.py:51
  778.2 13.8 %collective-permute-done.19 = f32[72,256]{0,1:T(8,128)S(1)} collective-permute-done((f32[72,256]{0,1:T(8,128)S(1)}, f32[72,256]{0,1:T(8,128)S(1)}, u32[]{:S(2)}, u32[]{:S(2)}) %collective-permute-start.19) | collective-permute-done | bytes 73760 | tf_op jit(solution)/shard_map/ppermute | solution.py:51
  792.0 16.5 %all_gather.27 = f32[72,2048]{0,1:T(8,128)S(1)} all-gather(f32[72,256]{0,1:T(8,128)S(1)} %add.129), channel_id=1, replica_groups=mesh['dp'=8,'layer'=4] {'dp'}, dimensions={1}, use_global_device_ids=true | all-gather | bytes 663552 | tf_op jit(solution)/shard_map/all_gather | solution.py:823
  809.6 2.4 copy.52
  812.0 33.0 %all-gather.17.cloned.1.call-done.refs_2_.refs_3_.refs_4_ = bf16[512,6144]{1,0:T(8,128)(2,1)} async-done(((bf16[128,6144]{1,0:T(8,128)(2,1)}), bf16[512,6144]{1,0:T(8,128)(2,1)}) %all-gather.17.cloned.1.call-update) | async-done | bytes 6291472 | tf_op jit(solution)/shard_map/all_gather | solution.py:741
  845.0 14.0 %shard_map.256 = (bf16[4,512,2048]{2,1,0:T(8,128)(2,1)}, f32[512,16]{1,0:T(8,128)S(1)}) custom-call(f32[512,16]{1,0:T(8,128)S(1)} %bitcast.22, bf16[4,512,2048]{2,1,0:T(8,128)(2,1)} %refs_1_.7, bf16[512,6144]{1,0:T(8,128)(2,1)} %all-gather.17.cloned.1.call-done.refs_2_.refs_3_.refs_4_, ...), custom_call_target="tpu_custom_call" | custom-call | tf_op jit(solution)/shard_map/pallas_call | solution.py:286
  859.7 2.6 shard_map.257
  (161 shorter events, 32.4 us)
Async XLA Ops:
  8.0 426.3 %copy-start = (f32[2048,68]{0,1:T(8,128)S(1)}, f32[2048,68]{0,1:T(8,128)}, u32[]{:S(2)}) copy-start(f32[2048,68]{0,1:T(8,128)} %param.24) | copy-start | bytes 1671172
  8.0 123.5 %reduce-scatter.7.cloned.1.call-start = ((), (), s32[]{:S(2)}) async-start(), calls=%async_computation.6 | async-start | bytes 7864320 | tf_op jit(solution)/shard_map/reduce_scatter | solution.py:744
  17.9 132.3 %all-gather.7.cloned.1.call-start = ((), (), s32[]{:S(2)}) async-start(), calls=%async_computation.7 | async-start | bytes 28311552 | tf_op jit(solution)/shard_map/all_gather | solution.py:755
  22.3 243.5 %all-gather.9.cloned.1.call-start = ((), (), s32[]{:S(2)}) async-start(), calls=%async_computation.8 | async-start | bytes 7864320 | tf_op jit(solution)/shard_map/all_gather | solution.py:741
  131.5 1.5 copy-start.3
  136.0 1.1 copy-start.8
  150.3 174.5 %reduce-scatter.9.cloned.1.call-start = ((), (), s32[]{:S(2)}) async-start(), calls=%async_computation.9 | async-start | bytes 2621440 | tf_op jit(solution)/shard_map/reduce_scatter | solution.py:744
  150.3 1.9 copy-start.2
  152.2 6.8 copy-start.29
  157.6 1.3 copy-start.9
  282.5 90.4 %all-gather.11.cloned.1.call-start = ((), (), s32[]{:S(2)}) async-start(), calls=%async_computation.10 | async-start | bytes 2621440 | tf_op jit(solution)/shard_map/all_gather | solution.py:741
  324.8 1.0 copy-start.6
  327.6 105.4 %reduce-scatter.11.cloned.1.call-start = ((), (), s32[]{:S(2)}) async-start(), calls=%async_computation.11 | async-start | bytes 2621440 | tf_op jit(solution)/shard_map/reduce_scatter | solution.py:744
  390.1 42.8 %copy-start.7 = (bf16[128,2048]{1,0:T(8,128)(2,1)S(1)}, bf16[128,2048]{1,0:T(8,128)(2,1)}, u32[]{:S(2)}) copy-start(bf16[128,2048]{1,0:T(8,128)(2,1)} %reduce-scatter.9.cloned.1.call-done.value_ref.refs_1_) | copy-start | bytes 1572868
  390.2 95.0 %all-gather.13.cloned.1.call-start = ((), (), s32[]{:S(2)}) async-start(), calls=%async_computation.12 | async-start | bytes 2621440 | tf_op jit(solution)/shard_map/all_gather | solution.py:741
  432.9 3.9 copy-start.15
  434.3 4.0 copy-start.17
  439.7 104.7 %reduce-scatter.13.cloned.1.call-start = ((), (), s32[]{:S(2)}) async-start(), calls=%async_computation.13 | async-start | bytes 2621440 | tf_op jit(solution)/shard_map/reduce_scatter | solution.py:744
  501.7 91.5 %all-gather.15.cloned.1.call-start = ((), (), s32[]{:S(2)}) async-start(), calls=%async_computation.14 | async-start | bytes 2621440 | tf_op jit(solution)/shard_map/all_gather | solution.py:741
  544.4 1.0 copy-start.13
  547.7 173.2 %reduce-scatter.15.cloned.1.call-start = ((), (), s32[]{:S(2)}) async-start(), calls=%async_computation.16 | async-start | bytes 19464192 | tf_op jit(solution)/shard_map/reduce_scatter | solution.py:798
  548.3 296.7 %all-gather.17.cloned.1.call-start = ((), (), s32[]{:S(2)}) async-start(), calls=%async_computation.15 | async-start | bytes 7864320 | tf_op jit(solution)/shard_map/all_gather | solution.py:741
  613.9 26.7 %copy-start.19 = (bf16[512,2048]{1,0:T(8,128)(2,1)S(1)}, bf16[512,2048]{1,0:T(8,128)(2,1)}, u32[]{:S(2)}) copy-start(bf16[512,2048]{1,0:T(8,128)(2,1)} %get-tuple-element.71) | copy-start | bytes 6291460
  613.9 5.6 collective-permute-start.3
  614.7 14.6 %collective-permute-start = (bf16[128,2048]{1,0:T(8,128)(2,1)}, bf16[128,2048]{1,0:T(8,128)(2,1)S(1)}, u32[]{:S(2)}, u32[]{:S(2)}) collective-permute-start(bf16[128,2048]{1,0:T(8,128)(2,1)} %get-tuple-element.69), channel_id=1, source_target_pairs={{0,1},{4,5},{8,9},{12,13},{16,17},{20,21},{24,25},{28,29}} | collective-permute-start | bytes 1572872 | tf_op jit(solution)/shard_map/ppermute | solution.py:85
  616.8 14.8 %collective-permute-start.9 = (bf16[128,2048]{1,0:T(8,128)(2,1)}, bf16[128,2048]{1,0:T(8,128)(2,1)S(1)}, u32[]{:S(2)}, u32[]{:S(2)}) collective-permute-start(bf16[128,2048]{1,0:T(8,128)(2,1)} %get-tuple-element.72), channel_id=1, source_target_pairs={{3,2},{7,6},{11,10},{15,14},{19,18},{23,22},{27,26},{31,30}} | collective-permute-start | bytes 1572872 | tf_op jit(solution)/shard_map/ppermute | solution.py:86
  617.5 23.2 %collective-permute-start.6 = (bf16[128,2048]{1,0:T(8,128)(2,1)}, bf16[128,2048]{1,0:T(8,128)(2,1)S(1)}, u32[]{:S(2)}, u32[]{:S(2)}) collective-permute-start(bf16[128,2048]{1,0:T(8,128)(2,1)} %get-tuple-element.73), channel_id=1, source_target_pairs={{0,1},{4,5},{8,9},{12,13},{16,17},{20,21},{24,25},{28,29}} | collective-permute-start | bytes 1572872 | tf_op jit(solution)/shard_map/ppermute | solution.py:85
  618.8 22.8 %collective-permute-start.15 = (bf16[128,2048]{1,0:T(8,128)(2,1)}, bf16[128,2048]{1,0:T(8,128)(2,1)S(1)}, u32[]{:S(2)}, u32[]{:S(2)}) collective-permute-start(bf16[128,2048]{1,0:T(8,128)(2,1)} %get-tuple-element.76), channel_id=1, source_target_pairs={{3,2},{7,6},{11,10},{15,14},{19,18},{23,22},{27,26},{31,30}} | collective-permute-start | bytes 1572872 | tf_op jit(solution)/shard_map/ppermute | solution.py:86
  619.5 32.4 %collective-permute-start.12 = (bf16[128,2048]{1,0:T(8,128)(2,1)}, bf16[128,2048]{1,0:T(8,128)(2,1)S(1)}, u32[]{:S(2)}, u32[]{:S(2)}) collective-permute-start(bf16[128,2048]{1,0:T(8,128)(2,1)} %get-tuple-element.77), channel_id=1, source_target_pairs={{0,1},{4,5},{8,9},{12,13},{16,17},{20,21},{24,25},{28,29}} | collective-permute-start | bytes 1572872 | tf_op jit(solution)/shard_map/ppermute | solution.py:85
  630.7 21.1 %copy-start.18 = (bf16[512,2048]{1,0:T(8,128)(2,1)S(1)}, bf16[512,2048]{1,0:T(8,128)(2,1)}, u32[]{:S(2)}) copy-start(bf16[512,2048]{1,0:T(8,128)(2,1)} %get-tuple-element.75) | copy-start | bytes 6291460
  630.8 22.1 %collective-permute-start.4 = (bf16[128,2048]{1,0:T(8,128)(2,1)S(1)}, bf16[128,2048]{1,0:T(8,128)(2,1)S(1)}, u32[]{:S(2)}, u32[]{:S(2)}) collective-permute-start(bf16[128,2048]{1,0:T(8,128)(2,1)S(1)} %get-tuple-element.136), channel_id=1, source_target_pairs={{2,1},{3,2},{6,5},{7,6},{10,9},{11,10},{14,13},{15,14},{18,17},{19... | collective-permute-start | bytes 1572872 | tf_op jit(solution)/shard_map/ppermute | solution.py:86
  631.6 31.4 %collective-permute-start.1 = (bf16[128,2048]{1,0:T(8,128)(2,1)S(1)}, bf16[128,2048]{1,0:T(8,128)(2,1)S(1)}, u32[]{:S(2)}, u32[]{:S(2)}) collective-permute-start(bf16[128,2048]{1,0:T(8,128)(2,1)S(1)} %get-tuple-element.137), channel_id=1, source_target_pairs={{0,1},{1,2},{4,5},{5,6},{8,9},{9,10},{12,13},{13,14},{16,17},{17,1... | collective-permute-start | bytes 1572872 | tf_op jit(solution)/shard_map/ppermute | solution.py:85
  640.8 20.1 %copy-start.25 = (bf16[128,2048]{1,0:T(8,128)(2,1)S(1)}, bf16[128,2048]{1,0:T(8,128)(2,1)}, u32[]{:S(2)}) copy-start(bf16[128,2048]{1,0:T(8,128)(2,1)} %get-tuple-element.69) | copy-start | bytes 1572868
  640.8 23.7 %collective-permute-start.10 = (bf16[128,2048]{1,0:T(8,128)(2,1)S(1)}, bf16[128,2048]{1,0:T(8,128)(2,1)S(1)}, u32[]{:S(2)}, u32[]{:S(2)}) collective-permute-start(bf16[128,2048]{1,0:T(8,128)(2,1)S(1)} %get-tuple-element.139), channel_id=1, source_target_pairs={{2,1},{3,2},{6,5},{7,6},{10,9},{11,10},{14,13},{15,14},{18,17},{19... | collective-permute-start | bytes 1572872 | tf_op jit(solution)/shard_map/ppermute | solution.py:86
  641.6 32.6 %collective-permute-start.7 = (bf16[128,2048]{1,0:T(8,128)(2,1)S(1)}, bf16[128,2048]{1,0:T(8,128)(2,1)S(1)}, u32[]{:S(2)}, u32[]{:S(2)}) collective-permute-start(bf16[128,2048]{1,0:T(8,128)(2,1)S(1)} %get-tuple-element.140), channel_id=1, source_target_pairs={{0,1},{1,2},{4,5},{5,6},{8,9},{9,10},{12,13},{13,14},{16,17},{17,1... | collective-permute-start | bytes 1572872 | tf_op jit(solution)/shard_map/ppermute | solution.py:85
  651.9 12.4 %copy-start.24 = (bf16[128,2048]{1,0:T(8,128)(2,1)S(1)}, bf16[128,2048]{1,0:T(8,128)(2,1)}, u32[]{:S(2)}) copy-start(bf16[128,2048]{1,0:T(8,128)(2,1)} %get-tuple-element.68) | copy-start | bytes 1572868
  652.0 20.9 %copy-start.23 = (bf16[128,2048]{1,0:T(8,128)(2,1)S(1)}, bf16[128,2048]{1,0:T(8,128)(2,1)}, u32[]{:S(2)}) copy-start(bf16[128,2048]{1,0:T(8,128)(2,1)} %get-tuple-element.73) | copy-start | bytes 1572868
  652.1 23.6 %collective-permute-start.16 = (bf16[128,2048]{1,0:T(8,128)(2,1)S(1)}, bf16[128,2048]{1,0:T(8,128)(2,1)S(1)}, u32[]{:S(2)}, u32[]{:S(2)}) collective-permute-start(bf16[128,2048]{1,0:T(8,128)(2,1)S(1)} %get-tuple-element.142), channel_id=1, source_target_pairs={{2,1},{3,2},{6,5},{7,6},{10,9},{11,10},{14,13},{15,14},{18,17},{19... | collective-permute-start | bytes 1572872 | tf_op jit(solution)/shard_map/ppermute | solution.py:86
  652.9 22.6 %copy-start.22 = (bf16[128,2048]{1,0:T(8,128)(2,1)S(1)}, bf16[128,2048]{1,0:T(8,128)(2,1)}, u32[]{:S(2)}) copy-start(bf16[128,2048]{1,0:T(8,128)(2,1)} %get-tuple-element.72) | copy-start | bytes 1572868
  652.9 32.5 %collective-permute-start.13 = (bf16[128,2048]{1,0:T(8,128)(2,1)S(1)}, bf16[128,2048]{1,0:T(8,128)(2,1)S(1)}, u32[]{:S(2)}, u32[]{:S(2)}) collective-permute-start(bf16[128,2048]{1,0:T(8,128)(2,1)S(1)} %get-tuple-element.143), channel_id=1, source_target_pairs={{0,1},{1,2},{4,5},{5,6},{8,9},{9,10},{12,13},{13,14},{16,17},{17,1... | collective-permute-start | bytes 1572872 | tf_op jit(solution)/shard_map/ppermute | solution.py:85
  661.0 22.9 %copy-start.21 = (bf16[128,2048]{1,0:T(8,128)(2,1)S(1)}, bf16[128,2048]{1,0:T(8,128)(2,1)}, u32[]{:S(2)}) copy-start(bf16[128,2048]{1,0:T(8,128)(2,1)} %get-tuple-element.77) | copy-start | bytes 1572868
  663.0 23.9 %collective-permute-start.5 = (bf16[128,2048]{1,0:T(8,128)(2,1)S(1)}, bf16[128,2048]{1,0:T(8,128)(2,1)S(1)}, u32[]{:S(2)}, u32[]{:S(2)}) collective-permute-start(bf16[128,2048]{1,0:T(8,128)(2,1)S(1)} %add.119), channel_id=1, source_target_pairs={{1,0},{2,1},{3,2},{5,4},{6,5},{7,6},{9,8},{10,9},{11,10},{13,12},{... | collective-permute-start | bytes 1572872 | tf_op jit(solution)/shard_map/ppermute | solution.py:86
  664.4 22.3 %copy-start.20 = (bf16[128,2048]{1,0:T(8,128)(2,1)S(1)}, bf16[128,2048]{1,0:T(8,128)(2,1)}, u32[]{:S(2)}) copy-start(bf16[128,2048]{1,0:T(8,128)(2,1)} %get-tuple-element.76) | copy-start | bytes 1572868
  664.4 32.3 %collective-permute-start.2 = (bf16[128,2048]{1,0:T(8,128)(2,1)S(1)}, bf16[128,2048]{1,0:T(8,128)(2,1)S(1)}, u32[]{:S(2)}, u32[]{:S(2)}) collective-permute-start(bf16[128,2048]{1,0:T(8,128)(2,1)S(1)} %add.117), channel_id=1, source_target_pairs={{0,1},{1,2},{2,3},{4,5},{5,6},{6,7},{8,9},{9,10},{10,11},{12,13},{... | collective-permute-start | bytes 1572872 | tf_op jit(solution)/shard_map/ppermute | solution.py:85
  673.1 23.6 %copy-start.4 = (bf16[128,6144]{1,0:T(8,128)(2,1)S(1)}, bf16[128,6144]{1,0:T(8,128)(2,1)}, u32[]{:S(2)}) copy-start(bf16[128,6144]{1,0:T(8,128)(2,1)} %reduce-scatter.7.cloned.1.call-done.value_ref.refs_1_) | copy-start | bytes 4718596
  674.2 24.0 %collective-permute-start.11 = (bf16[128,2048]{1,0:T(8,128)(2,1)S(1)}, bf16[128,2048]{1,0:T(8,128)(2,1)S(1)}, u32[]{:S(2)}, u32[]{:S(2)}) collective-permute-start(bf16[128,2048]{1,0:T(8,128)(2,1)S(1)} %add.123), channel_id=1, source_target_pairs={{1,0},{2,1},{3,2},{5,4},{6,5},{7,6},{9,8},{10,9},{11,10},{13,12},{... | collective-permute-start | bytes 1572872 | tf_op jit(solution)/shard_map/ppermute | solution.py:86
  675.7 32.3 %collective-permute-start.8 = (bf16[128,2048]{1,0:T(8,128)(2,1)S(1)}, bf16[128,2048]{1,0:T(8,128)(2,1)S(1)}, u32[]{:S(2)}, u32[]{:S(2)}) collective-permute-start(bf16[128,2048]{1,0:T(8,128)(2,1)S(1)} %add.121), channel_id=1, source_target_pairs={{0,1},{1,2},{2,3},{4,5},{5,6},{6,7},{8,9},{9,10},{10,11},{12,13},{... | collective-permute-start | bytes 1572872 | tf_op jit(solution)/shard_map/ppermute | solution.py:85
  685.5 24.0 %collective-permute-start.17 = (bf16[128,2048]{1,0:T(8,128)(2,1)S(1)}, bf16[128,2048]{1,0:T(8,128)(2,1)S(1)}, u32[]{:S(2)}, u32[]{:S(2)}) collective-permute-start(bf16[128,2048]{1,0:T(8,128)(2,1)S(1)} %add.127), channel_id=1, source_target_pairs={{1,0},{2,1},{3,2},{5,4},{6,5},{7,6},{9,8},{10,9},{11,10},{13,12},{... | collective-permute-start | bytes 1572872 | tf_op jit(solution)/shard_map/ppermute | solution.py:86
  686.9 30.8 %collective-permute-start.14 = (bf16[128,2048]{1,0:T(8,128)(2,1)S(1)}, bf16[128,2048]{1,0:T(8,128)(2,1)S(1)}, u32[]{:S(2)}, u32[]{:S(2)}) collective-permute-start(bf16[128,2048]{1,0:T(8,128)(2,1)S(1)} %add.125), channel_id=1, source_target_pairs={{0,1},{1,2},{2,3},{4,5},{5,6},{6,7},{8,9},{9,10},{10,11},{12,13},{... | collective-permute-start | bytes 1572872 | tf_op jit(solution)/shard_map/ppermute | solution.py:85
  698.2 21.1 %copy-start.10 = (bf16[128,2048]{1,0:T(8,128)(2,1)}, bf16[128,2048]{1,0:T(8,128)(2,1)S(1)}, u32[]{:S(2)}) copy-start(bf16[128,2048]{1,0:T(8,128)(2,1)S(1)} %get-tuple-element.70.refs_0_) | copy-start | bytes 1572868
  709.4 11.1 %copy-start.11 = (bf16[128,2048]{1,0:T(8,128)(2,1)}, bf16[128,2048]{1,0:T(8,128)(2,1)S(1)}, u32[]{:S(2)}) copy-start(bf16[128,2048]{1,0:T(8,128)(2,1)S(1)} %get-tuple-element.74.refs_1_) | copy-start | bytes 1572868
  719.2 1.3 copy-start.12
  720.6 139.2 %reduce-scatter.17.cloned.1.call-start = ((), (), s32[]{:S(2)}) async-start(), calls=%async_computation.17 | async-start | bytes 9437184 | tf_op jit(solution)/shard_map/reduce_scatter | solution.py:821
  733.5 11.8 %collective-permute-start.20 = (f32[8,2048]{1,0:T(8,128)S(1)}, f32[8,2048]{1,0:T(8,128)S(1)}, u32[]{:S(2)}, u32[]{:S(2)}) collective-permute-start(f32[8,2048]{1,0:T(8,128)S(1)} %concatenate.15), channel_id=1, source_target_pairs={{0,1},{1,0},{2,3},{3,2},{4,5},{5,4},{6,7},{7,6},{8,9},{9,8},{10,11... | collective-permute-start | bytes 196616 | tf_op jit(solution)/shard_map/ppermute | solution.py:51
  745.3 7.2 collective-permute-start.21
  752.5 5.2 collective-permute-start.22
  757.6 18.1 %collective-permute-start.18 = (f32[72,256]{0,1:T(8,128)S(1)}, f32[72,256]{0,1:T(8,128)S(1)}, u32[]{:S(2)}, u32[]{:S(2)}) collective-permute-start(f32[72,256]{0,1:T(8,128)S(1)} %copy.50), channel_id=1, source_target_pairs={{0,1},{1,0},{2,3},{3,2},{4,5},{5,4},{6,7},{7,6},{8,9},{9,8},{10,11... | collective-permute-start | bytes 221192 | tf_op jit(solution)/shard_map/ppermute | solution.py:51
  757.7 6.0 collective-permute-start.23
  763.7 13.0 %collective-permute-start.24 = (f32[8,2048]{1,0:T(8,128)S(1)}, f32[8,2048]{1,0:T(8,128)S(1)}, u32[]{:S(2)}, u32[]{:S(2)}) collective-permute-start(f32[8,2048]{1,0:T(8,128)S(1)} %add.133), channel_id=1, source_target_pairs={{0,16},{4,20},{8,24},{12,28},{16,0},{20,4},{24,8},{28,12},{1,17},{... | collective-permute-start | bytes 196616 | tf_op jit(solution)/shard_map/ppermute | solution.py:51
  775.7 16.3 %collective-permute-start.19 = (f32[72,256]{0,1:T(8,128)S(1)}, f32[72,256]{0,1:T(8,128)S(1)}, u32[]{:S(2)}, u32[]{:S(2)}) collective-permute-start(f32[72,256]{0,1:T(8,128)S(1)} %add.128), channel_id=1, source_target_pairs={{0,2},{1,3},{2,0},{3,1},{4,6},{5,7},{6,4},{7,5},{8,10},{9,11},{10,... | collective-permute-start | bytes 221192 | tf_op jit(solution)/shard_map/ppermute | solution.py:51
  776.7 68.3 %copy-start.14 = (f32[8,2048]{1,0:T(8,128)}, f32[8,2048]{1,0:T(8,128)S(1)}, u32[]{:S(2)}) copy-start(f32[8,2048]{1,0:T(8,128)S(1)} %add.134.refs_8_) | copy-start | bytes 196612
  808.5 36.5 %copy-start.5 = (bf16[512,2048]{1,0:T(8,128)(2,1)S(1)}, bf16[512,2048]{1,0:T(8,128)(2,1)}, u32[]{:S(2)}) copy-start(bf16[512,2048]{1,0:T(8,128)(2,1)} %all-gather.15.cloned.1.call-done.hidden_ref.refs_5_) | copy-start | bytes 6291460
  808.6 1.0 copy-start.16
  845.0 17.4 %copy-start.1 = (f32[2048,68]{0,1:T(8,128)S(1)}, f32[2048,68]{0,1:T(8,128)}, u32[]{:S(2)}) copy-start(f32[2048,68]{0,1:T(8,128)} %param.24) | copy-start | bytes 1671172
  (3 other events, 2.4 us)
Sparse Core Ops, SparseCore 0:
  18.1 113.4 reduce-scatter.6
  150.4 115.3 all-gather.8
  282.7 42.1 reduce-scatter.8
  327.7 45.2 all-gather.10
  390.3 42.6 reduce-scatter.10
  439.9 45.2 all-gather.12
  501.8 42.5 reduce-scatter.12
  547.9 45.2 all-gather.14
  720.7 124.2 all-gather.16
Sparse Core Ops, SparseCore 1:
  22.4 127.8 all-gather.6
  552.3 117.7 reduce-scatter.14
  733.0 77.2 reduce-scatter.16
